TPU v7x, 32 devices: a whole 2x2x4 slice. The times are simulated.
32 devices in a mesh: dp: 4 (over z), head: 8 (over y, x, core).
Axes of the slice: x: 2, y: 2, z: 4, core: 2. Of those that a mesh axis runs over, the one named last changes fastest.
Arguments:
- tokens: bfloat16 [2048, 4096], P('head', 'dp'), may hold values from -6 to 6
- lengths: int32 [32], P('dp'), may hold values from 0 to 1024, as said below
- attn_gain: bfloat16 [2048], P('head'), may hold values from 0.5 to 1.5
- w_query: bfloat16 [2048, 2048], P('head'), may hold values from -0.125 to 0.125
- w_key: bfloat16 [2048, 2048], P('head'), may hold values from -0.125 to 0.125
- w_value: bfloat16 [2048, 2048], P('head'), may hold values from -0.125 to 0.125
- w_gate: bfloat16 [2048, 2048], P('head'), may hold values from -0.125 to 0.125
- w_rate: bfloat16 [2048, 32], P(None, 'head'), may hold values from -0.0625 to 0.0625
- rate_bias: bfloat16 [32], P('head'), may hold values from -3.4 to 0.9
- inner_weight: bfloat16 [32, 64, 64], P('head'), may hold values from -0.75 to 0.75
- inner_bias: bfloat16 [32, 64], P('head'), may hold values from -3 to 3
- inner_gain: bfloat16 [32, 64], P('head'), may hold values from 0.5 to 1.5
- inner_shift: bfloat16 [32, 64], P('head'), may hold values from -2 to 2
- post_gain: bfloat16 [2048], P('head'), may hold values from 0.5 to 1.5
- post_shift: bfloat16 [2048], P('head'), may hold values from -2 to 2
- w_out: bfloat16 [2048, 2048], P('head'), may hold values from -0.1875 to 0.1875
- ffn_gain: bfloat16 [2048], P('head'), may hold values from 0.5 to 1.5
- w_hidden_gate: bfloat16 [5504, 2048], P('head'), may hold values from -0.125 to 0.125
- w_hidden_up: bfloat16 [5504, 2048], P('head'), may hold values from -0.125 to 0.125
- w_down: bfloat16 [5504, 2048], P('head'), may hold values from -0.15625 to 0.15625
- out_grad: bfloat16 [2048, 4096], P('head', 'dp'), may hold values from -6 to 6
Outputs:
- result: bfloat16 [2048, 4096], P('head', 'dp')
- grad_tokens: float32 [2048, 4096], P('head', 'dp')
- grad_attn_gain: float32 [2048], P('head')
- grad_w_query: float32 [2048, 2048], P('head')
- grad_w_key: float32 [2048, 2048], P('head')
- grad_w_value: float32 [2048, 2048], P('head')
- grad_w_gate: float32 [2048, 2048], P('head')
- grad_w_rate: float32 [2048, 32], P(None, 'head')
- grad_rate_bias: float32 [32], P('head')
- grad_inner_weight: float32 [32, 64, 64], P('head')
- grad_inner_bias: float32 [32, 64], P('head')
- grad_inner_gain: float32 [32, 64], P('head')
- grad_inner_shift: float32 [32, 64], P('head')
- grad_post_gain: float32 [2048], P('head')
- grad_post_shift: float32 [2048], P('head')
- grad_w_out: float32 [2048, 2048], P('head')
- grad_ffn_gain: float32 [2048], P('head')
- grad_w_hidden_gate: float32 [5504, 2048], P('head')
- grad_w_hidden_up: float32 [5504, 2048], P('head')
- grad_w_down: float32 [5504, 2048], P('head')
- mean_rate: float32 [], replicated
- max_rate: float32 [], replicated
Inputs may be any that keep to these rules, and one draw needn't show every extreme that they name: For each index of dp, its 8 lengths rounded up to multiples of 16 sum to at most 1024; in every draw some index of dp holds one sequence of exactly 1024 tokens and zeros.
All inputs are finite; a program needn't handle non-finite values.
Results may differ from a plain program's by a relative error of at most 0.018.
Values may be sent and summed in bfloat16 or wider, within the bound.
No kernel may reach another device: no remote copies, remote signals or barrier semaphores. Data moves between devices by JAX's collectives and lax.ppermute only.
A program may use at most 192 MiB of HBM per device.

v0:
```python
import jax
import jax.numpy as jnp
from jax import lax
from jax.sharding import PartitionSpec as P

HEADS = 32
HD = 64
MB = 16


EPS = 1e-06
BASE_RATE = 1.0


def rms_scale(values):
    return lax.rsqrt(jnp.mean(values * values, -1, keepdims=True) + EPS)


def layer_norm(values, norm_gain, norm_shift):
    center = values - jnp.mean(values, -1, keepdims=True)
    return (
        center * lax.rsqrt(jnp.mean(center * center, -1, keepdims=True) + EPS) * norm_gain
        + norm_shift
    )


def inner_grad(values, target, norm_gain, norm_shift):
    center = values - jnp.mean(values, -1, keepdims=True)
    inv_std = lax.rsqrt(jnp.mean(center * center, -1, keepdims=True) + EPS)
    normed = center * inv_std
    upward = (normed * norm_gain + norm_shift - target) * norm_gain
    return inv_std * (
        upward
        - jnp.mean(upward, -1, keepdims=True)
        - normed * jnp.mean(upward * normed, -1, keepdims=True)
    )


def post_mix(mixer_out, gate_in, norm_gain, norm_shift):
    return layer_norm(mixer_out, norm_gain, norm_shift) * jax.nn.gelu(gate_in, approximate=True)


def gelu_tanh(values):
    return jax.nn.gelu(values, approximate=True)


def head_block(
    weight,
    offset_vec,
    query_rows,
    key_rows,
    value_rows,
    step_rates,
    valid_rows,
    norm_gain,
    norm_shift,
):
    highest = lax.Precision.HIGHEST
    positions = 1.0 / (jnp.arange(MB).astype(jnp.float32) + 1.0)
    lower = jnp.tril(jnp.ones((MB, MB), jnp.float32))
    weights = lower * positions[:, None] * step_rates[None, :]
    grad_z = inner_grad(
        jnp.dot(key_rows, weight, precision=highest) + offset_vec,
        value_rows - key_rows,
        norm_gain,
        norm_shift,
    )
    scores = jnp.dot(query_rows, key_rows.T, precision=highest)
    zbar = (
        jnp.dot(query_rows, weight, precision=highest)
        - jnp.dot(weights * scores, grad_z, precision=highest)
        + offset_vec
        - jnp.dot(weights, grad_z, precision=highest)
    )
    output = (query_rows + layer_norm(zbar, norm_gain, norm_shift)) * valid_rows[:, None]
    last_rates = step_rates / MB
    new_weight = weight - jnp.dot((last_rates[:, None] * key_rows).T, grad_z, precision=highest)
    new_offset = offset_vec - jnp.dot(last_rates, grad_z, precision=highest)
    return (new_weight, new_offset, output)


def ttt_scan(
    queries,
    key_rows,
    value_rows,
    logits,
    valid_rows,
    reset_rows,
    init_weight,
    init_bias,
    norm_gain,
    norm_shift,
):
    row_count, head_count = logits.shape
    block_count = row_count // MB

    def blocks(array):
        return array.reshape(block_count, MB, head_count, HD).transpose(0, 2, 1, 3)

    step_rates = BASE_RATE / HD * jax.nn.sigmoid(logits) * valid_rows[:, None]
    rate_blocks = step_rates.reshape(block_count, MB, head_count).transpose(0, 2, 1)
    valid_blocks = valid_rows.reshape(block_count, MB)

    def advance(carry, pieces):
        weight, offset_vec = carry
        query_blk, key_blk, value_blk, rate_blk, valid_blk, reset_now = pieces
        weight = reset_now * init_weight + (1.0 - reset_now) * weight
        offset_vec = reset_now * init_bias + (1.0 - reset_now) * offset_vec
        new_weight, new_offset, output = jax.vmap(
            head_block, in_axes=(0, 0, 0, 0, 0, 0, None, 0, 0)
        )(
            weight,
            offset_vec,
            query_blk,
            key_blk,
            value_blk,
            rate_blk,
            valid_blk,
            norm_gain,
            norm_shift,
        )
        return ((new_weight, new_offset), output)

    carry_out, outputs = lax.scan(
        jax.checkpoint(advance),
        (init_weight, init_bias),
        (
            blocks(queries),
            blocks(key_rows),
            blocks(value_rows),
            rate_blocks,
            valid_blocks,
            reset_rows,
        ),
    )
    return outputs.transpose(0, 2, 1, 3).reshape(row_count, head_count * HD)


def layout(seq_lens, row_count):
    padded = (seq_lens + MB - 1) // MB * MB
    starts = jnp.cumsum(padded, axis=1) - padded
    positions = jnp.arange(row_count, dtype=jnp.int32)
    inside = (positions[None, None, :] >= starts[:, :, None]) & (
        positions[None, None, :] < (starts + seq_lens)[:, :, None]
    )
    valid_rows = jnp.any(inside, axis=1).astype(jnp.float32)
    block_first = jnp.arange(row_count // MB, dtype=jnp.int32) * MB
    begins = jnp.any(
        (starts[:, :, None] == block_first[None, None, :]) & (seq_lens[:, :, None] > 0), axis=1
    )
    begins = begins | (block_first[None, :] == 0)
    return (valid_rows, begins.astype(jnp.float32))


def matmul(left, right):
    return jnp.dot(left, right, preferred_element_type=jnp.float32)


def lead_product(left, right):
    return lax.dot_general(
        left, right, (((0,), (0,)), ((), ())), preferred_element_type=jnp.float32
    )


def tail_product(left, right):
    return lax.dot_general(
        left, right, (((1,), (1,)), ((), ())), preferred_element_type=jnp.float32
    )


def cross_product(left, right):
    return lax.dot_general(
        left, right, (((0,), (1,)), ((), ())), preferred_element_type=jnp.float32
    )


def columns(array, start, width_here, axis_here):
    return lax.dynamic_slice_in_dim(array, start, width_here, axis_here)


def on_device(
    tokens,
    lengths,
    attn_gain,
    w_query,
    w_key,
    w_value,
    w_gate,
    w_rate,
    rate_bias,
    inner_weight,
    inner_bias,
    inner_gain,
    inner_shift,
    post_gain,
    post_shift,
    w_out,
    ffn_gain,
    w_hidden_gate,
    w_hidden_up,
    w_down,
    out_grad,
):
    tok_rows = tokens.shape[1]
    own_cols = tokens.shape[0]
    col_start = lax.axis_index("head") * own_cols
    masks, resets = layout(lengths.reshape(1, -1), tok_rows)
    valid_rows = masks[0]
    reset_rows = resets[0]
    full_tokens, full_attn_gain = (
        lax.all_gather(tokens, "head", axis=0, tiled=True),
        lax.all_gather(attn_gain, "head", axis=0, tiled=True),
    )
    inputs_full = full_tokens.astype(jnp.float32).T
    full_width = inputs_full.shape[1]
    scale_in = rms_scale(inputs_full)
    gain_in = full_attn_gain.astype(jnp.float32)
    normed_in = (inputs_full * scale_in * gain_in).astype(jnp.bfloat16)
    queries = tail_product(normed_in, w_query)
    key_rows = tail_product(normed_in, w_key)
    value_rows = tail_product(normed_in, w_value)
    gate_pre = tail_product(normed_in, w_gate).astype(jnp.bfloat16)
    logits = matmul(normed_in, w_rate) + rate_bias.astype(jnp.float32)

    def mixer(queries_in, keys_in, values_in, logits_in, w_init, b_init, n_gain, n_shift):
        return ttt_scan(
            queries_in,
            keys_in,
            values_in,
            logits_in,
            valid_rows,
            reset_rows,
            w_init,
            b_init,
            n_gain,
            n_shift,
        )

    mixer_out, mixer_pull = jax.vjp(
        mixer,
        queries,
        key_rows,
        value_rows,
        logits,
        inner_weight.astype(jnp.float32),
        inner_bias.astype(jnp.float32),
        inner_gain.astype(jnp.float32),
        inner_shift.astype(jnp.float32),
    )
    masked_rates = jax.nn.sigmoid(logits) * valid_rows[:, None]
    rate_part = jnp.sum(masked_rates)
    max_rate = lax.pmax(jnp.max(masked_rates), ("dp", "head"))
    mixer_cols, gate_cols, full_post_gain, full_post_shift = (
        lax.all_gather(mixer_out.astype(jnp.bfloat16).T, "head", axis=0, tiled=True),
        lax.all_gather(gate_pre.T, "head", axis=0, tiled=True),
        lax.all_gather(post_gain, "head", axis=0, tiled=True),
        lax.all_gather(post_shift, "head", axis=0, tiled=True),
    )
    mixer_full = mixer_cols.T.astype(jnp.float32)
    mixed_gate, post_pull = jax.vjp(
        post_mix,
        mixer_full,
        gate_cols.T.astype(jnp.float32),
        full_post_gain.astype(jnp.float32),
        full_post_shift.astype(jnp.float32),
    )
    mixed_low = mixed_gate.astype(jnp.bfloat16)
    tokens_rows = tokens.astype(jnp.float32).T
    hidden = tokens_rows + tail_product(mixed_low, w_out)
    hidden_cols, full_ffn_gain = (
        lax.all_gather(hidden.astype(jnp.bfloat16).T, "head", axis=0, tiled=True),
        lax.all_gather(ffn_gain, "head", axis=0, tiled=True),
    )
    hidden_full = hidden_cols.astype(jnp.float32).T
    scale_mid = rms_scale(hidden_full)
    gain_mid = full_ffn_gain.astype(jnp.float32)
    normed_mid = (hidden_full * scale_mid * gain_mid).astype(jnp.bfloat16)
    gate_val = tail_product(normed_mid, w_hidden_gate)
    up_val = tail_product(normed_mid, w_hidden_up)
    sig_gate = jax.nn.sigmoid(gate_val)
    inner_act = (gate_val * sig_gate * up_val).astype(jnp.bfloat16)
    ffn_term = lax.psum_scatter(
        cross_product(
            columns(w_down, jnp.int32(0), own_cols * lax.axis_size("head"), 1), inner_act
        ).astype(jnp.bfloat16),
        "head",
        scatter_dimension=0,
        tiled=True,
    ).astype(jnp.float32)
    result = (hidden.T + ffn_term).astype(jnp.bfloat16)
    full_grad = lax.all_gather(out_grad, "head", axis=0, tiled=True)
    grad_down = cross_product(inner_act, full_grad)
    grad_act = cross_product(full_grad, w_down)
    grad_up = (grad_act * gate_val * sig_gate).astype(jnp.bfloat16)
    grad_gate = (grad_act * up_val * sig_gate * (1.0 + gate_val * (1.0 - sig_gate))).astype(
        jnp.bfloat16
    )
    grad_hgate = lead_product(grad_gate, normed_mid)
    grad_hup = lead_product(grad_up, normed_mid)
    start = jnp.int32(0)
    grad_normed_own = lax.psum_scatter(
        cross_product(columns(w_hidden_gate, start, own_cols * lax.axis_size("head"), 1), grad_gate)
        + cross_product(columns(w_hidden_up, start, own_cols * lax.axis_size("head"), 1), grad_up),
        "head",
        scatter_dimension=0,
        tiled=True,
    ).T
    hidden_own = columns(hidden_full, col_start, own_cols, 1)
    gain_mid_own = ffn_gain.astype(jnp.float32)
    own_mid = jnp.sum(hidden_own * gain_mid_own * grad_normed_own, -1)
    mid_sum, rate_head = lax.psum((own_mid, rate_part), "head")
    mid_dot = mid_sum[:, None]
    grad_ffn_gain = jnp.sum(grad_normed_own * hidden_own * scale_mid, 0)
    grad_hidden = (
        out_grad.astype(jnp.float32).T
        + scale_mid * gain_mid_own * grad_normed_own
        - hidden_own * scale_mid**3 * mid_dot / full_width
    )
    grad_branch = grad_hidden.astype(jnp.bfloat16)
    grad_out_w = lead_product(grad_branch, mixed_low)
    grad_mixed_own = lax.psum_scatter(
        cross_product(
            columns(w_out, jnp.int32(0), own_cols * lax.axis_size("head"), 1), grad_branch
        ),
        "head",
        scatter_dimension=0,
        tiled=True,
    ).T
    center = mixer_full - jnp.mean(mixer_full, -1, keepdims=True)
    inv_std = lax.rsqrt(jnp.mean(center * center, -1, keepdims=True) + EPS)
    normed_own = columns(center * inv_std, col_start, own_cols, 1)
    gain_post_own = post_gain.astype(jnp.float32)
    shift_post_own = post_shift.astype(jnp.float32)
    gelu_own, gelu_pull = jax.vjp(gelu_tanh, gate_pre.astype(jnp.float32))
    grad_post_gain = jnp.sum(grad_mixed_own * gelu_own * normed_own, 0)
    grad_post_shift = jnp.sum(grad_mixed_own * gelu_own, 0)
    grad_gate_pre = gelu_pull(grad_mixed_own * (normed_own * gain_post_own + shift_post_own))[
        0
    ].astype(jnp.bfloat16)
    grad_norm_own = grad_mixed_own * gelu_own * gain_post_own
    sum_plain, sum_normed = lax.psum(
        (jnp.sum(grad_norm_own, -1), jnp.sum(grad_norm_own * normed_own, -1)), "head"
    )
    grad_mixer = inv_std * (
        grad_norm_own
        - sum_plain[:, None] / full_width
        - normed_own * sum_normed[:, None] / full_width
    )
    inner_grads = mixer_pull(grad_mixer)
    grad_queries = inner_grads[0].astype(jnp.bfloat16)
    grad_keys = inner_grads[1].astype(jnp.bfloat16)
    grad_values = inner_grads[2].astype(jnp.bfloat16)
    grad_rate_bias = jnp.sum(inner_grads[3], 0)
    grad_logits = inner_grads[3].astype(jnp.bfloat16)
    grad_w_query = lead_product(grad_queries, normed_in)
    grad_w_key = lead_product(grad_keys, normed_in)
    grad_w_value = lead_product(grad_values, normed_in)
    grad_w_gate = lead_product(grad_gate_pre, normed_in)
    grad_w_rate = lead_product(normed_in, grad_logits)
    pairs = (
        (grad_queries, w_query),
        (grad_keys, w_key),
        (grad_values, w_value),
        (grad_gate_pre, w_gate),
    )
    input_part = tail_product(grad_logits, w_rate)
    for grad_piece, weight_piece in pairs:
        input_part = input_part + matmul(grad_piece, weight_piece)
    grad_input_norm = lax.psum(input_part.astype(jnp.bfloat16), "head").astype(jnp.float32)
    grad_attn_gain = columns(
        jnp.sum(grad_input_norm * inputs_full * scale_in, 0), col_start, own_cols, 0
    )
    in_dot = jnp.sum(inputs_full * gain_in * grad_input_norm, -1, keepdims=True)
    grad_in_full = (
        scale_in * gain_in * grad_input_norm - inputs_full * scale_in**3 * in_dot / full_width
    )
    grad_tokens = (grad_hidden + columns(grad_in_full, col_start, own_cols, 1)).T
    summed = (
        lax.psum(grad_attn_gain.astype(jnp.bfloat16), "dp").astype(jnp.float32),
        lax.psum(grad_w_query.astype(jnp.bfloat16), "dp").astype(jnp.float32),
        lax.psum(grad_w_key.astype(jnp.bfloat16), "dp").astype(jnp.float32),
        lax.psum(grad_w_value.astype(jnp.bfloat16), "dp").astype(jnp.float32),
        lax.psum(grad_w_gate.astype(jnp.bfloat16), "dp").astype(jnp.float32),
        lax.psum(grad_w_rate.astype(jnp.bfloat16), "dp").astype(jnp.float32),
        lax.psum(grad_rate_bias.astype(jnp.bfloat16), "dp").astype(jnp.float32),
        lax.psum(inner_grads[4].astype(jnp.bfloat16), "dp").astype(jnp.float32),
        lax.psum(inner_grads[5].astype(jnp.bfloat16), "dp").astype(jnp.float32),
        lax.psum(inner_grads[6].astype(jnp.bfloat16), "dp").astype(jnp.float32),
        lax.psum(inner_grads[7].astype(jnp.bfloat16), "dp").astype(jnp.float32),
        lax.psum(grad_post_gain.astype(jnp.bfloat16), "dp").astype(jnp.float32),
        lax.psum(grad_post_shift.astype(jnp.bfloat16), "dp").astype(jnp.float32),
        lax.psum(grad_out_w.astype(jnp.bfloat16), "dp").astype(jnp.float32),
        lax.psum(grad_ffn_gain.astype(jnp.bfloat16), "dp").astype(jnp.float32),
        lax.psum(grad_hgate.astype(jnp.bfloat16), "dp").astype(jnp.float32),
        lax.psum(grad_hup.astype(jnp.bfloat16), "dp").astype(jnp.float32),
        lax.psum(grad_down.astype(jnp.bfloat16), "dp").astype(jnp.float32),
        lax.psum(rate_head.astype(jnp.bfloat16), "dp").astype(jnp.float32),
    )
    mean_rate = summed[18] / (tok_rows * lax.axis_size("dp") * HEADS)
    return (
        result,
        grad_tokens,
        summed[0],
        summed[1],
        summed[2],
        summed[3],
        summed[4],
        summed[5],
        summed[6],
        summed[7],
        summed[8],
        summed[9],
        summed[10],
        summed[11],
        summed[12],
        summed[13],
        summed[14],
        summed[15],
        summed[16],
        summed[17],
        mean_rate,
        max_rate,
    )


def solution(mesh):
    placed = (
        P("head", "dp"),
        P("dp"),
        P("head"),
        P("head", None),
        P("head", None),
        P("head", None),
        P("head", None),
        P(None, "head"),
        P("head"),
        P("head", None, None),
        P("head", None),
        P("head", None),
        P("head", None),
        P("head"),
        P("head"),
        P("head", None),
        P("head"),
        P("head", None),
        P("head", None),
        P("head", None),
        P("head", "dp"),
    )
    return jax.shard_map(
        on_device,
        mesh=mesh,
        in_specs=placed,
        out_specs=(
            P("head", "dp"),
            P("head", "dp"),
            P("head"),
            P("head", None),
            P("head", None),
            P("head", None),
            P("head", None),
            P(None, "head"),
            P("head"),
            P("head", None, None),
            P("head", None),
            P("head", None),
            P("head", None),
            P("head"),
            P("head"),
            P("head", None),
            P("head"),
            P("head", None),
            P("head", None),
            P("head", None),
            P(),
            P(),
        ),
        check_vma=False,
    )
```

profile of v0, /device:TPU:0, one launch (start us, length us, event | category | flops | bytes accessed | tf_op | source)
XLA Modules:
  0.0 2860.7 jit_solution(5425787134414442879)
XLA Ops:
  10.2 10.3 all-gather
  26.0 24.7 all-gather.10.cloned.1.call-done
  50.7 3.2 fusion.103
  59.6 4.7 fusion.175
  64.3 3.3 reshape.557
  67.6 3.3 copy.127
  70.9 3.5 fusion.177
  74.4 3.0 reshape.559
  77.4 4.7 fusion.176
  82.2 3.0 reshape.558
  85.2 4.8 copy_bitcast_fusion.1
  91.2 746.5 %while.53 = (s32[]{:T(128)}, f32[4,64,64]{2,1,0:T(8,128)S(1)}, f32[4,64]{1,0:T(4,128)S(1)}, bf16[64,4,16,64]{3,2,1,0:T(8,128)(2,1)}, f32[64,4,64,64]{3,2,1,0:T(8...) while((s32[]{:T(128)}, f32[4,64,64]{2,1,0:T(8,128)S(1)}, ...), condition=%wide.region_11.12_spmd.clone, body=%wide.region_4.11_spmd.clone.sunk | while | flops 12059587 | bytes 1250561 | solution.py:124
  837.8 2.7 copy.105
  840.5 2.7 convert_element_type.321
  843.3 4.6 convolution_convert_fusion.9
  848.0 8.9 all-gather.2
  856.9 8.5 all-gather.1
  865.4 15.5 all-gather.12.cloned.1.call-done
  880.8 3.0 convert_reduce_fusion
  885.5 34.7 %all-gather.14.cloned.1.call-done = bf16[2048,1024]{0,1:T(8,128)(2,1)} async-done(((bf16[256,1024]{0,1:T(8,128)(2,1)}), bf16[2048,1024]{0,1:T(8,128)(2,1)}) %all-gather.14.cloned.1.call-update) | async-done | bytes 4194320 | tf_op jit(solution)/shard_map/all_gather | solution.py:255
  920.2 7.4 fusion.98
  930.8 8.8 all-gather.3
  939.6 28.1 all-gather.16.cloned.1.call-done
  967.7 3.2 multiply_reduce_fusion.18
  971.2 6.7 fusion.155
  977.9 4.7 fusion.154
  982.6 23.6 all-gather.18.cloned.1.call-done
  1006.2 8.4 multiply_convert_fusion.1
  1014.6 3.5 fusion.178
  1018.1 6.0 add_bitcast_fusion
  1026.2 7.1 convert_element_type.331
  1033.2 62.3 %reduce-scatter.6.cloned.1.call-done = f32[256,1024]{0,1:T(8,128)} async-done(((f32[2048,1024]{0,1:T(8,128)}), f32[256,1024]{0,1:T(8,128)}) %reduce-scatter.6.cloned.1.call-update) | async-done | bytes 1048592 | tf_op jit(solution)/shard_map/reduce_scatter | solution.py:301
  1097.5 12.7 psum.168
  1113.4 4.5 convolution_bitcast_fusion
  1118.1 6.7 fusion.87
  1124.8 5.3 convert_bitcast_fusion.1
  1131.7 7.5 convolution_convert_fusion.2
  1139.2 4.6 convolution_convert_fusion.1
  1143.9 45.4 %reduce-scatter.8.cloned.1.call-done = f32[256,1024]{0,1:T(8,128)} async-done(((f32[2048,1024]{0,1:T(8,128)}), f32[256,1024]{0,1:T(8,128)}) %reduce-scatter.8.cloned.1.call-update) | async-done | bytes 1048592 | tf_op jit(solution)/shard_map/reduce_scatter | solution.py:321
  1189.2 3.5 fusion.136
  1192.7 23.5 all-reduce
  1225.3 994.1 %while.54 = (s32[]{:T(128)}, f32[4,64,64]{2,1,0:T(8,128)S(1)}, f32[4,64]{1,0:T(4,128)S(1)}, f32[4,64]{1,0:T(4,128)S(1)}, f32[4,64]{1,0:T(4,128)S(1)}, /*index=5*...) while((s32[]{:T(128)}, f32[4,64,64]{2,1,0:T(8,128)S(1)}, ...), condition=%wide.region_47.48_spmd.clone, body=%wide.region_24.47_spmd.clone.sunk | while | flops 32213620 | bytes 2806072 | solution.py:124
  2219.5 2.7 copy.112
  2224.3 2.7 copy.111
  2230.8 14.2 convert_element_type.349
  2245.2 4.5 fusion.151
  2249.7 4.5 fusion.181
  2254.2 4.5 fusion.180
  2258.7 4.5 fusion.179
  2263.2 13.7 add_convert_fusion
  2277.0 7.4 convolution_convert_fusion
  2296.8 39.8 %pmax.7 = f32[]{:T(128)} all-reduce(f32[]{:T(128)} %get-tuple-element.1020), channel_id=1, replica_groups=mesh['dp'=4,'head'=8] {'dp','head'}, use_global_device_ids=true, to_apply=%region_77.78 | all-reduce | flops 1 | bytes 8 | tf_op jit(solution)/shard_map/pmax | solution.py:252
  2336.6 6.8 convert_bitcast_fusion
  2345.7 2.9 convolution_convert_fusion.8
  2348.6 9.8 all-reduce.6.cloned.1.call-done
  2358.4 5.6 fusion.109
  2364.1 30.0 %all-reduce.1 = (bf16[]{:T(256)}, bf16[256]{0:T(256)(128)(2,1)S(1)}, bf16[2048,4]{0,1:T(4,128)(2,1)S(1)}, bf16[4]{0:T(256)(128)(2,1)S(1)}, bf16[4,64,64]{2,1,0:T...) all-reduce(bf16[]{:T(256)} %get-tuple-element.1104, ...), channel_id=1, replica_groups=mesh['dp'=4,'head'=8] {'dp'}, use_global_device_ids=true, to_apply=%region_75.76 | all-reduce | flops 26373 | bytes 105492 | tf_op jit(solution)/shard_map/psum | solution.py:397
  2394.1 3.3 convert_element_type.359
  2406.9 425.3 %all-reduce.8.cloned.1.call-done = (bf16[256,2048]{1,0:T(8,128)(2,1)}, bf16[256,2048]{1,0:T(8,128)(2,1)}, bf16[256,2048]{1,0:T(8,128)(2,1)}, bf16[256,2048]{1,0:...) async-done(((bf16[256,2048]{1,0:T(8,128)(2,1)}, bf16[256,2048]{1,0:T(8,128)(2,1)}, ...) | async-done | bytes 13697040 | tf_op jit(solution)/shard_map/psum | solution.py:380
  2832.3 2.9 convert_element_type.363
  2835.2 2.9 convert_element_type.365
  2842.8 3.2 convert_element_type.391
  2846.0 3.2 convert_element_type.393
  2849.3 3.2 convert_element_type.395
  (5657 shorter events, 1707.7 us)
Async XLA Ops:
  7.2 999.0 %copy-start = (bf16[688,2048]{1,0:T(8,128)(2,1)S(1)}, bf16[688,2048]{1,0:T(8,128)(2,1)}, u32[]{:S(2)}) copy-start(bf16[688,2048]{1,0:T(8,128)(2,1)} %param.44) | copy-start | bytes 8454148
  7.2 43.5 %all-gather.10.cloned.1.call-start = ((), (), s32[]{:S(2)}) async-start(), calls=%async_computation.3 | async-start | bytes 4718592 | tf_op jit(solution)/shard_map/all_gather | solution.py:211
  9.5 871.4 %all-gather.12.cloned.1.call-start = ((), (), s32[]{:S(2)}) async-start(), calls=%async_computation.4 | async-start | bytes 4718592 | tf_op jit(solution)/shard_map/all_gather | solution.py:254
  20.5 35.0 %copy-start.34 = (f32[8,1,256]{2,1,0:T(1,128)}, f32[8,1,256]{2,1,0:T(1,128)S(1)}, u32[]{:S(2)}) copy-start(f32[8,1,256]{2,1,0:T(1,128)S(1)} %convert_element_type.400) | copy-start | bytes 24580
  50.7 3.8 copy-start.2
  54.5 1.0 copy-start.37
  54.5 3.1 copy-start.36
  55.5 2.0 copy-start.4
  67.6 3.3 copy-start.5
  843.3 4.7 copy-start.45
  843.3 13.6 copy-start.44
  843.3 76.9 %all-gather.14.cloned.1.call-start = ((), (), s32[]{:S(2)}) async-start(), calls=%async_computation.5 | async-start | bytes 4718592 | tf_op jit(solution)/shard_map/all_gather | solution.py:255
  847.9 119.8 %all-gather.16.cloned.1.call-start = ((), (), s32[]{:S(2)}) async-start(), calls=%async_computation.6 | async-start | bytes 4718592 | tf_op jit(solution)/shard_map/all_gather | solution.py:271
  880.8 3.4 copy-start.3
  920.2 7.4 copy-start.23
  920.2 7.4 copy-start.24
  927.6 2.5 copy-start.11
  927.6 3.1 copy-start.43
  930.1 76.1 %all-gather.18.cloned.1.call-start = ((), (), s32[]{:S(2)}) async-start(), calls=%async_computation.8 | async-start | bytes 4718592 | tf_op jit(solution)/shard_map/all_gather | solution.py:291
  930.7 164.8 %reduce-scatter.6.cloned.1.call-start = ((), (), s32[]{:S(2)}) async-start(), calls=%async_computation.9 | async-start | bytes 9437184 | tf_op jit(solution)/shard_map/reduce_scatter | solution.py:301
  967.7 3.4 copy-start.7
  971.2 6.7 copy-start.41
  1006.2 8.4 copy-start.40
  1014.6 3.5 copy-start.48
  1014.6 3.5 copy-start.46
  1014.6 3.5 copy-start.42
  1024.1 165.1 %reduce-scatter.8.cloned.1.call-start = ((), (), s32[]{:S(2)}) async-start(), calls=%async_computation.10 | async-start | bytes 9437184 | tf_op jit(solution)/shard_map/reduce_scatter | solution.py:321
  1110.2 3.2 copy-start.25
  1112.5 1.0 copy-start.9
  1117.9 1225.6 %reduce-scatter.4.cloned.1.call-start = ((), (), s32[]{:S(2)}) async-start(), calls=%async_computation.7 | async-start | bytes 4718592 | tf_op jit(solution)/shard_map/reduce_scatter | solution.py:282
  1118.0 6.7 copy-start.50
  1130.1 1.6 copy-start.49
  1130.1 1228.4 %all-reduce.6.cloned.1.call-start = ((), (), s32[]{:S(2)}) async-start(), calls=%async_computation.11 | async-start | bytes 8388608 | tf_op jit(solution)/shard_map/psum | solution.py:369
  1131.7 7.5 copy-start.8
  1131.7 7.5 copy-start.47
  1139.2 50.0 %copy-start.22 = (bf16[1024,256]{1,0:T(8,128)(2,1)S(1)}, bf16[1024,256]{1,0:T(8,128)(2,1)}, u32[]{:S(2)}) copy-start(bf16[1024,256]{1,0:T(8,128)(2,1)} %convolution_convert_fusion.9) | copy-start | bytes 1572868
  2229.1 25.1 copy-start.16
  2245.0 13.6 copy-start.18
  2245.2 4.5 copy-start.26
  2249.7 4.5 copy-start.27
  2254.2 4.5 copy-start.28
  2258.7 4.5 copy-start.20
  2258.7 4.5 copy-start.29
  2277.0 7.5 copy-start.10
  2277.0 555.3 %all-reduce.8.cloned.1.call-start = ((), (), s32[]{:S(2)}) async-start(), calls=%async_computation.12 | async-start | bytes 27394048 | tf_op jit(solution)/shard_map/psum | solution.py:380
  2277.0 7.5 copy-start.12
  2284.5 2.3 copy-start.6
  2284.5 2.5 copy-start.19
  2287.0 2.2 copy-start.17
  2291.5 2.3 copy-start.21
  2296.0 0.7 copy-start.35
  2336.6 6.8 copy-start.33
  2343.5 15.0 copy-start.38
  2394.1 3.3 copy-start.39
  2832.3 5.8 copy-start.32
  2832.3 7.4 copy-start.31
  2835.2 6.0 copy-start.30
  2838.1 4.7 copy-start.15
  2842.8 3.2 copy-start.14
  2846.0 3.3 copy-start.13
  2849.3 3.3 copy-start.1
Sparse Core Ops, SparseCore 0:
  10.5 40.1 all-gather.9
  843.4 37.4 all-gather.11
  882.7 37.4 all-gather.13
  930.2 37.4 all-gather.15
  969.4 36.7 all-gather.17
  1024.2 71.2 reduce-scatter.5
  1118.0 71.1 reduce-scatter.7
  1193.2 51.4 reduce-scatter.3
  2277.1 81.3 all-reduce.5
  2362.9 469.3 all-reduce.7
where the time goes:
time: 2900 us; the launch traced here: 2860 us
  matrix products  847 us (29%)
  waiting for transfers between devices  670 us (23%)
  other arithmetic  650 us (22%)
  local copies, waits for them, and re-layouts  428 us (15%)
  blocking collectives  143 us (5%)
  loops' own time  106 us (4%)
    psum x1, waiting for transfers between devices, on_device(): lax.psum(grad_w_query.astype(jnp.bfloat16), 'dp').astype(jnp.float32)  425 us
    dot_general x256, matrix products, head_block(): jnp.dot(key_rows, weight, precision=highest) + offset_vec  223 us
    squeeze x384, local copies, waits for them, and re-layouts, ttt_scan(): lax.scan(jax.checkpoint(advance), (init_weight, init_bias), (blocks(queri...  203 us
    dynamic_update_slice x192, other arithmetic, ttt_scan(): lax.scan(jax.checkpoint(advance), (init_weight, init_bias), (blocks(queri...  140 us
    dot_general x256, matrix products, head_block(): jnp.dot(query_rows, weight, precision=highest)  130 us
    dot_general x192, matrix products, head_block(): jnp.dot((last_rates[:, None] * key_rows).T, grad_z, precision=highest)  126 us
    another operation x2, loops' own time, ttt_scan(): lax.scan(jax.checkpoint(advance), (init_weight, init_bias), (blocks(queri...  106 us
    dot_general x256, matrix products, head_block(): scores = jnp.dot(query_rows, key_rows.T, precision=highest)  99.3 us

commit v1 on v0

v1 whole, which is shorter than its diff:
```python
import jax, jax.numpy as jnp
from jax import lax
from jax.experimental import pallas as pl
from jax.experimental.pallas import tpu as pltpu
import functools
HD=64; MB=16; EPS=1e-6
F32=jnp.float32; BF=jnp.bfloat16

def nn(a,b): return lax.dot_general(a,b,(((1,),(0,)),((),())),preferred_element_type=F32)
def nt(a,b): return lax.dot_general(a,b,(((1,),(1,)),((),())),preferred_element_type=F32)
def tn(a,b): return lax.dot_general(a,b,(((0,),(0,)),((),())),preferred_element_type=F32)

def avg(x): return jnp.sum(x,0,keepdims=True)*(1.0/HD)

def lane_heads(heads, rows):
    return lax.broadcasted_iota(jnp.int32,(rows,heads*MB),1)//MB

def spread(x, heads):
    ids=lane_heads(heads,HD)
    return jnp.concatenate([jnp.where(ids==h,x,jnp.zeros_like(x)) for h in range(heads)],0)

def gather_blocks(x, heads):
    ids=lane_heads(heads,HD)
    out=jnp.zeros((HD,heads*MB),F32)
    for h in range(heads):
        out=out+jnp.where(ids==h,x[h*HD:(h+1)*HD],0.0)
    return out

def split_heads(ref, group, heads):
    cols=[ref[h*HD:(h+1)*HD, pl.ds(pl.multiple_of(group*128,128),128)] for h in range(heads)]
    return [jnp.concatenate([c[:,p*MB:(p+1)*MB] for c in cols],1) for p in range(8)]

def merge_heads(ref, group, parts, heads):
    for h in range(heads):
        blk=jnp.concatenate([p[:,h*MB:(h+1)*MB] for p in parts],1)
        ref[h*HD:(h+1)*HD, pl.ds(pl.multiple_of(group*128,128),128)]=blk.astype(ref.dtype)

def padded(x):
    rows=lax.broadcasted_iota(jnp.int32,(MB,x.shape[1]),0)
    return jnp.concatenate([x,jnp.where(rows==0,1.0,0.0).astype(F32)],0)

def same_head(heads):
    L=heads*MB
    r=lax.broadcasted_iota(jnp.int32,(L,L),0); c=lax.broadcasted_iota(jnp.int32,(L,L),1)
    return r//MB==c//MB, r%MB, c%MB

def step_grad(zt, td, g, s):
    mu=avg(zt); cen=zt-mu
    r=lax.rsqrt(avg(cen*cen)+EPS)
    n=cen*r
    v=n*g+s-td
    u=v*g
    m1=avg(u); m2=avg(u*n)
    return r,n,v,u,m2,r*(u-m1-n*m2)

def fwd_kernel(heads, nb, reset, qT, kT, vT, er, vr, w0, c0, g_ref, s_ref, wi, ci,
               outT, zt_o, zb_o, td_o, qa_o, ka_o, wt_o, wo, co, mp, q32):
    L=heads*MB
    same,ri,ci_=same_head(heads)
    tri=jnp.where(same&(ri<=ci_), 16.0/(ci_.astype(F32)+1.0), 0.0)
    diag=jnp.where(same,1.0,0.0)
    def pre(gr,_):
        qs=split_heads(qT,gr,heads); ks=split_heads(kT,gr,heads); vs=split_heads(vT,gr,heads)
        for p in range(8):
            b=gr*8+p
            td_o[b]=vs[p]-ks[p]
            q32[b]=qs[p]
            qa_o[b]=padded(qs[p]).astype(BF)
            ka_o[b]=padded(ks[p]).astype(BF)
        return 0
    lax.fori_loop(0,nb//8,pre,0)
    def pre2(b,_):
        nxt=jnp.minimum(b+1,nb-1)
        ke=(ka_o[b].astype(F32)*(er[b]*(1.0/MB))).astype(BF)
        keep=jnp.where(reset[nxt]>0,0.0,1.0)
        m=tn(ke,ka_o[nxt])*(diag*keep)
        pt=tn(ke,qa_o[b])*tri
        mp[b]=jnp.concatenate([m,pt],1).astype(BF)
        return 0
    lax.fori_loop(0,nb,pre2,0,unroll=4)
    g=g_ref[...]; s=s_ref[...]
    ids=lane_heads(heads,L)
    rows=lax.broadcasted_iota(jnp.int32,(L,L),0)//MB
    def body(b,carry):
        zt,wt,ct=carry
        nxt=jnp.minimum(b+1,nb-1)
        rs=reset[nxt]>0
        wt_b=wt.astype(BF)
        wt_o[b]=wt_b; zt_o[b]=zt
        r,n,v,u,m2,gt=step_grad(zt,td_o[b],g,s)
        gb=gt.astype(BF)
        kn=spread(ka_o[nxt][:HD],heads)
        wsel=jnp.where(rs,w0[...],wt).astype(BF)
        csel=jnp.where(rs,c0[...],ct)
        yk=nn(wsel,kn)+csel
        yq=nn(wt_b,spread(qa_o[b][:HD],heads))+ct
        rr=nn(gb,mp[b])
        e16=er[b]*(1.0/MB)
        ke=(ka_o[b][:HD].astype(F32)*e16).astype(BF)
        rw=nt(gb,spread(ke,heads))
        ec=jnp.where(same,jnp.broadcast_to(e16,(L,L)),0.0).astype(BF)
        rc=nt(gb,ec)
        zb_o[b]=yq-rr[:,L:]
        z2=yk-rr[:,:L]
        wn=jnp.where(rs,w0[...],wt-rw)
        cn=jnp.where(rs,c0[...],ct-rc)
        @pl.when(b==nb-1)
        def _():
            wo[...]=wt-rw; co[...]=ct-rc
        return z2,wn,cn
    rs0=reset[0]>0
    wt=jnp.where(rs0,w0[...],wi[...]); ct=jnp.where(rs0,c0[...],ci[...])
    zt=nn(wt.astype(BF),spread(ka_o[0][:HD],heads))+ct
    lax.fori_loop(0,nb,body,(zt,wt,ct))
    def post(gr,_):
        outs=[]
        for p in range(8):
            b=gr*8+p
            zb=zb_o[b]; cen=zb-avg(zb)
            n=cen*lax.rsqrt(avg(cen*cen)+EPS)
            outs.append((q32[b]+n*g+s)*vr[b])
        merge_heads(outT,gr,outs,heads)
        return 0
    lax.fori_loop(0,nb//8,post,0)

VM=pl.BlockSpec(memory_space=pltpu.VMEM)
SM=pl.BlockSpec(memory_space=pltpu.SMEM)

def ttt_fwd(reset, qT,kT,vT, er, vr, w0,c0,g,s, wi,ci):
    T=qT.shape[1]; heads=qT.shape[0]//HD; nb=T//MB; L=heads*MB; S=jax.ShapeDtypeStruct
    outs=[S((heads*HD,T),BF),S((nb,HD,L),F32),S((nb,HD,L),F32),S((nb,HD,L),F32),S((nb,HD+MB,L),BF),S((nb,HD+MB,L),BF),
          S((nb,HD,heads*HD),BF),S((HD,heads*HD),F32),S((HD,L),F32)]
    return pl.pallas_call(functools.partial(fwd_kernel,heads,nb),out_shape=outs,
        in_specs=[SM]+[VM]*11,out_specs=[VM]*len(outs),
        scratch_shapes=[pltpu.VMEM((nb,L,2*L),BF),pltpu.VMEM((nb,HD,L),F32)],
        compiler_params=pltpu.CompilerParams(vmem_limit_bytes=56<<20), name="mix_forward")(reset,qT,kT,vT,er,vr,w0,c0,g,s,wi,ci)

def bwd_kernel(heads, nb, reset, dOT, zt_i, zb_i, td_i, qa_i, ka_i, wt_i, er, vr, g_ref, s_ref, li, lci,
               dqT, dkT, dvT, de_o, dg_o, ds_o, dw0_o, dc0_o, lo, lco,
               n_s, v_s, r_s, m2_s, gb_s, gh_s, nm_s, u_s, uc_s, dq_s, dk_s, du_s, dz_s, h_s, la_s):
    L=heads*MB
    g=g_ref[...]; s=s_ref[...]
    same,ri,cj=same_head(heads)
    tri=jnp.where(same&(cj<=ri),1.0/(ri.astype(F32)+1.0),0.0)
    diag=jnp.where(same,1.0,0.0)
    diag_b=diag.astype(BF)
    dg_o[...]=jnp.zeros((HD,L),F32); ds_o[...]=jnp.zeros((HD,L),F32)
    dw0_o[...]=jnp.zeros_like(dw0_o); dc0_o[...]=jnp.zeros_like(dc0_o)
    def pre(gr,_):
        dos=split_heads(dOT,gr,heads)
        dga=jnp.zeros((HD,L),F32); dsa=jnp.zeros((HD,L),F32)
        for p in range(8):
            b=gr*8+p
            dO=dos[p].astype(F32)*vr[b]
            zb=zb_i[b]; cen=zb-avg(zb); rb=lax.rsqrt(avg(cen*cen)+EPS); nbar=cen*rb
            dga=dga+dO*nbar; dsa=dsa+dO
            dn=dO*g
            dzb=rb*(dn-avg(dn)-nbar*avg(dn*nbar))
            dzb_b=dzb.astype(BF)
            r,n,v,u,m2,gt=step_grad(zt_i[b],td_i[b],g,s)
            gb=gt.astype(BF)
            n_s[b]=n; v_s[b]=v; r_s[b]=r; m2_s[b]=m2; gb_s[b]=gt
            e=er[b]
            ka=ka_i[b]; qa=qa_i[b]
            st=tn(qa,ka)*tri
            gh_s[b]=-nn(dzb_b,(st*e).astype(BF))
            dp=-tn(dzb_b,gb)
            de_o[b]=jnp.sum(dp*st,0,keepdims=True)
            dS=(dp*tri*e).astype(BF)
            dq_s[b]=dO+gather_blocks(tn(wt_i[b],dzb_b),heads)+nt(ka[:HD],dS)
            dk_s[b]=nn(qa[:HD],dS)
            prev=jnp.maximum(b-1,0)
            keep=jnp.where(reset[b]>0,0.0,1.0)
            nm_s[b]=(tn(ka,ka_i[prev])*(diag*keep)).astype(BF)
            u_s[b]=nt(dzb_b,spread(qa[:HD],heads))
            uc_s[b]=nn(dzb_b,diag_b)
        dg_o[...]+=dga; ds_o[...]+=dsa
        return 0
    lax.fori_loop(0,nb//8,pre,0)
    def body(k,carry):
        ht,la,lc=carry
        b=nb-1-k
        prev=jnp.maximum(b-1,0)
        rs=reset[b]>0
        n=n_s[b]; v=v_s[b]; r=r_s[b]; m2=m2_s[b]; gt=gb_s[b]
        h_s[b]=ht
        la_s[b]=la.astype(BF)
        dG=gh_s[b]-(er[b]*(1.0/MB))*ht
        da=r*dG
        m3=avg(da); m4=avg(da*n); m6a=avg(dG*gt)
        du=da-m3-n*m4
        dn=(du*g-v*m4)*g-da*m2
        m5=avg(dn); m6=m6a+avg(dn*n)
        dz=(r*(dn-m5-n*m6)).astype(BF)
        du_s[b]=du
        dz_s[b]=dz
        la2=la+u_s[b]; lc2=lc+uc_s[b]
        y=nn(la2.astype(BF),spread(ka_i[prev][:HD],heads))+lc2
        h2=jnp.where(rs,0.0,y)+nn(dz,nm_s[b])
        la3=la2+nt(dz,spread(ka_i[b][:HD],heads)); lc3=lc2+nn(dz,diag_b)
        @pl.when(rs)
        def _():
            dw0_o[...]+=la3; dc0_o[...]+=lc3
        return h2,jnp.where(rs,0.0,la3),jnp.where(rs,0.0,lc3)
    la=li[...]; lc=lci[...]
    ht=nn(la.astype(BF),spread(ka_i[nb-1][:HD],heads))+lc
    ht,la,lc=lax.fori_loop(0,nb,body,(ht,la,lc))
    lo[...]=la; lco[...]=lc
    def post(gr,_):
        dqs=[];dks=[];dvs=[]
        dga=jnp.zeros((HD,L),F32); dsa=jnp.zeros((HD,L),F32)
        for p in range(8):
            b=gr*8+p
            du=du_s[b]; dug=du*g; gt=gb_s[b]
            dga=dga+du*v_s[b]+dug*n_s[b]; dsa=dsa+dug
            dvs.append(-dug)
            dqs.append(dq_s[b])
            de_o[b]=de_o[b]-avg(gt*h_s[b])*(HD/MB)
            dks.append(dug+dk_s[b]-(er[b]*(1.0/MB))*gather_blocks(tn(la_s[b],gt.astype(BF)),heads)
                       +gather_blocks(tn(wt_i[b],dz_s[b]),heads))
        merge_heads(dqT,gr,dqs,heads); merge_heads(dkT,gr,dks,heads); merge_heads(dvT,gr,dvs,heads)
        dg_o[...]+=dga; ds_o[...]+=dsa
        return 0
    lax.fori_loop(0,nb//8,post,0)

def ttt_bwd(reset, dOT, zt,zb,td,qa,ka,wt,er,vr,g,s,li,lci):
    T=dOT.shape[1]; heads=dOT.shape[0]//HD; nb=T//MB; L=heads*MB; S=jax.ShapeDtypeStruct
    W=heads*HD
    outs=[S((W,T),BF)]*3+[S((nb,1,L),F32)]+[S((HD,L),F32)]*2+[S((HD,W),F32),S((HD,L),F32)]*2
    V=pltpu.VMEM
    scr=[V((nb,HD,L),F32),V((nb,HD,L),F32),V((nb,1,L),F32),V((nb,1,L),F32),V((nb,HD,L),F32),V((nb,HD,L),F32),
         V((nb,L,L),BF),V((nb,HD,W),F32),V((nb,HD,L),F32),V((nb,HD,L),F32),V((nb,HD,L),F32),V((nb,HD,L),F32),
         V((nb,HD,L),BF),V((nb,HD,L),F32),V((nb,HD,W),BF)]
    return pl.pallas_call(functools.partial(bwd_kernel,heads,nb),out_shape=outs,
        in_specs=[SM]+[VM]*13,out_specs=[VM]*len(outs),scratch_shapes=scr,
        compiler_params=pltpu.CompilerParams(vmem_limit_bytes=60<<20), name="mix_backward")(reset,dOT,zt,zb,td,qa,ka,wt,er,vr,g,s,li,lci)

def lane_rows(x, heads):
    T=x.shape[1]
    return x.reshape(heads,T//MB,MB).transpose(1,0,2).reshape(T//MB,1,heads*MB)
def lane_cols(x):
    return jnp.repeat(x.T,MB,axis=1)


from jax.sharding import PartitionSpec as P


def col_sum(x):
    return jnp.sum(x, 0, keepdims=True)


def gelu_tanh(values):
    return jax.nn.gelu(values, approximate=True)


def layout(seq_lens, row_count):
    padded = (seq_lens + MB - 1) // MB * MB
    starts = jnp.cumsum(padded) - padded
    positions = jnp.arange(row_count, dtype=jnp.int32)
    inside = (positions[None, :] >= starts[:, None]) & (positions[None, :] < (starts + seq_lens)[:, None])
    valid_rows = jnp.any(inside, axis=0).astype(F32)
    block_first = jnp.arange(row_count // MB, dtype=jnp.int32) * MB
    begins = jnp.any((starts[:, None] == block_first[None, :]) & (seq_lens[:, None] > 0), axis=0)
    return valid_rows, (begins | (block_first == 0)).astype(jnp.int32)


def on_device(
    tokens, lengths, attn_gain, w_query, w_key, w_value, w_gate, w_rate, rate_bias,
    inner_weight, inner_bias, inner_gain, inner_shift, post_gain, post_shift, w_out,
    ffn_gain, w_hidden_gate, w_hidden_up, w_down, out_grad,
):
    tok = tokens.shape[1]
    own = tokens.shape[0]
    heads = inner_weight.shape[0]
    devs = lax.axis_size("head")
    width = own * devs
    first = lax.axis_index("head") * own

    def gather(x):
        return lax.all_gather(x, "head", axis=0, tiled=True)

    def mine(x):
        return lax.dynamic_slice_in_dim(x, first, own, 0)

    valid, reset = layout(lengths, tok)
    vrow = valid[None, :]
    gains = lax.all_gather(jnp.stack([attn_gain, post_gain, post_shift, ffn_gain]), "head", axis=1, tiled=True)
    gains = gains.astype(F32)[:, :, None]
    x = gather(tokens).astype(F32)
    q1 = lax.rsqrt(col_sum(x * x) / width + EPS)
    nin = (x * q1 * gains[0]).astype(BF)
    q_t = nn(w_query, nin)
    k_t = nn(w_key, nin)
    v_t = nn(w_value, nin)
    gate = nn(w_gate, nin).astype(BF)
    logits = tn(w_rate, nin) + rate_bias.astype(F32)[:, None]
    sig = jax.nn.sigmoid(logits)
    masked = sig * vrow
    er = lane_rows(masked * (1.0 / HD), heads)
    vr = lane_rows(jnp.broadcast_to(vrow, (heads, tok)), heads)
    w0 = inner_weight.astype(F32).transpose(2, 0, 1).reshape(HD, own)
    c0 = lane_cols(inner_bias.astype(F32))
    ig = lane_cols(inner_gain.astype(F32))
    ish = lane_cols(inner_shift.astype(F32))
    zw = jnp.zeros_like(w0)
    zc = jnp.zeros_like(c0)
    mixer_own, zt, zb, td, qa, ka, wt, _, _ = ttt_fwd(reset, q_t, k_t, v_t, er, vr, w0, c0, ig, ish, zw, zc)
    rate_part = jnp.sum(masked)
    max_rate = lax.pmax(jnp.max(masked), ("dp", "head"))

    mix = gather(mixer_own).astype(F32)
    gates = gather(gate).astype(F32)
    cen = mix - col_sum(mix) / width
    r3 = lax.rsqrt(col_sum(cen * cen) / width + EPS)
    mixed = ((cen * r3 * gains[1] + gains[2]) * gelu_tanh(gates)).astype(BF)
    hidden = tokens.astype(F32) + nn(w_out, mixed)
    hid = gather(hidden.astype(BF)).astype(F32)
    q2 = lax.rsqrt(col_sum(hid * hid) / width + EPS)
    nmid = (hid * q2 * gains[3]).astype(BF)
    gate_val = nn(w_hidden_gate, nmid)
    up_val = nn(w_hidden_up, nmid)
    sg = jax.nn.sigmoid(gate_val)
    act = (gate_val * sg * up_val).astype(BF)
    ffn = lax.psum_scatter(tn(w_down, act).astype(BF), "head", scatter_dimension=0, tiled=True)
    result = (hidden + ffn.astype(F32)).astype(BF)

    g_full = gather(out_grad)
    g_down = nt(act, g_full)
    g_act = nn(w_down, g_full)
    g_up = (g_act * gate_val * sg).astype(BF)
    g_gate = (g_act * up_val * sg * (1.0 + gate_val * (1.0 - sg))).astype(BF)
    g_hgate = nt(g_gate, nmid)
    g_hup = nt(g_up, nmid)
    gn = lax.psum_scatter(
        tn(w_hidden_gate, g_gate) + tn(w_hidden_up, g_up), "head", scatter_dimension=0, tiled=True
    )
    hid_own = mine(hid)
    fg_own = ffn_gain.astype(F32)[:, None]
    mid_dot, rate_head = lax.psum((col_sum(hid_own * fg_own * gn), rate_part), "head")
    g_ffn_gain = jnp.sum(gn * hid_own * q2, 1)
    g_hidden = out_grad.astype(F32) + q2 * fg_own * gn - hid_own * q2**3 * mid_dot / width
    g_branch = g_hidden.astype(BF)
    g_w_out = nt(g_branch, mixed)
    gm = lax.psum_scatter(tn(w_out, g_branch), "head", scatter_dimension=0, tiled=True)
    n3 = mine(cen) * r3
    pg_own = post_gain.astype(F32)[:, None]
    ps_own = post_shift.astype(F32)[:, None]
    a_own, gelu_pull = jax.vjp(gelu_tanh, gate.astype(F32))
    g_post_gain = jnp.sum(gm * a_own * n3, 1)
    g_post_shift = jnp.sum(gm * a_own, 1)
    g_gate_pre = gelu_pull(gm * (n3 * pg_own + ps_own))[0].astype(BF)
    m = gm * a_own * pg_own
    s_plain, s_norm = lax.psum((col_sum(m), col_sum(m * n3)), "head")
    g_mixer = r3 * (m - s_plain / width - n3 * s_norm / width)
    dq, dk, dv, de, dgl, dsl, dw0, dc0, _, _ = ttt_bwd(
        reset, g_mixer, zt, zb, td, qa, ka, wt, er, vr, ig, ish, zw, zc
    )
    de_rows = de.reshape(tok // MB, heads, MB).transpose(1, 0, 2).reshape(heads, tok)
    g_logits = de_rows * vrow * (1.0 / HD) * sig * (1.0 - sig)
    gl = g_logits.astype(BF)
    g_inner_w = dw0.reshape(HD, heads, HD).transpose(1, 2, 0)
    g_inner_b = dc0.reshape(HD, heads, MB)[:, :, 0].T
    g_inner_g = dgl.reshape(HD, heads, MB).sum(-1).T
    g_inner_s = dsl.reshape(HD, heads, MB).sum(-1).T
    g_wq = nt(dq, nin)
    g_wk = nt(dk, nin)
    g_wv = nt(dv, nin)
    g_wg = nt(g_gate_pre, nin)
    g_wr = nt(nin, gl)
    part = tn(w_query, dq) + tn(w_key, dk) + tn(w_value, dv) + tn(w_gate, g_gate_pre) + nn(w_rate, gl)
    gi_full = lax.psum(part.astype(BF), "head").astype(F32)
    g_attn_gain = jnp.sum(mine(gi_full * x) * q1, 1)
    in_dot = col_sum(x * gains[0] * gi_full)
    x_own = tokens.astype(F32)
    g_tokens = (
        g_hidden + q1 * attn_gain.astype(F32)[:, None] * mine(gi_full) - x_own * q1**3 * in_dot / width
    )

    def over_dp(v):
        return lax.psum(v.astype(BF), "dp").astype(F32)

    mean_rate = over_dp(rate_head) / (tok * lax.axis_size("dp") * heads * devs)
    return (
        result, g_tokens, over_dp(g_attn_gain), over_dp(g_wq), over_dp(g_wk), over_dp(g_wv), over_dp(g_wg),
        over_dp(g_wr), over_dp(jnp.sum(g_logits, 1)), over_dp(g_inner_w), over_dp(g_inner_b),
        over_dp(g_inner_g), over_dp(g_inner_s), over_dp(g_post_gain), over_dp(g_post_shift), over_dp(g_w_out),
        over_dp(g_ffn_gain), over_dp(g_hgate), over_dp(g_hup), over_dp(g_down), mean_rate, max_rate,
    )


def solution(mesh):
    h = P("head")
    m = P("head", None)
    c = P("head", None, None)
    t = P("head", "dp")
    r = P(None, "head")
    ins = (t, P("dp"), h, m, m, m, m, r, h, c, m, m, m, h, h, m, h, m, m, m, t)
    outs = (t, t, h, m, m, m, m, r, h, c, m, m, m, h, h, m, h, m, m, m, P(), P())
    return jax.shard_map(on_device, mesh=mesh, in_specs=ins, out_specs=outs, check_vma=False)
```

time: 2900 us -> 1150 us (0.40); the launches traced: 2860 us -> 1150 us
  matrix products: 847 us -> 130 us
  other arithmetic: 650 us -> 87.9 us
  local copies, waits for them, and re-layouts: 428 us -> 21.1 us
  loops' own time: 106 us -> 0 us
  Pallas kernels: 0 us -> 82.1 us
    dot_general x1563 -> x27, matrix products: 847 us -> 130 us  [the longest x9 50.2 us: nn(): lax.dot_general(a, b, (((1,), (0,)), ((), ())), preferred_element_type=F32)]
    squeeze x384 -> x0, local copies, waits for them, and re-layouts: 203 us -> none  [ttt_scan(): lax.scan(jax.checkpoint(advance), (init_weight, init_bias), (blocks(queri...]
    reduce_sum x776 -> x10, other arithmetic: 193 us -> 18 us  [the longest x4 11.1 us: col_sum(): return jnp.sum(x, 0, keepdims=True)]
    add x256 -> x0, other arithmetic: 168 us -> none  [the longest x128 84.8 us: advance(): weight = reset_now * init_weight + (1.0 - reset_now) * weight]
    dynamic_update_slice x192 -> x0, other arithmetic: 140 us -> none  [ttt_scan(): lax.scan(jax.checkpoint(advance), (init_weight, init_bias), (blocks(queri...]
    another operation x2 -> x0, loops' own time: 106 us -> none  [ttt_scan(): lax.scan(jax.checkpoint(advance), (init_weight, init_bias), (blocks(queri...]
    pallas_call x0 -> x2, Pallas kernels: none -> 82.1 us  [the longest x1 44.4 us: ttt_bwd(): pl.pallas_call(functools.partial(bwd_kernel, heads, nb), out_shape=outs,...]
    dynamic_update_slice x128 -> x0, local copies, waits for them, and re-layouts: 79.5 us -> none  [ttt_scan(): lax.scan(jax.checkpoint(advance), (init_weight, init_bias), (blocks(queri...]
where the time goes in v1:
time: 1150 us
  waiting for transfers between devices  692 us (60%)
  matrix products  130 us (11%)
  blocking collectives  116 us (10%)
  other arithmetic  87.9 us (8%)
  Pallas kernels  82.1 us (7%)
  local copies, waits for them, and re-layouts  21.1 us (2%)
  between operations  16.8 us (1%)
    psum x1, waiting for transfers between devices, over_dp(): return lax.psum(v.astype(BF), 'dp').astype(F32)  428 us
    all_gather x5, waiting for transfers between devices, gather(): return lax.all_gather(x, 'head', axis=0, tiled=True)  141 us
    reduce_scatter x1, waiting for transfers between devices, on_device(): lax.psum_scatter(tn(w_hidden_gate, g_gate) + tn(w_hidden_up, g_up), 'head...  63.7 us
    dot_general x9, matrix products, nn(): lax.dot_general(a, b, (((1,), (0,)), ((), ())), preferred_element_type=F32)  50.2 us
    reduce_scatter x1, waiting for transfers between devices, on_device(): lax.psum_scatter(tn(w_out, g_branch), 'head', scatter_dimension=0, tiled=...  45.5 us
    pallas_call x1, Pallas kernels, ttt_bwd(): pl.pallas_call(functools.partial(bwd_kernel, heads, nb), out_shape=outs,...  44.4 us
    dot_general x9, matrix products, tn(): lax.dot_general(a, b, (((0,), (0,)), ((), ())), preferred_element_type=F32)  43.2 us
    pmax x1, blocking collectives, on_device(): max_rate = lax.pmax(jnp.max(masked), ('dp', 'head'))  39.5 us
  transfers between devices with their start and end apart: 10, of which 9 were waited for; matrix products, arithmetic and copies ran while one was open for 13% of the time, Pallas kernels for 4%

profile of v1, /device:TPU:0, one launch (start us, length us, event | category | flops | bytes accessed | tf_op | source)
XLA Modules:
  0.0 1146.4 jit_solution(9399536194465108509)
XLA Ops:
  19.5 10.4 all_gather.19
  31.2 18.2 %all-gather.6.cloned.1.call-done = bf16[2048,1024]{1,0:T(8,128)(2,1)} async-done(((bf16[256,1024]{1,0:T(8,128)(2,1)}), bf16[2048,1024]{1,0:T(8,128)(2,1)}) %all-gather.6.cloned.1.call-update) | async-done | bytes 4194320 | tf_op jit(solution)/shard_map/all_gather | solution.py:280
  49.4 3.3 multiply_reduce_fusion.3
  54.4 2.0 copy-done.4
  58.6 4.9 convolution_bitcast_fusion.4.qT
  63.5 2.2 convolution_bitcast_fusion.3.kT
  65.7 2.2 convolution_bitcast_fusion.2.vT
  69.2 37.7 %mix_forward.1 = (bf16[256,1024]{1,0:T(8,128)(2,1)}, f32[64,64,64]{2,1,0:T(8,128)}, f32[64,64,64]{2,1,0:T(8,128)}, f32[64,64,64]{2,1,0:T(8,128)}, bf16[64,80,64]...) custom-call(s32[64]{0:T(128)} %or_convert_fusion.reset, ...), custom_call_target="tpu_custom_call" | custom-call | tf_op jit(solution)/shard_map/mix_forward/pallas_call | solution.py:133
  107.0 4.6 fusion.19
  111.8 32.0 %all-gather.8.cloned.1.call-done = bf16[2048,1024]{1,0:T(8,128)(2,1)} async-done(((bf16[256,1024]{1,0:T(8,128)(2,1)}), bf16[2048,1024]{1,0:T(8,128)(2,1)}) %all-gather.8.cloned.1.call-update) | async-done | bytes 4194320 | tf_op jit(solution)/shard_map/all_gather | solution.py:280
  143.8 3.0 convert_reduce_fusion
  147.2 4.6 convert_subtract_fusion
  151.8 31.2 %all-gather.10.cloned.1.call-done = bf16[2048,1024]{1,0:T(8,128)(2,1)} async-done(((bf16[256,1024]{1,0:T(8,128)(2,1)}), bf16[2048,1024]{1,0:T(8,128)(2,1)}) %all-gather.10.cloned.1.call-update) | async-done | bytes 4194320 | tf_op jit(solution)/shard_map/all_gather | solution.py:280
  183.0 6.8 fusion.6
  189.8 1.9 copy-done.14
  191.8 2.4 fusion.55
  194.8 36.2 %all-gather.12.cloned.1.call-done = bf16[2048,1024]{1,0:T(8,128)(2,1)} async-done(((bf16[256,1024]{1,0:T(8,128)(2,1)}), bf16[2048,1024]{1,0:T(8,128)(2,1)}) %all-gather.12.cloned.1.call-update) | async-done | bytes 4194320 | tf_op jit(solution)/shard_map/all_gather | solution.py:280
  231.1 3.3 multiply_reduce_fusion.1
  234.5 6.7 fusion.49
  241.2 4.7 fusion.50
  245.9 23.6 %all-gather.14.cloned.1.call-done = bf16[2048,1024]{1,0:T(8,128)(2,1)} async-done(((bf16[256,1024]{1,0:T(8,128)(2,1)}), bf16[2048,1024]{1,0:T(8,128)(2,1)}) %all-gather.14.cloned.1.call-update) | async-done | bytes 4194320 | tf_op jit(solution)/shard_map/all_gather | solution.py:280
  269.6 8.7 fusion.17
  278.3 3.7 fusion.56
  282.1 6.0 add_bitcast_fusion
  288.8 7.1 convert_element_type.257
  295.9 63.7 %reduce-scatter.6.cloned.1.call-done = f32[256,1024]{1,0:T(8,128)} async-done(((f32[2048,1024]{1,0:T(8,128)}), f32[256,1024]{1,0:T(8,128)}) %reduce-scatter.6.cloned.1.call-update) | async-done | bytes 1048592 | tf_op jit(solution)/shard_map/reduce_scatter | solution.py:334
  359.5 1.8 multiply_reduce_fusion.4
  361.3 12.7 %psum.168 = f32[1024]{0:T(1024)S(1)} all-reduce(f32[1024]{0:T(1024)S(1)} %get-tuple-element.55), channel_id=1, replica_groups=mesh['dp'=4,'head'=8] {'head'}, use_global_device_ids=true, to_apply=%region_10.11 | all-reduce | flops 1024 | bytes 8192 | tf_op jit(solution)/shard_map/psum | solution.py:339
  374.0 1.9 multiply_subtract_fusion
  377.0 4.5 convolution_bitcast_fusion
  382.2 6.4 convert_bitcast_fusion
  390.2 7.8 convolution_convert_fusion
  398.0 4.7 convolution_convert_fusion.1
  402.7 4.7 convolution_convert_fusion.2
  407.4 45.5 %reduce-scatter.8.cloned.1.call-done = f32[256,1024]{1,0:T(8,128)} async-done(((f32[2048,1024]{1,0:T(8,128)}), f32[256,1024]{1,0:T(8,128)}) %reduce-scatter.8.cloned.1.call-update) | async-done | bytes 1048592 | tf_op jit(solution)/shard_map/reduce_scatter | solution.py:344
  452.9 2.3 multiply_reduce_fusion.5
  455.2 23.1 %all-reduce = (f32[1024]{0:T(1024)S(1)}, f32[1,1024]{1,0:T(1,128)S(1)}, bf16[]{:T(256)}) all-reduce(f32[1024]{0:T(1024)S(1)} %get-tuple-element.53, f32[1,1024]{1,0:T(1,128)S(1)} %bitcast.169, f32[]{:T(128)} %get-tuple-element.59), channel_id=1, replica_groups=mesh['dp'=4,'head'=8] {'head'}, use_global_device_ids=true, to_apply=%region_15.16 | all-reduce | flops 2049 | bytes 16390 | tf_op jit(solution)/shard_map/psum | solution.py:353
  478.2 2.7 subtract_multiply_fusion.dOT
  481.0 44.4 %mix_backward.1 = (bf16[256,1024]{1,0:T(8,128)(2,1)}, bf16[256,1024]{1,0:T(8,128)(2,1)}, bf16[256,1024]{1,0:T(8,128)(2,1)}, f32[64,1,64]{2,1,0:T(1,128)}, f32[64...) custom-call(s32[64]{0:T(128)} %or_convert_fusion.reset, ...), custom_call_target="tpu_custom_call" | custom-call | tf_op jit(solution)/shard_map/mix_backward/pallas_call | solution.py:234
  526.6 5.7 fusion.59
  532.3 4.5 fusion.58
  536.9 4.5 fusion.57
  541.4 6.5 fusion.47
  548.0 13.7 %fusion.7 = bf16[2048,1024]{1,0:T(8,128)(2,1)} fusion(bf16[2048,4]{0,1:T(4,128)(2,1)S(1)} %copy-done.38, f32[1024,2048]{0,1:T(8,128)} %fusion.47, f32[1024,2048]{0,1:T(8,128)} %fusion.59, f32[1024,2048]{0,1:T(8,128)} %fusion.57, f32[1024,2048]{0,1:T(8,128)} %fusion.58, bf16[4,1024]{1,0:T(4,128)(2,1)S(1)} %get-tuple-element.83), kind=kOutput, calls=%fused_computation.26 | convolution fusion | flops 27262976 | bytes 37773312 | tf_op jit(solution)/shard_map/dot_general | solution.py:9
  562.9 4.6 convolution_convert_fusion.3
  567.5 2.3 convolution_convert_fusion.7
  569.8 2.3 convolution_convert_fusion.6
  572.2 2.3 convolution_convert_fusion.5
  574.5 4.3 convolution_convert_fusion.4
  579.5 39.5 %pmax.7 = f32[]{:T(128)} all-reduce(f32[]{:T(128)} %get-tuple-element.58), channel_id=1, replica_groups=mesh['dp'=4,'head'=8] {'dp','head'}, use_global_device_ids=true, to_apply=%region_47.48 | all-reduce | flops 1 | bytes 8 | tf_op jit(solution)/shard_map/pmax | solution.py:309
  619.0 7.0 convert_element_type.244
  626.1 2.0 add_convert_fusion.1
  628.5 3.5 convolution_convert_fusion.8
  632.0 11.4 all-reduce.6.cloned.1.call-done
  643.4 3.4 convert_element_type.275
  649.7 2.7 fusion.38
  652.3 30.4 %all-reduce.1 = (bf16[256]{0:T(256)(128)(2,1)S(1)}, bf16[2048,4]{0,1:T(4,128)(2,1)S(1)}, bf16[4]{0:T(256)(128)(2,1)S(1)}, bf16[4,64,64]{2,1,0:T(8,128)(2,1)S(1)}...) all-reduce(bf16[256]{0:T(256)(128)(2,1)S(1)} %get-tuple-element.87,, ...), channel_id=1, replica_groups=mesh['dp'=4,'head'=8] {'dp'}, use_global_device_ids=true, to_apply=%region_19.20 | all-reduce | flops 26373 | bytes 105492 | tf_op jit(solution)/shard_map/psum | solution.py:380
  689.2 428.5 %all-reduce.8.cloned.1.call-done = (bf16[256,2048]{1,0:T(8,128)(2,1)}, bf16[256,2048]{1,0:T(8,128)(2,1)}, bf16[256,2048]{1,0:T(8,128)(2,1)}, bf16[256,2048]{1,0:...) async-done(((bf16[256,2048]{1,0:T(8,128)(2,1)}, bf16[256,2048]{1,0:T(8,128)(2,1)}, ...) | async-done | bytes 13697040 | tf_op jit(solution)/shard_map/psum | solution.py:380
  1117.7 2.9 convert_element_type.279
  1120.7 2.9 convert_element_type.281
  1126.7 1.6 convert_element_type.308
  1128.2 3.2 convert_element_type.312
  1131.5 3.2 convert_element_type.314
  1134.7 3.2 convert_element_type.316
  (209 shorter events, 39.5 us)
Async XLA Ops:
  7.2 262.4 %copy-start = (bf16[688,2048]{1,0:T(8,128)(2,1)S(1)}, bf16[688,2048]{1,0:T(8,128)(2,1)}, u32[]{:S(2)}) copy-start(bf16[688,2048]{1,0:T(8,128)(2,1)} %param.40) | copy-start | bytes 8454148
  7.2 42.2 %all-gather.6.cloned.1.call-start = ((), (), s32[]{:S(2)}) async-start(), calls=%async_computation.3 | async-start | bytes 4718592 | tf_op jit(solution)/shard_map/all_gather | solution.py:280
  7.9 135.8 %all-gather.8.cloned.1.call-start = ((), (), s32[]{:S(2)}) async-start(), calls=%async_computation.4 | async-start | bytes 4718592 | tf_op jit(solution)/shard_map/all_gather | solution.py:280
  49.4 3.9 copy-start.2
  53.3 1.1 copy-start.40
  53.3 3.1 copy-start.38
  54.4 2.0 copy-start.4
  58.6 4.9 copy-start.5
  58.6 4.9 copy-start.26
  63.5 2.2 copy-start.24
  106.9 76.1 %all-gather.10.cloned.1.call-start = ((), (), s32[]{:S(2)}) async-start(), calls=%async_computation.5 | async-start | bytes 4718592 | tf_op jit(solution)/shard_map/all_gather | solution.py:280
  111.5 119.5 %all-gather.12.cloned.1.call-start = ((), (), s32[]{:S(2)}) async-start(), calls=%async_computation.6 | async-start | bytes 4718592 | tf_op jit(solution)/shard_map/all_gather | solution.py:280
  143.8 3.4 copy-start.7
  183.0 8.8 copy-start.20
  183.0 8.8 copy-start.22
  189.8 1.9 copy-start.14
  194.2 75.4 %all-gather.14.cloned.1.call-start = ((), (), s32[]{:S(2)}) async-start(), calls=%async_computation.8 | async-start | bytes 4718592 | tf_op jit(solution)/shard_map/all_gather | solution.py:280
  194.8 164.8 %reduce-scatter.6.cloned.1.call-start = ((), (), s32[]{:S(2)}) async-start(), calls=%async_computation.9 | async-start | bytes 9437184 | tf_op jit(solution)/shard_map/reduce_scatter | solution.py:334
  231.1 3.4 copy-start.8
  234.5 6.7 copy-start.47
  269.6 8.8 copy-start.46
  278.3 3.8 copy-start.55
  278.3 3.8 copy-start.53
  278.3 3.8 copy-start.48
  288.1 164.7 %reduce-scatter.8.cloned.1.call-start = ((), (), s32[]{:S(2)}) async-start(), calls=%async_computation.10 | async-start | bytes 9437184 | tf_op jit(solution)/shard_map/reduce_scatter | solution.py:344
  288.8 85.3 %copy-start.19 = (bf16[256,1024]{1,0:T(8,128)(2,1)S(1)}, bf16[256,1024]{1,0:T(8,128)(2,1)}, u32[]{:S(2)}) copy-start(bf16[256,1024]{1,0:T(8,128)(2,1)} %param.41) | copy-start | bytes 1572868
  374.0 2.9 copy-start.23
  376.0 1.0 copy-start.11
  381.5 244.5 %reduce-scatter.4.cloned.1.call-start = ((), (), s32[]{:S(2)}) async-start(), calls=%async_computation.7 | async-start | bytes 4718592 | tf_op jit(solution)/shard_map/reduce_scatter | solution.py:324
  388.6 1.6 copy-start.57
  388.6 9.4 copy-start.54
  388.6 254.8 %all-reduce.6.cloned.1.call-start = ((), (), s32[]{:S(2)}) async-start(), calls=%async_computation.11 | async-start | bytes 8388608 | tf_op jit(solution)/shard_map/psum | solution.py:371
  390.2 7.8 copy-start.9
  398.0 4.7 copy-start.56
  402.7 50.2 %copy-start.13 = (bf16[256,1024]{1,0:T(8,128)(2,1)S(1)}, bf16[256,1024]{1,0:T(8,128)(2,1)}, u32[]{:S(2)}) copy-start(bf16[256,1024]{1,0:T(8,128)(2,1)} %fusion.19) | copy-start | bytes 1572868
  481.0 45.6 %copy-start.25 = (bf16[256,2048]{1,0:T(8,128)(2,1)S(1)}, bf16[256,2048]{1,0:T(8,128)(2,1)}, u32[]{:S(2)}) copy-start(bf16[256,2048]{1,0:T(8,128)(2,1)} %param.26) | copy-start | bytes 3145732
  526.6 5.7 copy-start.27
  526.6 5.7 copy-start.35
  532.3 4.6 copy-start.28
  532.3 4.6 copy-start.36
  536.9 4.6 copy-start.15
  536.9 4.6 copy-start.33
  561.7 1.2 copy-start.12
  561.7 556.0 %all-reduce.8.cloned.1.call-start = ((), (), s32[]{:S(2)}) async-start(), calls=%async_computation.12 | async-start | bytes 27394048 | tf_op jit(solution)/shard_map/psum | solution.py:380
  562.9 4.6 copy-start.6
  562.9 4.6 copy-start.37
  569.8 2.3 copy-start.34
  619.0 7.0 copy-start.32
  619.0 9.0 copy-start.42
  619.0 9.2 copy-start.39
  619.0 9.3 copy-start.44
  619.0 9.4 copy-start.43
  643.4 3.4 copy-start.3
  643.4 4.7 copy-start.10
  648.1 1.5 copy-start.21
  648.1 1.5 copy-start.41
  648.1 1.5 copy-start.45
  1117.7 5.8 copy-start.31
  1117.7 7.4 copy-start.30
  1120.7 6.0 copy-start.29
  1123.5 4.7 copy-start.18
  1128.2 3.2 copy-start.17
  1131.5 3.3 copy-start.16
  1134.7 3.3 copy-start.1
  (4 other events, 2.6 us)
Sparse Core Ops, SparseCore 0:
  9.9 39.4 all-gather.5
  107.0 36.7 all-gather.7
  146.2 36.7 all-gather.9
  194.3 36.7 all-gather.11
  232.8 36.7 all-gather.13
  288.3 71.2 reduce-scatter.5
  381.6 71.1 reduce-scatter.7
  456.8 51.3 reduce-scatter.3
  561.8 81.4 all-reduce.5
  647.8 469.8 all-reduce.7

commit v2 on v1

v2 whole, which is shorter than its diff:
```python
import jax, jax.numpy as jnp
from jax import lax
from jax.experimental import pallas as pl
from jax.experimental.pallas import tpu as pltpu
import functools
HD=64; MB=16; EPS=1e-6
F32=jnp.float32; BF=jnp.bfloat16

def nn(a,b): return lax.dot_general(a,b,(((1,),(0,)),((),())),preferred_element_type=F32)
def nt(a,b): return lax.dot_general(a,b,(((1,),(1,)),((),())),preferred_element_type=F32)
def tn(a,b): return lax.dot_general(a,b,(((0,),(0,)),((),())),preferred_element_type=F32)

def avg(x): return jnp.sum(x,0,keepdims=True)*(1.0/HD)

def lane_heads(heads, rows):
    return lax.broadcasted_iota(jnp.int32,(rows,heads*MB),1)//MB

def spread(x, heads):
    ids=lane_heads(heads,HD)
    return jnp.concatenate([jnp.where(ids==h,x,jnp.zeros_like(x)) for h in range(heads)],0)

def gather_blocks(x, heads):
    ids=lane_heads(heads,HD)
    out=jnp.zeros((HD,heads*MB),F32)
    for h in range(heads):
        out=out+jnp.where(ids==h,x[h*HD:(h+1)*HD],0.0)
    return out

def split_heads(ref, group, heads):
    cols=[ref[h*HD:(h+1)*HD, pl.ds(pl.multiple_of(group*128,128),128)] for h in range(heads)]
    return [jnp.concatenate([c[:,p*MB:(p+1)*MB] for c in cols],1) for p in range(8)]

def merge_heads(ref, group, parts, heads):
    for h in range(heads):
        blk=jnp.concatenate([p[:,h*MB:(h+1)*MB] for p in parts],1)
        ref[h*HD:(h+1)*HD, pl.ds(pl.multiple_of(group*128,128),128)]=blk.astype(ref.dtype)

def padded(x):
    rows=lax.broadcasted_iota(jnp.int32,(MB,x.shape[1]),0)
    return jnp.concatenate([x,jnp.where(rows==0,1.0,0.0).astype(F32)],0)

def same_head(heads):
    L=heads*MB
    r=lax.broadcasted_iota(jnp.int32,(L,L),0); c=lax.broadcasted_iota(jnp.int32,(L,L),1)
    return r//MB==c//MB, r%MB, c%MB

def step_grad(zt, td, g, s):
    mu=avg(zt); cen=zt-mu
    r=lax.rsqrt(avg(cen*cen)+EPS)
    n=cen*r
    v=n*g+s-td
    u=v*g
    m1=avg(u); m2=avg(u*n)
    return r,n,v,u,m2,r*(u-m1-n*m2)

def fwd_kernel(heads, nb, reset, qT, kT, vT, rows, consts,
               outT, zt_o, zb_o, td_o, qa_o, ka_o, wt_o, mp, q32):
    L=heads*MB
    same,ri,ci_=same_head(heads)
    tri=jnp.where(same&(ri<=ci_), 16.0/(ci_.astype(F32)+1.0), 0.0)
    diag=jnp.where(same,1.0,0.0)
    def pre(gr,_):
        qs=split_heads(qT,gr,heads); ks=split_heads(kT,gr,heads); vs=split_heads(vT,gr,heads)
        for p in range(8):
            b=gr*8+p
            td_o[b]=vs[p]-ks[p]
            q32[b]=qs[p]
            qa_o[b]=padded(qs[p]).astype(BF)
            ka_o[b]=padded(ks[p]).astype(BF)
        return 0
    lax.fori_loop(0,nb//8,pre,0)
    def pre2(b,_):
        nxt=jnp.minimum(b+1,nb-1)
        ke=(ka_o[b].astype(F32)*(rows[b,0:1]*(1.0/MB))).astype(BF)
        keep=jnp.where(reset[nxt]>0,0.0,1.0)
        m=tn(ke,ka_o[nxt])*(diag*keep)
        pt=tn(ke,qa_o[b])*tri
        mp[b]=jnp.concatenate([m,pt],1).astype(BF)
        return 0
    lax.fori_loop(0,nb,pre2,0,unroll=4)
    w0,c0,g,s=unpack_consts(consts,heads)
    def body(b,carry):
        zt,wt,ct=carry
        nxt=jnp.minimum(b+1,nb-1)
        rs=reset[nxt]>0
        wt_b=wt.astype(BF)
        wt_o[b]=wt_b; zt_o[b]=zt
        r,n,v,u,m2,gt=step_grad(zt,td_o[b],g,s)
        gb=gt.astype(BF)
        kn=spread(ka_o[nxt][:HD],heads)
        wsel=jnp.where(rs,w0,wt).astype(BF)
        csel=jnp.where(rs,c0,ct)
        yk=nn(wsel,kn)+csel
        yq=nn(wt_b,spread(qa_o[b][:HD],heads))+ct
        rr=nn(gb,mp[b])
        e16=rows[b,0:1]*(1.0/MB)
        ke=(ka_o[b][:HD].astype(F32)*e16).astype(BF)
        rw=nt(gb,spread(ke,heads))
        ec=jnp.where(same,jnp.broadcast_to(e16,(L,L)),0.0).astype(BF)
        rc=nt(gb,ec)
        zb_o[b]=yq-rr[:,L:]
        z2=yk-rr[:,:L]
        return z2,jnp.where(rs,w0,wt-rw),jnp.where(rs,c0,ct-rc)
    zt=nn(w0.astype(BF),spread(ka_o[0][:HD],heads))+c0
    lax.fori_loop(0,nb,body,(zt,w0,c0))
    def post(gr,_):
        outs=[]
        for p in range(8):
            b=gr*8+p
            zb=zb_o[b]; cen=zb-avg(zb)
            n=cen*lax.rsqrt(avg(cen*cen)+EPS)
            outs.append((q32[b]+n*g+s)*rows[b,1:2])
        merge_heads(outT,gr,outs,heads)
        return 0
    lax.fori_loop(0,nb//8,post,0)

VM=pl.BlockSpec(memory_space=pltpu.VMEM)
SM=pl.BlockSpec(memory_space=pltpu.SMEM)
AN=pl.BlockSpec(memory_space=pl.ANY)

def pack_consts(w0, c0, g, s):
    heads=w0.shape[0]
    cols=[w0.transpose(2,0,1).reshape(HD,heads*HD)]+[lane_cols(v) for v in (c0,g,s)]
    return jnp.concatenate([jnp.pad(v,((0,0),(0,-v.shape[1]%128))) for v in cols],1)

def unpack_consts(ref, heads):
    wide=(heads*HD+127)//128*128; step=(heads*MB+127)//128*128
    return [ref[:,:heads*HD]]+[ref[:,wide+i*step:wide+i*step+heads*MB] for i in range(3)]

def ttt_fwd(reset, qT,kT,vT, rows, consts):
    T=qT.shape[1]; heads=qT.shape[0]//HD; nb=T//MB; L=heads*MB; S=jax.ShapeDtypeStruct
    outs=[S((heads*HD,T),BF),S((nb,HD,L),F32),S((nb,HD,L),F32),S((nb,HD,L),F32),S((nb,HD+MB,L),BF),S((nb,HD+MB,L),BF),
          S((nb,HD,heads*HD),BF)]
    return pl.pallas_call(functools.partial(fwd_kernel,heads,nb),out_shape=outs,
        in_specs=[SM]+[VM]*5,out_specs=[VM]*len(outs),
        scratch_shapes=[pltpu.VMEM((nb,L,2*L),BF),pltpu.VMEM((nb,HD,L),F32)],
        compiler_params=pltpu.CompilerParams(vmem_limit_bytes=56<<20), name="mix_forward",
        cost_estimate=pl.CostEstimate(flops=T*heads*4000*64*50, bytes_accessed=T*heads*64*40, transcendentals=0))(
            reset,qT,kT,vT,rows,consts)

def bwd_kernel(heads, nb, base, last, reset, dOT, zt_i, zb_i, td_i, qa_i, ka_i, wt_i, rows, consts, *refs):
    if last:
        li=lci=None
    else:
        li,lci=refs[:2]; refs=refs[5:]
    (dqT, dkT, dvT, de_o, dg_o, ds_o, dw0_o, dc0_o, lo, lco,
               n_s, v_s, r_s, m2_s, gb_s, gh_s, nm_s, u_s, uc_s, dq_s, dk_s, du_s, dz_s, h_s, la_s)=refs
    L=heads*MB
    _,_,g,s=unpack_consts(consts,heads)
    same,ri,cj=same_head(heads)
    tri=jnp.where(same&(cj<=ri),1.0/(ri.astype(F32)+1.0),0.0)
    diag=jnp.where(same,1.0,0.0)
    diag_b=diag.astype(BF)
    dg_o[...]=jnp.zeros((HD,L),F32); ds_o[...]=jnp.zeros((HD,L),F32)
    dw0_o[...]=jnp.zeros_like(dw0_o); dc0_o[...]=jnp.zeros_like(dc0_o)
    def pre(gr,_):
        dos=split_heads(dOT,gr,heads)
        dga=jnp.zeros((HD,L),F32); dsa=jnp.zeros((HD,L),F32)
        for p in range(8):
            b=gr*8+p
            dO=dos[p].astype(F32)*rows[b,1:2]
            zb=zb_i[b]; cen=zb-avg(zb); rb=lax.rsqrt(avg(cen*cen)+EPS); nbar=cen*rb
            dga=dga+dO*nbar; dsa=dsa+dO
            dn=dO*g
            dzb=rb*(dn-avg(dn)-nbar*avg(dn*nbar))
            dzb_b=dzb.astype(BF)
            r,n,v,u,m2,gt=step_grad(zt_i[b],td_i[b],g,s)
            gb=gt.astype(BF)
            n_s[b]=n; v_s[b]=v; r_s[b]=r; m2_s[b]=m2; gb_s[b]=gt
            e=rows[b,0:1]
            ka=ka_i[b]; qa=qa_i[b]
            st=tn(qa,ka)*tri
            gh_s[b]=-nn(dzb_b,(st*e).astype(BF))
            dp=-tn(dzb_b,gb)
            de_o[b]=jnp.sum(dp*st,0,keepdims=True)
            dS=(dp*tri*e).astype(BF)
            dq_s[b]=dO+gather_blocks(tn(wt_i[b],dzb_b),heads)+nt(ka[:HD],dS)
            dk_s[b]=nn(qa[:HD],dS)
            prev=jnp.maximum(b-1,0)
            keep=jnp.where(reset[base+b]>0,0.0,1.0)
            nm_s[b]=(tn(ka,ka_i[prev])*(diag*keep)).astype(BF)
            u_s[b]=nt(dzb_b,spread(qa[:HD],heads))
            uc_s[b]=nn(dzb_b,diag_b)
        dg_o[...]+=dga; ds_o[...]+=dsa
        return 0
    lax.fori_loop(0,nb//8,pre,0)
    def body(k,carry):
        ht,la,lc=carry
        b=nb-1-k
        prev=jnp.maximum(b-1,0)
        rs=reset[base+b]>0
        n=n_s[b]; v=v_s[b]; r=r_s[b]; m2=m2_s[b]; gt=gb_s[b]
        h_s[b]=ht
        la_s[b]=la.astype(BF)
        dG=gh_s[b]-(rows[b,0:1]*(1.0/MB))*ht
        da=r*dG
        m3=avg(da); m4=avg(da*n); m6a=avg(dG*gt)
        du=da-m3-n*m4
        dn=(du*g-v*m4)*g-da*m2
        m5=avg(dn); m6=m6a+avg(dn*n)
        dz=(r*(dn-m5-n*m6)).astype(BF)
        du_s[b]=du
        dz_s[b]=dz
        la2=la+u_s[b]; lc2=lc+uc_s[b]
        y=nn(la2.astype(BF),spread(ka_i[prev][:HD],heads))+lc2
        h2=jnp.where(rs,0.0,y)+nn(dz,nm_s[b])
        la3=la2+nt(dz,spread(ka_i[b][:HD],heads)); lc3=lc2+nn(dz,diag_b)
        @pl.when(rs)
        def _():
            dw0_o[...]+=la3; dc0_o[...]+=lc3
        return h2,jnp.where(rs,0.0,la3),jnp.where(rs,0.0,lc3)
    la=jnp.zeros((HD,heads*HD),F32) if last else li[...]
    lc=jnp.zeros((HD,L),F32) if last else lci[...]
    ht=nn(la.astype(BF),spread(ka_i[nb-1][:HD],heads))+lc
    ht,la,lc=lax.fori_loop(0,nb,body,(ht,la,lc))
    lo[...]=la; lco[...]=lc
    def post(gr,_):
        dqs=[];dks=[];dvs=[]
        dga=jnp.zeros((HD,L),F32); dsa=jnp.zeros((HD,L),F32)
        for p in range(8):
            b=gr*8+p
            du=du_s[b]; dug=du*g; gt=gb_s[b]
            dga=dga+du*v_s[b]+dug*n_s[b]; dsa=dsa+dug
            dvs.append(-dug)
            dqs.append(dq_s[b])
            de_o[b]=de_o[b]-avg(gt*h_s[b])*(HD/MB)
            dks.append(dug+dk_s[b]-(rows[b,0:1]*(1.0/MB))*gather_blocks(tn(la_s[b],gt.astype(BF)),heads)
                       +gather_blocks(tn(wt_i[b],dz_s[b]),heads))
        merge_heads(dqT,gr,dqs,heads); merge_heads(dkT,gr,dks,heads); merge_heads(dvT,gr,dvs,heads)
        dg_o[...]+=dga; ds_o[...]+=dsa
        return 0
    lax.fori_loop(0,nb//8,post,0)

def ttt_bwd(part, parts, reset, dOT, zt,zb,td,qa,ka,wt,rows,consts, carry=None):
    T=dOT.shape[1]//parts; heads=dOT.shape[0]//HD; nb=T//MB; L=heads*MB; S=jax.ShapeDtypeStruct
    W=heads*HD; last=part==parts-1
    outs=[S((W,T*parts),BF)]*3+[S((nb,1,L),F32)]+[S((HD,L),F32)]*2+[S((HD,W),F32),S((HD,L),F32)]*2
    V=pltpu.VMEM
    scr=[V((nb,HD,L),F32),V((nb,HD,L),F32),V((nb,1,L),F32),V((nb,1,L),F32),V((nb,HD,L),F32),V((nb,HD,L),F32),
         V((nb,L,L),BF),V((nb,HD,W),F32),V((nb,HD,L),F32),V((nb,HD,L),F32),V((nb,HD,L),F32),V((nb,HD,L),F32),
         V((nb,HD,L),BF),V((nb,HD,L),F32),V((nb,HD,W),BF)]
    def whole(*dims): return pl.BlockSpec(dims,lambda i:(0,)*len(dims))
    def third(*dims): return pl.BlockSpec((nb,)+dims,lambda i:(part,)+(0,)*len(dims))
    nat=pl.BlockSpec((W,T),lambda i:(0,part))
    ins=[SM,nat]+[third(HD,L)]*3+[third(HD+MB,L)]*2+[third(HD,W),third(2,L),whole(*consts.shape)]
    args=[reset,dOT,zt,zb,td,qa,ka,wt,rows,consts]
    alias={}
    if not last:
        ins+=[whole(HD,W),whole(HD,L)]+[AN]*3
        alias={12:0,13:1,14:2}
        args+=list(carry)
    return pl.pallas_call(functools.partial(bwd_kernel,heads,nb,part*nb,last),out_shape=outs,grid=(1,),
        in_specs=ins,out_specs=[nat]*3+[whole(nb,1,L)]+[whole(HD,L)]*2+[whole(HD,W),whole(HD,L)]*2,
        scratch_shapes=scr,input_output_aliases=alias,
        compiler_params=pltpu.CompilerParams(vmem_limit_bytes=60<<20), name="mix_backward",
        cost_estimate=pl.CostEstimate(flops=T*heads*4000*64*60, bytes_accessed=T*heads*64*60, transcendentals=0))(*args)

def lane_rows(x, heads):
    T=x.shape[1]
    return x.reshape(heads,T//MB,MB).transpose(1,0,2).reshape(T//MB,1,heads*MB)
def lane_cols(x):
    return jnp.repeat(x.T,MB,axis=1)


ROWS = 64


def fetch(pieces, spots, buf, sems):
    copies = []
    for i, p in enumerate(pieces):
        at = pl.ds(pl.multiple_of(spots[i], 16), p.shape[0])
        copies.append(pltpu.make_async_copy(p, buf.at[at], sems.at[i]))
        copies[-1].start()
    for c in copies:
        c.wait()


def fold(buf, width, f):
    def add(i, acc):
        v = f(buf[pl.ds(pl.multiple_of(i * ROWS, ROWS), ROWS), :].astype(F32))
        return acc + jnp.sum(v.reshape(ROWS // 8, 8, v.shape[1]), 0)

    acc = lax.fori_loop(0, width // ROWS, add, jnp.zeros((8, buf.shape[1]), F32))
    return jnp.sum(acc, 0, keepdims=True)


def rms_kernel(n, lane, width, spots, gains, *refs):
    pieces, (out, scale_out, buf, sems) = refs[:n], refs[n:]
    fetch(pieces, spots, buf, sems)
    scale = lax.rsqrt(fold(buf, width, lambda v: v * v) * (1.0 / width) + EPS)
    scale_out[...] = scale

    def write(i, _):
        at = pl.ds(pl.multiple_of(i * ROWS, ROWS), ROWS)
        gain = gains[at, lane:lane + 1].astype(F32)
        out[at, :] = (buf[at, :].astype(F32) * scale * gain).astype(BF)
        return 0

    lax.fori_loop(0, width // ROWS, write, 0)


def mixed_kernel(n, width, spots, gains, gates, *refs):
    pieces, (out, mean_out, scale_out, buf, sems) = refs[:n], refs[n:]
    fetch(pieces, spots, buf, sems)
    mean = fold(buf, width, lambda v: v) * (1.0 / width)
    scale = lax.rsqrt(fold(buf, width, lambda v: (v - mean) * (v - mean)) * (1.0 / width) + EPS)
    mean_out[...] = mean
    scale_out[...] = scale

    def write(i, _):
        at = pl.ds(pl.multiple_of(i * ROWS, ROWS), ROWS)
        normed = (buf[at, :].astype(F32) - mean) * scale * gains[at, 1:2].astype(F32) + gains[at, 2:3].astype(F32)
        out[at, :] = (normed * jax.nn.gelu(gates[at, :].astype(F32), approximate=True)).astype(BF)
        return 0

    lax.fori_loop(0, width // ROWS, write, 0)


def rms_rows(pieces, spots, gains, lane, tok, width):
    n = len(pieces)
    return pl.pallas_call(
        functools.partial(rms_kernel, n, lane, width),
        out_shape=[jax.ShapeDtypeStruct((width, tok), BF), jax.ShapeDtypeStruct((1, tok), F32)],
        in_specs=[SM, VM] + [AN] * n, out_specs=[VM, VM],
        scratch_shapes=[pltpu.VMEM((width, tok), BF), pltpu.SemaphoreType.DMA((n,))],
        compiler_params=pltpu.CompilerParams(vmem_limit_bytes=40 << 20), name="rms_rows",
        cost_estimate=pl.CostEstimate(flops=8 * width * tok, bytes_accessed=4 * width * tok, transcendentals=0),
    )(spots, gains, *pieces)


def mixed_rows(pieces, spots, gates, gains, tok, width):
    n = len(pieces)
    return pl.pallas_call(
        functools.partial(mixed_kernel, n, width),
        out_shape=[jax.ShapeDtypeStruct((width, tok), BF)] + [jax.ShapeDtypeStruct((1, tok), F32)] * 2,
        in_specs=[SM, VM, VM] + [AN] * n, out_specs=[VM] * 3,
        scratch_shapes=[pltpu.VMEM((width, tok), BF), pltpu.SemaphoreType.DMA((n,))],
        compiler_params=pltpu.CompilerParams(vmem_limit_bytes=48 << 20), name="mixed_rows",
        cost_estimate=pl.CostEstimate(flops=20 * width * tok, bytes_accessed=6 * width * tok, transcendentals=0),
    )(spots, gains, gates, *pieces)


def hold(x, *deps):
    return lax.optimization_barrier((x,) + deps)[0]


def spread_pieces(x, devs, *deps):
    if devs != 8:
        return [lax.all_gather(x, "head", axis=0, tiled=True)]
    rows = x.shape[0]

    def swap(v, bit):
        return lax.ppermute(v, "head", [(i, i ^ bit) for i in range(8)])

    along_x = swap(x, 2)
    along_y = swap(x, 4)
    peer = swap(x, 1)
    if deps:
        along_x, along_y = hold(along_x, *deps), hold(along_y, *deps)
    diag_low = swap(along_x[:rows // 2], 4)
    diag_high = swap(along_y[rows // 2:], 2)
    return [x, peer, along_x, swap(along_x, 1), along_y, swap(along_y, 1),
            diag_low, diag_high, swap(diag_low, 1), swap(diag_high, 1)]


def piece_spots(own, devs):
    if devs != 8:
        return jnp.zeros((1,), jnp.int32)
    me = lax.axis_index("head")
    half = own // 2
    places = [(0, 0), (1, 0), (2, 0), (3, 0), (4, 0), (5, 0), (6, 0), (6, half), (7, 0), (7, half)]
    return jnp.stack([(me ^ bits) * own + off for bits, off in places]).astype(jnp.int32)


from jax.sharding import PartitionSpec as P


def col_sum(x):
    return jnp.sum(x, 0, keepdims=True)


def gelu_tanh(values):
    return jax.nn.gelu(values, approximate=True)


def layout(seq_lens, row_count):
    padded = (seq_lens + MB - 1) // MB * MB
    starts = jnp.cumsum(padded) - padded
    positions = jnp.arange(row_count, dtype=jnp.int32)
    inside = (positions[None, :] >= starts[:, None]) & (positions[None, :] < (starts + seq_lens)[:, None])
    valid_rows = jnp.any(inside, axis=0).astype(F32)
    block_first = jnp.arange(row_count // MB, dtype=jnp.int32) * MB
    begins = jnp.any((starts[:, None] == block_first[None, :]) & (seq_lens[:, None] > 0), axis=0)
    return valid_rows, (begins | (block_first == 0)).astype(jnp.int32)


class LineSum:
    def __init__(self, x):
        self.x = x
        self.near = lax.ppermute(x, "dp", [(0, 1), (3, 2)])

    def cross(self, *deps):
        near = hold(self.near, *deps) if deps else self.near
        self.half = (self.x.astype(F32) + near.astype(F32)).astype(BF)
        self.across = lax.ppermute(self.half, "dp", [(1, 2), (2, 1)])

    def back(self, *deps):
        across = hold(self.across, *deps) if deps else self.across
        self.total = (self.half.astype(F32) + across.astype(F32)).astype(BF)
        self.ends = lax.ppermute(self.total, "dp", [(1, 0), (2, 3)])

    def result(self, *deps):
        ends = hold(self.ends, *deps) if deps else self.ends
        at = lax.axis_index("dp")
        return jnp.where((at == 0) | (at == 3), ends, self.total).astype(F32)


class WholeSum:
    def __init__(self, x):
        self.x = self.half = self.total = x

    def cross(self, *deps):
        pass

    def back(self, *deps):
        pass

    def result(self, *deps):
        return lax.psum(self.x, "dp").astype(F32)


def on_device(
    tokens, lengths, attn_gain, w_query, w_key, w_value, w_gate, w_rate, rate_bias,
    inner_weight, inner_bias, inner_gain, inner_shift, post_gain, post_shift, w_out,
    ffn_gain, w_hidden_gate, w_hidden_up, w_down, out_grad,
):
    tok = tokens.shape[1]
    own = tokens.shape[0]
    heads = inner_weight.shape[0]
    devs = lax.axis_size("head")
    width = own * devs
    line = LineSum if lax.axis_size("dp") == 4 else WholeSum

    def gather(x):
        return lax.all_gather(x, "head", axis=0, tiled=True)

    valid, reset = layout(lengths, tok)
    vrow = valid[None, :]
    spots = piece_spots(own, devs)
    consts = pack_consts(*[v.astype(F32) for v in (inner_weight, inner_bias, inner_gain, inner_shift)])
    gains = lax.all_gather(jnp.stack([attn_gain, post_gain, post_shift, ffn_gain]), "head", axis=1, tiled=True)
    gains = jnp.pad(gains.T, ((0, 0), (0, 124)))
    tok_pieces = spread_pieces(tokens, devs, gains, consts)
    g_full = gather(hold(out_grad, *tok_pieces[-4:-2]))
    nin, q1 = rms_rows(tok_pieces, spots, gains, 0, tok, width)
    gate = nn(w_gate, nin).astype(BF)
    gates = gather(hold(gate, g_full) if devs != 8 else gate)
    nin_q = hold(nin, gate)
    q_t = nn(w_query, nin_q)
    k_t = nn(w_key, nin_q)
    v_t = nn(w_value, nin_q)
    logits = tn(w_rate, nin) + rate_bias.astype(F32)[:, None]
    sig = jax.nn.sigmoid(logits)
    masked = sig * vrow
    er = lane_rows(masked * (1.0 / HD), heads)
    vr = lane_rows(jnp.broadcast_to(vrow, (heads, tok)), heads)
    rows = jnp.concatenate([er, vr], 1)
    mixer_own, zt, zb, td, qa, ka, wt = ttt_fwd(reset, q_t, k_t, v_t, rows, consts)

    mixed, mean3, r3 = mixed_rows(spread_pieces(mixer_own, devs), spots, gates, gains, tok, width)
    hidden = tokens.astype(F32) + nn(w_out, mixed)
    hidden_low = hidden.astype(BF)
    nmid, q2 = rms_rows(spread_pieces(hidden_low, devs), spots, gains, 3, tok, width)
    gate_val = nn(w_hidden_gate, nmid)
    up_val = nn(w_hidden_up, nmid)
    sg = jax.nn.sigmoid(gate_val)
    act = (gate_val * sg * up_val).astype(BF)

    def halves(x):
        cut = x.shape[0] // 32 * 16
        return line(x[:cut]), line(x[cut:])

    d0, d1 = halves(nt(act, g_full).astype(BF))
    g_act = nn(w_down, hold(g_full, d0.x))
    g_up = (g_act * gate_val * sg).astype(BF)
    g_gate = (g_act * up_val * sg * (1.0 + gate_val * (1.0 - sg))).astype(BF)
    gn_part = (tn(w_hidden_gate, g_gate) + tn(w_hidden_up, g_up)).astype(BF)
    gn = lax.psum_scatter(gn_part, "head", scatter_dimension=0, tiled=True)
    h0, h1 = halves(nt(hold(g_gate, gn_part), nmid).astype(BF))
    u0, u1 = halves(nt(hold(g_up, gn_part), nmid).astype(BF))
    d0.cross(u1.x)
    gn = hold(gn, d0.half).astype(F32)
    hid_own = hidden_low.astype(F32)
    fg_own = ffn_gain.astype(F32)[:, None]
    here = lax.axis_index("head") + 1
    marks = lax.broadcasted_iota(jnp.int32, (1, 128), 1)
    rates = jnp.where(marks == 0, jnp.sum(masked), jnp.where(marks == here, jnp.max(masked), 0.0))
    mid_dot, rates = lax.psum((col_sum(hid_own * fg_own * gn), rates), "head")
    g_ffn_gain = jnp.sum(gn * hid_own * q2, 1)
    g_hidden = out_grad.astype(F32) + q2 * fg_own * gn - hid_own * q2**3 * mid_dot / width
    g_branch = g_hidden.astype(BF)
    gm_part = tn(w_out, g_branch).astype(BF)
    gm = lax.psum_scatter(gm_part, "head", scatter_dimension=0, tiled=True)
    d1.cross(gm_part)
    d0.back(gm_part, d1.half)
    so = line(nt(hold(g_branch, d0.total), mixed).astype(BF))
    ffn_part = tn(w_down, hold(act, so.x)).astype(BF)
    h0.cross(so.x, ffn_part)
    d1.back(h0.half)
    gm = hold(gm, d1.total).astype(F32)
    h1.cross(gm)
    h0.back(h1.half)
    n3 = (mixer_own.astype(F32) - mean3) * r3
    pg_own = post_gain.astype(F32)[:, None]
    ps_own = post_shift.astype(F32)[:, None]
    a_own, gelu_pull = jax.vjp(gelu_tanh, gate.astype(F32))
    g_post_gain = jnp.sum(gm * a_own * n3, 1)
    g_post_shift = jnp.sum(gm * a_own, 1)
    g_gate_pre = gelu_pull(gm * (n3 * pg_own + ps_own))[0].astype(BF)
    m = gm * a_own * pg_own
    s_plain, s_norm = lax.psum((col_sum(m), col_sum(m * n3)), "head")
    g_mixer = r3 * (m - s_plain / width - n3 * s_norm / width)
    ffn = lax.psum_scatter(hold(ffn_part, gm), "head", scatter_dimension=0, tiled=True)
    result = (hidden + ffn.astype(F32)).astype(BF)
    sg_w = line(nt(hold(g_gate_pre, s_plain), nin).astype(BF))
    g_mixer = hold(g_mixer, sg_w.x, h0.total)
    saved = (zt, zb, td, qa, ka, wt, rows, consts)
    b1 = ttt_bwd(1, 2, reset, g_mixer, *saved)
    u0.cross(b1[8])
    h1.back(b1[8], u0.half)
    lam, lam_c = hold(b1[8], h1.total), b1[9]
    b0 = ttt_bwd(0, 2, reset, g_mixer, *saved, carry=(lam, lam_c) + tuple(b1[:3]))
    dq, dk, dv = b0[:3]
    de = jnp.concatenate([b0[3], b1[3]], 0)
    dgl, dsl, dw0, dc0 = [b0[i] + b1[i] for i in range(4, 8)]
    u1.cross(dq)
    de_rows = de.reshape(tok // MB, heads, MB).transpose(1, 0, 2).reshape(heads, tok)
    g_logits = de_rows * vrow * (1.0 / HD) * sig * (1.0 - sig)
    gl = g_logits.astype(BF)
    g_inner_w = dw0.reshape(HD, heads, HD).transpose(1, 2, 0)
    g_inner_b = dc0.reshape(HD, heads, MB)[:, :, 0].T
    g_inner_g = dgl.reshape(HD, heads, MB).sum(-1).T
    g_inner_s = dsl.reshape(HD, heads, MB).sum(-1).T
    nin_l = hold(nin, u1.half)
    q = line(nt(dq, nin_l).astype(BF))
    k = line(nt(dk, nin_l).astype(BF))
    v0, v1 = halves(nt(dv, nin_l).astype(BF))
    u0.back(v1.x)
    gi_part = hold((tn(w_query, dq) + tn(w_key, dk) + tn(w_value, dv) + tn(w_gate, g_gate_pre) + nn(w_rate, gl)).astype(BF), u0.total)
    gi = lax.psum_scatter(gi_part, "head", scatter_dimension=0, tiled=True)
    so.cross(gi_part)
    g_wr = nt(gl, hold(nin_l, so.half))
    u1.back(g_wr)
    sg_w.cross(u1.total)
    so.back(sg_w.half)
    q.cross(so.total)
    gi = hold(gi, q.half).astype(F32)
    x_own = tokens.astype(F32)
    ag_own = attn_gain.astype(F32)[:, None]
    in_dot = lax.psum(col_sum(x_own * ag_own * gi), "head")
    sg_w.back(in_dot)
    k.cross(sg_w.total)
    g_attn_gain = jnp.sum(gi * x_own * q1, 1)
    g_tokens = g_hidden + q1 * ag_own * gi - x_own * q1**3 * in_dot / width
    there = lax.axis_index("dp") + 1
    top = jnp.max(jnp.where((marks > 0), rates, 0.0))
    rates = jnp.where(marks == 0, rates[0, 0], jnp.where(marks == there, top, 0.0))
    small = [g_attn_gain, g_wr, jnp.sum(g_logits, 1), g_inner_w, g_inner_b, g_inner_g, g_inner_s,
             g_post_gain, g_post_shift, g_ffn_gain]
    small = lax.psum([hold(x.astype(BF), k.half) for x in small] + [rates], "dp")
    rates = small.pop()
    s_attn, s_wr, s_rb, s_iw, s_ib, s_ig, s_is, s_pg, s_ps, s_fg = [x.astype(F32) for x in small]
    mean_rate = rates[0, 0] / (tok * lax.axis_size("dp") * heads * devs)
    max_rate = jnp.max(jnp.where(marks > 0, rates, 0.0))
    q.back(s_attn)
    v0.cross(q.total)
    v1.cross(v0.half)
    k.back(v1.half)
    v0.back(k.total)
    v1.back(v0.total)

    def joined(*parts):
        return jnp.concatenate([s.result() for s in parts], 0)

    return (
        result, g_tokens, s_attn, q.result(), k.result(), joined(v0, v1), sg_w.result(),
        s_wr.T, s_rb, s_iw, s_ib, s_ig, s_is, s_pg, s_ps, so.result(),
        s_fg, joined(h0, h1), joined(u0, u1), joined(d0, d1), mean_rate, max_rate,
    )


def solution(mesh):
    h = P("head")
    m = P("head", None)
    c = P("head", None, None)
    t = P("head", "dp")
    r = P(None, "head")
    ins = (t, P("dp"), h, m, m, m, m, r, h, c, m, m, m, h, h, m, h, m, m, m, t)
    outs = (t, t, h, m, m, m, m, r, h, c, m, m, m, h, h, m, h, m, m, m, P(), P())
    return jax.shard_map(on_device, mesh=mesh, in_specs=ins, out_specs=outs, check_vma=False)
```

time: 1150 us -> 821 us (0.71)
  waiting for transfers between devices: 692 us -> 212 us
  starting transfers between devices: 0.84 us -> 102 us
  other arithmetic: 87.9 us -> 120 us
  Pallas kernels: 82.1 us -> 106 us
  local copies, waits for them, and re-layouts: 21.1 us -> 38.6 us
  matrix products: 130 us -> 114 us
  blocking collectives: 116 us -> 103 us
    psum x2 -> x0, waiting for transfers between devices: 440 us -> none  [the longest x1 428 us: over_dp(): return lax.psum(v.astype(BF), 'dp').astype(F32)]
    ppermute x0 -> x63, waiting for transfers between devices: none -> 200 us  [the longest x12 101 us: back(): self.ends = lax.ppermute(self.total, 'dp', [(1, 0), (2, 3)])]
    all_gather x5 -> x2, waiting for transfers between devices: 141 us -> 0.02 us  [gather(): return lax.all_gather(x, 'head', axis=0, tiled=True)]
    ppermute x0 -> x63, starting transfers between devices: none -> 102 us  [the longest x12 48.4 us: __init__(): self.near = lax.ppermute(x, 'dp', [(0, 1), (3, 2)])]
    reduce_scatter x3 -> x4, waiting for transfers between devices: 109 us -> 11.9 us  [the longest x1 11.9 us: on_device(): gn = lax.psum_scatter(gn_part, 'head', scatter_dimension=0, tiled=True)]
    pmax x1 -> x0, blocking collectives: 39.5 us -> none  [on_device(): max_rate = lax.pmax(jnp.max(masked), ('dp', 'head'))]
    psum x2 -> x4, blocking collectives: 43.1 us -> 78.8 us  [the longest x2 54.1 us: on_device(): lax.psum([hold(x.astype(BF), k.half) for x in small] + [rates], 'dp')]
    convert_element_type x25 -> x40, other arithmetic: 51.4 us -> 77.2 us  [the longest x12 31.3 us: back(): self.total = (self.half.astype(F32) + across.astype(F32)).astype(BF)]
  transfers between devices with their start and end apart: 10 -> 69, of which waited for: 9 -> 19; matrix products, arithmetic and copies ran while one was open for 13% -> 28% of each run, Pallas kernels for 4% -> 12%
where the time goes in v2:
time: 821 us; the launch traced here: 813 us
  waiting for transfers between devices  212 us (26%)
  other arithmetic  120 us (15%)
  matrix products  114 us (14%)
  Pallas kernels  106 us (13%)
  blocking collectives  103 us (13%)
  starting transfers between devices  102 us (12%)
  local copies, waits for them, and re-layouts  38.6 us (5%)
  between operations  17 us (2%)
    ppermute x12, waiting for transfers between devices, back(): self.ends = lax.ppermute(self.total, 'dp', [(1, 0), (2, 3)])  101 us
    ppermute x27, waiting for transfers between devices, swap(): return lax.ppermute(v, 'head', [(i, i ^ bit) for i in range(8)])  56.8 us
    psum x2, blocking collectives, on_device(): lax.psum([hold(x.astype(BF), k.half) for x in small] + [rates], 'dp')  54.1 us
    ppermute x12, starting transfers between devices, __init__(): self.near = lax.ppermute(x, 'dp', [(0, 1), (3, 2)])  48.4 us
    pallas_call x2, Pallas kernels, ttt_bwd(): pl.pallas_call(functools.partial(bwd_kernel, heads, nb, part * nb, last),...  46.3 us
    ppermute x12, waiting for transfers between devices, __init__(): self.near = lax.ppermute(x, 'dp', [(0, 1), (3, 2)])  42.3 us
    dot_general x9, matrix products, nn(): lax.dot_general(a, b, (((1,), (0,)), ((), ())), preferred_element_type=F32)  41.7 us
    dot_general x9, matrix products, tn(): lax.dot_general(a, b, (((0,), (0,)), ((), ())), preferred_element_type=F32)  38.6 us
  transfers between devices with their start and end apart: 69, of which 19 were waited for; matrix products, arithmetic and copies ran while one was open for 28% of the time, Pallas kernels for 12%

profile of v2, /device:TPU:0, one launch (start us, length us, event | category | flops | bytes accessed | tf_op | source)
XLA Modules:
  0.0 812.7 jit_solution(1906849870722394812)
XLA Ops:
  17.9 12.0 %all_gather.9 = bf16[4,2048]{0,1:T(8,128)(2,1)S(1)} all-gather(bf16[4,256]{0,1:T(8,128)(2,1)S(1)} %copy.161), channel_id=1, replica_groups=mesh['dp'=4,'head'=8] {'head'}, dimensions={1}, use_global_device_ids=true | all-gather | bytes 18432 | tf_op jit(solution)/shard_map/all_gather | solution.py:451
  35.3 5.6 collective-permute-done.5.refs_6_
  45.1 6.0 rms_rows.2
  56.6 4.9 convolution_bitcast_fusion.3.qT
  68.2 37.5 %mix_forward.1 = (bf16[256,1024]{1,0:T(8,128)(2,1)}, f32[64,64,64]{2,1,0:T(8,128)}, f32[64,64,64]{2,1,0:T(8,128)}, f32[64,64,64]{2,1,0:T(8,128)}, bf16[64,80,64]...) custom-call(s32[64]{0:T(128)} %or_convert_fusion.reset, ...), custom_call_target="tpu_custom_call" | custom-call | flops 52428800000 | bytes 10485760 | tf_op jit(solution)/shard_map/mix_forward/pallas_call | solution.py:134
  107.7 16.0 %collective-permute-done.10.refs_2_ = bf16[256,1024]{1,0:T(8,128)(2,1)S(1)} collective-permute-done((bf16[256,1024]{1,0:T(8,128)(2,1)}, bf16[256,1024]{1,0:T(8,128)(2,1)S(1)}, u32[]{:S(2)}, u32[]{:S(2)}) %collective-permute-start.10) | collective-permute-done | bytes 524320 | tf_op jit(solution)/shard_map/ppermute | solution.py:353
  126.4 11.6 %collective-permute-done.14.refs_6_ = bf16[128,1024]{1,0:T(8,128)(2,1)S(1)} collective-permute-done((bf16[128,1024]{1,0:T(8,128)(2,1)S(1)}, bf16[128,1024]{1,0:T(8,128)(2,1)S(1)}, u32[]{:S(2)}, u32[]{:S(2)}) %collective-permute-start.14) | collective-permute-done | bytes 262176 | tf_op jit(solution)/shard_map/ppermute | solution.py:353
  153.9 12.4 %mixed_rows.1 = (bf16[2048,1024]{1,0:T(8,128)(2,1)}, f32[1,1024]{1,0:T(1,128)S(1)}, f32[1,1024]{1,0:T(1,128)S(1)}) custom-call(s32[10]{0:T(128)S(1)} %stack.58.spots, bf16[2048,128]{1,0:T(8,128)(2,1)S(1)} %pad.14.gains, bf16[2048,1024]{1,0:T(8,128)(2,1)} %all-gather.3.cloned.1.call-done.gates, bf16[256,1024]{1,0:T(8,128)(2,1)S(1)} %copy-done.12, ...), custom_call_target="tpu_custom_call" | custom-call | flops 41943040 | bytes 12582912 | tf_op jit(solution)/shard_map/mixed_rows/pallas_call | solution.py:333
  166.3 4.5 fusion.57
  172.8 11.8 %collective-permute-done.19.refs_2_ = bf16[256,1024]{1,0:T(8,128)(2,1)S(1)} collective-permute-done((bf16[256,1024]{1,0:T(8,128)(2,1)S(1)}, bf16[256,1024]{1,0:T(8,128)(2,1)S(1)}, u32[]{:S(2)}, u32[]{:S(2)}) %collective-permute-start.19) | collective-permute-done | bytes 524320 | tf_op jit(solution)/shard_map/ppermute | solution.py:353
  187.3 4.7 collective-permute-done.23.refs_6_
  196.0 4.3 rms_rows.3
  200.3 3.1 fusion.63
  205.0 5.1 fusion.7
  210.1 5.9 convolution_convert_fusion.2
  217.4 3.9 fusion.6
  221.3 3.7 fusion.58
  225.1 5.4 fusion
  230.6 3.8 collective-permute-start.27
  235.7 6.2 convolution_convert_fusion.1
  245.6 19.6 %collective-permute-done.27 = bf16[336,2048]{1,0:T(8,128)(2,1)S(1)} collective-permute-done((bf16[336,2048]{1,0:T(8,128)(2,1)}, bf16[336,2048]{1,0:T(8,128)(2,1)S(1)}, u32[]{:S(2)}, u32[]{:S(2)}) %collective-permute-start.27) | collective-permute-done | bytes 1376288 | tf_op jit(solution)/shard_map/ppermute | solution.py:400
  269.8 11.9 %reduce-scatter.5.cloned.1.call-done = bf16[256,1024]{1,0:T(8,128)(2,1)} async-done(((bf16[2048,1024]{1,0:T(8,128)(2,1)}), bf16[256,1024]{1,0:T(8,128)(2,1)}) %reduce-scatter.5.cloned.1.call-update) | async-done | bytes 524304 | tf_op jit(solution)/shard_map/reduce_scatter | solution.py:488
  283.7 12.7 %psum.112 = f32[1024]{0:T(1024)S(1)} all-reduce(f32[1024]{0:T(1024)S(1)} %get-tuple-element.196), channel_id=1, replica_groups=mesh['dp'=4,'head'=8] {'head'}, use_global_device_ids=true, to_apply=%region_5.6 | all-reduce | flops 1024 | bytes 8192 | tf_op jit(solution)/shard_map/psum | solution.py:498
  298.9 3.3 convert_bitcast_fusion.1
  302.3 5.9 convolution_convert_fusion
  309.5 4.5 collective-permute-start.31
  314.0 3.2 add_convert_fusion.7
  319.2 3.4 add_convert_fusion.12
  326.5 5.2 convert_bitcast_fusion
  331.7 10.1 %collective-permute-done.31 = bf16[336,2048]{1,0:T(8,128)(2,1)} collective-permute-done((bf16[336,2048]{1,0:T(8,128)(2,1)}, bf16[336,2048]{1,0:T(8,128)(2,1)}, u32[]{:S(2)}, u32[]{:S(2)}) %collective-permute-start.31) | collective-permute-done | bytes 1376288 | tf_op jit(solution)/shard_map/ppermute | solution.py:400
  341.8 3.5 add_convert_fusion.11
  345.3 3.5 add_convert_fusion.6
  354.2 9.2 %collective-permute-start.37 = (bf16[352,2048]{1,0:T(8,128)(2,1)}, bf16[352,2048]{1,0:T(8,128)(2,1)}, u32[]{:S(2)}, u32[]{:S(2)}) collective-permute-start(bf16[352,2048]{1,0:T(8,128)(2,1)} %slice.74), channel_id=1, source_target_pairs={{0,8},{24,16},{1,9},{25,17},{2,10},{26,18},{3,11},{27,19},{4,12},{... | collective-permute-start | bytes 4325384 | tf_op jit(solution)/shard_map/ppermute | solution.py:400
  371.4 15.3 %collective-permute-done.62 = bf16[352,2048]{1,0:T(8,128)(2,1)} collective-permute-done((bf16[352,2048]{1,0:T(8,128)(2,1)}, bf16[352,2048]{1,0:T(8,128)(2,1)}, u32[]{:S(2)}, u32[]{:S(2)}) %collective-permute-start.62) | collective-permute-done | bytes 1441824 | tf_op jit(solution)/shard_map/ppermute | solution.py:410
  390.7 3.2 maximum_convert_fusion.2
  397.1 12.0 %all-reduce.5 = (f32[1024]{0:T(1024)S(1)}, f32[1,1024]{1,0:T(1,128)S(1)}) all-reduce(f32[1024]{0:T(1024)S(1)} %get-tuple-element.193, f32[1,1024]{1,0:T(1,128)S(1)} %bitcast.210), channel_id=1, replica_groups=mesh['dp'=4,'head'=8] {'head'}, use_global_device_ids=true, to_apply=%region_11.12 | all-reduce | flops 2048 | bytes 16384 | tf_op jit(solution)/shard_map/psum | solution.py:521
  409.1 3.7 subtract_multiply_fusion
  412.9 12.6 %collective-permute-done.33 = bf16[352,2048]{1,0:T(8,128)(2,1)} collective-permute-done((bf16[352,2048]{1,0:T(8,128)(2,1)}, bf16[352,2048]{1,0:T(8,128)(2,1)}, u32[]{:S(2)}, u32[]{:S(2)}) %collective-permute-start.33) | collective-permute-done | bytes 1441824 | tf_op jit(solution)/shard_map/ppermute | solution.py:400
  432.4 3.4 add_convert_fusion.10
  437.1 23.2 %mix_backward.2 = (bf16[256,1024]{1,0:T(8,128)(2,1)}, bf16[256,1024]{1,0:T(8,128)(2,1)}, bf16[256,1024]{1,0:T(8,128)(2,1)}, f32[32,1,64]{2,1,0:T(1,128)}, f32[64...) custom-call(s32[64]{0:T(128)} %or_convert_fusion.reset, ...), custom_call_target="tpu_custom_call" | custom-call | flops 31457280000 | bytes 7864320 | tf_op jit(solution)/shard_map/mix_backward/pallas_call | solution.py:252
  460.3 8.8 %collective-permute-start.41 = (bf16[256,2048]{1,0:T(8,128)(2,1)}, bf16[256,2048]{1,0:T(8,128)(2,1)}, u32[]{:S(2)}, u32[]{:S(2)}) collective-permute-start(bf16[256,2048]{1,0:T(8,128)(2,1)} %convolution_convert_fusion.6), channel_id=1, source_target_pairs={{0,8},{24,16},{1,9},{25,17},{2,10},{26,18},{3,11},{27,19},{4,12},{... | collective-permute-start | bytes 3145736 | tf_op jit(solution)/shard_map/ppermute | solution.py:400
  469.0 5.9 fusion.62
  482.1 3.5 add_convert_fusion.4
  485.6 23.2 %mix_backward.3 = (bf16[256,1024]{1,0:T(8,128)(2,1)}, bf16[256,1024]{1,0:T(8,128)(2,1)}, bf16[256,1024]{1,0:T(8,128)(2,1)}, f32[32,1,64]{2,1,0:T(1,128)}, f32[64...) custom-call(s32[64]{0:T(128)} %or_convert_fusion.reset, ...), custom_call_target="tpu_custom_call", output_to_operand_aliasing={{0}: (12, {}), {1}: (13, {}), {2}: (14, {})} | custom-call | flops 31457280000 | bytes 7864320 | tf_op jit(solution)/shard_map/mix_backward/pallas_call | solution.py:252
  508.9 3.0 add_convert_fusion.3
  514.0 3.5 convolution_convert_fusion.5
  518.6 3.6 collective-permute-start.48
  526.8 4.6 fusion.61
  531.5 4.6 fusion.59
  536.1 4.5 fusion.60
  540.7 13.8 %fusion.1 = bf16[2048,1024]{1,0:T(8,128)(2,1)} fusion(bf16[2048,4]{0,1:T(4,128)(2,1)S(1)} %copy-done.64, f32[1024,2048]{0,1:T(8,128)} %fusion.62, f32[1024,2048]{0,1:T(8,128)} %fusion.61, f32[1024,2048]{0,1:T(8,128)} %fusion.59, f32[1024,2048]{0,1:T(8,128)} %fusion.60, bf16[4,1024]{1,0:T(4,128)(2,1)S(1)} %get-tuple-element.227), kind=kOutput, calls=%fused_computation.8 | convolution fusion | flops 27262976 | bytes 37773312 | tf_op jit(solution)/shard_map/dot_general | solution.py:9
  554.5 3.0 add_convert_fusion.21
  559.7 3.6 fusion.47
  571.1 5.4 collective-permute-start.38
  587.6 14.2 %collective-permute-done.58 = bf16[352,2048]{1,0:T(8,128)(2,1)S(1)} collective-permute-done((bf16[352,2048]{1,0:T(8,128)(2,1)S(1)}, bf16[352,2048]{1,0:T(8,128)(2,1)S(1)}, u32[]{:S(2)}, u32[]{:S(2)}) %collective-permute-start.58) | collective-permute-done | bytes 1441824 | tf_op jit(solution)/shard_map/ppermute | solution.py:410
  604.6 3.2 maximum_convert_fusion
  609.2 20.6 %collective-permute-done.56 = bf16[256,2048]{1,0:T(8,128)(2,1)S(1)} collective-permute-done((bf16[256,2048]{1,0:T(8,128)(2,1)S(1)}, bf16[256,2048]{1,0:T(8,128)(2,1)S(1)}, u32[]{:S(2)}, u32[]{:S(2)}) %collective-permute-start.56) | collective-permute-done | bytes 1048608 | tf_op jit(solution)/shard_map/ppermute | solution.py:410
  633.0 18.6 %collective-permute-done.60 = bf16[352,2048]{1,0:T(8,128)(2,1)S(1)} collective-permute-done((bf16[352,2048]{1,0:T(8,128)(2,1)S(1)}, bf16[352,2048]{1,0:T(8,128)(2,1)S(1)}, u32[]{:S(2)}, u32[]{:S(2)}) %collective-permute-start.60) | collective-permute-done | bytes 1441824 | tf_op jit(solution)/shard_map/ppermute | solution.py:410
  653.4 3.2 maximum_convert_fusion.1
  660.5 12.0 %all-reduce.4 = (f32[1,1024]{1,0:T(1,128)S(1)}, f32[1,128]{1,0:T(1,128)S(1)}) all-reduce(f32[1,1024]{1,0:T(1,128)S(1)} %bitcast.211, f32[1,128]{1,0:T(1,128)S(1)} %compare_select_fusion.8), channel_id=1, replica_groups=mesh['dp'=4,'head'=8] {'head'}, use_global_device_ids=true, to_apply=%region_14.15 | all-reduce | flops 1152 | bytes 9216 | tf_op jit(solution)/shard_map/psum | solution.py:560
  681.3 39.0 %all-reduce.6 = (bf16[256]{0:T(256)(128)(2,1)S(1)}, bf16[2048,4]{0,1:T(4,128)(2,1)S(1)}, bf16[4]{0:T(256)(128)(2,1)S(1)}, bf16[4,64,64]{2,1,0:T(8,128)(2,1)S(1)}...) all-reduce(bf16[256]{0:T(256)(128)(2,1)S(1)} %get-tuple-element.168, ...), channel_id=1, replica_groups=mesh['dp'=4,'head'=8] {'dp'}, use_global_device_ids=true, to_apply=%region_16.17 | all-reduce | flops 26372 | bytes 105488 | tf_op jit(solution)/shard_map/psum | solution.py:570
  721.0 3.0 add_convert_fusion.15
  737.3 15.1 %psum.127 = f32[1,128]{1,0:T(1,128)S(1)} all-reduce(f32[1,128]{1,0:T(1,128)S(1)} %compare_select_fusion.7), channel_id=1, replica_groups=mesh['dp'=4,'head'=8] {'dp'}, use_global_device_ids=true, to_apply=%region_36.37 | all-reduce | flops 128 | bytes 1024 | tf_op jit(solution)/shard_map/psum | solution.py:570
  769.5 31.8 %collective-permute-done.54 = bf16[128,2048]{1,0:T(8,128)(2,1)S(1)} collective-permute-done((bf16[128,2048]{1,0:T(8,128)(2,1)S(1)}, bf16[128,2048]{1,0:T(8,128)(2,1)S(1)}, u32[]{:S(2)}, u32[]{:S(2)}) %collective-permute-start.54) | collective-permute-done | bytes 524320 | tf_op jit(solution)/shard_map/ppermute | solution.py:410
  (459 shorter events, 206.1 us)
Async XLA Ops:
  7.2 136.6 %all-gather.3.cloned.1.call-start = ((), (), s32[]{:S(2)}) async-start(), calls=%async_computation.4 | async-start | bytes 4718592 | tf_op jit(solution)/shard_map/all_gather | solution.py:445
  7.3 35.0 %collective-permute-start = (bf16[256,1024]{1,0:T(8,128)(2,1)}, bf16[256,1024]{1,0:T(8,128)(2,1)}, u32[]{:S(2)}, u32[]{:S(2)}) collective-permute-start(bf16[256,1024]{1,0:T(8,128)(2,1)} %refs_0_.1), channel_id=1, source_target_pairs={{0,1},{1,0},{2,3},{3,2},{4,5},{5,4},{6,7},{7,6},{8,9},{9,8},{10,11... | collective-permute-start | bytes 1572872 | tf_op jit(solution)/shard_map/ppermute | solution.py:353
  7.8 22.9 %collective-permute-start.1 = (bf16[256,1024]{1,0:T(8,128)(2,1)}, bf16[256,1024]{1,0:T(8,128)(2,1)}, u32[]{:S(2)}, u32[]{:S(2)}) collective-permute-start(bf16[256,1024]{1,0:T(8,128)(2,1)} %refs_0_.1), channel_id=1, source_target_pairs={{0,2},{1,3},{2,0},{3,1},{4,6},{5,7},{6,4},{7,5},{8,10},{9,11},{10,... | collective-permute-start | bytes 1572872 | tf_op jit(solution)/shard_map/ppermute | solution.py:353
  10.3 21.7 %collective-permute-start.3 = (bf16[256,1024]{1,0:T(8,128)(2,1)}, bf16[256,1024]{1,0:T(8,128)(2,1)}, u32[]{:S(2)}, u32[]{:S(2)}) collective-permute-start(bf16[256,1024]{1,0:T(8,128)(2,1)} %refs_0_.1), channel_id=1, source_target_pairs={{0,4},{1,5},{2,6},{3,7},{4,0},{5,1},{6,2},{7,3},{8,12},{9,13},{10,... | collective-permute-start | bytes 1572872 | tf_op jit(solution)/shard_map/ppermute | solution.py:353
  30.7 11.6 %collective-permute-start.2 = (bf16[256,1024]{1,0:T(8,128)(2,1)}, bf16[256,1024]{1,0:T(8,128)(2,1)}, u32[]{:S(2)}, u32[]{:S(2)}) collective-permute-start(bf16[256,1024]{1,0:T(8,128)(2,1)} %collective-permute-done.1.refs_2_), channel_id=1, source_target_pairs={{0,1},{1,0},{2,3},{3,2},{4,5},{5,4},{6,7},{7,6},{8,9},{9,8},{10,11... | collective-permute-start | bytes 1572872 | tf_op jit(solution)/shard_map/ppermute | solution.py:353
  32.0 10.3 %collective-permute-start.4 = (bf16[256,1024]{1,0:T(8,128)(2,1)}, bf16[256,1024]{1,0:T(8,128)(2,1)}, u32[]{:S(2)}, u32[]{:S(2)}) collective-permute-start(bf16[256,1024]{1,0:T(8,128)(2,1)} %collective-permute-done.3.refs_4_), channel_id=1, source_target_pairs={{0,1},{1,0},{2,3},{3,2},{4,5},{5,4},{6,7},{7,6},{8,9},{9,8},{10,11... | collective-permute-start | bytes 1572872 | tf_op jit(solution)/shard_map/ppermute | solution.py:353
  32.2 8.7 %collective-permute-start.5 = (bf16[128,1024]{1,0:T(8,128)(2,1)S(1)}, bf16[128,1024]{1,0:T(8,128)(2,1)}, u32[]{:S(2)}, u32[]{:S(2)}) collective-permute-start(bf16[128,1024]{1,0:T(8,128)(2,1)S(1)} %slice.52), channel_id=1, source_target_pairs={{0,4},{1,5},{2,6},{3,7},{4,0},{5,1},{6,2},{7,3},{8,12},{9,13},{10,... | collective-permute-start | bytes 786440 | tf_op jit(solution)/shard_map/ppermute | solution.py:353
  33.7 8.5 %collective-permute-start.6 = (bf16[128,1024]{1,0:T(8,128)(2,1)S(1)}, bf16[128,1024]{1,0:T(8,128)(2,1)}, u32[]{:S(2)}, u32[]{:S(2)}) collective-permute-start(bf16[128,1024]{1,0:T(8,128)(2,1)S(1)} %slice.53), channel_id=1, source_target_pairs={{0,2},{1,3},{2,0},{3,1},{4,6},{5,7},{6,4},{7,5},{8,10},{9,11},{10,... | collective-permute-start | bytes 786440 | tf_op jit(solution)/shard_map/ppermute | solution.py:353
  55.2 154.9 %all-gather.5.cloned.1.call-start = ((), (), s32[]{:S(2)}) async-start(), calls=%async_computation.5 | async-start | bytes 4718592 | tf_op jit(solution)/shard_map/all_gather | solution.py:445
  56.5 225.1 %reduce-scatter.5.cloned.1.call-start = ((), (), s32[]{:S(2)}) async-start(), calls=%async_computation.6 | async-start | bytes 4718592 | tf_op jit(solution)/shard_map/reduce_scatter | solution.py:488
  105.7 18.0 %collective-permute-start.10 = (bf16[256,1024]{1,0:T(8,128)(2,1)}, bf16[256,1024]{1,0:T(8,128)(2,1)S(1)}, u32[]{:S(2)}, u32[]{:S(2)}) collective-permute-start(bf16[256,1024]{1,0:T(8,128)(2,1)} %get-tuple-element.111.refs_0_), channel_id=1, source_target_pairs={{0,2},{1,3},{2,0},{3,1},{4,6},{5,7},{6,4},{7,5},{8,10},{9,11},{10,... | collective-permute-start | bytes 1572872 | tf_op jit(solution)/shard_map/ppermute | solution.py:353
  107.2 18.1 %collective-permute-start.12 = (bf16[256,1024]{1,0:T(8,128)(2,1)}, bf16[256,1024]{1,0:T(8,128)(2,1)S(1)}, u32[]{:S(2)}, u32[]{:S(2)}) collective-permute-start(bf16[256,1024]{1,0:T(8,128)(2,1)} %get-tuple-element.111.refs_0_), channel_id=1, source_target_pairs={{0,4},{1,5},{2,6},{3,7},{4,0},{5,1},{6,2},{7,3},{8,12},{9,13},{10,... | collective-permute-start | bytes 1572872 | tf_op jit(solution)/shard_map/ppermute | solution.py:353
  107.7 32.3 %collective-permute-start.9 = (bf16[256,1024]{1,0:T(8,128)(2,1)}, bf16[256,1024]{1,0:T(8,128)(2,1)S(1)}, u32[]{:S(2)}, u32[]{:S(2)}) collective-permute-start(bf16[256,1024]{1,0:T(8,128)(2,1)} %get-tuple-element.111.refs_0_), channel_id=1, source_target_pairs={{0,1},{1,0},{2,3},{3,2},{4,5},{5,4},{6,7},{7,6},{8,9},{9,8},{10,11... | collective-permute-start | bytes 1572872 | tf_op jit(solution)/shard_map/ppermute | solution.py:353
  123.7 14.3 %collective-permute-start.14 = (bf16[128,1024]{1,0:T(8,128)(2,1)S(1)}, bf16[128,1024]{1,0:T(8,128)(2,1)S(1)}, u32[]{:S(2)}, u32[]{:S(2)}) collective-permute-start(bf16[128,1024]{1,0:T(8,128)(2,1)S(1)} %slice.69), channel_id=1, source_target_pairs={{0,4},{1,5},{2,6},{3,7},{4,0},{5,1},{6,2},{7,3},{8,12},{9,13},{10,... | collective-permute-start | bytes 786440 | tf_op jit(solution)/shard_map/ppermute | solution.py:353
  125.3 13.5 %collective-permute-start.15 = (bf16[128,1024]{1,0:T(8,128)(2,1)S(1)}, bf16[128,1024]{1,0:T(8,128)(2,1)S(1)}, u32[]{:S(2)}, u32[]{:S(2)}) collective-permute-start(bf16[128,1024]{1,0:T(8,128)(2,1)S(1)} %slice.70), channel_id=1, source_target_pairs={{0,2},{1,3},{2,0},{3,1},{4,6},{5,7},{6,4},{7,5},{8,10},{9,11},{10,... | collective-permute-start | bytes 786440 | tf_op jit(solution)/shard_map/ppermute | solution.py:353
  125.9 16.3 %collective-permute-start.11 = (bf16[256,1024]{1,0:T(8,128)(2,1)S(1)}, bf16[256,1024]{1,0:T(8,128)(2,1)S(1)}, u32[]{:S(2)}, u32[]{:S(2)}) collective-permute-start(bf16[256,1024]{1,0:T(8,128)(2,1)S(1)} %collective-permute-done.10.refs_2_), channel_id=1, source_target_pairs={{0,1},{1,0},{2,3},{3,2},{4,5},{5,4},{6,7},{7,6},{8,9},{9,8},{10,11... | collective-permute-start | bytes 1572872 | tf_op jit(solution)/shard_map/ppermute | solution.py:353
  125.9 17.1 %collective-permute-start.13 = (bf16[256,1024]{1,0:T(8,128)(2,1)S(1)}, bf16[256,1024]{1,0:T(8,128)(2,1)S(1)}, u32[]{:S(2)}, u32[]{:S(2)}) collective-permute-start(bf16[256,1024]{1,0:T(8,128)(2,1)S(1)} %collective-permute-done.12.refs_4_), channel_id=1, source_target_pairs={{0,1},{1,0},{2,3},{3,2},{4,5},{5,4},{6,7},{7,6},{8,9},{9,8},{10,11... | collective-permute-start | bytes 1572872 | tf_op jit(solution)/shard_map/ppermute | solution.py:353
  138.0 2.7 collective-permute-start.16
  170.8 13.8 %collective-permute-start.19 = (bf16[256,1024]{1,0:T(8,128)(2,1)S(1)}, bf16[256,1024]{1,0:T(8,128)(2,1)S(1)}, u32[]{:S(2)}, u32[]{:S(2)}) collective-permute-start(bf16[256,1024]{1,0:T(8,128)(2,1)S(1)} %get-tuple-element.230.refs_0_), channel_id=1, source_target_pairs={{0,2},{1,3},{2,0},{3,1},{4,6},{5,7},{6,4},{7,5},{8,10},{9,11},{10,... | collective-permute-start | bytes 1572872 | tf_op jit(solution)/shard_map/ppermute | solution.py:353
  171.1 14.5 %collective-permute-start.21 = (bf16[256,1024]{1,0:T(8,128)(2,1)S(1)}, bf16[256,1024]{1,0:T(8,128)(2,1)S(1)}, u32[]{:S(2)}, u32[]{:S(2)}) collective-permute-start(bf16[256,1024]{1,0:T(8,128)(2,1)S(1)} %get-tuple-element.230.refs_0_), channel_id=1, source_target_pairs={{0,4},{1,5},{2,6},{3,7},{4,0},{5,1},{6,2},{7,3},{8,12},{9,13},{10,... | collective-permute-start | bytes 1572872 | tf_op jit(solution)/shard_map/ppermute | solution.py:353
  172.8 21.7 %collective-permute-start.18 = (bf16[256,1024]{1,0:T(8,128)(2,1)S(1)}, bf16[256,1024]{1,0:T(8,128)(2,1)S(1)}, u32[]{:S(2)}, u32[]{:S(2)}) collective-permute-start(bf16[256,1024]{1,0:T(8,128)(2,1)S(1)} %get-tuple-element.230.refs_0_), channel_id=1, source_target_pairs={{0,1},{1,0},{2,3},{3,2},{4,5},{5,4},{6,7},{7,6},{8,9},{9,8},{10,11... | collective-permute-start | bytes 1572872 | tf_op jit(solution)/shard_map/ppermute | solution.py:353
  184.6 7.4 collective-permute-start.23
  185.7 8.8 %collective-permute-start.20 = (bf16[256,1024]{1,0:T(8,128)(2,1)S(1)}, bf16[256,1024]{1,0:T(8,128)(2,1)S(1)}, u32[]{:S(2)}, u32[]{:S(2)}) collective-permute-start(bf16[256,1024]{1,0:T(8,128)(2,1)S(1)} %collective-permute-done.19.refs_2_), channel_id=1, source_target_pairs={{0,1},{1,0},{2,3},{3,2},{4,5},{5,4},{6,7},{7,6},{8,9},{9,8},{10,11... | collective-permute-start | bytes 1572872 | tf_op jit(solution)/shard_map/ppermute | solution.py:353
  185.7 8.8 %collective-permute-start.22 = (bf16[256,1024]{1,0:T(8,128)(2,1)S(1)}, bf16[256,1024]{1,0:T(8,128)(2,1)S(1)}, u32[]{:S(2)}, u32[]{:S(2)}) collective-permute-start(bf16[256,1024]{1,0:T(8,128)(2,1)S(1)} %collective-permute-done.21.refs_4_), channel_id=1, source_target_pairs={{0,1},{1,0},{2,3},{3,2},{4,5},{5,4},{6,7},{7,6},{8,9},{9,8},{10,11... | collective-permute-start | bytes 1572872 | tf_op jit(solution)/shard_map/ppermute | solution.py:353
  186.2 8.3 %collective-permute-start.24 = (bf16[128,1024]{1,0:T(8,128)(2,1)S(1)}, bf16[128,1024]{1,0:T(8,128)(2,1)S(1)}, u32[]{:S(2)}, u32[]{:S(2)}) collective-permute-start(bf16[128,1024]{1,0:T(8,128)(2,1)S(1)} %slice.72), channel_id=1, source_target_pairs={{0,2},{1,3},{2,0},{3,1},{4,6},{5,7},{6,4},{7,5},{8,10},{9,11},{10,... | collective-permute-start | bytes 786440 | tf_op jit(solution)/shard_map/ppermute | solution.py:353
  230.5 163.4 %reduce-scatter.7.cloned.1.call-start = ((), (), s32[]{:S(2)}) async-start(), calls=%async_computation.7 | async-start | bytes 4718592 | tf_op jit(solution)/shard_map/reduce_scatter | solution.py:503
  230.6 34.6 %collective-permute-start.27 = (bf16[336,2048]{1,0:T(8,128)(2,1)}, bf16[336,2048]{1,0:T(8,128)(2,1)S(1)}, u32[]{:S(2)}, u32[]{:S(2)}) collective-permute-start(bf16[336,2048]{1,0:T(8,128)(2,1)} %slice.73), channel_id=1, source_target_pairs={{0,8},{24,16},{1,9},{25,17},{2,10},{26,18},{3,11},{27,19},{4,12},{... | collective-permute-start | bytes 4128776 | tf_op jit(solution)/shard_map/ppermute | solution.py:400
  243.2 70.8 %collective-permute-start.29 = (bf16[352,2048]{1,0:T(8,128)(2,1)}, bf16[352,2048]{1,0:T(8,128)(2,1)}, u32[]{:S(2)}, u32[]{:S(2)}) collective-permute-start(bf16[352,2048]{1,0:T(8,128)(2,1)} %slice.75), channel_id=1, source_target_pairs={{0,8},{24,16},{1,9},{25,17},{2,10},{26,18},{3,11},{27,19},{4,12},{... | collective-permute-start | bytes 4325384 | tf_op jit(solution)/shard_map/ppermute | solution.py:400
  268.0 51.2 %collective-permute-start.28 = (bf16[336,2048]{1,0:T(8,128)(2,1)}, bf16[336,2048]{1,0:T(8,128)(2,1)}, u32[]{:S(2)}, u32[]{:S(2)}) collective-permute-start(bf16[336,2048]{1,0:T(8,128)(2,1)} %add_convert_fusion.13), channel_id=1, source_target_pairs={{8,16},{16,8},{9,17},{17,9},{10,18},{18,10},{11,19},{19,11},{12,20... | collective-permute-start | bytes 4128776 | tf_op jit(solution)/shard_map/ppermute | solution.py:405
  302.2 354.4 %reduce-scatter.9.cloned.1.call-start = ((), (), s32[]{:S(2)}) async-start(), calls=%async_computation.8 | async-start | bytes 4718592 | tf_op jit(solution)/shard_map/reduce_scatter | solution.py:523
  309.5 32.3 %collective-permute-start.31 = (bf16[336,2048]{1,0:T(8,128)(2,1)}, bf16[336,2048]{1,0:T(8,128)(2,1)}, u32[]{:S(2)}, u32[]{:S(2)}) collective-permute-start(bf16[336,2048]{1,0:T(8,128)(2,1)} %slice.76), channel_id=1, source_target_pairs={{0,8},{24,16},{1,9},{25,17},{2,10},{26,18},{3,11},{27,19},{4,12},{... | collective-permute-start | bytes 4128776 | tf_op jit(solution)/shard_map/ppermute | solution.py:400
  317.3 28.1 %collective-permute-start.30 = (bf16[352,2048]{1,0:T(8,128)(2,1)}, bf16[352,2048]{1,0:T(8,128)(2,1)}, u32[]{:S(2)}, u32[]{:S(2)}) collective-permute-start(bf16[352,2048]{1,0:T(8,128)(2,1)} %add_convert_fusion.7), channel_id=1, source_target_pairs={{8,16},{16,8},{9,17},{17,9},{10,18},{18,10},{11,19},{19,11},{12,20... | collective-permute-start | bytes 4325384 | tf_op jit(solution)/shard_map/ppermute | solution.py:405
  322.6 45.5 %collective-permute-start.61 = (bf16[336,2048]{1,0:T(8,128)(2,1)}, bf16[336,2048]{1,0:T(8,128)(2,1)}, u32[]{:S(2)}, u32[]{:S(2)}) collective-permute-start(bf16[336,2048]{1,0:T(8,128)(2,1)} %add_convert_fusion.12), channel_id=1, source_target_pairs={{8,0},{16,24},{9,1},{17,25},{10,2},{18,26},{11,3},{19,27},{12,4},{... | collective-permute-start | bytes 4128776 | tf_op jit(solution)/shard_map/ppermute | solution.py:410
  348.9 37.9 %collective-permute-start.62 = (bf16[352,2048]{1,0:T(8,128)(2,1)}, bf16[352,2048]{1,0:T(8,128)(2,1)}, u32[]{:S(2)}, u32[]{:S(2)}) collective-permute-start(bf16[352,2048]{1,0:T(8,128)(2,1)} %add_convert_fusion.6), channel_id=1, source_target_pairs={{8,0},{16,24},{9,1},{17,25},{10,2},{18,26},{11,3},{19,27},{12,4},{... | collective-permute-start | bytes 4325384 | tf_op jit(solution)/shard_map/ppermute | solution.py:410
  354.2 154.7 %collective-permute-start.37 = (bf16[352,2048]{1,0:T(8,128)(2,1)}, bf16[352,2048]{1,0:T(8,128)(2,1)}, u32[]{:S(2)}, u32[]{:S(2)}) collective-permute-start(bf16[352,2048]{1,0:T(8,128)(2,1)} %slice.74), channel_id=1, source_target_pairs={{0,8},{24,16},{1,9},{25,17},{2,10},{26,18},{3,11},{27,19},{4,12},{... | collective-permute-start | bytes 4325384 | tf_op jit(solution)/shard_map/ppermute | solution.py:400
  363.3 62.1 %collective-permute-start.33 = (bf16[352,2048]{1,0:T(8,128)(2,1)}, bf16[352,2048]{1,0:T(8,128)(2,1)}, u32[]{:S(2)}, u32[]{:S(2)}) collective-permute-start(bf16[352,2048]{1,0:T(8,128)(2,1)} %slice.77), channel_id=1, source_target_pairs={{0,8},{24,16},{1,9},{25,17},{2,10},{26,18},{3,11},{27,19},{4,12},{... | collective-permute-start | bytes 4325384 | tf_op jit(solution)/shard_map/ppermute | solution.py:400
  365.8 94.5 %collective-permute-start.35 = (bf16[336,2048]{1,0:T(8,128)(2,1)}, bf16[336,2048]{1,0:T(8,128)(2,1)}, u32[]{:S(2)}, u32[]{:S(2)}) collective-permute-start(bf16[336,2048]{1,0:T(8,128)(2,1)} %slice.78), channel_id=1, source_target_pairs={{0,8},{24,16},{1,9},{25,17},{2,10},{26,18},{3,11},{27,19},{4,12},{... | collective-permute-start | bytes 4128776 | tf_op jit(solution)/shard_map/ppermute | solution.py:400
  368.1 64.3 %collective-permute-start.32 = (bf16[336,2048]{1,0:T(8,128)(2,1)}, bf16[336,2048]{1,0:T(8,128)(2,1)}, u32[]{:S(2)}, u32[]{:S(2)}) collective-permute-start(bf16[336,2048]{1,0:T(8,128)(2,1)} %add_convert_fusion.11), channel_id=1, source_target_pairs={{8,16},{16,8},{9,17},{17,9},{10,18},{18,10},{11,19},{19,11},{12,20... | collective-permute-start | bytes 4128776 | tf_op jit(solution)/shard_map/ppermute | solution.py:405
  386.7 167.8 %collective-permute-start.39 = (bf16[256,2048]{1,0:T(8,128)(2,1)}, bf16[256,2048]{1,0:T(8,128)(2,1)}, u32[]{:S(2)}, u32[]{:S(2)}) collective-permute-start(bf16[256,2048]{1,0:T(8,128)(2,1)} %convolution_convert_fusion.7), channel_id=1, source_target_pairs={{0,8},{24,16},{1,9},{25,17},{2,10},{26,18},{3,11},{27,19},{4,12},{... | collective-permute-start | bytes 3145736 | tf_op jit(solution)/shard_map/ppermute | solution.py:400
  393.9 265.1 %reduce-scatter.11.cloned.1.call-start = ((), (), s32[]{:S(2)}) async-start(), calls=%async_computation.9 | async-start | bytes 4718592 | tf_op jit(solution)/shard_map/reduce_scatter | solution.py:550
  428.4 53.8 %collective-permute-start.34 = (bf16[352,2048]{1,0:T(8,128)(2,1)}, bf16[352,2048]{1,0:T(8,128)(2,1)}, u32[]{:S(2)}, u32[]{:S(2)}) collective-permute-start(bf16[352,2048]{1,0:T(8,128)(2,1)} %add_convert_fusion.5), channel_id=1, source_target_pairs={{8,16},{16,8},{9,17},{17,9},{10,18},{18,10},{11,19},{19,11},{12,20... | collective-permute-start | bytes 4325384 | tf_op jit(solution)/shard_map/ppermute | solution.py:405
  435.8 42.0 %collective-permute-start.57 = (bf16[336,2048]{1,0:T(8,128)(2,1)}, bf16[336,2048]{1,0:T(8,128)(2,1)}, u32[]{:S(2)}, u32[]{:S(2)}) collective-permute-start(bf16[336,2048]{1,0:T(8,128)(2,1)} %add_convert_fusion.10), channel_id=1, source_target_pairs={{8,0},{16,24},{9,1},{17,25},{10,2},{18,26},{11,3},{19,27},{12,4},{... | collective-permute-start | bytes 4128776 | tf_op jit(solution)/shard_map/ppermute | solution.py:410
  460.3 119.2 %collective-permute-start.41 = (bf16[256,2048]{1,0:T(8,128)(2,1)}, bf16[256,2048]{1,0:T(8,128)(2,1)}, u32[]{:S(2)}, u32[]{:S(2)}) collective-permute-start(bf16[256,2048]{1,0:T(8,128)(2,1)} %convolution_convert_fusion.6), channel_id=1, source_target_pairs={{0,8},{24,16},{1,9},{25,17},{2,10},{26,18},{3,11},{27,19},{4,12},{... | collective-permute-start | bytes 3145736 | tf_op jit(solution)/shard_map/ppermute | solution.py:400
  477.8 44.4 %collective-permute-start.36 = (bf16[336,2048]{1,0:T(8,128)(2,1)}, bf16[336,2048]{1,0:T(8,128)(2,1)}, u32[]{:S(2)}, u32[]{:S(2)}) collective-permute-start(bf16[336,2048]{1,0:T(8,128)(2,1)} %add_convert_fusion.9), channel_id=1, source_target_pairs={{8,16},{16,8},{9,17},{17,9},{10,18},{18,10},{11,19},{19,11},{12,20... | collective-permute-start | bytes 4128776 | tf_op jit(solution)/shard_map/ppermute | solution.py:405
  511.9 59.2 %collective-permute-start.42 = (bf16[352,2048]{1,0:T(8,128)(2,1)}, bf16[352,2048]{1,0:T(8,128)(2,1)}, u32[]{:S(2)}, u32[]{:S(2)}) collective-permute-start(bf16[352,2048]{1,0:T(8,128)(2,1)} %add_convert_fusion.3), channel_id=1, source_target_pairs={{8,16},{16,8},{9,17},{17,9},{10,18},{18,10},{11,19},{19,11},{12,20... | collective-permute-start | bytes 4325384 | tf_op jit(solution)/shard_map/ppermute | solution.py:405
  518.6 209.4 %collective-permute-start.48 = (bf16[128,2048]{1,0:T(8,128)(2,1)}, bf16[128,2048]{1,0:T(8,128)(2,1)}, u32[]{:S(2)}, u32[]{:S(2)}) collective-permute-start(bf16[128,2048]{1,0:T(8,128)(2,1)} %get-tuple-element.225), channel_id=1, source_target_pairs={{0,8},{24,16},{1,9},{25,17},{2,10},{26,18},{3,11},{27,19},{4,12},{... | collective-permute-start | bytes 1572872 | tf_op jit(solution)/shard_map/ppermute | solution.py:400
  524.4 43.9 %collective-permute-start.59 = (bf16[336,2048]{1,0:T(8,128)(2,1)S(1)}, bf16[336,2048]{1,0:T(8,128)(2,1)}, u32[]{:S(2)}, u32[]{:S(2)}) collective-permute-start(bf16[336,2048]{1,0:T(8,128)(2,1)S(1)} %add_convert_fusion.8), channel_id=1, source_target_pairs={{8,0},{16,24},{9,1},{17,25},{10,2},{18,26},{11,3},{19,27},{12,4},{... | collective-permute-start | bytes 4128776 | tf_op jit(solution)/shard_map/ppermute | solution.py:410
  557.5 26.7 %collective-permute-start.40 = (bf16[256,2048]{1,0:T(8,128)(2,1)}, bf16[256,2048]{1,0:T(8,128)(2,1)}, u32[]{:S(2)}, u32[]{:S(2)}) collective-permute-start(bf16[256,2048]{1,0:T(8,128)(2,1)} %add_convert_fusion.21), channel_id=1, source_target_pairs={{8,16},{16,8},{9,17},{17,9},{10,18},{18,10},{11,19},{19,11},{12,20... | collective-permute-start | bytes 3145736 | tf_op jit(solution)/shard_map/ppermute | solution.py:405
  568.3 33.5 %collective-permute-start.58 = (bf16[352,2048]{1,0:T(8,128)(2,1)S(1)}, bf16[352,2048]{1,0:T(8,128)(2,1)S(1)}, u32[]{:S(2)}, u32[]{:S(2)}) collective-permute-start(bf16[352,2048]{1,0:T(8,128)(2,1)S(1)} %copy-done.40), channel_id=1, source_target_pairs={{8,0},{16,24},{9,1},{17,25},{10,2},{18,26},{11,3},{19,27},{12,4},{... | collective-permute-start | bytes 4325384 | tf_op jit(solution)/shard_map/ppermute | solution.py:410
  571.1 32.2 %collective-permute-start.38 = (bf16[256,2048]{1,0:T(8,128)(2,1)S(1)}, bf16[256,2048]{1,0:T(8,128)(2,1)S(1)}, u32[]{:S(2)}, u32[]{:S(2)}) collective-permute-start(bf16[256,2048]{1,0:T(8,128)(2,1)S(1)} %convolution_convert_fusion.4), channel_id=1, source_target_pairs={{0,8},{24,16},{1,9},{25,17},{2,10},{26,18},{3,11},{27,19},{4,12},{... | collective-permute-start | bytes 3145736 | tf_op jit(solution)/shard_map/ppermute | solution.py:400
  579.4 96.0 %collective-permute-start.43 = (bf16[256,2048]{1,0:T(8,128)(2,1)}, bf16[256,2048]{1,0:T(8,128)(2,1)}, u32[]{:S(2)}, u32[]{:S(2)}) collective-permute-start(bf16[256,2048]{1,0:T(8,128)(2,1)} %convolution_convert_fusion.3), channel_id=1, source_target_pairs={{0,8},{24,16},{1,9},{25,17},{2,10},{26,18},{3,11},{27,19},{4,12},{... | collective-permute-start | bytes 3145736 | tf_op jit(solution)/shard_map/ppermute | solution.py:400
  584.2 141.0 %collective-permute-start.49 = (bf16[128,2048]{1,0:T(8,128)(2,1)}, bf16[128,2048]{1,0:T(8,128)(2,1)S(1)}, u32[]{:S(2)}, u32[]{:S(2)}) collective-permute-start(bf16[128,2048]{1,0:T(8,128)(2,1)} %get-tuple-element.224), channel_id=1, source_target_pairs={{0,8},{24,16},{1,9},{25,17},{2,10},{26,18},{3,11},{27,19},{4,12},{... | collective-permute-start | bytes 1572872 | tf_op jit(solution)/shard_map/ppermute | solution.py:400
  601.8 28.0 %collective-permute-start.56 = (bf16[256,2048]{1,0:T(8,128)(2,1)S(1)}, bf16[256,2048]{1,0:T(8,128)(2,1)S(1)}, u32[]{:S(2)}, u32[]{:S(2)}) collective-permute-start(bf16[256,2048]{1,0:T(8,128)(2,1)S(1)} %add_convert_fusion.19), channel_id=1, source_target_pairs={{8,0},{16,24},{9,1},{17,25},{10,2},{18,26},{11,3},{19,27},{12,4},{... | collective-permute-start | bytes 3145736 | tf_op jit(solution)/shard_map/ppermute | solution.py:410
  603.3 48.3 %collective-permute-start.60 = (bf16[352,2048]{1,0:T(8,128)(2,1)S(1)}, bf16[352,2048]{1,0:T(8,128)(2,1)S(1)}, u32[]{:S(2)}, u32[]{:S(2)}) collective-permute-start(bf16[352,2048]{1,0:T(8,128)(2,1)S(1)} %add_convert_fusion.2), channel_id=1, source_target_pairs={{8,0},{16,24},{9,1},{17,25},{10,2},{18,26},{11,3},{19,27},{12,4},{... | collective-permute-start | bytes 4325384 | tf_op jit(solution)/shard_map/ppermute | solution.py:410
  629.8 42.7 %collective-permute-start.44 = (bf16[256,2048]{1,0:T(8,128)(2,1)}, bf16[256,2048]{1,0:T(8,128)(2,1)}, u32[]{:S(2)}, u32[]{:S(2)}) collective-permute-start(bf16[256,2048]{1,0:T(8,128)(2,1)} %add_convert_fusion.20), channel_id=1, source_target_pairs={{8,16},{16,8},{9,17},{17,9},{10,18},{18,10},{11,19},{19,11},{12,20... | collective-permute-start | bytes 3145736 | tf_op jit(solution)/shard_map/ppermute | solution.py:405
  651.7 69.3 %collective-permute-start.45 = (bf16[256,2048]{1,0:T(8,128)(2,1)}, bf16[256,2048]{1,0:T(8,128)(2,1)}, u32[]{:S(2)}, u32[]{:S(2)}) collective-permute-start(bf16[256,2048]{1,0:T(8,128)(2,1)} %add_convert_fusion.18), channel_id=1, source_target_pairs={{8,16},{16,8},{9,17},{17,9},{10,18},{18,10},{11,19},{19,11},{12,20... | collective-permute-start | bytes 3145736 | tf_op jit(solution)/shard_map/ppermute | solution.py:405
  678.4 77.5 %collective-permute-start.47 = (bf16[256,2048]{1,0:T(8,128)(2,1)}, bf16[256,2048]{1,0:T(8,128)(2,1)}, u32[]{:S(2)}, u32[]{:S(2)}) collective-permute-start(bf16[256,2048]{1,0:T(8,128)(2,1)} %add_convert_fusion.16), channel_id=1, source_target_pairs={{8,16},{16,8},{9,17},{17,9},{10,18},{18,10},{11,19},{19,11},{12,20... | collective-permute-start | bytes 3145736 | tf_op jit(solution)/shard_map/ppermute | solution.py:405
  680.0 86.8 %collective-permute-start.55 = (bf16[256,2048]{1,0:T(8,128)(2,1)}, bf16[256,2048]{1,0:T(8,128)(2,1)}, u32[]{:S(2)}, u32[]{:S(2)}) collective-permute-start(bf16[256,2048]{1,0:T(8,128)(2,1)} %add_convert_fusion.17), channel_id=1, source_target_pairs={{8,0},{16,24},{9,1},{17,25},{10,2},{18,26},{11,3},{19,27},{12,4},{... | collective-permute-start | bytes 3145736 | tf_op jit(solution)/shard_map/ppermute | solution.py:410
  724.0 40.2 %collective-permute-start.46 = (bf16[256,2048]{1,0:T(8,128)(2,1)}, bf16[256,2048]{1,0:T(8,128)(2,1)}, u32[]{:S(2)}, u32[]{:S(2)}) collective-permute-start(bf16[256,2048]{1,0:T(8,128)(2,1)} %add_convert_fusion.15), channel_id=1, source_target_pairs={{8,0},{16,24},{9,1},{17,25},{10,2},{18,26},{11,3},{19,27},{12,4},{... | collective-permute-start | bytes 3145736 | tf_op jit(solution)/shard_map/ppermute | solution.py:410
  726.5 32.5 %collective-permute-start.51 = (bf16[128,2048]{1,0:T(8,128)(2,1)S(1)}, bf16[128,2048]{1,0:T(8,128)(2,1)}, u32[]{:S(2)}, u32[]{:S(2)}) collective-permute-start(bf16[128,2048]{1,0:T(8,128)(2,1)S(1)} %add_convert_fusion.25), channel_id=1, source_target_pairs={{8,16},{16,8},{9,17},{17,9},{10,18},{18,10},{11,19},{19,11},{12,20... | collective-permute-start | bytes 1572872 | tf_op jit(solution)/shard_map/ppermute | solution.py:405
  729.3 32.3 %collective-permute-start.53 = (bf16[128,2048]{1,0:T(8,128)(2,1)S(1)}, bf16[128,2048]{1,0:T(8,128)(2,1)}, u32[]{:S(2)}, u32[]{:S(2)}) collective-permute-start(bf16[128,2048]{1,0:T(8,128)(2,1)S(1)} %add_convert_fusion.24), channel_id=1, source_target_pairs={{8,16},{16,8},{9,17},{17,9},{10,18},{18,10},{11,19},{19,11},{12,20... | collective-permute-start | bytes 1572872 | tf_op jit(solution)/shard_map/ppermute | solution.py:405
  757.8 45.3 %collective-permute-start.50 = (bf16[256,2048]{1,0:T(8,128)(2,1)S(1)}, bf16[256,2048]{1,0:T(8,128)(2,1)S(1)}, u32[]{:S(2)}, u32[]{:S(2)}) collective-permute-start(bf16[256,2048]{1,0:T(8,128)(2,1)S(1)} %add_convert_fusion.14), channel_id=1, source_target_pairs={{8,0},{16,24},{9,1},{17,25},{10,2},{18,26},{11,3},{19,27},{12,4},{... | collective-permute-start | bytes 3145736 | tf_op jit(solution)/shard_map/ppermute | solution.py:410
  760.3 41.1 %collective-permute-start.52 = (bf16[128,2048]{1,0:T(8,128)(2,1)S(1)}, bf16[128,2048]{1,0:T(8,128)(2,1)S(1)}, u32[]{:S(2)}, u32[]{:S(2)}) collective-permute-start(bf16[128,2048]{1,0:T(8,128)(2,1)S(1)} %add_convert_fusion.23), channel_id=1, source_target_pairs={{8,0},{16,24},{9,1},{17,25},{10,2},{18,26},{11,3},{19,27},{12,4},{... | collective-permute-start | bytes 1572872 | tf_op jit(solution)/shard_map/ppermute | solution.py:410
  762.8 38.5 %collective-permute-start.54 = (bf16[128,2048]{1,0:T(8,128)(2,1)S(1)}, bf16[128,2048]{1,0:T(8,128)(2,1)S(1)}, u32[]{:S(2)}, u32[]{:S(2)}) collective-permute-start(bf16[128,2048]{1,0:T(8,128)(2,1)S(1)} %add_convert_fusion.22), channel_id=1, source_target_pairs={{8,0},{16,24},{9,1},{17,25},{10,2},{18,26},{11,3},{19,27},{12,4},{... | collective-permute-start | bytes 1572872 | tf_op jit(solution)/shard_map/ppermute | solution.py:410
  (107 other events, 1183.0 us)
Sparse Core Ops, SparseCore 0:
  55.4 37.0 all-gather.2
  94.4 45.8 all-gather.4
  230.6 51.0 reduce-scatter.4
  302.4 51.2 reduce-scatter.6
  394.0 50.3 reduce-scatter.8
  554.6 51.6 reduce-scatter.10

commit v3 on v2

v3 whole, which is shorter than its diff:
```python
import jax, jax.numpy as jnp
from jax import lax
from jax.experimental import pallas as pl
from jax.experimental.pallas import tpu as pltpu
import functools
HD=64; MB=16; EPS=1e-6
F32=jnp.float32; BF=jnp.bfloat16

def nn(a,b): return lax.dot_general(a,b,(((1,),(0,)),((),())),preferred_element_type=F32)
def nt(a,b): return lax.dot_general(a,b,(((1,),(1,)),((),())),preferred_element_type=F32)
def tn(a,b): return lax.dot_general(a,b,(((0,),(0,)),((),())),preferred_element_type=F32)

def avg(x): return jnp.sum(x,0,keepdims=True)*(1.0/HD)

def lane_heads(heads, rows):
    return lax.broadcasted_iota(jnp.int32,(rows,heads*MB),1)//MB

def spread(x, heads):
    ids=lane_heads(heads,HD)
    return jnp.concatenate([jnp.where(ids==h,x,jnp.zeros_like(x)) for h in range(heads)],0)

def gather_blocks(x, heads):
    ids=lane_heads(heads,HD)
    out=jnp.zeros((HD,heads*MB),F32)
    for h in range(heads):
        out=out+jnp.where(ids==h,x[h*HD:(h+1)*HD],0.0)
    return out

def split_heads(ref, group, heads):
    cols=[ref[h*HD:(h+1)*HD, pl.ds(pl.multiple_of(group*128,128),128)] for h in range(heads)]
    return [jnp.concatenate([c[:,p*MB:(p+1)*MB] for c in cols],1) for p in range(8)]

def merge_heads(ref, group, parts, heads):
    for h in range(heads):
        blk=jnp.concatenate([p[:,h*MB:(h+1)*MB] for p in parts],1)
        ref[h*HD:(h+1)*HD, pl.ds(pl.multiple_of(group*128,128),128)]=blk.astype(ref.dtype)

def padded(x):
    rows=lax.broadcasted_iota(jnp.int32,(MB,x.shape[1]),0)
    return jnp.concatenate([x,jnp.where(rows==0,1.0,0.0).astype(F32)],0)

def same_head(heads):
    L=heads*MB
    r=lax.broadcasted_iota(jnp.int32,(L,L),0); c=lax.broadcasted_iota(jnp.int32,(L,L),1)
    return r//MB==c//MB, r%MB, c%MB

def step_grad(zt, td, g, s):
    mu=avg(zt); cen=zt-mu
    r=lax.rsqrt(avg(cen*cen)+EPS)
    n=cen*r
    v=n*g+s-td
    u=v*g
    m1=avg(u); m2=avg(u*n)
    return r,n,v,u,m2,r*(u-m1-n*m2)

def fwd_kernel(heads, nb, reset, qT, kT, vT, rate, valid, consts,
               outT, zt_o, zb_o, td_o, qa_o, ka_o, wt_o, rows, mp, q32):
    L=heads*MB
    same,ri,ci_=same_head(heads)
    tri=jnp.where(same&(ri<=ci_), 16.0/(ci_.astype(F32)+1.0), 0.0)
    diag=jnp.where(same,1.0,0.0)
    def pre(gr,_):
        qs=split_heads(qT,gr,heads); ks=split_heads(kT,gr,heads); vs=split_heads(vT,gr,heads)
        at=pl.ds(pl.multiple_of(gr*128,128),128)
        rt=rate[:,at]; vl=valid[:,at]
        for p in range(8):
            b=gr*8+p
            cut=slice(p*MB,(p+1)*MB)
            rows[b]=jnp.concatenate([jnp.concatenate([rt[h:h+1,cut] for h in range(heads)],1),
                                     jnp.concatenate([vl[:,cut]]*heads,1)],0)
            td_o[b]=vs[p]-ks[p]
            q32[b]=qs[p]
            qa_o[b]=padded(qs[p]).astype(BF)
            ka_o[b]=padded(ks[p]).astype(BF)
        return 0
    lax.fori_loop(0,nb//8,pre,0)
    def pre2(b,_):
        nxt=jnp.minimum(b+1,nb-1)
        ke=(ka_o[b].astype(F32)*(rows[b,0:1]*(1.0/MB))).astype(BF)
        keep=jnp.where(reset[nxt]>0,0.0,1.0)
        m=tn(ke,ka_o[nxt])*(diag*keep)
        pt=tn(ke,qa_o[b])*tri
        mp[b]=jnp.concatenate([m,pt],1).astype(BF)
        return 0
    lax.fori_loop(0,nb,pre2,0,unroll=4)
    w0,c0,g,s=unpack_consts(consts,heads)
    def body(b,carry):
        zt,wt,ct=carry
        nxt=jnp.minimum(b+1,nb-1)
        rs=reset[nxt]>0
        wt_b=wt.astype(BF)
        wt_o[b]=wt_b; zt_o[b]=zt
        r,n,v,u,m2,gt=step_grad(zt,td_o[b],g,s)
        gb=gt.astype(BF)
        kn=spread(ka_o[nxt][:HD],heads)
        wsel=jnp.where(rs,w0,wt).astype(BF)
        csel=jnp.where(rs,c0,ct)
        yk=nn(wsel,kn)+csel
        yq=nn(wt_b,spread(qa_o[b][:HD],heads))+ct
        rr=nn(gb,mp[b])
        e16=rows[b,0:1]*(1.0/MB)
        ke=(ka_o[b][:HD].astype(F32)*e16).astype(BF)
        rw=nt(gb,spread(ke,heads))
        ec=jnp.where(same,jnp.broadcast_to(e16,(L,L)),0.0).astype(BF)
        rc=nt(gb,ec)
        zb_o[b]=yq-rr[:,L:]
        z2=yk-rr[:,:L]
        return z2,jnp.where(rs,w0,wt-rw),jnp.where(rs,c0,ct-rc)
    zt=nn(w0.astype(BF),spread(ka_o[0][:HD],heads))+c0
    lax.fori_loop(0,nb,body,(zt,w0,c0))
    def post(gr,_):
        outs=[]
        for p in range(8):
            b=gr*8+p
            zb=zb_o[b]; cen=zb-avg(zb)
            n=cen*lax.rsqrt(avg(cen*cen)+EPS)
            outs.append((q32[b]+n*g+s)*rows[b,1:2])
        merge_heads(outT,gr,outs,heads)
        return 0
    lax.fori_loop(0,nb//8,post,0)

VM=pl.BlockSpec(memory_space=pltpu.VMEM)
SM=pl.BlockSpec(memory_space=pltpu.SMEM)
AN=pl.BlockSpec(memory_space=pl.ANY)

def pack_consts(w0, c0, g, s):
    heads=w0.shape[0]
    cols=[w0.transpose(2,0,1).reshape(HD,heads*HD)]+[lane_cols(v) for v in (c0,g,s)]
    return jnp.concatenate([jnp.pad(v,((0,0),(0,-v.shape[1]%128))) for v in cols],1)

def unpack_consts(ref, heads):
    wide=(heads*HD+127)//128*128; step=(heads*MB+127)//128*128
    return [ref[:,:heads*HD]]+[ref[:,wide+i*step:wide+i*step+heads*MB] for i in range(3)]

def ttt_fwd(reset, qT,kT,vT, rate, valid, consts):
    T=qT.shape[1]; heads=qT.shape[0]//HD; nb=T//MB; L=heads*MB; S=jax.ShapeDtypeStruct
    outs=[S((heads*HD,T),BF),S((nb,HD,L),F32),S((nb,HD,L),F32),S((nb,HD,L),F32),S((nb,HD+MB,L),BF),S((nb,HD+MB,L),BF),
          S((nb,HD,heads*HD),BF),S((nb,2,L),F32)]
    def whole(v): return pl.BlockSpec(v.shape,lambda i:(0,)*len(v.shape))
    args=[qT,kT,vT,rate,valid,consts]
    return pl.pallas_call(functools.partial(fwd_kernel,heads,nb),out_shape=outs,grid=(1,),
        in_specs=[SM]+[whole(v) for v in args],out_specs=[whole(v) for v in outs],
        scratch_shapes=[pltpu.VMEM((nb,L,2*L),BF),pltpu.VMEM((nb,HD,L),F32)],
        compiler_params=pltpu.CompilerParams(vmem_limit_bytes=44<<20), name="mix_forward",
        cost_estimate=pl.CostEstimate(flops=T*heads*4000*64*50, bytes_accessed=T*heads*64*40, transcendentals=0))(
            reset,*args)

def bwd_kernel(heads, nb, base, last, reset, dOT, zt_i, zb_i, td_i, qa_i, ka_i, wt_i, rows, consts, *refs):
    if last:
        li=lci=None
    else:
        li,lci=refs[:2]; refs=refs[5:]
    (dqT, dkT, dvT, de_o, dg_o, ds_o, dw0_o, dc0_o, lo, lco,
               n_s, v_s, r_s, m2_s, gb_s, gh_s, nm_s, u_s, uc_s, dq_s, dk_s, du_s, dz_s, h_s, la_s, de_s)=refs
    L=heads*MB
    _,_,g,s=unpack_consts(consts,heads)
    same,ri,cj=same_head(heads)
    tri=jnp.where(same&(cj<=ri),1.0/(ri.astype(F32)+1.0),0.0)
    diag=jnp.where(same,1.0,0.0)
    diag_b=diag.astype(BF)
    dg_o[...]=jnp.zeros((HD,L),F32); ds_o[...]=jnp.zeros((HD,L),F32)
    dw0_o[...]=jnp.zeros_like(dw0_o); dc0_o[...]=jnp.zeros_like(dc0_o)
    def pre(gr,_):
        dos=split_heads(dOT,gr,heads)
        dga=jnp.zeros((HD,L),F32); dsa=jnp.zeros((HD,L),F32)
        for p in range(8):
            b=gr*8+p
            dO=dos[p].astype(F32)*rows[b,1:2]
            zb=zb_i[b]; cen=zb-avg(zb); rb=lax.rsqrt(avg(cen*cen)+EPS); nbar=cen*rb
            dga=dga+dO*nbar; dsa=dsa+dO
            dn=dO*g
            dzb=rb*(dn-avg(dn)-nbar*avg(dn*nbar))
            dzb_b=dzb.astype(BF)
            r,n,v,u,m2,gt=step_grad(zt_i[b],td_i[b],g,s)
            gb=gt.astype(BF)
            n_s[b]=n; v_s[b]=v; r_s[b]=r; m2_s[b]=m2; gb_s[b]=gt
            e=rows[b,0:1]
            ka=ka_i[b]; qa=qa_i[b]
            st=tn(qa,ka)*tri
            gh_s[b]=-nn(dzb_b,(st*e).astype(BF))
            dp=-tn(dzb_b,gb)
            de_s[b]=jnp.sum(dp*st,0,keepdims=True)
            dS=(dp*tri*e).astype(BF)
            dq_s[b]=dO+gather_blocks(tn(wt_i[b],dzb_b),heads)+nt(ka[:HD],dS)
            dk_s[b]=nn(qa[:HD],dS)
            prev=jnp.maximum(b-1,0)
            keep=jnp.where(reset[base+b]>0,0.0,1.0)
            nm_s[b]=(tn(ka,ka_i[prev])*(diag*keep)).astype(BF)
            u_s[b]=nt(dzb_b,spread(qa[:HD],heads))
            uc_s[b]=nn(dzb_b,diag_b)
        dg_o[...]+=dga; ds_o[...]+=dsa
        return 0
    lax.fori_loop(0,nb//8,pre,0)
    def body(k,carry):
        ht,la,lc=carry
        b=nb-1-k
        prev=jnp.maximum(b-1,0)
        rs=reset[base+b]>0
        n=n_s[b]; v=v_s[b]; r=r_s[b]; m2=m2_s[b]; gt=gb_s[b]
        h_s[b]=ht
        la_s[b]=la.astype(BF)
        dG=gh_s[b]-(rows[b,0:1]*(1.0/MB))*ht
        da=r*dG
        m3=avg(da); m4=avg(da*n); m6a=avg(dG*gt)
        du=da-m3-n*m4
        dn=(du*g-v*m4)*g-da*m2
        m5=avg(dn); m6=m6a+avg(dn*n)
        dz=(r*(dn-m5-n*m6)).astype(BF)
        du_s[b]=du
        dz_s[b]=dz
        la2=la+u_s[b]; lc2=lc+uc_s[b]
        y=nn(la2.astype(BF),spread(ka_i[prev][:HD],heads))+lc2
        h2=jnp.where(rs,0.0,y)+nn(dz,nm_s[b])
        la3=la2+nt(dz,spread(ka_i[b][:HD],heads)); lc3=lc2+nn(dz,diag_b)
        @pl.when(rs)
        def _():
            dw0_o[...]+=la3; dc0_o[...]+=lc3
        return h2,jnp.where(rs,0.0,la3),jnp.where(rs,0.0,lc3)
    la=jnp.zeros((HD,heads*HD),F32) if last else li[...]
    lc=jnp.zeros((HD,L),F32) if last else lci[...]
    ht=nn(la.astype(BF),spread(ka_i[nb-1][:HD],heads))+lc
    ht,la,lc=lax.fori_loop(0,nb,body,(ht,la,lc))
    lo[...]=la; lco[...]=lc
    def post(gr,_):
        dqs=[];dks=[];dvs=[];des=[]
        dga=jnp.zeros((HD,L),F32); dsa=jnp.zeros((HD,L),F32)
        for p in range(8):
            b=gr*8+p
            du=du_s[b]; dug=du*g; gt=gb_s[b]
            dga=dga+du*v_s[b]+dug*n_s[b]; dsa=dsa+dug
            dvs.append(-dug)
            dqs.append(dq_s[b])
            des.append(de_s[b]-avg(gt*h_s[b])*(HD/MB))
            dks.append(dug+dk_s[b]-(rows[b,0:1]*(1.0/MB))*gather_blocks(tn(la_s[b],gt.astype(BF)),heads)
                       +gather_blocks(tn(wt_i[b],dz_s[b]),heads))
        de_o[:,pl.ds(pl.multiple_of(gr*128,128),128)]=jnp.concatenate(
            [jnp.concatenate([d[:,h*MB:(h+1)*MB] for d in des],1) for h in range(heads)],0)
        merge_heads(dqT,gr,dqs,heads); merge_heads(dkT,gr,dks,heads); merge_heads(dvT,gr,dvs,heads)
        dg_o[...]+=dga; ds_o[...]+=dsa
        return 0
    lax.fori_loop(0,nb//8,post,0)

def ttt_bwd(part, parts, reset, dOT, zt,zb,td,qa,ka,wt,rows,consts, carry=None):
    T=dOT.shape[1]//parts; heads=dOT.shape[0]//HD; nb=T//MB; L=heads*MB; S=jax.ShapeDtypeStruct
    W=heads*HD; last=part==parts-1
    outs=[S((W,T*parts),BF)]*3+[S((heads,T),F32)]+[S((HD,L),F32)]*2+[S((HD,W),F32),S((HD,L),F32)]*2
    V=pltpu.VMEM
    scr=[V((nb,HD,L),F32),V((nb,HD,L),F32),V((nb,1,L),F32),V((nb,1,L),F32),V((nb,HD,L),F32),V((nb,HD,L),F32),
         V((nb,L,L),BF),V((nb,HD,W),F32),V((nb,HD,L),F32),V((nb,HD,L),F32),V((nb,HD,L),F32),V((nb,HD,L),F32),
         V((nb,HD,L),BF),V((nb,HD,L),F32),V((nb,HD,W),BF),V((nb,1,L),F32)]
    def whole(*dims): return pl.BlockSpec(dims,lambda i:(0,)*len(dims))
    def third(*dims): return pl.BlockSpec((nb,)+dims,lambda i:(part,)+(0,)*len(dims))
    nat=pl.BlockSpec((W,T),lambda i:(0,part))
    ins=[SM,nat]+[third(HD,L)]*3+[third(HD+MB,L)]*2+[third(HD,W),third(2,L),whole(*consts.shape)]
    args=[reset,dOT,zt,zb,td,qa,ka,wt,rows,consts]
    alias={}
    if not last:
        ins+=[whole(HD,W),whole(HD,L)]+[AN]*3
        alias={12:0,13:1,14:2}
        args+=list(carry)
    return pl.pallas_call(functools.partial(bwd_kernel,heads,nb,part*nb,last),out_shape=outs,grid=(1,),
        in_specs=ins,out_specs=[nat]*3+[whole(heads,T)]+[whole(HD,L)]*2+[whole(HD,W),whole(HD,L)]*2,
        scratch_shapes=scr,input_output_aliases=alias,
        compiler_params=pltpu.CompilerParams(vmem_limit_bytes=36<<20), name="mix_backward",
        cost_estimate=pl.CostEstimate(flops=T*heads*64, bytes_accessed=T*heads, transcendentals=0))(*args)

def lane_cols(x):
    return jnp.repeat(x.T,MB,axis=1)


ROWS = 64


def fetch(pieces, spots, buf, sems):
    copies = []
    for i, p in enumerate(pieces):
        at = pl.ds(pl.multiple_of(spots[i], 16), p.shape[0])
        copies.append(pltpu.make_async_copy(p, buf.at[at], sems.at[i]))
        copies[-1].start()
    for c in copies:
        c.wait()


def fold(buf, width, f):
    def add(i, acc):
        v = f(buf[pl.ds(pl.multiple_of(i * ROWS, ROWS), ROWS), :].astype(F32))
        return acc + jnp.sum(v.reshape(ROWS // 8, 8, v.shape[1]), 0)

    acc = lax.fori_loop(0, width // ROWS, add, jnp.zeros((8, buf.shape[1]), F32))
    return jnp.sum(acc, 0, keepdims=True)


def rms_kernel(n, lane, width, fresh, spots, blocks, *refs):
    pieces, (out, scale_out, gains, buf, sems, gain_sems) = refs[:n], refs[n:]
    if fresh:
        copies = []
        for i in range(blocks.shape[0]):
            at = pl.ds(pl.multiple_of(spots[i if i < 7 else 8], 16), blocks.shape[1])
            copies.append(pltpu.make_async_copy(blocks.at[i], gains.at[at], gain_sems.at[i]))
            copies[-1].start()
        fetch(pieces, spots, buf, sems)
        for c in copies:
            c.wait()
    else:
        fetch(pieces, spots, buf, sems)
    scale = lax.rsqrt(fold(buf, width, lambda v: v * v) * (1.0 / width) + EPS)
    scale_out[...] = scale
    source = gains if fresh else blocks

    def write(i, _):
        at = pl.ds(pl.multiple_of(i * ROWS, ROWS), ROWS)
        gain = source[at, lane:lane + 1].astype(F32)
        out[at, :] = (buf[at, :].astype(F32) * scale * gain).astype(BF)
        return 0

    lax.fori_loop(0, width // ROWS, write, 0)
    if not fresh:
        gains[...] = jnp.zeros_like(gains)


def moments_kernel(n, width, spots, *refs):
    pieces, (out, mean_out, scale_out, sems) = refs[:n], refs[n:]
    fetch(pieces, spots, out, sems)
    mean = fold(out, width, lambda v: v) * (1.0 / width)
    mean_out[...] = mean
    scale_out[...] = lax.rsqrt(fold(out, width, lambda v: (v - mean) * (v - mean)) * (1.0 / width) + EPS)


def rms_rows(pieces, spots, gains, lane, tok, width):
    n = len(pieces)
    fresh = gains.ndim == 3
    count = gains.shape[0] if fresh else 1
    S = jax.ShapeDtypeStruct
    return pl.pallas_call(
        functools.partial(rms_kernel, n, lane, width, fresh),
        out_shape=[S((width, tok), BF), S((1, tok), F32), S((width, 128) if fresh else (16, 128), BF)],
        in_specs=[SM, AN if fresh else VM] + [AN] * n, out_specs=[VM, VM, VM],
        scratch_shapes=[pltpu.VMEM((width, tok), BF), pltpu.SemaphoreType.DMA((n,)), pltpu.SemaphoreType.DMA((count,))],
        compiler_params=pltpu.CompilerParams(vmem_limit_bytes=16 << 20), name="rms_rows",
        cost_estimate=pl.CostEstimate(flops=8 * width * tok, bytes_accessed=4 * width * tok, transcendentals=0),
    )(spots, gains, *pieces)


def moments_rows(pieces, spots, tok, width):
    n = len(pieces)
    return pl.pallas_call(
        functools.partial(moments_kernel, n, width),
        out_shape=[jax.ShapeDtypeStruct((width, tok), BF)] + [jax.ShapeDtypeStruct((1, tok), F32)] * 2,
        in_specs=[SM] + [AN] * n, out_specs=[VM] * 3,
        scratch_shapes=[pltpu.SemaphoreType.DMA((n,))],
        compiler_params=pltpu.CompilerParams(vmem_limit_bytes=16 << 20), name="moments_rows",
        cost_estimate=pl.CostEstimate(flops=8 * width * tok, bytes_accessed=4 * width * tok, transcendentals=0),
    )(spots, *pieces)


def hold(x, *deps):
    return lax.optimization_barrier((x,) + deps)[0]


class Pieces:
    def __init__(self, x, devs):
        if devs != 8:
            self.direct = self.diag = (x,)
            self.all = [lax.all_gather(x, "head", axis=0, tiled=True)]
            return
        rows = x.shape[0]

        def swap(v, bit):
            return lax.ppermute(v, "head", [(i, i ^ bit) for i in range(8)])

        along_x = swap(x, 2)
        along_y = swap(x, 4)
        peer = swap(x, 1)
        low = swap(along_x[:rows // 2], 4)
        high = swap(along_y[rows // 2:], 2)
        self.direct = (along_x, along_y)
        self.diag = (low, high)
        self.all = [x, peer, along_x, swap(along_x, 1), along_y, swap(along_y, 1), low, high, swap(low, 1), swap(high, 1)]


class Scatter:
    def __init__(self, left, right, rows, own, devs):
        self.own, self.devs = own, devs
        self.terms = None
        if devs != 8:
            total = sum(tn(a, b) for a, b in zip(left, right)).astype(BF)
            self.pair = (total, total[:16])
            self.dot = jnp.sum(total.astype(F32) * rows.astype(F32), 0, keepdims=True)
            return
        me = lax.axis_index("head")
        self.chip = me // 2
        keep, give, self.dot = parts((me % 2).reshape(1), left, right, rows, own)
        self.pair = (keep, give)

    def swap(self, v, bit):
        return lax.ppermute(v, "head", [(i, i ^ bit) for i in range(8)])

    def add(self, a, b):
        return (a.astype(F32) + b.astype(F32)).astype(BF)

    def spread(self):
        if self.devs != 8:
            return
        half = self.own // 2
        self.acc = self.add(self.pair[0], self.swap(self.pair[1], 1))
        far, to_x, to_y, home = [lax.dynamic_index_in_dim(self.acc, self.chip ^ k, 0, keepdims=False) for k in (3, 1, 2, 0)]
        low, high = self.swap(far[:half], 2), self.swap(far[half:], 4)
        x_low, y_high = self.swap(to_x[:half], 2), self.swap(to_y[half:], 4)
        x_high, y_low = self.swap(self.add(to_x[half:], high), 2), self.swap(self.add(to_y[:half], low), 4)
        self.terms = (home, (x_low, x_high), (y_low, y_high))

    def result(self):
        if self.devs != 8:
            return lax.psum_scatter(self.pair[0], "head", scatter_dimension=0, tiled=True).astype(F32)
        if self.terms is None:
            self.spread()
        home, *pairs = self.terms
        total = home.astype(F32)
        for pair in pairs:
            total = total + jnp.concatenate([v.astype(F32) for v in pair], 0)
        return total


def spread_gains(cols, devs):
    cols = jnp.pad(cols, ((0, 0), (0, 128 - cols.shape[1])))[None]
    if devs != 8:
        return lax.all_gather(cols, "head", axis=1, tiled=True)
    for bit in (1, 2, 4):
        cols = jnp.concatenate([cols, lax.ppermute(cols, "head", [(i, i ^ bit) for i in range(8)])], 0)
    return cols


def piece_spots(own, devs):
    if devs != 8:
        return jnp.zeros((1,), jnp.int32)
    me = lax.axis_index("head")
    half = own // 2
    places = [(0, 0), (1, 0), (2, 0), (3, 0), (4, 0), (5, 0), (6, 0), (6, half), (7, 0), (7, half)]
    return jnp.stack([(me ^ bits) * own + off for bits, off in places]).astype(jnp.int32)


FREE = pl.CostEstimate(flops=0, bytes_accessed=0, transcendentals=0)
COLS = 512


def wide_params(mib):
    return pltpu.CompilerParams(vmem_limit_bytes=mib << 20)


def wgrad_kernel(a, b, out):
    out[...] = nt(a[...], b[...]).astype(BF)


def wgrad(a, b):
    rows, tok = a.shape
    n = b.shape[0]
    return pl.pallas_call(
        wgrad_kernel, grid=(n // COLS,), out_shape=jax.ShapeDtypeStruct((rows, n), BF),
        in_specs=[pl.BlockSpec((rows, tok), lambda i: (0, 0)), pl.BlockSpec((COLS, tok), lambda i: (i, 0))],
        out_specs=pl.BlockSpec((rows, COLS), lambda i: (0, i)),
        compiler_params=wide_params(24), cost_estimate=FREE, name="weight_gradient")(a, b)


def column_blocks(v):
    return pl.BlockSpec((v.shape[0], COLS), lambda i: (0, i))


def half_kernel(x, air, out):
    out[...] = (x[...].astype(F32) + air[:x.shape[0], :].astype(F32)).astype(BF)


def half_sum(x, air):
    return pl.pallas_call(
        half_kernel, grid=(x.shape[1] // COLS,), out_shape=jax.ShapeDtypeStruct(x.shape, BF),
        in_specs=[column_blocks(x), column_blocks(air)], out_specs=column_blocks(x),
        compiler_params=wide_params(16), cost_estimate=FREE, name="half_sum")(x, air)


def outgoing_kernel(end, x, half, air, out):
    def put(v):
        out[:v.shape[0], :] = v
        if v.shape[0] < out.shape[0]:
            out[v.shape[0]:, :] = jnp.zeros((out.shape[0] - v.shape[0], out.shape[1]), BF)

    @pl.when(end[0] > 0)
    def _():
        put(x[...])

    @pl.when(end[0] == 0)
    def _():
        put((half[...].astype(F32) + air[...].astype(F32)).astype(BF))


def outgoing(end, x, half, air):
    out = jax.ShapeDtypeStruct((max(x.shape[0], half.shape[0]), x.shape[1]), BF)
    return pl.pallas_call(
        outgoing_kernel, grid=(x.shape[1] // COLS,), out_shape=out,
        in_specs=[SM] + [column_blocks(v) for v in (x, half, air)], out_specs=column_blocks(out),
        compiler_params=wide_params(16), cost_estimate=FREE, name="outgoing")(end, x, half, air)


def finish_kernel(sizes, end, *refs):
    n = len(sizes)
    airs, sents, out = refs[:n], refs[n:2 * n], refs[2 * n]
    for chosen, kind in ((airs, 1), (sents, 0)):
        @pl.when(end[0] == kind)
        def _():
            at = 0
            for v, rows in zip(chosen, sizes):
                out[at:at + rows, :] = v[:rows, :].astype(F32)
                at += rows


def finish(end, jobs):
    sizes = [job.x.shape[0] for job in jobs]
    vals = [job.landed for job in jobs] + [job.sent for job in jobs]
    out = jax.ShapeDtypeStruct((sum(sizes), vals[0].shape[1]), F32)
    return pl.pallas_call(
        functools.partial(finish_kernel, sizes), grid=(out.shape[1] // COLS,), out_shape=out,
        in_specs=[SM] + [column_blocks(v) for v in vals], out_specs=column_blocks(out),
        compiler_params=wide_params(24), cost_estimate=FREE, name="finish")(end, *vals)


def parts_kernel(n, core, *refs):
    left, right, (rows, keep, give, dot) = refs[:n], refs[n:2 * n], refs[2 * n:]
    which = pl.program_id(1)
    total = tn(left[0][...], right[0][...])
    for a, b in zip(left[1:], right[1:]):
        total = total + tn(a[...], b[...])
    low = total.astype(BF)

    @pl.when((pl.program_id(0) == 0) & (which == 0))
    def _():
        dot[...] = jnp.zeros_like(dot)

    dot[...] += jnp.sum(low.astype(F32) * rows[...].astype(F32), 0, keepdims=True)

    @pl.when(which == 0)
    def _():
        keep[0] = low

    @pl.when(which == 1)
    def _():
        give[0] = low


def parts(core, left, right, rows, own):
    tok = right[0].shape[1]
    n = len(left)
    chips = left[0].shape[1] // (2 * own)
    block = lambda c, w, core: c * 2 + (core[0] ^ w)
    S = jax.ShapeDtypeStruct
    spec = pltpu.PrefetchScalarGridSpec(
        num_scalar_prefetch=1, grid=(chips, 2),
        in_specs=[pl.BlockSpec((v.shape[0], own), lambda c, w, core: (0, block(c, w, core))) for v in left]
        + [pl.BlockSpec(v.shape, lambda c, w, core: (0, 0)) for v in right]
        + [pl.BlockSpec((own, tok), lambda c, w, core: (block(c, w, core), 0))],
        out_specs=[pl.BlockSpec((1, own, tok), lambda c, w, core: (c, 0, 0))] * 2
        + [pl.BlockSpec((1, tok), lambda c, w, core: (0, 0))])
    return pl.pallas_call(
        functools.partial(parts_kernel, n), grid_spec=spec,
        out_shape=[S((chips, own, tok), BF)] * 2 + [S((1, tok), F32)],
        compiler_params=wide_params(32), name="parts",
        cost_estimate=pl.CostEstimate(flops=10**10, bytes_accessed=10**7, transcendentals=0))(core, *left, *right, rows)


from jax.sharding import PartitionSpec as P


def col_sum(x):
    return jnp.sum(x, 0, keepdims=True)


def gelu_tanh(values):
    return jax.nn.gelu(values, approximate=True)


def layout(seq_lens, row_count):
    padded = (seq_lens + MB - 1) // MB * MB
    starts = jnp.cumsum(padded) - padded
    positions = jnp.arange(row_count, dtype=jnp.int32)
    inside = (positions[None, :] >= starts[:, None]) & (positions[None, :] < (starts + seq_lens)[:, None])
    valid_rows = jnp.any(inside, axis=0).astype(F32)
    block_first = jnp.arange(row_count // MB, dtype=jnp.int32) * MB
    begins = jnp.any((starts[:, None] == block_first[None, :]) & (seq_lens[:, None] > 0), axis=0)
    return valid_rows, (begins | (block_first == 0)).astype(jnp.int32)


def tie(*values):
    return lax.optimization_barrier(values)


class Sum:
    def __init__(self, x):
        self.x = x
        self.half = self.air = self.sent = self.landed = None


class Belt:
    def __init__(self):
        self.line = lax.axis_size("dp") == 4
        at = lax.axis_index("dp")
        self.end = ((at == 0) | (at == 3)).astype(jnp.int32).reshape(1)
        self.outer = self.inner = None

    def load(self, job, back):
        if back is None:
            return job.x
        if job is None:
            return half_sum(back.half, back.air)
        return outgoing(self.end, job.x, back.half, back.air)

    def tick(self, x, *values):
        job = Sum(x) if x is not None else None
        if not self.line:
            return (job,) + tuple(tie(*values)) if values else (job,)
        airs = ([self.outer[2]] if self.outer else []) + ([self.inner.air] if self.inner else [])
        held = tie(*airs, *([x] if job else []), *values)
        if job:
            job.x = held[len(airs)]
        values = held[len(airs) + (1 if job else 0):]
        back, self.inner = self.inner, None
        if back:
            back.air = held[len(airs) - 1]
        if self.outer:
            sent, gone, _ = self.outer
            if gone:
                gone.landed = held[0]
            if sent:
                sent.half = half_sum(sent.x, held[0])
                sent.air = lax.ppermute(sent.half, "dp", [(1, 2), (2, 1)])
                self.inner = sent
        self.outer = None
        if job or back:
            load = self.load(job, back)
            self.outer = (job, back, lax.ppermute(load, "dp", [(0, 1), (1, 0), (2, 3), (3, 2)]))
            if back:
                back.sent = load
        return (job,) + tuple(values)

    def drain(self):
        while self.outer or self.inner:
            self.tick(None)

    def result(self, *jobs):
        if not self.line:
            return lax.psum(jnp.concatenate([job.x for job in jobs], 0), "dp").astype(F32)
        return finish(self.end, jobs)


def on_device(
    tokens, lengths, attn_gain, w_query, w_key, w_value, w_gate, w_rate, rate_bias,
    inner_weight, inner_bias, inner_gain, inner_shift, post_gain, post_shift, w_out,
    ffn_gain, w_hidden_gate, w_hidden_up, w_down, out_grad,
):
    tok = tokens.shape[1]
    own = tokens.shape[0]
    heads = inner_weight.shape[0]
    devs = lax.axis_size("head")
    width = own * devs
    belt = Belt()

    def gather(x):
        return lax.all_gather(x, "head", axis=0, tiled=True)

    def head_sum(v):
        if devs != 8:
            return lax.psum(v, "head")
        for bit in (1, 2, 4):
            v = v + lax.ppermute(v, "head", [(i, i ^ bit) for i in range(8)])
        return v

    valid, reset = layout(lengths, tok)
    vrow = valid[None, :]
    spots = piece_spots(own, devs)
    stacked = jnp.concatenate([w_query, w_key, w_value, w_gate, jnp.pad(w_rate.T, ((0, 16 - heads), (0, 0)))], 0)
    tok_pieces = Pieces(tokens, devs)
    gain_blocks = spread_gains(jnp.stack([attn_gain, post_gain, post_shift, ffn_gain], 1), devs)
    consts = [hold(v, *tok_pieces.direct).astype(F32) for v in (inner_weight, inner_bias, inner_gain, inner_shift)]
    consts = pack_consts(*consts)
    nin, q1, gains = rms_rows(tok_pieces.all, spots, gain_blocks, 0, tok, width)
    g_full = gather(hold(out_grad, q1))
    gate = nn(w_gate, nin).astype(BF)
    gates = gather(gate)
    nin_q = hold(nin, gate)
    q_t = nn(w_query, nin_q)
    k_t = nn(w_key, nin_q)
    v_t = nn(w_value, nin_q)
    logits = tn(w_rate, nin) + rate_bias.astype(F32)[:, None]
    sig = jax.nn.sigmoid(logits)
    masked = sig * vrow
    mixer_own, zt, zb, td, qa, ka, wt, rows = ttt_fwd(
        reset, q_t, k_t, v_t, masked * (1.0 / HD), vrow, consts)

    mixer_own, g_full = tie(mixer_own, g_full)
    mix_pieces = Pieces(mixer_own, devs)
    mix, mean3, r3 = moments_rows(mix_pieces.all, spots, tok, width)
    gain_cols = gains.astype(F32)
    mixed = (((mix.astype(F32) - mean3) * r3 * gain_cols[:, 1:2] + gain_cols[:, 2:3])
             * gelu_tanh(gates.astype(F32))).astype(BF)
    hidden = tokens.astype(F32) + nn(w_out, mixed)
    hidden_low = hidden.astype(BF)
    nmid, q2, _ = rms_rows(Pieces(hidden_low, devs).all, spots, gains, 3, tok, width)
    gate_val = nn(w_hidden_gate, nmid)
    up_val = nn(w_hidden_up, nmid)
    sg = jax.nn.sigmoid(gate_val)
    act = (gate_val * sg * up_val).astype(BF)

    def halves(x, other):
        cut = (x.shape[0] // 2 + 7) // 8 * 8
        return wgrad(x[:cut], other), wgrad(x[cut:], other)

    down = halves(act, g_full)
    here = lax.axis_index("head") + 1
    marks = lax.broadcasted_iota(jnp.int32, (1, tok), 1)
    rates = jnp.where(marks == 0, jnp.sum(masked), jnp.where(marks == here, jnp.max(masked), 0.0))
    d0, g_full, rates = belt.tick(down[0], g_full, rates)
    g_act = nn(w_down, g_full)
    g_up = (g_act * gate_val * sg).astype(BF)
    g_gate = (g_act * up_val * sg * (1.0 + gate_val * (1.0 - sg))).astype(BF)
    gn = Scatter([w_hidden_gate, w_hidden_up], [g_gate, g_up], nmid, own, devs)
    d1, *gn.pair, gn.dot, rates, g_up, g_gate = belt.tick(down[1], *gn.pair, gn.dot, rates, g_up, g_gate)
    gn.spread()
    hgate = halves(g_gate, nmid)
    sums = head_sum(jnp.concatenate([gn.dot, rates], 0))
    mid_dot, rates = sums[:1], sums[1:]
    gn = gn.result()
    h0, gn, mid_dot, rates, g_up, h1_x = belt.tick(hgate[0], gn, mid_dot, rates, g_up, hgate[1])
    hid_own = hidden_low.astype(F32)
    fg_own = ffn_gain.astype(F32)[:, None]
    g_ffn_gain = jnp.sum(gn * hid_own * q2, 1)
    g_hidden = out_grad.astype(F32) + q2 * fg_own * gn - hid_own * q2**2 * mid_dot / width
    g_branch = g_hidden.astype(BF)
    gm = Scatter([w_out], [g_branch], mixed, own, devs)
    hup = halves(g_up, nmid)
    h1, *gm.pair, g_branch, u0_x = belt.tick(h1_x, *gm.pair, g_branch, hup[0])
    gm.spread()
    out_w = wgrad(g_branch, mixed)
    gm = gm.result()
    u0, gm, out_w, u1_x = belt.tick(u0_x, gm, out_w, hup[1])
    n3 = (mixer_own.astype(F32) - mean3) * r3
    pg_own = post_gain.astype(F32)[:, None]
    ps_own = post_shift.astype(F32)[:, None]
    a_own, gelu_pull = jax.vjp(gelu_tanh, gate.astype(F32))
    g_post_gain = jnp.sum(gm * a_own * n3, 1)
    g_post_shift = jnp.sum(gm * a_own, 1)
    g_gate_pre = gelu_pull(gm * (n3 * pg_own + ps_own))[0].astype(BF)
    m = gm * a_own * pg_own
    sums = head_sum(jnp.concatenate([col_sum(m), col_sum(m * n3)], 0))
    s_plain, s_norm = sums[:1], sums[1:]
    g_mixer = r3 * (m - s_plain / width - n3 * s_norm / width)
    u1, g_mixer, g_gate_pre, out_w = belt.tick(u1_x, g_mixer, g_gate_pre, out_w)
    gate_w = wgrad(g_gate_pre, nin)
    saved = (zt, zb, td, qa, ka, wt, rows, consts)
    b1 = ttt_bwd(1, 2, reset, g_mixer, *saved)
    so, lam, lam_c, gate_w = belt.tick(out_w, b1[8], b1[9], gate_w)
    b0 = ttt_bwd(0, 2, reset, g_mixer, *saved, carry=(lam, lam_c) + tuple(b1[:3]))
    dq, dk, dv = b0[:3]
    de_rows = jnp.concatenate([b0[3], b1[3]], 1)
    dgl, dsl, dw0, dc0 = [b0[i] + b1[i] for i in range(4, 8)]
    g_logits = de_rows * vrow * (1.0 / HD) * sig * (1.0 - sig)
    gl = g_logits.astype(BF)
    g_inner_w = dw0.reshape(HD, heads, HD).transpose(1, 2, 0)
    g_inner_b = dc0.reshape(HD, heads, MB)[:, :, 0].T
    g_inner_g = dgl.reshape(HD, heads, MB).sum(-1).T
    g_inner_s = dsl.reshape(HD, heads, MB).sum(-1).T
    wide_q, wide_k, wide_v = [wgrad(v, nin) for v in (dq, dk, dv)]
    wg, dq, dk, dv, gl, wide_q, wide_k, wide_v = belt.tick(gate_w, dq, dk, dv, gl, wide_q, wide_k, wide_v)
    tall = jnp.concatenate([dq, dk, dv, g_gate_pre, jnp.pad(gl, ((0, 16 - heads), (0, 0)))], 0)
    gi = Scatter([stacked], [tall], nin, own, devs)
    q, *gi.pair, gi.dot, act, wide_k = belt.tick(wide_q, *gi.pair, gi.dot, act, wide_k)
    gi.spread()
    in_dot = head_sum(gi.dot)
    gi = gi.result()
    g_wr = nt(gl, nin)
    ffn_part = tn(w_down, act).astype(BF)
    ffn = lax.psum_scatter(ffn_part, "head", scatter_dimension=0, tiled=True)
    result = (hidden + ffn.astype(F32)).astype(BF)
    k, gi, in_dot, g_wr = belt.tick(wide_k, gi, in_dot, g_wr)
    x_own = tokens.astype(F32)
    ag_own = attn_gain.astype(F32)[:, None]
    g_attn_gain = jnp.sum(gi * x_own * q1, 1)
    g_tokens = g_hidden + q1 * ag_own * gi - x_own * q1**2 * in_dot / width
    top = jnp.max(jnp.where(marks > 0, rates, 0.0))
    both = jnp.stack([rates[0, 0], top])
    cut = []
    for _ in range(3):
        cut.append(lax.reduce_precision(both, 8, 7))
        both = both - cut[-1]
    dps = lax.axis_size("dp")
    slot = (jnp.arange(dps) == lax.axis_index("dp")).astype(F32)
    slots = (slot[:, None, None] * jnp.stack(cut)[None]).reshape(-1)
    vectors = [g_attn_gain, g_post_gain, g_post_shift, g_ffn_gain, g_inner_b, g_inner_g, g_inner_s,
               jnp.sum(g_logits, 1), slots]
    vectors = [jnp.pad(u.reshape(-1), (0, own - u.size)) for u in vectors]
    small = jnp.concatenate([u.astype(BF).reshape(-1) for u in vectors + [g_inner_w, g_wr]])
    count = small.shape[0]
    small = jnp.pad(small, (0, -count % (16 * width))).reshape(-1, width)
    v, = belt.tick(jnp.concatenate([wide_v, small], 0))
    belt.drain()
    s_wv = belt.result(v)
    s_wv, small = s_wv[:own], s_wv[own:].reshape(-1)
    s_attn, s_pg, s_ps, s_fg, s_ib, s_ig, s_is, s_rb, slots = [small[i * own:(i + 1) * own] for i in range(9)]
    s_ib, s_ig, s_is = [v.reshape(heads, HD) for v in (s_ib, s_ig, s_is)]
    s_rb = s_rb[:heads]
    wide = 9 * own + heads * HD * HD
    s_iw = small[9 * own:wide].reshape(heads, HD, HD)
    s_wr = small[wide:count].reshape(heads, width)
    slots = jnp.sum(slots[:dps * 6].reshape(dps, 3, 2), 1)
    mean_rate = jnp.sum(slots[:, 0]) / (tok * dps * heads * devs)
    max_rate = jnp.max(slots[:, 1])

    return (
        result, g_tokens, s_attn, belt.result(q), belt.result(k), s_wv, belt.result(wg),
        s_wr.T, s_rb, s_iw, s_ib, s_ig, s_is, s_pg, s_ps, belt.result(so),
        s_fg, belt.result(h0, h1), belt.result(u0, u1), belt.result(d0, d1), mean_rate, max_rate,
    )


def solution(mesh):
    h = P("head")
    m = P("head", None)
    c = P("head", None, None)
    t = P("head", "dp")
    r = P(None, "head")
    ins = (t, P("dp"), h, m, m, m, m, r, h, c, m, m, m, h, h, m, h, m, m, m, t)
    outs = (t, t, h, m, m, m, m, r, h, c, m, m, m, h, h, m, h, m, m, m, P(), P())
    return jax.shard_map(on_device, mesh=mesh, in_specs=ins, out_specs=outs, check_vma=False)
```

time: 821 us -> 706 us (0.86)
  Pallas kernels: 106 us -> 212 us
  blocking collectives: 103 us -> 0 us
  matrix products: 114 us -> 37.1 us
  other arithmetic: 120 us -> 45.6 us
  local copies, waits for them, and re-layouts: 38.6 us -> 59.1 us
  waiting for transfers between devices: 212 us -> 225 us
    pallas_call x3 -> x47, Pallas kernels: 22.7 us -> 137 us  [the longest x3 28.2 us: parts(): pl.pallas_call(functools.partial(parts_kernel, n), grid_spec=spec, out_sh...]
    psum x5 -> x0, blocking collectives: 90.9 us -> none  [the longest x2 54.1 us: on_device(): lax.psum([hold(x.astype(BF), k.half) for x in small] + [rates], 'dp')]
    convert_element_type x38 -> x10, other arithmetic: 75.5 us -> 18.1 us  [the longest x6 8.99 us: add(): return (a.astype(F32) + b.astype(F32)).astype(BF)]
    dot_general x9 -> x1, matrix products: 33.2 us -> 4.01 us  [nt(): lax.dot_general(a, b, (((1,), (1,)), ((), ())), preferred_element_type=F32)]
    dot_general x9 -> x2, matrix products: 38.6 us -> 10.7 us  [tn(): lax.dot_general(a, b, (((0,), (0,)), ((), ())), preferred_element_type=F32)]
    ppermute x27 -> x48, waiting for transfers between devices: 56.8 us -> 77.8 us  [swap(): return lax.ppermute(v, 'head', [(i, i ^ bit) for i in range(8)])]
    dot_general x9 -> x8, matrix products: 41.7 us -> 22.4 us  [nn(): lax.dot_general(a, b, (((1,), (0,)), ((), ())), preferred_element_type=F32)]
    ppermute x36, starting transfers between devices: 84.9 us -> 65.7 us  [the longest x13 42.6 us: tick(): lax.ppermute(load, 'dp', [(0, 1), (1, 0), (2, 3), (3, 2)])]
  transfers between devices with their start and end apart: 69 -> 87, of which waited for: 19 -> 35; matrix products, arithmetic and copies ran while one was open for 28% -> 13% of each run, Pallas kernels for 12% -> 27%
where the time goes in v3:
time: 706 us; the launch traced here: 698 us
  waiting for transfers between devices  225 us (32%)
  Pallas kernels  212 us (30%)
  starting transfers between devices  101 us (14%)
  local copies, waits for them, and re-layouts  59.1 us (8%)
  other arithmetic  45.6 us (6%)
  matrix products  37.1 us (5%)
  between operations  18.3 us (3%)
    ppermute x13, waiting for transfers between devices, tick(): lax.ppermute(load, 'dp', [(0, 1), (1, 0), (2, 3), (3, 2)])  118 us
    ppermute x48, waiting for transfers between devices, swap(): return lax.ppermute(v, 'head', [(i, i ^ bit) for i in range(8)])  77.8 us
    ppermute x13, starting transfers between devices, tick(): lax.ppermute(load, 'dp', [(0, 1), (1, 0), (2, 3), (3, 2)])  42.6 us
    pallas_call x2, Pallas kernels, ttt_bwd(): pl.pallas_call(functools.partial(bwd_kernel, heads, nb, part * nb, last),...  40.5 us
    unnamed x293, local copies, waits for them, and re-layouts  35.4 us
    ppermute x48, starting transfers between devices, swap(): return lax.ppermute(v, 'head', [(i, i ^ bit) for i in range(8)])  35.3 us
    pallas_call x1, Pallas kernels, ttt_fwd(): pl.pallas_call(functools.partial(fwd_kernel, heads, nb), out_shape=outs,...  34.9 us
    pallas_call x3, Pallas kernels, parts(): pl.pallas_call(functools.partial(parts_kernel, n), grid_spec=spec, out_sh...  28.2 us
  transfers between devices with their start and end apart: 87, of which 35 were waited for; matrix products, arithmetic and copies ran while one was open for 13% of the time, Pallas kernels for 27%

profile of v3, /device:TPU:0, one launch (start us, length us, event | category | flops | bytes accessed | tf_op | source)
XLA Modules:
  0.0 698.1 jit_solution(4542018589823461428)
XLA Ops:
  15.6 13.4 %collective-permute-done.1 = bf16[2,256,128]{2,1,0:T(8,128)(2,1)S(1)} collective-permute-done((bf16[2,256,128]{2,1,0:T(8,128)(2,1)S(1)}, bf16[2,256,128]{2,1,0:T(8,128)(2,1)S(1)}, u32[]{:S(2)}, u32[]{:S(2)}) %collective-permute-start.1) | collective-permute-done | bytes 131104 | tf_op jit(solution)/shard_map/ppermute | solution.py:429
  35.6 3.3 collective-permute-done.2
  38.9 4.6 collective-permute-done.8.refs_6_
  45.8 6.8 rms_rows.2
  56.4 4.6 fusion.18
  61.1 4.3 multiply_reduce_fusion.4
  65.3 2.6 convolution_bitcast_fusion.1.vT
  70.6 34.9 %mix_forward.1 = (bf16[256,1024]{1,0:T(8,128)(2,1)S(1)}, f32[64,64,64]{2,1,0:T(8,128)S(1)}, f32[64,64,64]{2,1,0:T(8,128)}, f32[64,64,64]{2,1,0:T(8,128)}, bf16[6...) custom-call(s32[64]{0:T(128)S(1)} %or_convert_fusion.reset, ...), custom_call_target="tpu_custom_call" | custom-call | flops 52428800000 | bytes 10485760 | tf_op jit(solution)/shard_map/mix_forward/pallas_call | solution.py:141
  112.7 15.7 %collective-permute-done.13.refs_2_ = bf16[256,1024]{1,0:T(8,128)(2,1)S(1)} collective-permute-done((bf16[256,1024]{1,0:T(8,128)(2,1)S(1)}, bf16[256,1024]{1,0:T(8,128)(2,1)S(1)}, u32[]{:S(2)}, u32[]{:S(2)}) %collective-permute-start.13) | collective-permute-done | bytes 524320 | tf_op jit(solution)/shard_map/ppermute | solution.py:369
  133.0 8.8 %collective-permute-done.17.refs_6_ = bf16[128,1024]{1,0:T(8,128)(2,1)S(1)} collective-permute-done((bf16[128,1024]{1,0:T(8,128)(2,1)S(1)}, bf16[128,1024]{1,0:T(8,128)(2,1)S(1)}, u32[]{:S(2)}, u32[]{:S(2)}) %collective-permute-start.17) | collective-permute-done | bytes 262176 | tf_op jit(solution)/shard_map/ppermute | solution.py:369
  144.6 3.3 moments_rows.1
  150.0 6.8 fusion.6.refs_2_.b
  161.2 11.9 %collective-permute-done.22.refs_2_ = bf16[256,1024]{1,0:T(8,128)(2,1)} collective-permute-done((bf16[256,1024]{1,0:T(8,128)(2,1)S(1)}, bf16[256,1024]{1,0:T(8,128)(2,1)}, u32[]{:S(2)}, u32[]{:S(2)}) %collective-permute-start.22) | collective-permute-done | bytes 524320 | tf_op jit(solution)/shard_map/ppermute | solution.py:369
  177.7 3.9 collective-permute-done.26.refs_6_
  186.8 6.9 rms_rows.3
  193.7 3.1 fusion.78
  197.0 3.4 fusion.12
  201.5 2.8 weight_gradient.11.x
  205.9 3.9 fusion.11
  209.9 3.6 weight_gradient.12.x
  213.5 12.0 %parts.3 = (bf16[4,256,1024]{2,1,0:T(8,128)(2,1)S(1)}, bf16[4,256,1024]{2,1,0:T(8,128)(2,1)}, f32[1,1024]{1,0:T(1,128)S(1)}) custom-call(s32[1]{0:T(128)} %bitcast.33.core, bf16[688,2048]{1,0:T(8,128)(2,1)S(1)} %copy-done.94, bf16[688,2048]{1,0:T(8,128)(2,1)S(1)} %copy-done.95, bf16[688,1024]{1,0:T(8,128)(2,1)S(1)} %get-tuple-element.171.refs_2_, ...), custom_call_target="tpu_custom_call" | custom-call | flops 10000000000 | bytes 10000000 | tf_op jit(solution)/shard_map/parts/pallas_call | solution.py:560
  226.8 10.5 %collective-permute-done.30.air = bf16[344,2048]{1,0:T(8,128)(2,1)S(1)} collective-permute-done((bf16[344,2048]{1,0:T(8,128)(2,1)S(1)}, bf16[344,2048]{1,0:T(8,128)(2,1)S(1)}, u32[]{:S(2)}, u32[]{:S(2)}) %collective-permute-start.30) | collective-permute-done | bytes 1409056 | tf_op jit(solution)/shard_map/ppermute | solution.py:636
  245.5 3.4 collective-permute-start.31
  257.6 4.5 collective-permute-done.41
  280.4 3.0 half_sum.14.half
  284.2 2.7 outgoing.9.refs_2_
  287.0 3.3 collective-permute-start.43
  293.3 5.6 parts.4
  298.9 20.5 %collective-permute-done.43.air.refs_0_ = bf16[344,2048]{1,0:T(8,128)(2,1)S(1)} collective-permute-done((bf16[344,2048]{1,0:T(8,128)(2,1)S(1)}, bf16[344,2048]{1,0:T(8,128)(2,1)S(1)}, u32[]{:S(2)}, u32[]{:S(2)}) %collective-permute-start.43) | collective-permute-done | bytes 1409056 | tf_op jit(solution)/shard_map/ppermute | solution.py:636
  321.7 4.7 collective-permute-start.45
  330.1 5.6 collective-permute-done.49
  338.0 4.8 collective-permute-done.48
  349.5 8.2 %collective-permute-done.45.air.refs_1_ = bf16[344,2048]{1,0:T(8,128)(2,1)S(1)} collective-permute-done((bf16[344,2048]{1,0:T(8,128)(2,1)S(1)}, bf16[344,2048]{1,0:T(8,128)(2,1)S(1)}, u32[]{:S(2)}, u32[]{:S(2)}) %collective-permute-start.45) | collective-permute-done | bytes 1409056 | tf_op jit(solution)/shard_map/ppermute | solution.py:636
  359.9 3.7 collective-permute-start.54
  363.6 2.9 multiply_reduce_fusion
  368.4 3.1 collective-permute-done.57
  372.1 3.2 collective-permute-done.58
  375.6 18.2 %collective-permute-done.54.air.refs_0_ = bf16[344,2048]{1,0:T(8,128)(2,1)S(1)} collective-permute-done((bf16[344,2048]{1,0:T(8,128)(2,1)S(1)}, bf16[344,2048]{1,0:T(8,128)(2,1)S(1)}, u32[]{:S(2)}, u32[]{:S(2)}) %collective-permute-start.54) | collective-permute-done | bytes 1409056 | tf_op jit(solution)/shard_map/ppermute | solution.py:636
  398.3 3.8 collective-permute-start.59
  403.5 20.0 %mix_backward.2 = (bf16[256,1024]{1,0:T(8,128)(2,1)S(1)}, bf16[256,1024]{1,0:T(8,128)(2,1)S(1)}, bf16[256,1024]{1,0:T(8,128)(2,1)S(1)}, f32[4,512]{1,0:T(4,128)S...) custom-call(s32[64]{0:T(128)S(1)} %or_convert_fusion.reset, ...), custom_call_target="tpu_custom_call" | custom-call | flops 131072 | bytes 2048 | tf_op jit(solution)/shard_map/mix_backward/pallas_call | solution.py:261
  425.6 5.7 collective-permute-done.59.air.refs_1_
  434.0 3.8 outgoing.13.refs_2_
  437.8 2.6 collective-permute-start.61
  443.3 20.5 %mix_backward.3 = (bf16[256,1024]{1,0:T(8,128)(2,1)S(1)}, bf16[256,1024]{1,0:T(8,128)(2,1)S(1)}, bf16[256,1024]{1,0:T(8,128)(2,1)S(1)}, f32[4,512]{1,0:T(4,128)S...) custom-call(s32[64]{0:T(128)S(1)} %or_convert_fusion.reset, ...), custom_call_target="tpu_custom_call", output_to_operand_aliasing={{0}: (12, {}), {1}: (13, {}), {2}: (14, {})} | custom-call | flops 131072 | bytes 2048 | tf_op jit(solution)/shard_map/mix_backward/pallas_call | solution.py:261
  474.7 3.8 collective-permute-start.63
  478.7 10.7 %parts.5 = (bf16[4,256,1024]{2,1,0:T(8,128)(2,1)S(1)}, bf16[4,256,1024]{2,1,0:T(8,128)(2,1)}, f32[1,1024]{1,0:T(1,128)S(1)}) custom-call(s32[1]{0:T(128)} %bitcast.33.core, bf16[1040,2048]{1,0:T(8,128)(2,1)S(1)} %bitcast.216, bf16[1040,1024]{1,0:T(8,128)(2,1)S(1)} %pad_dynamic-update-slice_fusion.1.refs_1_, bf16[2048,1024]{1,0:T(8,128)(2,1)S(1)} %copy-done.3), custom_call_target="tpu_custom_call" | custom-call | flops 10000000000 | bytes 10000000 | tf_op jit(solution)/shard_map/parts/pallas_call | solution.py:560
  491.7 14.3 %collective-permute-done.63.air.refs_1_ = bf16[344,2048]{1,0:T(8,128)(2,1)S(1)} collective-permute-done((bf16[344,2048]{1,0:T(8,128)(2,1)S(1)}, bf16[344,2048]{1,0:T(8,128)(2,1)S(1)}, u32[]{:S(2)}, u32[]{:S(2)}) %collective-permute-start.63) | collective-permute-done | bytes 1409056 | tf_op jit(solution)/shard_map/ppermute | solution.py:636
  509.9 6.4 convert_bitcast_fusion
  526.6 3.2 collective-permute-start.65
  542.4 5.9 collective-permute-done.69
  555.3 5.9 collective-permute-done.68
  562.7 4.0 fusion.77
  570.1 3.5 half_sum.21.half
  575.4 3.6 outgoing.16.refs_1_
  584.7 3.8 fusion.28
  594.6 5.9 collective-permute-done.77.air.refs_0_
  607.7 17.0 %collective-permute-done.79.air.refs_0_ = bf16[272,2048]{1,0:T(8,128)(2,1)S(1)} collective-permute-done((bf16[272,2048]{1,0:T(8,128)(2,1)S(1)}, bf16[272,2048]{1,0:T(8,128)(2,1)S(1)}, u32[]{:S(2)}, u32[]{:S(2)}) %collective-permute-start.79) | collective-permute-done | bytes 1114144 | tf_op jit(solution)/shard_map/ppermute | solution.py:636
  626.7 6.7 collective-permute-start.81
  633.5 17.5 %collective-permute-done.81.refs_0_ = bf16[256,2048]{1,0:T(8,128)(2,1)S(1)} collective-permute-done((bf16[256,2048]{1,0:T(8,128)(2,1)S(1)}, bf16[256,2048]{1,0:T(8,128)(2,1)S(1)}, u32[]{:S(2)}, u32[]{:S(2)}) %collective-permute-start.81) | collective-permute-done | bytes 1048608 | tf_op jit(solution)/shard_map/ppermute | solution.py:636
  655.0 3.2 finish.15
  658.2 4.7 finish.13
  663.0 4.5 finish.14
  667.4 3.8 finish.12
  671.2 3.8 finish.11
  (597 shorter events, 222.9 us)
Async XLA Ops:
  7.2 102.5 %all-gather.3.cloned.1.call-start = ((), (), s32[]{:S(2)}) async-start(), calls=%async_computation.1 | async-start | bytes 4718592 | tf_op jit(solution)/shard_map/all_gather | solution.py:664
  10.9 20.6 %collective-permute-start.4 = (bf16[256,1024]{1,0:T(8,128)(2,1)}, bf16[256,1024]{1,0:T(8,128)(2,1)}, u32[]{:S(2)}, u32[]{:S(2)}) collective-permute-start(bf16[256,1024]{1,0:T(8,128)(2,1)} %refs_0_.3), channel_id=1, source_target_pairs={{0,2},{1,3},{2,0},{3,1},{4,6},{5,7},{6,4},{7,5},{8,10},{9,11},{10,... | collective-permute-start | bytes 1572872 | tf_op jit(solution)/shard_map/ppermute | solution.py:369
  13.5 19.4 %collective-permute-start.6 = (bf16[256,1024]{1,0:T(8,128)(2,1)}, bf16[256,1024]{1,0:T(8,128)(2,1)}, u32[]{:S(2)}, u32[]{:S(2)}) collective-permute-start(bf16[256,1024]{1,0:T(8,128)(2,1)} %refs_0_.3), channel_id=1, source_target_pairs={{0,4},{1,5},{2,6},{3,7},{4,0},{5,1},{6,2},{7,3},{8,12},{9,13},{10,... | collective-permute-start | bytes 1572872 | tf_op jit(solution)/shard_map/ppermute | solution.py:369
  15.0 14.0 %collective-permute-start.1 = (bf16[2,256,128]{2,1,0:T(8,128)(2,1)S(1)}, bf16[2,256,128]{2,1,0:T(8,128)(2,1)S(1)}, u32[]{:S(2)}, u32[]{:S(2)}) collective-permute-start(bf16[2,256,128]{2,1,0:T(8,128)(2,1)S(1)} %pad_maximum_fusion.3), channel_id=1, source_target_pairs={{0,2},{1,3},{2,0},{3,1},{4,6},{5,7},{6,4},{7,5},{8,10},{9,11},{10,... | collective-permute-start | bytes 393224 | tf_op jit(solution)/shard_map/ppermute | solution.py:429
  29.7 9.3 %collective-permute-start.2 = (bf16[4,256,128]{2,1,0:T(8,128)(2,1)S(1)}, bf16[4,256,128]{2,1,0:T(8,128)(2,1)S(1)}, u32[]{:S(2)}, u32[]{:S(2)}) collective-permute-start(bf16[4,256,128]{2,1,0:T(8,128)(2,1)S(1)} %pad_maximum_fusion.2), channel_id=1, source_target_pairs={{0,4},{1,5},{2,6},{3,7},{4,0},{5,1},{6,2},{7,3},{8,12},{9,13},{10,... | collective-permute-start | bytes 786440 | tf_op jit(solution)/shard_map/ppermute | solution.py:429
  31.5 13.7 %collective-permute-start.3 = (bf16[256,1024]{1,0:T(8,128)(2,1)}, bf16[256,1024]{1,0:T(8,128)(2,1)}, u32[]{:S(2)}, u32[]{:S(2)}) collective-permute-start(bf16[256,1024]{1,0:T(8,128)(2,1)} %refs_0_.3), channel_id=1, source_target_pairs={{0,1},{1,0},{2,3},{3,2},{4,5},{5,4},{6,7},{7,6},{8,9},{9,8},{10,11... | collective-permute-start | bytes 1572872 | tf_op jit(solution)/shard_map/ppermute | solution.py:369
  32.5 11.0 %collective-permute-start.8 = (bf16[128,1024]{1,0:T(8,128)(2,1)S(1)}, bf16[128,1024]{1,0:T(8,128)(2,1)}, u32[]{:S(2)}, u32[]{:S(2)}) collective-permute-start(bf16[128,1024]{1,0:T(8,128)(2,1)S(1)} %slice.277), channel_id=1, source_target_pairs={{0,4},{1,5},{2,6},{3,7},{4,0},{5,1},{6,2},{7,3},{8,12},{9,13},{10,... | collective-permute-start | bytes 786440 | tf_op jit(solution)/shard_map/ppermute | solution.py:369
  33.8 9.7 %collective-permute-start.9 = (bf16[128,1024]{1,0:T(8,128)(2,1)S(1)}, bf16[128,1024]{1,0:T(8,128)(2,1)}, u32[]{:S(2)}, u32[]{:S(2)}) collective-permute-start(bf16[128,1024]{1,0:T(8,128)(2,1)S(1)} %slice.278), channel_id=1, source_target_pairs={{0,2},{1,3},{2,0},{3,1},{4,6},{5,7},{6,4},{7,5},{8,10},{9,11},{10,... | collective-permute-start | bytes 786440 | tf_op jit(solution)/shard_map/ppermute | solution.py:369
  35.6 10.2 %collective-permute-start.5 = (bf16[256,1024]{1,0:T(8,128)(2,1)}, bf16[256,1024]{1,0:T(8,128)(2,1)}, u32[]{:S(2)}, u32[]{:S(2)}) collective-permute-start(bf16[256,1024]{1,0:T(8,128)(2,1)} %collective-permute-done.4.refs_2_), channel_id=1, source_target_pairs={{0,1},{1,0},{2,3},{3,2},{4,5},{5,4},{6,7},{7,6},{8,9},{9,8},{10,11... | collective-permute-start | bytes 1572872 | tf_op jit(solution)/shard_map/ppermute | solution.py:369
  55.4 94.5 %all-gather.5.cloned.1.call-start = ((), (), s32[]{:S(2)}) async-start(), calls=%async_computation.2 | async-start | bytes 4718592 | tf_op jit(solution)/shard_map/all_gather | solution.py:664
  61.0 617.9 %reduce-scatter.2.cloned.1.call-start = ((), (), s32[]{:S(2)}) async-start(), calls=%async_computation.3 | async-start | bytes 4718592 | tf_op jit(solution)/shard_map/reduce_scatter | solution.py:777
  109.7 18.7 %collective-permute-start.13 = (bf16[256,1024]{1,0:T(8,128)(2,1)S(1)}, bf16[256,1024]{1,0:T(8,128)(2,1)S(1)}, u32[]{:S(2)}, u32[]{:S(2)}) collective-permute-start(bf16[256,1024]{1,0:T(8,128)(2,1)S(1)} %get-tuple-element.156.refs_0_), channel_id=1, source_target_pairs={{0,2},{1,3},{2,0},{3,1},{4,6},{5,7},{6,4},{7,5},{8,10},{9,11},{10,... | collective-permute-start | bytes 1572872 | tf_op jit(solution)/shard_map/ppermute | solution.py:369
  111.2 21.1 %collective-permute-start.15 = (bf16[256,1024]{1,0:T(8,128)(2,1)S(1)}, bf16[256,1024]{1,0:T(8,128)(2,1)S(1)}, u32[]{:S(2)}, u32[]{:S(2)}) collective-permute-start(bf16[256,1024]{1,0:T(8,128)(2,1)S(1)} %get-tuple-element.156.refs_0_), channel_id=1, source_target_pairs={{0,4},{1,5},{2,6},{3,7},{4,0},{5,1},{6,2},{7,3},{8,12},{9,13},{10,... | collective-permute-start | bytes 1572872 | tf_op jit(solution)/shard_map/ppermute | solution.py:369
  112.7 31.9 %collective-permute-start.12 = (bf16[256,1024]{1,0:T(8,128)(2,1)S(1)}, bf16[256,1024]{1,0:T(8,128)(2,1)S(1)}, u32[]{:S(2)}, u32[]{:S(2)}) collective-permute-start(bf16[256,1024]{1,0:T(8,128)(2,1)S(1)} %get-tuple-element.156.refs_0_), channel_id=1, source_target_pairs={{0,1},{1,0},{2,3},{3,2},{4,5},{5,4},{6,7},{7,6},{8,9},{9,8},{10,11... | collective-permute-start | bytes 1572872 | tf_op jit(solution)/shard_map/ppermute | solution.py:369
  128.4 13.4 %collective-permute-start.17 = (bf16[128,1024]{1,0:T(8,128)(2,1)S(1)}, bf16[128,1024]{1,0:T(8,128)(2,1)S(1)}, u32[]{:S(2)}, u32[]{:S(2)}) collective-permute-start(bf16[128,1024]{1,0:T(8,128)(2,1)S(1)} %slice.279), channel_id=1, source_target_pairs={{0,4},{1,5},{2,6},{3,7},{4,0},{5,1},{6,2},{7,3},{8,12},{9,13},{10,... | collective-permute-start | bytes 786440 | tf_op jit(solution)/shard_map/ppermute | solution.py:369
  132.3 9.5 %collective-permute-start.18 = (bf16[128,1024]{1,0:T(8,128)(2,1)S(1)}, bf16[128,1024]{1,0:T(8,128)(2,1)S(1)}, u32[]{:S(2)}, u32[]{:S(2)}) collective-permute-start(bf16[128,1024]{1,0:T(8,128)(2,1)S(1)} %slice.280), channel_id=1, source_target_pairs={{0,2},{1,3},{2,0},{3,1},{4,6},{5,7},{6,4},{7,5},{8,10},{9,11},{10,... | collective-permute-start | bytes 786440 | tf_op jit(solution)/shard_map/ppermute | solution.py:369
  132.4 12.2 %collective-permute-start.14 = (bf16[256,1024]{1,0:T(8,128)(2,1)S(1)}, bf16[256,1024]{1,0:T(8,128)(2,1)S(1)}, u32[]{:S(2)}, u32[]{:S(2)}) collective-permute-start(bf16[256,1024]{1,0:T(8,128)(2,1)S(1)} %collective-permute-done.13.refs_2_), channel_id=1, source_target_pairs={{0,1},{1,0},{2,3},{3,2},{4,5},{5,4},{6,7},{7,6},{8,9},{9,8},{10,11... | collective-permute-start | bytes 1572872 | tf_op jit(solution)/shard_map/ppermute | solution.py:369
  132.5 12.2 %collective-permute-start.16 = (bf16[256,1024]{1,0:T(8,128)(2,1)S(1)}, bf16[256,1024]{1,0:T(8,128)(2,1)S(1)}, u32[]{:S(2)}, u32[]{:S(2)}) collective-permute-start(bf16[256,1024]{1,0:T(8,128)(2,1)S(1)} %collective-permute-done.15.refs_4_), channel_id=1, source_target_pairs={{0,1},{1,0},{2,3},{3,2},{4,5},{5,4},{6,7},{7,6},{8,9},{9,8},{10,11... | collective-permute-start | bytes 1572872 | tf_op jit(solution)/shard_map/ppermute | solution.py:369
  159.2 13.9 %collective-permute-start.22 = (bf16[256,1024]{1,0:T(8,128)(2,1)S(1)}, bf16[256,1024]{1,0:T(8,128)(2,1)}, u32[]{:S(2)}, u32[]{:S(2)}) collective-permute-start(bf16[256,1024]{1,0:T(8,128)(2,1)S(1)} %get-tuple-element.336.refs_0_), channel_id=1, source_target_pairs={{0,2},{1,3},{2,0},{3,1},{4,6},{5,7},{6,4},{7,5},{8,10},{9,11},{10,... | collective-permute-start | bytes 1572872 | tf_op jit(solution)/shard_map/ppermute | solution.py:369
  159.6 16.1 %collective-permute-start.24 = (bf16[256,1024]{1,0:T(8,128)(2,1)S(1)}, bf16[256,1024]{1,0:T(8,128)(2,1)}, u32[]{:S(2)}, u32[]{:S(2)}) collective-permute-start(bf16[256,1024]{1,0:T(8,128)(2,1)S(1)} %get-tuple-element.336.refs_0_), channel_id=1, source_target_pairs={{0,4},{1,5},{2,6},{3,7},{4,0},{5,1},{6,2},{7,3},{8,12},{9,13},{10,... | collective-permute-start | bytes 1572872 | tf_op jit(solution)/shard_map/ppermute | solution.py:369
  161.2 24.0 %collective-permute-start.21 = (bf16[256,1024]{1,0:T(8,128)(2,1)S(1)}, bf16[256,1024]{1,0:T(8,128)(2,1)}, u32[]{:S(2)}, u32[]{:S(2)}) collective-permute-start(bf16[256,1024]{1,0:T(8,128)(2,1)S(1)} %get-tuple-element.336.refs_0_), channel_id=1, source_target_pairs={{0,1},{1,0},{2,3},{3,2},{4,5},{5,4},{6,7},{7,6},{8,9},{9,8},{10,11... | collective-permute-start | bytes 1572872 | tf_op jit(solution)/shard_map/ppermute | solution.py:369
  177.2 8.5 %collective-permute-start.23 = (bf16[256,1024]{1,0:T(8,128)(2,1)}, bf16[256,1024]{1,0:T(8,128)(2,1)}, u32[]{:S(2)}, u32[]{:S(2)}) collective-permute-start(bf16[256,1024]{1,0:T(8,128)(2,1)} %collective-permute-done.22.refs_2_), channel_id=1, source_target_pairs={{0,1},{1,0},{2,3},{3,2},{4,5},{5,4},{6,7},{7,6},{8,9},{9,8},{10,11... | collective-permute-start | bytes 1572872 | tf_op jit(solution)/shard_map/ppermute | solution.py:369
  177.2 8.5 %collective-permute-start.25 = (bf16[256,1024]{1,0:T(8,128)(2,1)}, bf16[256,1024]{1,0:T(8,128)(2,1)}, u32[]{:S(2)}, u32[]{:S(2)}) collective-permute-start(bf16[256,1024]{1,0:T(8,128)(2,1)} %collective-permute-done.24.refs_4_), channel_id=1, source_target_pairs={{0,1},{1,0},{2,3},{3,2},{4,5},{5,4},{6,7},{7,6},{8,9},{9,8},{10,11... | collective-permute-start | bytes 1572872 | tf_op jit(solution)/shard_map/ppermute | solution.py:369
  204.3 33.0 %collective-permute-start.30 = (bf16[344,2048]{1,0:T(8,128)(2,1)S(1)}, bf16[344,2048]{1,0:T(8,128)(2,1)S(1)}, u32[]{:S(2)}, u32[]{:S(2)}) collective-permute-start(bf16[344,2048]{1,0:T(8,128)(2,1)S(1)} %weight_gradient.11.x), channel_id=1, source_target_pairs={{0,8},{8,0},{16,24},{24,16},{1,9},{9,1},{17,25},{25,17},{2,10},{10... | collective-permute-start | bytes 4227080 | tf_op jit(solution)/shard_map/ppermute | solution.py:636
  238.4 10.5 %collective-permute-start.33 = (bf16[4,256,1024]{2,1,0:T(8,128)(2,1)}, bf16[4,256,1024]{2,1,0:T(8,128)(2,1)}, u32[]{:S(2)}, u32[]{:S(2)}) collective-permute-start(bf16[4,256,1024]{2,1,0:T(8,128)(2,1)} %get-tuple-element.173), channel_id=1, source_target_pairs={{0,1},{1,0},{2,3},{3,2},{4,5},{5,4},{6,7},{7,6},{8,9},{9,8},{10,11... | collective-permute-start | bytes 6291464 | tf_op jit(solution)/shard_map/ppermute | solution.py:396
  238.4 16.3 %collective-permute-start.40 = (f32[2,1024]{1,0:T(2,128)S(1)}, f32[2,1024]{1,0:T(2,128)S(1)}, u32[]{:S(2)}, u32[]{:S(2)}) collective-permute-start(f32[2,1024]{1,0:T(2,128)S(1)} %pad_maximum_fusion.4), channel_id=1, source_target_pairs={{0,1},{1,0},{2,3},{3,2},{4,5},{5,4},{6,7},{7,6},{8,9},{9,8},{10,11... | collective-permute-start | bytes 24584 | tf_op jit(solution)/shard_map/ppermute | solution.py:670
  243.7 36.7 %collective-permute-start.32 = (bf16[344,2048]{1,0:T(8,128)(2,1)}, bf16[344,2048]{1,0:T(8,128)(2,1)}, u32[]{:S(2)}, u32[]{:S(2)}) collective-permute-start(bf16[344,2048]{1,0:T(8,128)(2,1)} %half_sum.13.half), channel_id=1, source_target_pairs={{8,16},{16,8},{9,17},{17,9},{10,18},{18,10},{11,19},{19,11},{12,20... | collective-permute-start | bytes 4227080 | tf_op jit(solution)/shard_map/ppermute | solution.py:631
  245.5 34.9 %collective-permute-start.31 = (bf16[344,2048]{1,0:T(8,128)(2,1)}, bf16[344,2048]{1,0:T(8,128)(2,1)}, u32[]{:S(2)}, u32[]{:S(2)}) collective-permute-start(bf16[344,2048]{1,0:T(8,128)(2,1)} %weight_gradient.12.x), channel_id=1, source_target_pairs={{0,8},{8,0},{16,24},{24,16},{1,9},{9,1},{17,25},{25,17},{2,10},{10... | collective-permute-start | bytes 4227080 | tf_op jit(solution)/shard_map/ppermute | solution.py:636
  253.7 9.6 %collective-permute-start.35 = (bf16[128,1024]{1,0:T(8,128)(2,1)}, bf16[128,1024]{1,0:T(8,128)(2,1)}, u32[]{:S(2)}, u32[]{:S(2)}) collective-permute-start(bf16[128,1024]{1,0:T(8,128)(2,1)} %get-tuple-element.309), channel_id=1, source_target_pairs={{0,4},{1,5},{2,6},{3,7},{4,0},{5,1},{6,2},{7,3},{8,12},{9,13},{10,... | collective-permute-start | bytes 786440 | tf_op jit(solution)/shard_map/ppermute | solution.py:396
  254.2 10.7 %collective-permute-start.37 = (bf16[128,1024]{1,0:T(8,128)(2,1)}, bf16[128,1024]{1,0:T(8,128)(2,1)}, u32[]{:S(2)}, u32[]{:S(2)}) collective-permute-start(bf16[128,1024]{1,0:T(8,128)(2,1)} %get-tuple-element.308), channel_id=1, source_target_pairs={{0,2},{1,3},{2,0},{3,1},{4,6},{5,7},{6,4},{7,5},{8,10},{9,11},{10,... | collective-permute-start | bytes 786440 | tf_op jit(solution)/shard_map/ppermute | solution.py:396
  265.0 14.1 %collective-permute-start.39 = (bf16[128,1024]{1,0:T(8,128)(2,1)}, bf16[128,1024]{1,0:T(8,128)(2,1)S(1)}, u32[]{:S(2)}, u32[]{:S(2)}) collective-permute-start(bf16[128,1024]{1,0:T(8,128)(2,1)} %get-tuple-element.311), channel_id=1, source_target_pairs={{0,4},{1,5},{2,6},{3,7},{4,0},{5,1},{6,2},{7,3},{8,12},{9,13},{10,... | collective-permute-start | bytes 786440 | tf_op jit(solution)/shard_map/ppermute | solution.py:396
  267.2 11.8 %collective-permute-start.36 = (bf16[128,1024]{1,0:T(8,128)(2,1)S(1)}, bf16[128,1024]{1,0:T(8,128)(2,1)S(1)}, u32[]{:S(2)}, u32[]{:S(2)}) collective-permute-start(bf16[128,1024]{1,0:T(8,128)(2,1)S(1)} %get-tuple-element.307), channel_id=1, source_target_pairs={{0,2},{1,3},{2,0},{3,1},{4,6},{5,7},{6,4},{7,5},{8,10},{9,11},{10,... | collective-permute-start | bytes 786440 | tf_op jit(solution)/shard_map/ppermute | solution.py:396
  283.4 15.4 %collective-permute-start.44 = (bf16[344,2048]{1,0:T(8,128)(2,1)S(1)}, bf16[344,2048]{1,0:T(8,128)(2,1)S(1)}, u32[]{:S(2)}, u32[]{:S(2)}) collective-permute-start(bf16[344,2048]{1,0:T(8,128)(2,1)S(1)} %half_sum.14.half), channel_id=1, source_target_pairs={{8,16},{16,8},{9,17},{17,9},{10,18},{18,10},{11,19},{19,11},{12,20... | collective-permute-start | bytes 4227080 | tf_op jit(solution)/shard_map/ppermute | solution.py:631
  287.0 32.4 %collective-permute-start.43 = (bf16[344,2048]{1,0:T(8,128)(2,1)S(1)}, bf16[344,2048]{1,0:T(8,128)(2,1)S(1)}, u32[]{:S(2)}, u32[]{:S(2)}) collective-permute-start(bf16[344,2048]{1,0:T(8,128)(2,1)S(1)} %outgoing.9.refs_2_), channel_id=1, source_target_pairs={{0,8},{8,0},{16,24},{24,16},{1,9},{9,1},{17,25},{25,17},{2,10},{10... | collective-permute-start | bytes 4227080 | tf_op jit(solution)/shard_map/ppermute | solution.py:636
  320.1 29.4 %collective-permute-start.46 = (bf16[344,2048]{1,0:T(8,128)(2,1)S(1)}, bf16[344,2048]{1,0:T(8,128)(2,1)S(1)}, u32[]{:S(2)}, u32[]{:S(2)}) collective-permute-start(bf16[344,2048]{1,0:T(8,128)(2,1)S(1)} %half_sum.15.half), channel_id=1, source_target_pairs={{8,16},{16,8},{9,17},{17,9},{10,18},{18,10},{11,19},{19,11},{12,20... | collective-permute-start | bytes 4227080 | tf_op jit(solution)/shard_map/ppermute | solution.py:631
  321.7 36.0 %collective-permute-start.45 = (bf16[344,2048]{1,0:T(8,128)(2,1)S(1)}, bf16[344,2048]{1,0:T(8,128)(2,1)S(1)}, u32[]{:S(2)}, u32[]{:S(2)}) collective-permute-start(bf16[344,2048]{1,0:T(8,128)(2,1)S(1)} %outgoing.10.refs_3_), channel_id=1, source_target_pairs={{0,8},{8,0},{16,24},{24,16},{1,9},{9,1},{17,25},{25,17},{2,10},{10... | collective-permute-start | bytes 4227080 | tf_op jit(solution)/shard_map/ppermute | solution.py:636
  328.0 9.2 %collective-permute-start.51 = (bf16[128,1024]{1,0:T(8,128)(2,1)S(1)}, bf16[128,1024]{1,0:T(8,128)(2,1)S(1)}, u32[]{:S(2)}, u32[]{:S(2)}) collective-permute-start(bf16[128,1024]{1,0:T(8,128)(2,1)S(1)} %get-tuple-element.302), channel_id=1, source_target_pairs={{0,2},{1,3},{2,0},{3,1},{4,6},{5,7},{6,4},{7,5},{8,10},{9,11},{10,... | collective-permute-start | bytes 786440 | tf_op jit(solution)/shard_map/ppermute | solution.py:396
  328.6 14.3 %collective-permute-start.48 = (bf16[128,1024]{1,0:T(8,128)(2,1)S(1)}, bf16[128,1024]{1,0:T(8,128)(2,1)S(1)}, u32[]{:S(2)}, u32[]{:S(2)}) collective-permute-start(bf16[128,1024]{1,0:T(8,128)(2,1)S(1)} %get-tuple-element.304), channel_id=1, source_target_pairs={{0,2},{1,3},{2,0},{3,1},{4,6},{5,7},{6,4},{7,5},{8,10},{9,11},{10,... | collective-permute-start | bytes 786440 | tf_op jit(solution)/shard_map/ppermute | solution.py:396
  335.7 13.1 %collective-permute-start.53 = (bf16[128,1024]{1,0:T(8,128)(2,1)S(1)}, bf16[128,1024]{1,0:T(8,128)(2,1)S(1)}, u32[]{:S(2)}, u32[]{:S(2)}) collective-permute-start(bf16[128,1024]{1,0:T(8,128)(2,1)S(1)} %get-tuple-element.305), channel_id=1, source_target_pairs={{0,4},{1,5},{2,6},{3,7},{4,0},{5,1},{6,2},{7,3},{8,12},{9,13},{10,... | collective-permute-start | bytes 786440 | tf_op jit(solution)/shard_map/ppermute | solution.py:396
  337.4 11.4 %collective-permute-start.50 = (bf16[128,1024]{1,0:T(8,128)(2,1)S(1)}, bf16[128,1024]{1,0:T(8,128)(2,1)S(1)}, u32[]{:S(2)}, u32[]{:S(2)}) collective-permute-start(bf16[128,1024]{1,0:T(8,128)(2,1)S(1)} %get-tuple-element.301), channel_id=1, source_target_pairs={{0,2},{1,3},{2,0},{3,1},{4,6},{5,7},{6,4},{7,5},{8,10},{9,11},{10,... | collective-permute-start | bytes 786440 | tf_op jit(solution)/shard_map/ppermute | solution.py:396
  358.4 17.3 %collective-permute-start.55 = (bf16[344,2048]{1,0:T(8,128)(2,1)S(1)}, bf16[344,2048]{1,0:T(8,128)(2,1)S(1)}, u32[]{:S(2)}, u32[]{:S(2)}) collective-permute-start(bf16[344,2048]{1,0:T(8,128)(2,1)S(1)} %half_sum.16.half), channel_id=1, source_target_pairs={{8,16},{16,8},{9,17},{17,9},{10,18},{18,10},{11,19},{19,11},{12,20... | collective-permute-start | bytes 4227080 | tf_op jit(solution)/shard_map/ppermute | solution.py:631
  359.9 33.9 %collective-permute-start.54 = (bf16[344,2048]{1,0:T(8,128)(2,1)S(1)}, bf16[344,2048]{1,0:T(8,128)(2,1)S(1)}, u32[]{:S(2)}, u32[]{:S(2)}) collective-permute-start(bf16[344,2048]{1,0:T(8,128)(2,1)S(1)} %outgoing.11.refs_2_), channel_id=1, source_target_pairs={{0,8},{8,0},{16,24},{24,16},{1,9},{9,1},{17,25},{25,17},{2,10},{10... | collective-permute-start | bytes 4227080 | tf_op jit(solution)/shard_map/ppermute | solution.py:636
  394.6 31.0 %collective-permute-start.60 = (bf16[344,2048]{1,0:T(8,128)(2,1)S(1)}, bf16[344,2048]{1,0:T(8,128)(2,1)}, u32[]{:S(2)}, u32[]{:S(2)}) collective-permute-start(bf16[344,2048]{1,0:T(8,128)(2,1)S(1)} %half_sum.17.half), channel_id=1, source_target_pairs={{8,16},{16,8},{9,17},{17,9},{10,18},{18,10},{11,19},{19,11},{12,20... | collective-permute-start | bytes 4227080 | tf_op jit(solution)/shard_map/ppermute | solution.py:631
  398.3 33.0 %collective-permute-start.59 = (bf16[344,2048]{1,0:T(8,128)(2,1)}, bf16[344,2048]{1,0:T(8,128)(2,1)S(1)}, u32[]{:S(2)}, u32[]{:S(2)}) collective-permute-start(bf16[344,2048]{1,0:T(8,128)(2,1)} %outgoing.12.refs_3_), channel_id=1, source_target_pairs={{0,8},{8,0},{16,24},{24,16},{1,9},{9,1},{17,25},{25,17},{2,10},{10... | collective-permute-start | bytes 4227080 | tf_op jit(solution)/shard_map/ppermute | solution.py:636
  432.1 38.6 %collective-permute-start.62 = (bf16[344,2048]{1,0:T(8,128)(2,1)S(1)}, bf16[344,2048]{1,0:T(8,128)(2,1)}, u32[]{:S(2)}, u32[]{:S(2)}) collective-permute-start(bf16[344,2048]{1,0:T(8,128)(2,1)S(1)} %half_sum.18.half), channel_id=1, source_target_pairs={{8,16},{16,8},{9,17},{17,9},{10,18},{18,10},{11,19},{19,11},{12,20... | collective-permute-start | bytes 4227080 | tf_op jit(solution)/shard_map/ppermute | solution.py:631
  437.8 32.9 %collective-permute-start.61 = (bf16[344,2048]{1,0:T(8,128)(2,1)}, bf16[344,2048]{1,0:T(8,128)(2,1)S(1)}, u32[]{:S(2)}, u32[]{:S(2)}) collective-permute-start(bf16[344,2048]{1,0:T(8,128)(2,1)} %outgoing.13.refs_2_), channel_id=1, source_target_pairs={{0,8},{8,0},{16,24},{24,16},{1,9},{9,1},{17,25},{25,17},{2,10},{10... | collective-permute-start | bytes 4227080 | tf_op jit(solution)/shard_map/ppermute | solution.py:636
  471.4 19.3 %collective-permute-start.64 = (bf16[256,2048]{1,0:T(8,128)(2,1)S(1)}, bf16[256,2048]{1,0:T(8,128)(2,1)S(1)}, u32[]{:S(2)}, u32[]{:S(2)}) collective-permute-start(bf16[256,2048]{1,0:T(8,128)(2,1)S(1)} %half_sum.19.half), channel_id=1, source_target_pairs={{8,16},{16,8},{9,17},{17,9},{10,18},{18,10},{11,19},{19,11},{12,20... | collective-permute-start | bytes 3145736 | tf_op jit(solution)/shard_map/ppermute | solution.py:631
  474.7 31.3 %collective-permute-start.63 = (bf16[344,2048]{1,0:T(8,128)(2,1)S(1)}, bf16[344,2048]{1,0:T(8,128)(2,1)S(1)}, u32[]{:S(2)}, u32[]{:S(2)}) collective-permute-start(bf16[344,2048]{1,0:T(8,128)(2,1)S(1)} %outgoing.14.refs_3_), channel_id=1, source_target_pairs={{0,8},{8,0},{16,24},{24,16},{1,9},{9,1},{17,25},{25,17},{2,10},{10... | collective-permute-start | bytes 4227080 | tf_op jit(solution)/shard_map/ppermute | solution.py:636
  507.1 23.0 %collective-permute-start.67 = (bf16[4,256,1024]{2,1,0:T(8,128)(2,1)}, bf16[4,256,1024]{2,1,0:T(8,128)(2,1)}, u32[]{:S(2)}, u32[]{:S(2)}) collective-permute-start(bf16[4,256,1024]{2,1,0:T(8,128)(2,1)} %get-tuple-element.247), channel_id=1, source_target_pairs={{0,1},{1,0},{2,3},{3,2},{4,5},{5,4},{6,7},{7,6},{8,9},{9,8},{10,11... | collective-permute-start | bytes 6291464 | tf_op jit(solution)/shard_map/ppermute | solution.py:396
  517.8 12.0 %collective-permute-start.74 = (f32[1,1024]{1,0:T(1,128)S(1)}, f32[1,1024]{1,0:T(1,128)S(1)}, u32[]{:S(2)}, u32[]{:S(2)}) collective-permute-start(f32[1,1024]{1,0:T(1,128)S(1)} %get-tuple-element.248), channel_id=1, source_target_pairs={{0,1},{1,0},{2,3},{3,2},{4,5},{5,4},{6,7},{7,6},{8,9},{9,8},{10,11... | collective-permute-start | bytes 12296 | tf_op jit(solution)/shard_map/ppermute | solution.py:670
  522.7 47.4 %collective-permute-start.66 = (bf16[256,2048]{1,0:T(8,128)(2,1)}, bf16[256,2048]{1,0:T(8,128)(2,1)}, u32[]{:S(2)}, u32[]{:S(2)}) collective-permute-start(bf16[256,2048]{1,0:T(8,128)(2,1)} %half_sum.20.half), channel_id=1, source_target_pairs={{8,16},{16,8},{9,17},{17,9},{10,18},{18,10},{11,19},{19,11},{12,20... | collective-permute-start | bytes 3145736 | tf_op jit(solution)/shard_map/ppermute | solution.py:631
  526.6 43.5 %collective-permute-start.65 = (bf16[256,2048]{1,0:T(8,128)(2,1)}, bf16[256,2048]{1,0:T(8,128)(2,1)}, u32[]{:S(2)}, u32[]{:S(2)}) collective-permute-start(bf16[256,2048]{1,0:T(8,128)(2,1)} %outgoing.15.refs_1_), channel_id=1, source_target_pairs={{0,8},{8,0},{16,24},{24,16},{1,9},{9,1},{17,25},{25,17},{2,10},{10... | collective-permute-start | bytes 3145736 | tf_op jit(solution)/shard_map/ppermute | solution.py:636
  529.8 9.0 %collective-permute-start.75 = (f32[1,1024]{1,0:T(1,128)S(1)}, f32[1,1024]{1,0:T(1,128)}, u32[]{:S(2)}, u32[]{:S(2)}) collective-permute-start(f32[1,1024]{1,0:T(1,128)S(1)} %add.265), channel_id=1, source_target_pairs={{0,2},{1,3},{2,0},{3,1},{4,6},{5,7},{6,4},{7,5},{8,10},{9,11},{10,... | collective-permute-start | bytes 12296 | tf_op jit(solution)/shard_map/ppermute | solution.py:670
  535.0 13.4 %collective-permute-start.69 = (bf16[128,1024]{1,0:T(8,128)(2,1)}, bf16[128,1024]{1,0:T(8,128)(2,1)}, u32[]{:S(2)}, u32[]{:S(2)}) collective-permute-start(bf16[128,1024]{1,0:T(8,128)(2,1)} %get-tuple-element.297), channel_id=1, source_target_pairs={{0,4},{1,5},{2,6},{3,7},{4,0},{5,1},{6,2},{7,3},{8,12},{9,13},{10,... | collective-permute-start | bytes 786440 | tf_op jit(solution)/shard_map/ppermute | solution.py:396
  535.3 14.6 %collective-permute-start.71 = (bf16[128,1024]{1,0:T(8,128)(2,1)}, bf16[128,1024]{1,0:T(8,128)(2,1)}, u32[]{:S(2)}, u32[]{:S(2)}) collective-permute-start(bf16[128,1024]{1,0:T(8,128)(2,1)} %get-tuple-element.296), channel_id=1, source_target_pairs={{0,2},{1,3},{2,0},{3,1},{4,6},{5,7},{6,4},{7,5},{8,10},{9,11},{10,... | collective-permute-start | bytes 786440 | tf_op jit(solution)/shard_map/ppermute | solution.py:396
  538.8 22.4 %collective-permute-start.68 = (bf16[128,1024]{1,0:T(8,128)(2,1)}, bf16[128,1024]{1,0:T(8,128)(2,1)}, u32[]{:S(2)}, u32[]{:S(2)}) collective-permute-start(bf16[128,1024]{1,0:T(8,128)(2,1)} %get-tuple-element.298), channel_id=1, source_target_pairs={{0,2},{1,3},{2,0},{3,1},{4,6},{5,7},{6,4},{7,5},{8,10},{9,11},{10,... | collective-permute-start | bytes 786440 | tf_op jit(solution)/shard_map/ppermute | solution.py:396
  550.0 17.3 %collective-permute-start.73 = (bf16[128,1024]{1,0:T(8,128)(2,1)}, bf16[128,1024]{1,0:T(8,128)(2,1)S(1)}, u32[]{:S(2)}, u32[]{:S(2)}) collective-permute-start(bf16[128,1024]{1,0:T(8,128)(2,1)} %get-tuple-element.299), channel_id=1, source_target_pairs={{0,4},{1,5},{2,6},{3,7},{4,0},{5,1},{6,2},{7,3},{8,12},{9,13},{10,... | collective-permute-start | bytes 786440 | tf_op jit(solution)/shard_map/ppermute | solution.py:396
  552.9 14.4 %collective-permute-start.70 = (bf16[128,1024]{1,0:T(8,128)(2,1)S(1)}, bf16[128,1024]{1,0:T(8,128)(2,1)S(1)}, u32[]{:S(2)}, u32[]{:S(2)}) collective-permute-start(bf16[128,1024]{1,0:T(8,128)(2,1)S(1)} %get-tuple-element.295), channel_id=1, source_target_pairs={{0,2},{1,3},{2,0},{3,1},{4,6},{5,7},{6,4},{7,5},{8,10},{9,11},{10,... | collective-permute-start | bytes 786440 | tf_op jit(solution)/shard_map/ppermute | solution.py:396
  573.6 21.0 %collective-permute-start.78 = (bf16[256,2048]{1,0:T(8,128)(2,1)}, bf16[256,2048]{1,0:T(8,128)(2,1)}, u32[]{:S(2)}, u32[]{:S(2)}) collective-permute-start(bf16[256,2048]{1,0:T(8,128)(2,1)} %half_sum.21.half), channel_id=1, source_target_pairs={{8,16},{16,8},{9,17},{17,9},{10,18},{18,10},{11,19},{19,11},{12,20... | collective-permute-start | bytes 3145736 | tf_op jit(solution)/shard_map/ppermute | solution.py:631
  579.0 21.5 %collective-permute-start.77 = (bf16[256,2048]{1,0:T(8,128)(2,1)}, bf16[256,2048]{1,0:T(8,128)(2,1)}, u32[]{:S(2)}, u32[]{:S(2)}) collective-permute-start(bf16[256,2048]{1,0:T(8,128)(2,1)} %outgoing.16.refs_1_), channel_id=1, source_target_pairs={{0,8},{8,0},{16,24},{24,16},{1,9},{9,1},{17,25},{25,17},{2,10},{10... | collective-permute-start | bytes 3145736 | tf_op jit(solution)/shard_map/ppermute | solution.py:636
  603.0 21.7 %collective-permute-start.79 = (bf16[272,2048]{1,0:T(8,128)(2,1)S(1)}, bf16[272,2048]{1,0:T(8,128)(2,1)S(1)}, u32[]{:S(2)}, u32[]{:S(2)}) collective-permute-start(bf16[272,2048]{1,0:T(8,128)(2,1)S(1)} %outgoing.17.refs_1_), channel_id=1, source_target_pairs={{0,8},{8,0},{16,24},{24,16},{1,9},{9,1},{17,25},{25,17},{2,10},{10... | collective-permute-start | bytes 3342344 | tf_op jit(solution)/shard_map/ppermute | solution.py:636
  625.3 25.6 %collective-permute-start.82 = (bf16[272,2048]{1,0:T(8,128)(2,1)S(1)}, bf16[272,2048]{1,0:T(8,128)(2,1)S(1)}, u32[]{:S(2)}, u32[]{:S(2)}) collective-permute-start(bf16[272,2048]{1,0:T(8,128)(2,1)S(1)} %half_sum.23.x), channel_id=1, source_target_pairs={{8,16},{16,8},{9,17},{17,9},{10,18},{18,10},{11,19},{19,11},{12,20... | collective-permute-start | bytes 3342344 | tf_op jit(solution)/shard_map/ppermute | solution.py:631
  626.7 24.2 %collective-permute-start.81 = (bf16[256,2048]{1,0:T(8,128)(2,1)S(1)}, bf16[256,2048]{1,0:T(8,128)(2,1)S(1)}, u32[]{:S(2)}, u32[]{:S(2)}) collective-permute-start(bf16[256,2048]{1,0:T(8,128)(2,1)S(1)} %half_sum.24.refs_1_), channel_id=1, source_target_pairs={{0,8},{8,0},{16,24},{24,16},{1,9},{9,1},{17,25},{25,17},{2,10},{10... | collective-permute-start | bytes 3145736 | tf_op jit(solution)/shard_map/ppermute | solution.py:636
  652.8 28.5 %collective-permute-start.83 = (bf16[272,2048]{1,0:T(8,128)(2,1)}, bf16[272,2048]{1,0:T(8,128)(2,1)}, u32[]{:S(2)}, u32[]{:S(2)}) collective-permute-start(bf16[272,2048]{1,0:T(8,128)(2,1)} %half_sum.25.refs_1_), channel_id=1, source_target_pairs={{0,8},{8,0},{16,24},{24,16},{1,9},{9,1},{17,25},{25,17},{2,10},{10... | collective-permute-start | bytes 3342344 | tf_op jit(solution)/shard_map/ppermute | solution.py:636
  (159 other events, 1385.7 us)
Sparse Core Ops, SparseCore 0:
  55.6 38.0 all-gather.2
  96.1 47.4 all-gather.4
  516.4 60.2 reduce-scatter.1

commit v4 on v3

--- a/solution.py
+++ b/solution.py
@@ -142,7 +142,7 @@
         in_specs=[SM]+[whole(v) for v in args],out_specs=[whole(v) for v in outs],
         scratch_shapes=[pltpu.VMEM((nb,L,2*L),BF),pltpu.VMEM((nb,HD,L),F32)],
         compiler_params=pltpu.CompilerParams(vmem_limit_bytes=44<<20), name="mix_forward",
-        cost_estimate=pl.CostEstimate(flops=T*heads*4000*64*50, bytes_accessed=T*heads*64*40, transcendentals=0))(
+        cost_estimate=pl.CostEstimate(flops=T*heads*64, bytes_accessed=T*heads, transcendentals=0))(
             reset,*args)
 
 def bwd_kernel(heads, nb, base, last, reset, dOT, zt_i, zb_i, td_i, qa_i, ka_i, wt_i, rows, consts, *refs):
@@ -271,23 +271,25 @@
 ROWS = 64
 
 
-def fetch(pieces, spots, buf, sems):
+def fetch(pieces, spots, buf, sems, f):
     copies = []
     for i, p in enumerate(pieces):
         at = pl.ds(pl.multiple_of(spots[i], 16), p.shape[0])
         copies.append(pltpu.make_async_copy(p, buf.at[at], sems.at[i]))
         copies[-1].start()
-    for c in copies:
+    acc = jnp.zeros((8, buf.shape[1]), F32)
+    for i, c in enumerate(copies):
         c.wait()
-
-
-def fold(buf, width, f):
+        acc = fold(buf, spots[i], pieces[i].shape[0], f, acc)
+    return jnp.sum(acc, 0, keepdims=True)
+
+
+def fold(buf, first, rows, f, acc):
     def add(i, acc):
-        v = f(buf[pl.ds(pl.multiple_of(i * ROWS, ROWS), ROWS), :].astype(F32))
+        v = f(buf[pl.ds(pl.multiple_of(first + i * ROWS, ROWS), ROWS), :].astype(F32))
         return acc + jnp.sum(v.reshape(ROWS // 8, 8, v.shape[1]), 0)
 
-    acc = lax.fori_loop(0, width // ROWS, add, jnp.zeros((8, buf.shape[1]), F32))
-    return jnp.sum(acc, 0, keepdims=True)
+    return lax.fori_loop(0, rows // ROWS, add, acc)
 
 
 def rms_kernel(n, lane, width, fresh, spots, blocks, *refs):
@@ -298,12 +300,10 @@
             at = pl.ds(pl.multiple_of(spots[i if i < 7 else 8], 16), blocks.shape[1])
             copies.append(pltpu.make_async_copy(blocks.at[i], gains.at[at], gain_sems.at[i]))
             copies[-1].start()
-        fetch(pieces, spots, buf, sems)
+    scale = lax.rsqrt(fetch(pieces, spots, buf, sems, lambda v: v * v) * (1.0 / width) + EPS)
+    if fresh:
         for c in copies:
             c.wait()
-    else:
-        fetch(pieces, spots, buf, sems)
-    scale = lax.rsqrt(fold(buf, width, lambda v: v * v) * (1.0 / width) + EPS)
     scale_out[...] = scale
     source = gains if fresh else blocks
 
@@ -320,10 +320,10 @@
 
 def moments_kernel(n, width, spots, *refs):
     pieces, (out, mean_out, scale_out, sems) = refs[:n], refs[n:]
-    fetch(pieces, spots, out, sems)
-    mean = fold(out, width, lambda v: v) * (1.0 / width)
+    mean = fetch(pieces, spots, out, sems, lambda v: v) * (1.0 / width)
     mean_out[...] = mean
-    scale_out[...] = lax.rsqrt(fold(out, width, lambda v: (v - mean) * (v - mean)) * (1.0 / width) + EPS)
+    acc = fold(out, 0, width, lambda v: (v - mean) * (v - mean), jnp.zeros((8, out.shape[1]), F32))
+    scale_out[...] = lax.rsqrt(jnp.sum(acc, 0, keepdims=True) * (1.0 / width) + EPS)
 
 
 def rms_rows(pieces, spots, gains, lane, tok, width):
@@ -465,38 +465,50 @@
     return pl.BlockSpec((v.shape[0], COLS), lambda i: (0, i))
 
 
-def half_kernel(x, air, out):
-    out[...] = (x[...].astype(F32) + air[:x.shape[0], :].astype(F32)).astype(BF)
-
-
-def half_sum(x, air):
-    return pl.pallas_call(
-        half_kernel, grid=(x.shape[1] // COLS,), out_shape=jax.ShapeDtypeStruct(x.shape, BF),
-        in_specs=[column_blocks(x), column_blocks(air)], out_specs=column_blocks(x),
-        compiler_params=wide_params(16), cost_estimate=FREE, name="half_sum")(x, air)
-
-
-def outgoing_kernel(end, x, half, air, out):
-    def put(v):
-        out[:v.shape[0], :] = v
-        if v.shape[0] < out.shape[0]:
-            out[v.shape[0]:, :] = jnp.zeros((out.shape[0] - v.shape[0], out.shape[1]), BF)
-
-    @pl.when(end[0] > 0)
-    def _():
-        put(x[...])
-
-    @pl.when(end[0] == 0)
-    def _():
-        put((half[...].astype(F32) + air[...].astype(F32)).astype(BF))
-
-
-def outgoing(end, x, half, air):
-    out = jax.ShapeDtypeStruct((max(x.shape[0], half.shape[0]), x.shape[1]), BF)
-    return pl.pallas_call(
-        outgoing_kernel, grid=(x.shape[1] // COLS,), out_shape=out,
-        in_specs=[SM] + [column_blocks(v) for v in (x, half, air)], out_specs=column_blocks(out),
-        compiler_params=wide_params(16), cost_estimate=FREE, name="outgoing")(end, x, half, air)
+def turn_kernel(landed, job, back, end, *refs):
+    refs = list(refs)
+    ins = [refs.pop(0) for _ in range(2 * landed + job * back + 2 * back)]
+    if landed:
+        x, air = ins.pop(0), ins.pop(0)
+        half = refs.pop(0)
+        half[...] = (x[...].astype(F32) + air[:x.shape[0], :].astype(F32)).astype(BF)
+    if back:
+        out = refs.pop(0)
+
+        def put(v):
+            out[:v.shape[0], :] = v
+            if v.shape[0] < out.shape[0]:
+                out[v.shape[0]:, :] = jnp.zeros((out.shape[0] - v.shape[0], out.shape[1]), BF)
+
+        half, air = ins[-2:]
+
+        def total():
+            put((half[...].astype(F32) + air[...].astype(F32)).astype(BF))
+
+        if job:
+            pl.when(end[0] > 0)(lambda: put(ins[0][...]))
+            pl.when(end[0] == 0)(total)
+        else:
+            total()
+
+
+def turn(end, sent, came, job, back):
+    ins = ([sent.x, came] if sent else []) + ([job.x] if job and back else []) + ([back.half, back.air] if back else [])
+    outs = []
+    if sent:
+        outs.append(jax.ShapeDtypeStruct(sent.x.shape, BF))
+    if back:
+        rows = max(job.x.shape[0] if job else 0, back.half.shape[0])
+        outs.append(jax.ShapeDtypeStruct((rows, back.half.shape[1]), BF))
+    res = []
+    if outs:
+        res = list(pl.pallas_call(
+            functools.partial(turn_kernel, bool(sent), bool(job), bool(back)), grid=(outs[0].shape[1] // COLS,),
+            out_shape=outs, in_specs=[SM] + [column_blocks(v) for v in ins], out_specs=[column_blocks(v) for v in outs],
+            compiler_params=wide_params(24), cost_estimate=FREE, name="turn")(end, *ins))
+    half = res.pop(0) if sent else None
+    load = res.pop(0) if back else (job.x if job else None)
+    return half, load
 
 
 def finish_kernel(sizes, end, *refs):
@@ -602,50 +614,65 @@
         at = lax.axis_index("dp")
         self.end = ((at == 0) | (at == 3)).astype(jnp.int32).reshape(1)
         self.outer = self.inner = None
-
-    def load(self, job, back):
-        if back is None:
-            return job.x
-        if job is None:
-            return half_sum(back.half, back.air)
-        return outgoing(self.end, job.x, back.half, back.air)
+        self.groups = []
+        self.idle = False
 
     def tick(self, x, *values):
         job = Sum(x) if x is not None else None
         if not self.line:
             return (job,) + tuple(tie(*values)) if values else (job,)
         airs = ([self.outer[2]] if self.outer else []) + ([self.inner.air] if self.inner else [])
-        held = tie(*airs, *([x] if job else []), *values)
+        done = []
+        if self.idle:
+            done = [g for g in self.groups if g.out is None and all(s.landed is not None for s in g.jobs)]
+            for g in done:
+                g.out = finish(self.end, g.jobs)
+        held = tie(*airs, *([x] if job else []), *values, *[g.out for g in done])
+        for g, out in zip(reversed(done), reversed(held)):
+            g.out = out
         if job:
             job.x = held[len(airs)]
-        values = held[len(airs) + (1 if job else 0):]
+        values = held[len(airs) + (1 if job else 0):len(held) - len(done)]
         back, self.inner = self.inner, None
         if back:
             back.air = held[len(airs) - 1]
-        if self.outer:
-            sent, gone, _ = self.outer
-            if gone:
-                gone.landed = held[0]
-            if sent:
-                sent.half = half_sum(sent.x, held[0])
-                sent.air = lax.ppermute(sent.half, "dp", [(1, 2), (2, 1)])
-                self.inner = sent
+        sent, gone = self.outer[:2] if self.outer else (None, None)
+        if gone:
+            gone.landed = held[0]
+        half, load = turn(self.end, sent, held[0], job, back)
+        if sent:
+            sent.half = half
+            sent.air = lax.ppermute(half, "dp", [(1, 2), (2, 1)])
+            self.inner = sent
         self.outer = None
-        if job or back:
-            load = self.load(job, back)
+        if load is not None:
             self.outer = (job, back, lax.ppermute(load, "dp", [(0, 1), (1, 0), (2, 3), (3, 2)]))
             if back:
                 back.sent = load
+        loads = [v for v in (half, load) if v is not None]
+        if values and loads:
+            values = tie(*values, *loads)[:len(values)]
         return (job,) + tuple(values)
 
     def drain(self):
+        self.idle = True
         while self.outer or self.inner:
             self.tick(None)
 
-    def result(self, *jobs):
+    def group(self, *jobs):
+        self.groups.append(Group(jobs))
+        return self.groups[-1]
+
+    def result(self, group):
         if not self.line:
-            return lax.psum(jnp.concatenate([job.x for job in jobs], 0), "dp").astype(F32)
-        return finish(self.end, jobs)
+            return lax.psum(jnp.concatenate([s.x for s in group.jobs], 0), "dp").astype(F32)
+        return finish(self.end, group.jobs) if group.out is None else group.out
+
+
+class Group:
+    def __init__(self, jobs):
+        self.jobs = jobs
+        self.out = None
 
 
 def on_device(
@@ -678,10 +705,11 @@
     gain_blocks = spread_gains(jnp.stack([attn_gain, post_gain, post_shift, ffn_gain], 1), devs)
     consts = [hold(v, *tok_pieces.direct).astype(F32) for v in (inner_weight, inner_bias, inner_gain, inner_shift)]
     consts = pack_consts(*consts)
+    g_full = gather(hold(out_grad, gain_blocks, *tok_pieces.diag))
     nin, q1, gains = rms_rows(tok_pieces.all, spots, gain_blocks, 0, tok, width)
-    g_full = gather(hold(out_grad, q1))
     gate = nn(w_gate, nin).astype(BF)
-    gates = gather(gate)
+    gelu_own = gelu_tanh(gate.astype(F32))
+    gates = gather(gelu_own.astype(BF))
     nin_q = hold(nin, gate)
     q_t = nn(w_query, nin_q)
     k_t = nn(w_key, nin_q)
@@ -697,7 +725,7 @@
     mix, mean3, r3 = moments_rows(mix_pieces.all, spots, tok, width)
     gain_cols = gains.astype(F32)
     mixed = (((mix.astype(F32) - mean3) * r3 * gain_cols[:, 1:2] + gain_cols[:, 2:3])
-             * gelu_tanh(gates.astype(F32))).astype(BF)
+             * gates.astype(F32)).astype(BF)
     hidden = tokens.astype(F32) + nn(w_out, mixed)
     hidden_low = hidden.astype(BF)
     nmid, q2, _ = rms_rows(Pieces(hidden_low, devs).all, spots, gains, 3, tok, width)
@@ -737,7 +765,8 @@
     gm.spread()
     out_w = wgrad(g_branch, mixed)
     gm = gm.result()
-    u0, gm, out_w, u1_x = belt.tick(u0_x, gm, out_w, hup[1])
+    u0, gm, out_w, u1_x, act = belt.tick(u0_x, gm, out_w, hup[1], act)
+    ffn_part = tn(w_down, act).astype(BF)
     n3 = (mixer_own.astype(F32) - mean3) * r3
     pg_own = post_gain.astype(F32)[:, None]
     ps_own = post_shift.astype(F32)[:, None]
@@ -749,7 +778,8 @@
     sums = head_sum(jnp.concatenate([col_sum(m), col_sum(m * n3)], 0))
     s_plain, s_norm = sums[:1], sums[1:]
     g_mixer = r3 * (m - s_plain / width - n3 * s_norm / width)
-    u1, g_mixer, g_gate_pre, out_w = belt.tick(u1_x, g_mixer, g_gate_pre, out_w)
+    u1, g_mixer, g_gate_pre, out_w, ffn_part = belt.tick(u1_x, g_mixer, g_gate_pre, out_w, ffn_part)
+    ffn = lax.psum_scatter(ffn_part, "head", scatter_dimension=0, tiled=True)
     gate_w = wgrad(g_gate_pre, nin)
     saved = (zt, zb, td, qa, ka, wt, rows, consts)
     b1 = ttt_bwd(1, 2, reset, g_mixer, *saved)
@@ -765,17 +795,16 @@
     g_inner_g = dgl.reshape(HD, heads, MB).sum(-1).T
     g_inner_s = dsl.reshape(HD, heads, MB).sum(-1).T
     wide_q, wide_k, wide_v = [wgrad(v, nin) for v in (dq, dk, dv)]
-    wg, dq, dk, dv, gl, wide_q, wide_k, wide_v = belt.tick(gate_w, dq, dk, dv, gl, wide_q, wide_k, wide_v)
+    wg, dq, dk, dv, gl, wide_q, wide_k, wide_v, ffn = belt.tick(
+        gate_w, dq, dk, dv, gl, wide_q, wide_k, wide_v, ffn)
+    result = (hidden + ffn.astype(F32)).astype(BF)
     tall = jnp.concatenate([dq, dk, dv, g_gate_pre, jnp.pad(gl, ((0, 16 - heads), (0, 0)))], 0)
     gi = Scatter([stacked], [tall], nin, own, devs)
-    q, *gi.pair, gi.dot, act, wide_k = belt.tick(wide_q, *gi.pair, gi.dot, act, wide_k)
+    q, *gi.pair, gi.dot, wide_k = belt.tick(wide_q, *gi.pair, gi.dot, wide_k)
     gi.spread()
     in_dot = head_sum(gi.dot)
     gi = gi.result()
     g_wr = nt(gl, nin)
-    ffn_part = tn(w_down, act).astype(BF)
-    ffn = lax.psum_scatter(ffn_part, "head", scatter_dimension=0, tiled=True)
-    result = (hidden + ffn.astype(F32)).astype(BF)
     k, gi, in_dot, g_wr = belt.tick(wide_k, gi, in_dot, g_wr)
     x_own = tokens.astype(F32)
     ag_own = attn_gain.astype(F32)[:, None]
@@ -797,8 +826,9 @@
     count = small.shape[0]
     small = jnp.pad(small, (0, -count % (16 * width))).reshape(-1, width)
     v, = belt.tick(jnp.concatenate([wide_v, small], 0))
+    sums = [belt.group(*jobs) for jobs in ((d0, d1), (h0, h1), (u0, u1), (so,), (wg,), (q,), (k,), (v,))]
     belt.drain()
-    s_wv = belt.result(v)
+    s_down, s_hgate, s_hup, s_out, s_wg, s_wq, s_wk, s_wv = [belt.result(g) for g in sums]
     s_wv, small = s_wv[:own], s_wv[own:].reshape(-1)
     s_attn, s_pg, s_ps, s_fg, s_ib, s_ig, s_is, s_rb, slots = [small[i * own:(i + 1) * own] for i in range(9)]
     s_ib, s_ig, s_is = [v.reshape(heads, HD) for v in (s_ib, s_ig, s_is)]
@@ -811,9 +841,9 @@
     max_rate = jnp.max(slots[:, 1])
 
     return (
-        result, g_tokens, s_attn, belt.result(q), belt.result(k), s_wv, belt.result(wg),
-        s_wr.T, s_rb, s_iw, s_ib, s_ig, s_is, s_pg, s_ps, belt.result(so),
-        s_fg, belt.result(h0, h1), belt.result(u0, u1), belt.result(d0, d1), mean_rate, max_rate,
+        result, g_tokens, s_attn, s_wq, s_wk, s_wv, s_wg,
+        s_wr.T, s_rb, s_iw, s_ib, s_ig, s_is, s_pg, s_ps, s_out,
+        s_fg, s_hgate, s_hup, s_down, mean_rate, max_rate,
     )
 
 

time: 706 us -> 676 us (0.958)
  Pallas kernels: 212 us -> 193 us
  local copies, waits for them, and re-layouts: 59.1 us -> 68.3 us
  starting transfers between devices: 101 us -> 93.3 us
    unnamed x293 -> x345, local copies, waits for them, and re-layouts: 35.4 us -> 50.8 us
    pallas_call x22 -> x12, Pallas kernels: 39.3 us -> 24.5 us  [turn(): pl.pallas_call(functools.partial(turn_kernel, bool(sent), bool(job), bool...]
    ppermute x13, starting transfers between devices: 42.6 us -> 35.5 us  [tick(): lax.ppermute(load, 'dp', [(0, 1), (1, 0), (2, 3), (3, 2)])]
  transfers between devices with their start and end apart: 87 -> 87, of which waited for: 35 -> 35; matrix products, arithmetic and copies ran while one was open for 13% -> 10% of each run, Pallas kernels for 27% -> 24%
where the time goes in v4:
time: 676 us; the launch traced here: 669 us
  waiting for transfers between devices  222 us (33%)
  Pallas kernels  193 us (29%)
  starting transfers between devices  93.3 us (14%)
  local copies, waits for them, and re-layouts  68.3 us (10%)
  other arithmetic  40.6 us (6%)
  matrix products  33.1 us (5%)
  between operations  18.6 us (3%)
    ppermute x13, waiting for transfers between devices, tick(): lax.ppermute(load, 'dp', [(0, 1), (1, 0), (2, 3), (3, 2)])  121 us
    ppermute x48, waiting for transfers between devices, swap(): return lax.ppermute(v, 'head', [(i, i ^ bit) for i in range(8)])  77 us
    unnamed x345, local copies, waits for them, and re-layouts  50.8 us
    pallas_call x2, Pallas kernels, ttt_bwd(): pl.pallas_call(functools.partial(bwd_kernel, heads, nb, part * nb, last),...  40.7 us
    ppermute x13, starting transfers between devices, tick(): lax.ppermute(load, 'dp', [(0, 1), (1, 0), (2, 3), (3, 2)])  35.5 us
    pallas_call x1, Pallas kernels, ttt_fwd(): pl.pallas_call(functools.partial(fwd_kernel, heads, nb), out_shape=outs,...  34.9 us
    ppermute x48, starting transfers between devices, swap(): return lax.ppermute(v, 'head', [(i, i ^ bit) for i in range(8)])  33.6 us
    pallas_call x3, Pallas kernels, parts(): pl.pallas_call(functools.partial(parts_kernel, n), grid_spec=spec, out_sh...  27.4 us
  transfers between devices with their start and end apart: 87, of which 35 were waited for; matrix products, arithmetic and copies ran while one was open for 10% of the time, Pallas kernels for 24%

profile of v4, /device:TPU:0, one launch (start us, length us, event | category | flops | bytes accessed | tf_op | source)
XLA Modules:
  0.0 668.5 jit_solution(1754929105100874816)
XLA Ops:
  10.9 2.6 collective-permute-start.4
  15.6 13.4 %collective-permute-done.1 = bf16[2,256,128]{2,1,0:T(8,128)(2,1)S(1)} collective-permute-done((bf16[2,256,128]{2,1,0:T(8,128)(2,1)S(1)}, bf16[2,256,128]{2,1,0:T(8,128)(2,1)S(1)}, u32[]{:S(2)}, u32[]{:S(2)}) %collective-permute-start.1) | collective-permute-done | bytes 131104 | tf_op jit(solution)/shard_map/ppermute | solution.py:429
  34.6 3.6 collective-permute-done.2
  39.1 3.7 collective-permute-done.8.refs_6_
  50.7 6.2 rms_rows.2
  60.5 4.2 multiply_reduce_fusion.4
  64.7 2.6 convolution_bitcast_fusion.1.vT
  69.9 34.9 %mix_forward.1 = (bf16[256,1024]{1,0:T(8,128)(2,1)S(1)}, f32[64,64,64]{2,1,0:T(8,128)S(1)}, f32[64,64,64]{2,1,0:T(8,128)}, f32[64,64,64]{2,1,0:T(8,128)}, bf16[6...) custom-call(s32[64]{0:T(128)S(1)} %or_convert_fusion.reset, ...), custom_call_target="tpu_custom_call" | custom-call | flops 262144 | bytes 4096 | tf_op jit(solution)/shard_map/mix_forward/pallas_call | solution.py:141
  112.1 17.8 %collective-permute-done.13.refs_2_ = bf16[256,1024]{1,0:T(8,128)(2,1)S(1)} collective-permute-done((bf16[256,1024]{1,0:T(8,128)(2,1)S(1)}, bf16[256,1024]{1,0:T(8,128)(2,1)S(1)}, u32[]{:S(2)}, u32[]{:S(2)}) %collective-permute-start.13) | collective-permute-done | bytes 524320 | tf_op jit(solution)/shard_map/ppermute | solution.py:369
  132.6 5.4 collective-permute-done.17.refs_6_
  141.7 3.3 moments_rows.1
  147.1 4.7 multiply_convert_fusion.refs_2_.b
  155.4 13.2 %collective-permute-done.22.refs_2_ = bf16[256,1024]{1,0:T(8,128)(2,1)} collective-permute-done((bf16[256,1024]{1,0:T(8,128)(2,1)S(1)}, bf16[256,1024]{1,0:T(8,128)(2,1)}, u32[]{:S(2)}, u32[]{:S(2)}) %collective-permute-start.22) | collective-permute-done | bytes 524320 | tf_op jit(solution)/shard_map/ppermute | solution.py:369
  172.0 5.6 collective-permute-done.26.refs_6_
  181.7 6.4 rms_rows.3
  188.1 3.1 fusion.72
  191.4 3.4 fusion.5
  195.9 2.8 weight_gradient.11.refs_0_
  200.3 3.9 fusion.4
  207.7 12.0 %parts.3 = (bf16[4,256,1024]{2,1,0:T(8,128)(2,1)S(1)}, bf16[4,256,1024]{2,1,0:T(8,128)(2,1)}, f32[1,1024]{1,0:T(1,128)S(1)}) custom-call(s32[1]{0:T(128)} %bitcast.33.core, bf16[688,2048]{1,0:T(8,128)(2,1)S(1)} %copy-done.117, bf16[688,2048]{1,0:T(8,128)(2,1)S(1)} %copy-done.118, bf16[688,1024]{1,0:T(8,128)(2,1)S(1)} %get-tuple-element.251.refs_2_, ...), custom_call_target="tpu_custom_call" | custom-call | flops 10000000000 | bytes 10000000 | tf_op jit(solution)/shard_map/parts/pallas_call | solution.py:572
  219.7 12.0 %collective-permute-done.30.refs_1_ = bf16[344,2048]{1,0:T(8,128)(2,1)S(1)} collective-permute-done((bf16[344,2048]{1,0:T(8,128)(2,1)S(1)}, bf16[344,2048]{1,0:T(8,128)(2,1)S(1)}, u32[]{:S(2)}, u32[]{:S(2)}) %collective-permute-start.30) | collective-permute-done | bytes 1409056 | tf_op jit(solution)/shard_map/ppermute | solution.py:649
  235.4 3.1 collective-permute-start.31
  238.6 3.2 add_convert_fusion.2
  249.2 5.6 collective-permute-done.41
  261.4 2.8 collective-permute-done.34
  272.9 3.3 turn.13
  277.6 2.6 weight_gradient.15.refs_2_.refs_0_
  280.7 5.6 parts.4
  286.3 19.4 %collective-permute-done.43.refs_1_.refs_0_ = bf16[344,2048]{1,0:T(8,128)(2,1)S(1)} collective-permute-done((bf16[344,2048]{1,0:T(8,128)(2,1)S(1)}, bf16[344,2048]{1,0:T(8,128)(2,1)S(1)}, u32[]{:S(2)}, u32[]{:S(2)}) %collective-permute-start.43) | collective-permute-done | bytes 1409056 | tf_op jit(solution)/shard_map/ppermute | solution.py:649
  307.1 3.9 collective-permute-start.45
  316.6 4.7 collective-permute-done.49
  324.8 4.6 collective-permute-done.48
  336.0 6.4 collective-permute-done.45.refs_1_
  342.5 2.7 turn.15
  345.2 3.1 multiply_reduce_fusion
  350.2 3.7 collective-permute-start.54
  357.7 5.1 convert_bitcast_fusion
  363.6 2.7 subtract_multiply_fusion.dOT
  366.3 18.9 %collective-permute-done.54.refs_1_.refs_0_ = bf16[344,2048]{1,0:T(8,128)(2,1)} collective-permute-done((bf16[344,2048]{1,0:T(8,128)(2,1)}, bf16[344,2048]{1,0:T(8,128)(2,1)}, u32[]{:S(2)}, u32[]{:S(2)}) %collective-permute-start.54) | collective-permute-done | bytes 1409056 | tf_op jit(solution)/shard_map/ppermute | solution.py:649
  386.6 3.2 turn.16
  392.0 3.8 collective-permute-start.59
  405.8 20.2 %mix_backward.2 = (bf16[256,1024]{1,0:T(8,128)(2,1)S(1)}, bf16[256,1024]{1,0:T(8,128)(2,1)S(1)}, bf16[256,1024]{1,0:T(8,128)(2,1)S(1)}, f32[4,512]{1,0:T(4,128)S...) custom-call(s32[64]{0:T(128)S(1)} %or_convert_fusion.reset, ...), custom_call_target="tpu_custom_call" | custom-call | flops 131072 | bytes 2048 | tf_op jit(solution)/shard_map/mix_backward/pallas_call | solution.py:261
  429.6 3.2 collective-permute-start.61
  436.6 20.5 %mix_backward.3 = (bf16[256,1024]{1,0:T(8,128)(2,1)S(1)}, bf16[256,1024]{1,0:T(8,128)(2,1)S(1)}, bf16[256,1024]{1,0:T(8,128)(2,1)S(1)}, f32[4,512]{1,0:T(4,128)S...) custom-call(s32[64]{0:T(128)S(1)} %or_convert_fusion.reset, ...), custom_call_target="tpu_custom_call", output_to_operand_aliasing={{0}: (12, {}), {1}: (13, {}), {2}: (14, {})} | custom-call | flops 131072 | bytes 2048 | tf_op jit(solution)/shard_map/mix_backward/pallas_call | solution.py:261
  479.7 9.8 %parts.5 = (bf16[4,256,1024]{2,1,0:T(8,128)(2,1)S(1)}, bf16[4,256,1024]{2,1,0:T(8,128)(2,1)S(1)}, f32[1,1024]{1,0:T(1,128)S(1)}) custom-call(s32[1]{0:T(128)} %bitcast.33.core, bf16[1040,2048]{1,0:T(8,128)(2,1)S(1)} %copy-done.102, bf16[1040,1024]{1,0:T(8,128)(2,1)S(1)} %pad_dynamic-update-slice_fusion.1.refs_1_, bf16[2048,1024]{1,0:T(8,128)(2,1)S(1)} %copy-done.5), custom_call_target="tpu_custom_call" | custom-call | flops 10000000000 | bytes 10000000 | tf_op jit(solution)/shard_map/parts/pallas_call | solution.py:572
  489.5 17.9 %collective-permute-done.63.refs_1_ = bf16[344,2048]{1,0:T(8,128)(2,1)S(1)} collective-permute-done((bf16[344,2048]{1,0:T(8,128)(2,1)S(1)}, bf16[344,2048]{1,0:T(8,128)(2,1)S(1)}, u32[]{:S(2)}, u32[]{:S(2)}) %collective-permute-start.63) | collective-permute-done | bytes 1409056 | tf_op jit(solution)/shard_map/ppermute | solution.py:649
  518.4 3.2 add_convert_fusion
  527.0 3.6 collective-permute-done.69
  536.0 3.5 collective-permute-done.68
  539.6 3.5 fusion.71
  543.3 2.7 collective-permute-done.72
  548.4 4.2 turn.20
  557.1 3.6 fusion.21
  565.0 10.6 %collective-permute-done.77.refs_1_.refs_0_ = bf16[256,2048]{1,0:T(8,128)(2,1)S(1)} collective-permute-done((bf16[256,2048]{1,0:T(8,128)(2,1)}, bf16[256,2048]{1,0:T(8,128)(2,1)S(1)}, u32[]{:S(2)}, u32[]{:S(2)}) %collective-permute-start.77) | collective-permute-done | bytes 1048608 | tf_op jit(solution)/shard_map/ppermute | solution.py:649
  577.8 2.8 turn.21
  580.6 2.9 collective-permute-start.79
  584.5 3.2 finish.8
  587.7 5.9 finish.9
  593.6 3.2 finish.10
  596.8 3.9 finish.11
  600.6 3.6 finish.12
  606.4 4.8 collective-permute-start.81
  613.2 18.0 %collective-permute-done.81.refs_0_ = bf16[256,2048]{1,0:T(8,128)(2,1)S(1)} collective-permute-done((bf16[256,2048]{1,0:T(8,128)(2,1)S(1)}, bf16[256,2048]{1,0:T(8,128)(2,1)S(1)}, u32[]{:S(2)}, u32[]{:S(2)}) %collective-permute-start.81) | collective-permute-done | bytes 1048608 | tf_op jit(solution)/shard_map/ppermute | solution.py:649
  636.5 17.1 %collective-permute-done.83.refs_0_ = bf16[272,2048]{1,0:T(8,128)(2,1)S(1)} collective-permute-done((bf16[272,2048]{1,0:T(8,128)(2,1)S(1)}, bf16[272,2048]{1,0:T(8,128)(2,1)S(1)}, u32[]{:S(2)}, u32[]{:S(2)}) %collective-permute-start.83) | collective-permute-done | bytes 1114144 | tf_op jit(solution)/shard_map/ppermute | solution.py:649
  (638 shorter events, 204.6 us)
Async XLA Ops:
  7.2 101.8 %all-gather.3.cloned.1.call-start = ((), (), s32[]{:S(2)}) async-start(), calls=%async_computation.1 | async-start | bytes 4718592 | tf_op jit(solution)/shard_map/all_gather | solution.py:691
  10.9 20.0 %collective-permute-start.4 = (bf16[256,1024]{1,0:T(8,128)(2,1)}, bf16[256,1024]{1,0:T(8,128)(2,1)S(1)}, u32[]{:S(2)}, u32[]{:S(2)}) collective-permute-start(bf16[256,1024]{1,0:T(8,128)(2,1)} %refs_0_.3), channel_id=1, source_target_pairs={{0,2},{1,3},{2,0},{3,1},{4,6},{5,7},{6,4},{7,5},{8,10},{9,11},{10,... | collective-permute-start | bytes 1572872 | tf_op jit(solution)/shard_map/ppermute | solution.py:369
  13.5 18.5 %collective-permute-start.6 = (bf16[256,1024]{1,0:T(8,128)(2,1)}, bf16[256,1024]{1,0:T(8,128)(2,1)S(1)}, u32[]{:S(2)}, u32[]{:S(2)}) collective-permute-start(bf16[256,1024]{1,0:T(8,128)(2,1)} %refs_0_.3), channel_id=1, source_target_pairs={{0,4},{1,5},{2,6},{3,7},{4,0},{5,1},{6,2},{7,3},{8,12},{9,13},{10,... | collective-permute-start | bytes 1572872 | tf_op jit(solution)/shard_map/ppermute | solution.py:369
  15.0 14.0 %collective-permute-start.1 = (bf16[2,256,128]{2,1,0:T(8,128)(2,1)S(1)}, bf16[2,256,128]{2,1,0:T(8,128)(2,1)S(1)}, u32[]{:S(2)}, u32[]{:S(2)}) collective-permute-start(bf16[2,256,128]{2,1,0:T(8,128)(2,1)S(1)} %pad_maximum_fusion.3), channel_id=1, source_target_pairs={{0,2},{1,3},{2,0},{3,1},{4,6},{5,7},{6,4},{7,5},{8,10},{9,11},{10,... | collective-permute-start | bytes 393224 | tf_op jit(solution)/shard_map/ppermute | solution.py:429
  29.0 9.3 %collective-permute-start.2 = (bf16[4,256,128]{2,1,0:T(8,128)(2,1)S(1)}, bf16[4,256,128]{2,1,0:T(8,128)(2,1)S(1)}, u32[]{:S(2)}, u32[]{:S(2)}) collective-permute-start(bf16[4,256,128]{2,1,0:T(8,128)(2,1)S(1)} %pad_maximum_fusion.2), channel_id=1, source_target_pairs={{0,4},{1,5},{2,6},{3,7},{4,0},{5,1},{6,2},{7,3},{8,12},{9,13},{10,... | collective-permute-start | bytes 786440 | tf_op jit(solution)/shard_map/ppermute | solution.py:429
  31.7 11.2 %collective-permute-start.8 = (bf16[128,1024]{1,0:T(8,128)(2,1)S(1)}, bf16[128,1024]{1,0:T(8,128)(2,1)}, u32[]{:S(2)}, u32[]{:S(2)}) collective-permute-start(bf16[128,1024]{1,0:T(8,128)(2,1)S(1)} %slice.277), channel_id=1, source_target_pairs={{0,4},{1,5},{2,6},{3,7},{4,0},{5,1},{6,2},{7,3},{8,12},{9,13},{10,... | collective-permute-start | bytes 786440 | tf_op jit(solution)/shard_map/ppermute | solution.py:369
  32.8 10.1 %collective-permute-start.9 = (bf16[128,1024]{1,0:T(8,128)(2,1)S(1)}, bf16[128,1024]{1,0:T(8,128)(2,1)}, u32[]{:S(2)}, u32[]{:S(2)}) collective-permute-start(bf16[128,1024]{1,0:T(8,128)(2,1)S(1)} %slice.278), channel_id=1, source_target_pairs={{0,2},{1,3},{2,0},{3,1},{4,6},{5,7},{6,4},{7,5},{8,10},{9,11},{10,... | collective-permute-start | bytes 786440 | tf_op jit(solution)/shard_map/ppermute | solution.py:369
  42.9 104.2 %all-gather.5.cloned.1.call-start = ((), (), s32[]{:S(2)}) async-start(), calls=%async_computation.2 | async-start | bytes 4718592 | tf_op jit(solution)/shard_map/all_gather | solution.py:691
  59.5 409.0 %reduce-scatter.2.cloned.1.call-start = ((), (), s32[]{:S(2)}) async-start(), calls=%async_computation.3 | async-start | bytes 4718592 | tf_op jit(solution)/shard_map/reduce_scatter | solution.py:782
  109.0 20.9 %collective-permute-start.13 = (bf16[256,1024]{1,0:T(8,128)(2,1)S(1)}, bf16[256,1024]{1,0:T(8,128)(2,1)S(1)}, u32[]{:S(2)}, u32[]{:S(2)}) collective-permute-start(bf16[256,1024]{1,0:T(8,128)(2,1)S(1)} %get-tuple-element.228.refs_0_), channel_id=1, source_target_pairs={{0,2},{1,3},{2,0},{3,1},{4,6},{5,7},{6,4},{7,5},{8,10},{9,11},{10,... | collective-permute-start | bytes 1572872 | tf_op jit(solution)/shard_map/ppermute | solution.py:369
  110.6 20.9 %collective-permute-start.15 = (bf16[256,1024]{1,0:T(8,128)(2,1)S(1)}, bf16[256,1024]{1,0:T(8,128)(2,1)S(1)}, u32[]{:S(2)}, u32[]{:S(2)}) collective-permute-start(bf16[256,1024]{1,0:T(8,128)(2,1)S(1)} %get-tuple-element.228.refs_0_), channel_id=1, source_target_pairs={{0,4},{1,5},{2,6},{3,7},{4,0},{5,1},{6,2},{7,3},{8,12},{9,13},{10,... | collective-permute-start | bytes 1572872 | tf_op jit(solution)/shard_map/ppermute | solution.py:369
  112.1 29.5 %collective-permute-start.12 = (bf16[256,1024]{1,0:T(8,128)(2,1)S(1)}, bf16[256,1024]{1,0:T(8,128)(2,1)S(1)}, u32[]{:S(2)}, u32[]{:S(2)}) collective-permute-start(bf16[256,1024]{1,0:T(8,128)(2,1)S(1)} %get-tuple-element.228.refs_0_), channel_id=1, source_target_pairs={{0,1},{1,0},{2,3},{3,2},{4,5},{5,4},{6,7},{7,6},{8,9},{9,8},{10,11... | collective-permute-start | bytes 1572872 | tf_op jit(solution)/shard_map/ppermute | solution.py:369
  129.9 8.1 %collective-permute-start.17 = (bf16[128,1024]{1,0:T(8,128)(2,1)S(1)}, bf16[128,1024]{1,0:T(8,128)(2,1)S(1)}, u32[]{:S(2)}, u32[]{:S(2)}) collective-permute-start(bf16[128,1024]{1,0:T(8,128)(2,1)S(1)} %slice.279), channel_id=1, source_target_pairs={{0,4},{1,5},{2,6},{3,7},{4,0},{5,1},{6,2},{7,3},{8,12},{9,13},{10,... | collective-permute-start | bytes 786440 | tf_op jit(solution)/shard_map/ppermute | solution.py:369
  131.5 7.8 %collective-permute-start.18 = (bf16[128,1024]{1,0:T(8,128)(2,1)S(1)}, bf16[128,1024]{1,0:T(8,128)(2,1)S(1)}, u32[]{:S(2)}, u32[]{:S(2)}) collective-permute-start(bf16[128,1024]{1,0:T(8,128)(2,1)S(1)} %slice.280), channel_id=1, source_target_pairs={{0,2},{1,3},{2,0},{3,1},{4,6},{5,7},{6,4},{7,5},{8,10},{9,11},{10,... | collective-permute-start | bytes 786440 | tf_op jit(solution)/shard_map/ppermute | solution.py:369
  132.1 9.6 %collective-permute-start.14 = (bf16[256,1024]{1,0:T(8,128)(2,1)S(1)}, bf16[256,1024]{1,0:T(8,128)(2,1)S(1)}, u32[]{:S(2)}, u32[]{:S(2)}) collective-permute-start(bf16[256,1024]{1,0:T(8,128)(2,1)S(1)} %collective-permute-done.13.refs_2_), channel_id=1, source_target_pairs={{0,1},{1,0},{2,3},{3,2},{4,5},{5,4},{6,7},{7,6},{8,9},{9,8},{10,11... | collective-permute-start | bytes 1572872 | tf_op jit(solution)/shard_map/ppermute | solution.py:369
  132.1 9.6 %collective-permute-start.16 = (bf16[256,1024]{1,0:T(8,128)(2,1)S(1)}, bf16[256,1024]{1,0:T(8,128)(2,1)S(1)}, u32[]{:S(2)}, u32[]{:S(2)}) collective-permute-start(bf16[256,1024]{1,0:T(8,128)(2,1)S(1)} %collective-permute-done.15.refs_4_), channel_id=1, source_target_pairs={{0,1},{1,0},{2,3},{3,2},{4,5},{5,4},{6,7},{7,6},{8,9},{9,8},{10,11... | collective-permute-start | bytes 1572872 | tf_op jit(solution)/shard_map/ppermute | solution.py:369
  154.1 14.4 %collective-permute-start.22 = (bf16[256,1024]{1,0:T(8,128)(2,1)S(1)}, bf16[256,1024]{1,0:T(8,128)(2,1)}, u32[]{:S(2)}, u32[]{:S(2)}) collective-permute-start(bf16[256,1024]{1,0:T(8,128)(2,1)S(1)} %get-tuple-element.484.refs_0_), channel_id=1, source_target_pairs={{0,2},{1,3},{2,0},{3,1},{4,6},{5,7},{6,4},{7,5},{8,10},{9,11},{10,... | collective-permute-start | bytes 1572872 | tf_op jit(solution)/shard_map/ppermute | solution.py:369
  154.7 15.5 %collective-permute-start.24 = (bf16[256,1024]{1,0:T(8,128)(2,1)S(1)}, bf16[256,1024]{1,0:T(8,128)(2,1)}, u32[]{:S(2)}, u32[]{:S(2)}) collective-permute-start(bf16[256,1024]{1,0:T(8,128)(2,1)S(1)} %get-tuple-element.484.refs_0_), channel_id=1, source_target_pairs={{0,4},{1,5},{2,6},{3,7},{4,0},{5,1},{6,2},{7,3},{8,12},{9,13},{10,... | collective-permute-start | bytes 1572872 | tf_op jit(solution)/shard_map/ppermute | solution.py:369
  155.4 24.7 %collective-permute-start.21 = (bf16[256,1024]{1,0:T(8,128)(2,1)S(1)}, bf16[256,1024]{1,0:T(8,128)(2,1)}, u32[]{:S(2)}, u32[]{:S(2)}) collective-permute-start(bf16[256,1024]{1,0:T(8,128)(2,1)S(1)} %get-tuple-element.484.refs_0_), channel_id=1, source_target_pairs={{0,1},{1,0},{2,3},{3,2},{4,5},{5,4},{6,7},{7,6},{8,9},{9,8},{10,11... | collective-permute-start | bytes 1572872 | tf_op jit(solution)/shard_map/ppermute | solution.py:369
  169.5 8.1 %collective-permute-start.26 = (bf16[128,1024]{1,0:T(8,128)(2,1)S(1)}, bf16[128,1024]{1,0:T(8,128)(2,1)}, u32[]{:S(2)}, u32[]{:S(2)}) collective-permute-start(bf16[128,1024]{1,0:T(8,128)(2,1)S(1)} %slice.283), channel_id=1, source_target_pairs={{0,4},{1,5},{2,6},{3,7},{4,0},{5,1},{6,2},{7,3},{8,12},{9,13},{10,... | collective-permute-start | bytes 786440 | tf_op jit(solution)/shard_map/ppermute | solution.py:369
  171.5 9.1 %collective-permute-start.23 = (bf16[256,1024]{1,0:T(8,128)(2,1)}, bf16[256,1024]{1,0:T(8,128)(2,1)}, u32[]{:S(2)}, u32[]{:S(2)}) collective-permute-start(bf16[256,1024]{1,0:T(8,128)(2,1)} %collective-permute-done.22.refs_2_), channel_id=1, source_target_pairs={{0,1},{1,0},{2,3},{3,2},{4,5},{5,4},{6,7},{7,6},{8,9},{9,8},{10,11... | collective-permute-start | bytes 1572872 | tf_op jit(solution)/shard_map/ppermute | solution.py:369
  171.5 9.1 %collective-permute-start.25 = (bf16[256,1024]{1,0:T(8,128)(2,1)}, bf16[256,1024]{1,0:T(8,128)(2,1)}, u32[]{:S(2)}, u32[]{:S(2)}) collective-permute-start(bf16[256,1024]{1,0:T(8,128)(2,1)} %collective-permute-done.24.refs_4_), channel_id=1, source_target_pairs={{0,1},{1,0},{2,3},{3,2},{4,5},{5,4},{6,7},{7,6},{8,9},{9,8},{10,11... | collective-permute-start | bytes 1572872 | tf_op jit(solution)/shard_map/ppermute | solution.py:369
  198.7 33.0 %collective-permute-start.30 = (bf16[344,2048]{1,0:T(8,128)(2,1)S(1)}, bf16[344,2048]{1,0:T(8,128)(2,1)S(1)}, u32[]{:S(2)}, u32[]{:S(2)}) collective-permute-start(bf16[344,2048]{1,0:T(8,128)(2,1)S(1)} %weight_gradient.11.refs_0_), channel_id=1, source_target_pairs={{0,8},{8,0},{16,24},{24,16},{1,9},{9,1},{17,25},{25,17},{2,10},{10... | collective-permute-start | bytes 4227080 | tf_op jit(solution)/shard_map/ppermute | solution.py:649
  233.6 39.3 %collective-permute-start.32 = (bf16[344,2048]{1,0:T(8,128)(2,1)}, bf16[344,2048]{1,0:T(8,128)(2,1)}, u32[]{:S(2)}, u32[]{:S(2)}) collective-permute-start(bf16[344,2048]{1,0:T(8,128)(2,1)} %copy-done.34), channel_id=1, source_target_pairs={{8,16},{16,8},{9,17},{17,9},{10,18},{18,10},{11,19},{19,11},{12,20... | collective-permute-start | bytes 4227080 | tf_op jit(solution)/shard_map/ppermute | solution.py:645
  235.4 37.5 %collective-permute-start.31 = (bf16[344,2048]{1,0:T(8,128)(2,1)}, bf16[344,2048]{1,0:T(8,128)(2,1)}, u32[]{:S(2)}, u32[]{:S(2)}) collective-permute-start(bf16[344,2048]{1,0:T(8,128)(2,1)} %copy-done.40), channel_id=1, source_target_pairs={{0,8},{8,0},{16,24},{24,16},{1,9},{9,1},{17,25},{25,17},{2,10},{10... | collective-permute-start | bytes 4227080 | tf_op jit(solution)/shard_map/ppermute | solution.py:649
  238.5 7.9 %collective-permute-start.40 = (f32[2,1024]{1,0:T(2,128)S(1)}, f32[2,1024]{1,0:T(2,128)S(1)}, u32[]{:S(2)}, u32[]{:S(2)}) collective-permute-start(f32[2,1024]{1,0:T(2,128)S(1)} %pad_maximum_fusion.4), channel_id=1, source_target_pairs={{0,1},{1,0},{2,3},{3,2},{4,5},{5,4},{6,7},{7,6},{8,9},{9,8},{10,11... | collective-permute-start | bytes 24584 | tf_op jit(solution)/shard_map/ppermute | solution.py:697
  244.2 11.9 %collective-permute-start.35 = (bf16[128,1024]{1,0:T(8,128)(2,1)}, bf16[128,1024]{1,0:T(8,128)(2,1)}, u32[]{:S(2)}, u32[]{:S(2)}) collective-permute-start(bf16[128,1024]{1,0:T(8,128)(2,1)} %get-tuple-element.455), channel_id=1, source_target_pairs={{0,4},{1,5},{2,6},{3,7},{4,0},{5,1},{6,2},{7,3},{8,12},{9,13},{10,... | collective-permute-start | bytes 786440 | tf_op jit(solution)/shard_map/ppermute | solution.py:396
  245.8 10.7 %collective-permute-start.37 = (bf16[128,1024]{1,0:T(8,128)(2,1)}, bf16[128,1024]{1,0:T(8,128)(2,1)}, u32[]{:S(2)}, u32[]{:S(2)}) collective-permute-start(bf16[128,1024]{1,0:T(8,128)(2,1)} %get-tuple-element.454), channel_id=1, source_target_pairs={{0,2},{1,3},{2,0},{3,1},{4,6},{5,7},{6,4},{7,5},{8,10},{9,11},{10,... | collective-permute-start | bytes 786440 | tf_op jit(solution)/shard_map/ppermute | solution.py:396
  246.4 8.3 %collective-permute-start.41 = (f32[2,1024]{1,0:T(2,128)S(1)}, f32[2,1024]{1,0:T(2,128)}, u32[]{:S(2)}, u32[]{:S(2)}) collective-permute-start(f32[2,1024]{1,0:T(2,128)S(1)} %fusion.56), channel_id=1, source_target_pairs={{0,2},{1,3},{2,0},{3,1},{4,6},{5,7},{6,4},{7,5},{8,10},{9,11},{10,... | collective-permute-start | bytes 24584 | tf_op jit(solution)/shard_map/ppermute | solution.py:697
  254.8 9.5 %collective-permute-start.34 = (bf16[128,1024]{1,0:T(8,128)(2,1)}, bf16[128,1024]{1,0:T(8,128)(2,1)S(1)}, u32[]{:S(2)}, u32[]{:S(2)}) collective-permute-start(bf16[128,1024]{1,0:T(8,128)(2,1)} %get-tuple-element.456), channel_id=1, source_target_pairs={{0,2},{1,3},{2,0},{3,1},{4,6},{5,7},{6,4},{7,5},{8,10},{9,11},{10,... | collective-permute-start | bytes 786440 | tf_op jit(solution)/shard_map/ppermute | solution.py:396
  256.5 15.0 %collective-permute-start.39 = (bf16[128,1024]{1,0:T(8,128)(2,1)}, bf16[128,1024]{1,0:T(8,128)(2,1)S(1)}, u32[]{:S(2)}, u32[]{:S(2)}) collective-permute-start(bf16[128,1024]{1,0:T(8,128)(2,1)} %get-tuple-element.457), channel_id=1, source_target_pairs={{0,4},{1,5},{2,6},{3,7},{4,0},{5,1},{6,2},{7,3},{8,12},{9,13},{10,... | collective-permute-start | bytes 786440 | tf_op jit(solution)/shard_map/ppermute | solution.py:396
  259.9 11.6 %collective-permute-start.36 = (bf16[128,1024]{1,0:T(8,128)(2,1)S(1)}, bf16[128,1024]{1,0:T(8,128)(2,1)S(1)}, u32[]{:S(2)}, u32[]{:S(2)}) collective-permute-start(bf16[128,1024]{1,0:T(8,128)(2,1)S(1)} %get-tuple-element.453), channel_id=1, source_target_pairs={{0,2},{1,3},{2,0},{3,1},{4,6},{5,7},{6,4},{7,5},{8,10},{9,11},{10,... | collective-permute-start | bytes 786440 | tf_op jit(solution)/shard_map/ppermute | solution.py:396
  276.2 29.5 %collective-permute-start.43 = (bf16[344,2048]{1,0:T(8,128)(2,1)S(1)}, bf16[344,2048]{1,0:T(8,128)(2,1)S(1)}, u32[]{:S(2)}, u32[]{:S(2)}) collective-permute-start(bf16[344,2048]{1,0:T(8,128)(2,1)S(1)} %get-tuple-element.260.refs_2_), channel_id=1, source_target_pairs={{0,8},{8,0},{16,24},{24,16},{1,9},{9,1},{17,25},{25,17},{2,10},{10... | collective-permute-start | bytes 4227080 | tf_op jit(solution)/shard_map/ppermute | solution.py:649
  276.7 29.0 %collective-permute-start.44 = (bf16[344,2048]{1,0:T(8,128)(2,1)S(1)}, bf16[344,2048]{1,0:T(8,128)(2,1)S(1)}, u32[]{:S(2)}, u32[]{:S(2)}) collective-permute-start(bf16[344,2048]{1,0:T(8,128)(2,1)S(1)} %get-tuple-element.261.refs_3_), channel_id=1, source_target_pairs={{8,16},{16,8},{9,17},{17,9},{10,18},{18,10},{11,19},{19,11},{12,20... | collective-permute-start | bytes 4227080 | tf_op jit(solution)/shard_map/ppermute | solution.py:645
  307.1 35.4 %collective-permute-start.45 = (bf16[344,2048]{1,0:T(8,128)(2,1)S(1)}, bf16[344,2048]{1,0:T(8,128)(2,1)S(1)}, u32[]{:S(2)}, u32[]{:S(2)}) collective-permute-start(bf16[344,2048]{1,0:T(8,128)(2,1)S(1)} %get-tuple-element.277.refs_3_), channel_id=1, source_target_pairs={{0,8},{8,0},{16,24},{24,16},{1,9},{9,1},{17,25},{25,17},{2,10},{10... | collective-permute-start | bytes 4227080 | tf_op jit(solution)/shard_map/ppermute | solution.py:649
  311.0 31.5 %collective-permute-start.46 = (bf16[344,2048]{1,0:T(8,128)(2,1)S(1)}, bf16[344,2048]{1,0:T(8,128)(2,1)S(1)}, u32[]{:S(2)}, u32[]{:S(2)}) collective-permute-start(bf16[344,2048]{1,0:T(8,128)(2,1)S(1)} %get-tuple-element.278.refs_3_), channel_id=1, source_target_pairs={{8,16},{16,8},{9,17},{17,9},{10,18},{18,10},{11,19},{19,11},{12,20... | collective-permute-start | bytes 4227080 | tf_op jit(solution)/shard_map/ppermute | solution.py:645
  312.9 8.4 %collective-permute-start.49 = (bf16[128,1024]{1,0:T(8,128)(2,1)S(1)}, bf16[128,1024]{1,0:T(8,128)(2,1)S(1)}, u32[]{:S(2)}, u32[]{:S(2)}) collective-permute-start(bf16[128,1024]{1,0:T(8,128)(2,1)S(1)} %get-tuple-element.449), channel_id=1, source_target_pairs={{0,4},{1,5},{2,6},{3,7},{4,0},{5,1},{6,2},{7,3},{8,12},{9,13},{10,... | collective-permute-start | bytes 786440 | tf_op jit(solution)/shard_map/ppermute | solution.py:396
  314.6 9.2 %collective-permute-start.51 = (bf16[128,1024]{1,0:T(8,128)(2,1)S(1)}, bf16[128,1024]{1,0:T(8,128)(2,1)S(1)}, u32[]{:S(2)}, u32[]{:S(2)}) collective-permute-start(bf16[128,1024]{1,0:T(8,128)(2,1)S(1)} %get-tuple-element.448), channel_id=1, source_target_pairs={{0,2},{1,3},{2,0},{3,1},{4,6},{5,7},{6,4},{7,5},{8,10},{9,11},{10,... | collective-permute-start | bytes 786440 | tf_op jit(solution)/shard_map/ppermute | solution.py:396
  315.4 14.0 %collective-permute-start.48 = (bf16[128,1024]{1,0:T(8,128)(2,1)S(1)}, bf16[128,1024]{1,0:T(8,128)(2,1)S(1)}, u32[]{:S(2)}, u32[]{:S(2)}) collective-permute-start(bf16[128,1024]{1,0:T(8,128)(2,1)S(1)} %get-tuple-element.450), channel_id=1, source_target_pairs={{0,2},{1,3},{2,0},{3,1},{4,6},{5,7},{6,4},{7,5},{8,10},{9,11},{10,... | collective-permute-start | bytes 786440 | tf_op jit(solution)/shard_map/ppermute | solution.py:396
  321.3 14.0 %collective-permute-start.53 = (bf16[128,1024]{1,0:T(8,128)(2,1)S(1)}, bf16[128,1024]{1,0:T(8,128)(2,1)S(1)}, u32[]{:S(2)}, u32[]{:S(2)}) collective-permute-start(bf16[128,1024]{1,0:T(8,128)(2,1)S(1)} %get-tuple-element.451), channel_id=1, source_target_pairs={{0,4},{1,5},{2,6},{3,7},{4,0},{5,1},{6,2},{7,3},{8,12},{9,13},{10,... | collective-permute-start | bytes 786440 | tf_op jit(solution)/shard_map/ppermute | solution.py:396
  324.0 11.3 %collective-permute-start.50 = (bf16[128,1024]{1,0:T(8,128)(2,1)S(1)}, bf16[128,1024]{1,0:T(8,128)(2,1)S(1)}, u32[]{:S(2)}, u32[]{:S(2)}) collective-permute-start(bf16[128,1024]{1,0:T(8,128)(2,1)S(1)} %get-tuple-element.447), channel_id=1, source_target_pairs={{0,2},{1,3},{2,0},{3,1},{4,6},{5,7},{6,4},{7,5},{8,10},{9,11},{10,... | collective-permute-start | bytes 786440 | tf_op jit(solution)/shard_map/ppermute | solution.py:396
  350.2 35.0 %collective-permute-start.54 = (bf16[344,2048]{1,0:T(8,128)(2,1)}, bf16[344,2048]{1,0:T(8,128)(2,1)}, u32[]{:S(2)}, u32[]{:S(2)}) collective-permute-start(bf16[344,2048]{1,0:T(8,128)(2,1)} %get-tuple-element.290.refs_2_), channel_id=1, source_target_pairs={{0,8},{8,0},{16,24},{24,16},{1,9},{9,1},{17,25},{25,17},{2,10},{10... | collective-permute-start | bytes 4227080 | tf_op jit(solution)/shard_map/ppermute | solution.py:649
  354.0 31.2 %collective-permute-start.55 = (bf16[344,2048]{1,0:T(8,128)(2,1)}, bf16[344,2048]{1,0:T(8,128)(2,1)}, u32[]{:S(2)}, u32[]{:S(2)}) collective-permute-start(bf16[344,2048]{1,0:T(8,128)(2,1)} %get-tuple-element.291.refs_3_), channel_id=1, source_target_pairs={{8,16},{16,8},{9,17},{17,9},{10,18},{18,10},{11,19},{19,11},{12,20... | collective-permute-start | bytes 4227080 | tf_op jit(solution)/shard_map/ppermute | solution.py:645
  392.0 36.1 %collective-permute-start.59 = (bf16[344,2048]{1,0:T(8,128)(2,1)}, bf16[344,2048]{1,0:T(8,128)(2,1)S(1)}, u32[]{:S(2)}, u32[]{:S(2)}) collective-permute-start(bf16[344,2048]{1,0:T(8,128)(2,1)} %copy-done.85), channel_id=1, source_target_pairs={{0,8},{8,0},{16,24},{24,16},{1,9},{9,1},{17,25},{25,17},{2,10},{10... | collective-permute-start | bytes 4227080 | tf_op jit(solution)/shard_map/ppermute | solution.py:649
  395.8 32.3 %collective-permute-start.60 = (bf16[344,2048]{1,0:T(8,128)(2,1)}, bf16[344,2048]{1,0:T(8,128)(2,1)S(1)}, u32[]{:S(2)}, u32[]{:S(2)}) collective-permute-start(bf16[344,2048]{1,0:T(8,128)(2,1)} %copy-done.76), channel_id=1, source_target_pairs={{8,16},{16,8},{9,17},{17,9},{10,18},{18,10},{11,19},{19,11},{12,20... | collective-permute-start | bytes 4227080 | tf_op jit(solution)/shard_map/ppermute | solution.py:645
  429.6 36.8 %collective-permute-start.61 = (bf16[344,2048]{1,0:T(8,128)(2,1)S(1)}, bf16[344,2048]{1,0:T(8,128)(2,1)S(1)}, u32[]{:S(2)}, u32[]{:S(2)}) collective-permute-start(bf16[344,2048]{1,0:T(8,128)(2,1)S(1)} %get-tuple-element.324.refs_2_), channel_id=1, source_target_pairs={{0,8},{8,0},{16,24},{24,16},{1,9},{9,1},{17,25},{25,17},{2,10},{10... | collective-permute-start | bytes 4227080 | tf_op jit(solution)/shard_map/ppermute | solution.py:649
  432.8 34.6 %collective-permute-start.62 = (bf16[344,2048]{1,0:T(8,128)(2,1)S(1)}, bf16[344,2048]{1,0:T(8,128)(2,1)S(1)}, u32[]{:S(2)}, u32[]{:S(2)}) collective-permute-start(bf16[344,2048]{1,0:T(8,128)(2,1)S(1)} %get-tuple-element.325.refs_3_), channel_id=1, source_target_pairs={{8,16},{16,8},{9,17},{17,9},{10,18},{18,10},{11,19},{19,11},{12,20... | collective-permute-start | bytes 4227080 | tf_op jit(solution)/shard_map/ppermute | solution.py:645
  476.2 31.3 %collective-permute-start.63 = (bf16[344,2048]{1,0:T(8,128)(2,1)S(1)}, bf16[344,2048]{1,0:T(8,128)(2,1)S(1)}, u32[]{:S(2)}, u32[]{:S(2)}) collective-permute-start(bf16[344,2048]{1,0:T(8,128)(2,1)S(1)} %get-tuple-element.353.refs_3_), channel_id=1, source_target_pairs={{0,8},{8,0},{16,24},{24,16},{1,9},{9,1},{17,25},{25,17},{2,10},{10... | collective-permute-start | bytes 4227080 | tf_op jit(solution)/shard_map/ppermute | solution.py:649
  478.1 11.5 %collective-permute-start.64 = (bf16[256,2048]{1,0:T(8,128)(2,1)S(1)}, bf16[256,2048]{1,0:T(8,128)(2,1)S(1)}, u32[]{:S(2)}, u32[]{:S(2)}) collective-permute-start(bf16[256,2048]{1,0:T(8,128)(2,1)S(1)} %get-tuple-element.352.refs_3_), channel_id=1, source_target_pairs={{8,16},{16,8},{9,17},{17,9},{10,18},{18,10},{11,19},{19,11},{12,20... | collective-permute-start | bytes 3145736 | tf_op jit(solution)/shard_map/ppermute | solution.py:645
  509.9 8.5 %collective-permute-start.67 = (bf16[4,256,1024]{2,1,0:T(8,128)(2,1)S(1)}, bf16[4,256,1024]{2,1,0:T(8,128)(2,1)}, u32[]{:S(2)}, u32[]{:S(2)}) collective-permute-start(bf16[4,256,1024]{2,1,0:T(8,128)(2,1)S(1)} %get-tuple-element.376), channel_id=1, source_target_pairs={{0,1},{1,0},{2,3},{3,2},{4,5},{5,4},{6,7},{7,6},{8,9},{9,8},{10,11... | collective-permute-start | bytes 6291464 | tf_op jit(solution)/shard_map/ppermute | solution.py:396
  513.0 35.4 %collective-permute-start.65 = (bf16[256,2048]{1,0:T(8,128)(2,1)}, bf16[256,2048]{1,0:T(8,128)(2,1)}, u32[]{:S(2)}, u32[]{:S(2)}) collective-permute-start(bf16[256,2048]{1,0:T(8,128)(2,1)} %get-tuple-element.368.refs_1_), channel_id=1, source_target_pairs={{0,8},{8,0},{16,24},{24,16},{1,9},{9,1},{17,25},{25,17},{2,10},{10... | collective-permute-start | bytes 3145736 | tf_op jit(solution)/shard_map/ppermute | solution.py:649
  514.8 33.5 %collective-permute-start.66 = (bf16[256,2048]{1,0:T(8,128)(2,1)}, bf16[256,2048]{1,0:T(8,128)(2,1)}, u32[]{:S(2)}, u32[]{:S(2)}) collective-permute-start(bf16[256,2048]{1,0:T(8,128)(2,1)} %get-tuple-element.369.refs_3_), channel_id=1, source_target_pairs={{8,16},{16,8},{9,17},{17,9},{10,18},{18,10},{11,19},{19,11},{12,20... | collective-permute-start | bytes 3145736 | tf_op jit(solution)/shard_map/ppermute | solution.py:645
  516.8 8.4 %collective-permute-start.75 = (f32[1,1024]{1,0:T(1,128)S(1)}, f32[1,1024]{1,0:T(1,128)S(1)}, u32[]{:S(2)}, u32[]{:S(2)}) collective-permute-start(f32[1,1024]{1,0:T(1,128)S(1)} %add.255), channel_id=1, source_target_pairs={{0,2},{1,3},{2,0},{3,1},{4,6},{5,7},{6,4},{7,5},{8,10},{9,11},{10,... | collective-permute-start | bytes 12296 | tf_op jit(solution)/shard_map/ppermute | solution.py:697
  522.7 8.0 %collective-permute-start.69 = (bf16[128,1024]{1,0:T(8,128)(2,1)}, bf16[128,1024]{1,0:T(8,128)(2,1)}, u32[]{:S(2)}, u32[]{:S(2)}) collective-permute-start(bf16[128,1024]{1,0:T(8,128)(2,1)} %get-tuple-element.443), channel_id=1, source_target_pairs={{0,4},{1,5},{2,6},{3,7},{4,0},{5,1},{6,2},{7,3},{8,12},{9,13},{10,... | collective-permute-start | bytes 786440 | tf_op jit(solution)/shard_map/ppermute | solution.py:396
  524.4 9.6 %collective-permute-start.71 = (bf16[128,1024]{1,0:T(8,128)(2,1)}, bf16[128,1024]{1,0:T(8,128)(2,1)}, u32[]{:S(2)}, u32[]{:S(2)}) collective-permute-start(bf16[128,1024]{1,0:T(8,128)(2,1)} %get-tuple-element.442), channel_id=1, source_target_pairs={{0,2},{1,3},{2,0},{3,1},{4,6},{5,7},{6,4},{7,5},{8,10},{9,11},{10,... | collective-permute-start | bytes 786440 | tf_op jit(solution)/shard_map/ppermute | solution.py:396
  525.2 14.4 %collective-permute-start.68 = (bf16[128,1024]{1,0:T(8,128)(2,1)S(1)}, bf16[128,1024]{1,0:T(8,128)(2,1)}, u32[]{:S(2)}, u32[]{:S(2)}) collective-permute-start(bf16[128,1024]{1,0:T(8,128)(2,1)S(1)} %get-tuple-element.444), channel_id=1, source_target_pairs={{0,2},{1,3},{2,0},{3,1},{4,6},{5,7},{6,4},{7,5},{8,10},{9,11},{10,... | collective-permute-start | bytes 786440 | tf_op jit(solution)/shard_map/ppermute | solution.py:396
  534.0 9.2 %collective-permute-start.73 = (bf16[128,1024]{1,0:T(8,128)(2,1)S(1)}, bf16[128,1024]{1,0:T(8,128)(2,1)S(1)}, u32[]{:S(2)}, u32[]{:S(2)}) collective-permute-start(bf16[128,1024]{1,0:T(8,128)(2,1)S(1)} %get-tuple-element.445), channel_id=1, source_target_pairs={{0,4},{1,5},{2,6},{3,7},{4,0},{5,1},{6,2},{7,3},{8,12},{9,13},{10,... | collective-permute-start | bytes 786440 | tf_op jit(solution)/shard_map/ppermute | solution.py:396
  552.6 22.9 %collective-permute-start.77 = (bf16[256,2048]{1,0:T(8,128)(2,1)}, bf16[256,2048]{1,0:T(8,128)(2,1)S(1)}, u32[]{:S(2)}, u32[]{:S(2)}) collective-permute-start(bf16[256,2048]{1,0:T(8,128)(2,1)} %get-tuple-element.385.refs_1_), channel_id=1, source_target_pairs={{0,8},{8,0},{16,24},{24,16},{1,9},{9,1},{17,25},{25,17},{2,10},{10... | collective-permute-start | bytes 3145736 | tf_op jit(solution)/shard_map/ppermute | solution.py:649
  554.8 21.8 %collective-permute-start.78 = (bf16[256,2048]{1,0:T(8,128)(2,1)}, bf16[256,2048]{1,0:T(8,128)(2,1)}, u32[]{:S(2)}, u32[]{:S(2)}) collective-permute-start(bf16[256,2048]{1,0:T(8,128)(2,1)} %get-tuple-element.384.refs_3_), channel_id=1, source_target_pairs={{8,16},{16,8},{9,17},{17,9},{10,18},{18,10},{11,19},{19,11},{12,20... | collective-permute-start | bytes 3145736 | tf_op jit(solution)/shard_map/ppermute | solution.py:645
  580.6 23.9 %collective-permute-start.79 = (bf16[272,2048]{1,0:T(8,128)(2,1)S(1)}, bf16[272,2048]{1,0:T(8,128)(2,1)S(1)}, u32[]{:S(2)}, u32[]{:S(2)}) collective-permute-start(bf16[272,2048]{1,0:T(8,128)(2,1)S(1)} %get-tuple-element.402.refs_1_), channel_id=1, source_target_pairs={{0,8},{8,0},{16,24},{24,16},{1,9},{9,1},{17,25},{25,17},{2,10},{10... | collective-permute-start | bytes 3342344 | tf_op jit(solution)/shard_map/ppermute | solution.py:649
  583.6 20.7 %collective-permute-start.80 = (bf16[256,2048]{1,0:T(8,128)(2,1)S(1)}, bf16[256,2048]{1,0:T(8,128)(2,1)S(1)}, u32[]{:S(2)}, u32[]{:S(2)}) collective-permute-start(bf16[256,2048]{1,0:T(8,128)(2,1)S(1)} %get-tuple-element.403.refs_2_), channel_id=1, source_target_pairs={{8,16},{16,8},{9,17},{17,9},{10,18},{18,10},{11,19},{19,11},{12,20... | collective-permute-start | bytes 3145736 | tf_op jit(solution)/shard_map/ppermute | solution.py:645
  605.6 25.6 %collective-permute-start.82 = (bf16[272,2048]{1,0:T(8,128)(2,1)S(1)}, bf16[272,2048]{1,0:T(8,128)(2,1)S(1)}, u32[]{:S(2)}, u32[]{:S(2)}) collective-permute-start(bf16[272,2048]{1,0:T(8,128)(2,1)S(1)} %get-tuple-element.406.refs_0_), channel_id=1, source_target_pairs={{8,16},{16,8},{9,17},{17,9},{10,18},{18,10},{11,19},{19,11},{12,20... | collective-permute-start | bytes 3342344 | tf_op jit(solution)/shard_map/ppermute | solution.py:645
  606.4 24.8 %collective-permute-start.81 = (bf16[256,2048]{1,0:T(8,128)(2,1)S(1)}, bf16[256,2048]{1,0:T(8,128)(2,1)S(1)}, u32[]{:S(2)}, u32[]{:S(2)}) collective-permute-start(bf16[256,2048]{1,0:T(8,128)(2,1)S(1)} %get-tuple-element.407.refs_1_), channel_id=1, source_target_pairs={{0,8},{8,0},{16,24},{24,16},{1,9},{9,1},{17,25},{25,17},{2,10},{10... | collective-permute-start | bytes 3145736 | tf_op jit(solution)/shard_map/ppermute | solution.py:649
  631.8 21.8 %collective-permute-start.83 = (bf16[272,2048]{1,0:T(8,128)(2,1)S(1)}, bf16[272,2048]{1,0:T(8,128)(2,1)S(1)}, u32[]{:S(2)}, u32[]{:S(2)}) collective-permute-start(bf16[272,2048]{1,0:T(8,128)(2,1)S(1)} %turn.23.refs_1_), channel_id=1, source_target_pairs={{0,8},{8,0},{16,24},{24,16},{1,9},{9,1},{17,25},{25,17},{2,10},{10... | collective-permute-start | bytes 3342344 | tf_op jit(solution)/shard_map/ppermute | solution.py:649
  (185 other events, 1421.1 us)
Sparse Core Ops, SparseCore 0:
  43.0 38.0 all-gather.2
  83.6 43.5 all-gather.4
  392.1 53.5 reduce-scatter.1

commit v5 on v4

--- a/solution.py
+++ b/solution.py
@@ -82,7 +82,7 @@
         pt=tn(ke,qa_o[b])*tri
         mp[b]=jnp.concatenate([m,pt],1).astype(BF)
         return 0
-    lax.fori_loop(0,nb,pre2,0,unroll=4)
+    lax.fori_loop(0,nb,pre2,0,unroll=8)
     w0,c0,g,s=unpack_consts(consts,heads)
     def body(b,carry):
         zt,wt,ct=carry
@@ -107,7 +107,7 @@
         z2=yk-rr[:,:L]
         return z2,jnp.where(rs,w0,wt-rw),jnp.where(rs,c0,ct-rc)
     zt=nn(w0.astype(BF),spread(ka_o[0][:HD],heads))+c0
-    lax.fori_loop(0,nb,body,(zt,w0,c0))
+    lax.fori_loop(0,nb,body,(zt,w0,c0),unroll=4)
     def post(gr,_):
         outs=[]
         for p in range(8):
@@ -141,7 +141,7 @@
     return pl.pallas_call(functools.partial(fwd_kernel,heads,nb),out_shape=outs,grid=(1,),
         in_specs=[SM]+[whole(v) for v in args],out_specs=[whole(v) for v in outs],
         scratch_shapes=[pltpu.VMEM((nb,L,2*L),BF),pltpu.VMEM((nb,HD,L),F32)],
-        compiler_params=pltpu.CompilerParams(vmem_limit_bytes=44<<20), name="mix_forward",
+        compiler_params=pltpu.CompilerParams(vmem_limit_bytes=34<<20), name="mix_forward",
         cost_estimate=pl.CostEstimate(flops=T*heads*64, bytes_accessed=T*heads, transcendentals=0))(
             reset,*args)
 
@@ -261,7 +261,7 @@
     return pl.pallas_call(functools.partial(bwd_kernel,heads,nb,part*nb,last),out_shape=outs,grid=(1,),
         in_specs=ins,out_specs=[nat]*3+[whole(heads,T)]+[whole(HD,L)]*2+[whole(HD,W),whole(HD,L)]*2,
         scratch_shapes=scr,input_output_aliases=alias,
-        compiler_params=pltpu.CompilerParams(vmem_limit_bytes=36<<20), name="mix_backward",
+        compiler_params=pltpu.CompilerParams(vmem_limit_bytes=30<<20), name="mix_backward",
         cost_estimate=pl.CostEstimate(flops=T*heads*64, bytes_accessed=T*heads, transcendentals=0))(*args)
 
 def lane_cols(x):
@@ -318,12 +318,15 @@
         gains[...] = jnp.zeros_like(gains)
 
 
-def moments_kernel(n, width, spots, *refs):
-    pieces, (out, mean_out, scale_out, sems) = refs[:n], refs[n:]
-    mean = fetch(pieces, spots, out, sems, lambda v: v) * (1.0 / width)
-    mean_out[...] = mean
-    acc = fold(out, 0, width, lambda v: (v - mean) * (v - mean), jnp.zeros((8, out.shape[1]), F32))
-    scale_out[...] = lax.rsqrt(jnp.sum(acc, 0, keepdims=True) * (1.0 / width) + EPS)
+def collect_kernel(n, spots, *refs):
+    pieces, (out, sems) = refs[:n], refs[n:]
+    copies = []
+    for i, p in enumerate(pieces):
+        at = pl.ds(pl.multiple_of(spots[i], 16), p.shape[0])
+        copies.append(pltpu.make_async_copy(p, out.at[at], sems.at[i]))
+        copies[-1].start()
+    for c in copies:
+        c.wait()
 
 
 def rms_rows(pieces, spots, gains, lane, tok, width):
@@ -336,20 +339,18 @@
         out_shape=[S((width, tok), BF), S((1, tok), F32), S((width, 128) if fresh else (16, 128), BF)],
         in_specs=[SM, AN if fresh else VM] + [AN] * n, out_specs=[VM, VM, VM],
         scratch_shapes=[pltpu.VMEM((width, tok), BF), pltpu.SemaphoreType.DMA((n,)), pltpu.SemaphoreType.DMA((count,))],
-        compiler_params=pltpu.CompilerParams(vmem_limit_bytes=16 << 20), name="rms_rows",
+        compiler_params=pltpu.CompilerParams(vmem_limit_bytes=10 << 20), name="rms_rows",
         cost_estimate=pl.CostEstimate(flops=8 * width * tok, bytes_accessed=4 * width * tok, transcendentals=0),
     )(spots, gains, *pieces)
 
 
-def moments_rows(pieces, spots, tok, width):
+def collect(pieces, spots, tok, width):
     n = len(pieces)
     return pl.pallas_call(
-        functools.partial(moments_kernel, n, width),
-        out_shape=[jax.ShapeDtypeStruct((width, tok), BF)] + [jax.ShapeDtypeStruct((1, tok), F32)] * 2,
-        in_specs=[SM] + [AN] * n, out_specs=[VM] * 3,
-        scratch_shapes=[pltpu.SemaphoreType.DMA((n,))],
-        compiler_params=pltpu.CompilerParams(vmem_limit_bytes=16 << 20), name="moments_rows",
-        cost_estimate=pl.CostEstimate(flops=8 * width * tok, bytes_accessed=4 * width * tok, transcendentals=0),
+        functools.partial(collect_kernel, n), out_shape=jax.ShapeDtypeStruct((width, tok), BF),
+        in_specs=[SM] + [AN] * n, out_specs=VM, scratch_shapes=[pltpu.SemaphoreType.DMA((n,))],
+        compiler_params=pltpu.CompilerParams(vmem_limit_bytes=10 << 20), name="collect",
+        cost_estimate=pl.CostEstimate(flops=0, bytes_accessed=4 * width * tok, transcendentals=0),
     )(spots, *pieces)
 
 
@@ -458,7 +459,7 @@
         wgrad_kernel, grid=(n // COLS,), out_shape=jax.ShapeDtypeStruct((rows, n), BF),
         in_specs=[pl.BlockSpec((rows, tok), lambda i: (0, 0)), pl.BlockSpec((COLS, tok), lambda i: (i, 0))],
         out_specs=pl.BlockSpec((rows, COLS), lambda i: (0, i)),
-        compiler_params=wide_params(24), cost_estimate=FREE, name="weight_gradient")(a, b)
+        compiler_params=wide_params(10), cost_estimate=FREE, name="weight_gradient")(a, b)
 
 
 def column_blocks(v):
@@ -505,7 +506,7 @@
         res = list(pl.pallas_call(
             functools.partial(turn_kernel, bool(sent), bool(job), bool(back)), grid=(outs[0].shape[1] // COLS,),
             out_shape=outs, in_specs=[SM] + [column_blocks(v) for v in ins], out_specs=[column_blocks(v) for v in outs],
-            compiler_params=wide_params(24), cost_estimate=FREE, name="turn")(end, *ins))
+            compiler_params=wide_params(10), cost_estimate=FREE, name="turn")(end, *ins))
     half = res.pop(0) if sent else None
     load = res.pop(0) if back else (job.x if job else None)
     return half, load
@@ -530,7 +531,7 @@
     return pl.pallas_call(
         functools.partial(finish_kernel, sizes), grid=(out.shape[1] // COLS,), out_shape=out,
         in_specs=[SM] + [column_blocks(v) for v in vals], out_specs=column_blocks(out),
-        compiler_params=wide_params(24), cost_estimate=FREE, name="finish")(end, *vals)
+        compiler_params=wide_params(12), cost_estimate=FREE, name="finish")(end, *vals)
 
 
 def parts_kernel(n, core, *refs):
@@ -572,7 +573,7 @@
     return pl.pallas_call(
         functools.partial(parts_kernel, n), grid_spec=spec,
         out_shape=[S((chips, own, tok), BF)] * 2 + [S((1, tok), F32)],
-        compiler_params=wide_params(32), name="parts",
+        compiler_params=wide_params(18), name="parts",
         cost_estimate=pl.CostEstimate(flops=10**10, bytes_accessed=10**7, transcendentals=0))(core, *left, *right, rows)
 
 
@@ -709,7 +710,6 @@
     nin, q1, gains = rms_rows(tok_pieces.all, spots, gain_blocks, 0, tok, width)
     gate = nn(w_gate, nin).astype(BF)
     gelu_own = gelu_tanh(gate.astype(F32))
-    gates = gather(gelu_own.astype(BF))
     nin_q = hold(nin, gate)
     q_t = nn(w_query, nin_q)
     k_t = nn(w_key, nin_q)
@@ -720,12 +720,28 @@
     mixer_own, zt, zb, td, qa, ka, wt, rows = ttt_fwd(
         reset, q_t, k_t, v_t, masked * (1.0 / HD), vrow, consts)
 
-    mixer_own, g_full = tie(mixer_own, g_full)
-    mix_pieces = Pieces(mixer_own, devs)
-    mix, mean3, r3 = moments_rows(mix_pieces.all, spots, tok, width)
-    gain_cols = gains.astype(F32)
-    mixed = (((mix.astype(F32) - mean3) * r3 * gain_cols[:, 1:2] + gain_cols[:, 2:3])
-             * gates.astype(F32)).astype(BF)
+    mixer_own, g_full, gelu_own = tie(mixer_own, g_full, gelu_own)
+    mixer_rows = mixer_own.astype(F32)
+    mean3 = col_sum(mixer_rows) / own
+    spread3 = col_sum((mixer_rows - mean3) * (mixer_rows - mean3))
+    if devs == 8:
+        count = own
+        for bit in (1, 2, 4):
+            both = jnp.concatenate([mean3, spread3], 0)
+            other = lax.ppermute(both, "head", [(i, i ^ bit) for i in range(8)])
+            gap = other[:1] - mean3
+            mean3 = (mean3 + other[:1]) * 0.5
+            spread3 = spread3 + other[1:] + gap * gap * (count * 0.5)
+            count *= 2
+    else:
+        mean3 = lax.psum(mean3, "head") / devs
+        spread3 = lax.psum(col_sum((mixer_rows - mean3) * (mixer_rows - mean3)), "head")
+    r3 = lax.rsqrt(spread3 / width + EPS)
+    n3 = (mixer_rows - mean3) * r3
+    pg_own = post_gain.astype(F32)[:, None]
+    ps_own = post_shift.astype(F32)[:, None]
+    mixed_own = ((n3 * pg_own + ps_own) * gelu_own).astype(BF)
+    mixed = collect(Pieces(mixed_own, devs).all, spots, tok, width)
     hidden = tokens.astype(F32) + nn(w_out, mixed)
     hidden_low = hidden.astype(BF)
     nmid, q2, _ = rms_rows(Pieces(hidden_low, devs).all, spots, gains, 3, tok, width)
@@ -767,9 +783,6 @@
     gm = gm.result()
     u0, gm, out_w, u1_x, act = belt.tick(u0_x, gm, out_w, hup[1], act)
     ffn_part = tn(w_down, act).astype(BF)
-    n3 = (mixer_own.astype(F32) - mean3) * r3
-    pg_own = post_gain.astype(F32)[:, None]
-    ps_own = post_shift.astype(F32)[:, None]
     a_own, gelu_pull = jax.vjp(gelu_tanh, gate.astype(F32))
     g_post_gain = jnp.sum(gm * a_own * n3, 1)
     g_post_shift = jnp.sum(gm * a_own, 1)

time: 676 us -> 664 us (0.982)
  Pallas kernels: 193 us -> 182 us
  waiting for transfers between devices: 222 us -> 215 us
    ppermute x48, waiting for transfers between devices: 77 us -> 64.7 us  [swap(): return lax.ppermute(v, 'head', [(i, i ^ bit) for i in range(8)])]
    pallas_call x1, Pallas kernels: 34.9 us -> 26.9 us  [ttt_fwd(): pl.pallas_call(functools.partial(fwd_kernel, heads, nb), out_shape=outs,...]
    unnamed x345 -> x337, local copies, waits for them, and re-layouts: 50.8 us -> 52.2 us
  transfers between devices with their start and end apart: 87 -> 89, of which waited for: 35 -> 37; matrix products, arithmetic and copies ran while one was open for 10% -> 11% of each run, Pallas kernels for 24% -> 23%
where the time goes in v5:
time: 664 us; the launch traced here: 653 us
  waiting for transfers between devices  215 us (32%)
  Pallas kernels  182 us (27%)
  starting transfers between devices  96.4 us (15%)
  local copies, waits for them, and re-layouts  71 us (11%)
  other arithmetic  40.4 us (6%)
  matrix products  29.6 us (4%)
  between operations  18.8 us (3%)
    ppermute x13, waiting for transfers between devices, tick(): lax.ppermute(load, 'dp', [(0, 1), (1, 0), (2, 3), (3, 2)])  122 us
    ppermute x48, waiting for transfers between devices, swap(): return lax.ppermute(v, 'head', [(i, i ^ bit) for i in range(8)])  64.7 us
    unnamed x337, local copies, waits for them, and re-layouts  52.2 us
    pallas_call x2, Pallas kernels, ttt_bwd(): pl.pallas_call(functools.partial(bwd_kernel, heads, nb, part * nb, last),...  40.5 us
    ppermute x13, starting transfers between devices, tick(): lax.ppermute(load, 'dp', [(0, 1), (1, 0), (2, 3), (3, 2)])  35.3 us
    ppermute x48, starting transfers between devices, swap(): return lax.ppermute(v, 'head', [(i, i ^ bit) for i in range(8)])  34.3 us
    pallas_call x3, Pallas kernels, parts(): pl.pallas_call(functools.partial(parts_kernel, n), grid_spec=spec, out_sh...  27.5 us
    pallas_call x1, Pallas kernels, ttt_fwd(): pl.pallas_call(functools.partial(fwd_kernel, heads, nb), out_shape=outs,...  26.9 us
  transfers between devices with their start and end apart: 89, of which 37 were waited for; matrix products, arithmetic and copies ran while one was open for 11% of the time, Pallas kernels for 23%

profile of v5, /device:TPU:0, one launch (start us, length us, event | category | flops | bytes accessed | tf_op | source)
XLA Modules:
  0.0 653.1 jit_solution(16834549559015378283)
XLA Ops:
  10.9 2.6 collective-permute-start.4
  15.6 13.4 %collective-permute-done.1 = bf16[2,256,128]{2,1,0:T(8,128)(2,1)S(1)} collective-permute-done((bf16[2,256,128]{2,1,0:T(8,128)(2,1)S(1)}, bf16[2,256,128]{2,1,0:T(8,128)(2,1)S(1)}, u32[]{:S(2)}, u32[]{:S(2)}) %collective-permute-start.1) | collective-permute-done | bytes 131104 | tf_op jit(solution)/shard_map/ppermute | solution.py:430
  34.7 3.6 collective-permute-done.2
  39.2 3.7 collective-permute-done.8.refs_6_
  53.0 6.0 rms_rows.2
  59.8 2.6 convert_multiply_fusion.1
  68.5 26.9 %mix_forward.1 = (bf16[256,1024]{1,0:T(8,128)(2,1)S(1)}, f32[64,64,64]{2,1,0:T(8,128)S(1)}, f32[64,64,64]{2,1,0:T(8,128)S(1)}, f32[64,64,64]{2,1,0:T(8,128)S(1)}...) custom-call(s32[64]{0:T(128)S(1)} %or_convert_fusion.reset, ...), custom_call_target="tpu_custom_call" | custom-call | flops 262144 | bytes 4096 | tf_op jit(solution)/shard_map/mix_forward/pallas_call | solution.py:141
  117.3 8.9 %collective-permute-done.16.refs_2_ = bf16[256,1024]{1,0:T(8,128)(2,1)S(1)} collective-permute-done((bf16[256,1024]{1,0:T(8,128)(2,1)S(1)}, bf16[256,1024]{1,0:T(8,128)(2,1)S(1)}, u32[]{:S(2)}, u32[]{:S(2)}) %collective-permute-start.16) | collective-permute-done | bytes 524320 | tf_op jit(solution)/shard_map/ppermute | solution.py:370
  129.9 3.2 collective-permute-done.20.refs_6_
  137.8 2.5 fusion.88
  141.8 12.7 %collective-permute-done.25.refs_2_ = bf16[256,1024]{1,0:T(8,128)(2,1)} collective-permute-done((bf16[256,1024]{1,0:T(8,128)(2,1)}, bf16[256,1024]{1,0:T(8,128)(2,1)}, u32[]{:S(2)}, u32[]{:S(2)}) %collective-permute-start.25) | collective-permute-done | bytes 524320 | tf_op jit(solution)/shard_map/ppermute | solution.py:370
  159.0 4.2 collective-permute-done.29.refs_6_
  168.5 6.8 %rms_rows.3 = (bf16[2048,1024]{1,0:T(8,128)(2,1)S(1)}, f32[1,1024]{1,0:T(1,128)S(1)}, bf16[16,128]{1,0:T(8,128)(2,1)}) custom-call(s32[10]{0:T(128)S(1)} %stack.70.spots, bf16[2048,128]{1,0:T(8,128)(2,1)S(1)} %copy-done.95, bf16[256,1024]{1,0:T(8,128)(2,1)} %get-tuple-element.484.refs_0_, bf16[256,1024]{1,0:T(8,128)(2,1)} %collective-permute-done.24.refs_1_, ...), custom_call_target="tpu_custom_call" | custom-call | flops 16777216 | bytes 8388608 | tf_op jit(solution)/shard_map/rms_rows/pallas_call | solution.py:337
  175.3 3.1 fusion.90
  178.6 3.3 fusion.5
  182.0 2.4 weight_gradient.11.refs_0_
  186.0 3.9 fusion.4
  190.0 2.4 weight_gradient.12.refs_0_
  193.5 12.0 %parts.3 = (bf16[4,256,1024]{2,1,0:T(8,128)(2,1)S(1)}, bf16[4,256,1024]{2,1,0:T(8,128)(2,1)}, f32[1,1024]{1,0:T(1,128)S(1)}) custom-call(s32[1]{0:T(128)} %bitcast.35.core, bf16[688,2048]{1,0:T(8,128)(2,1)S(1)} %copy-done.114, bf16[688,2048]{1,0:T(8,128)(2,1)S(1)} %copy-done.115, bf16[688,1024]{1,0:T(8,128)(2,1)S(1)} %get-tuple-element.247.refs_2_, ...), custom_call_target="tpu_custom_call" | custom-call | flops 10000000000 | bytes 10000000 | tf_op jit(solution)/shard_map/parts/pallas_call | solution.py:573
  205.5 11.9 %collective-permute-done.33.refs_1_ = bf16[344,2048]{1,0:T(8,128)(2,1)S(1)} collective-permute-done((bf16[344,2048]{1,0:T(8,128)(2,1)S(1)}, bf16[344,2048]{1,0:T(8,128)(2,1)S(1)}, u32[]{:S(2)}, u32[]{:S(2)}) %collective-permute-start.33) | collective-permute-done | bytes 1409056 | tf_op jit(solution)/shard_map/ppermute | solution.py:650
  221.4 3.3 collective-permute-start.34
  224.8 3.2 add_convert_fusion.2
  234.1 5.7 collective-permute-done.44
  246.3 3.0 collective-permute-done.37
  254.6 2.4 weight_gradient.13.refs_2_.refs_0_
  259.0 3.3 turn.13
  263.3 2.4 weight_gradient.15.refs_2_.refs_0_
  267.8 5.7 parts.4
  273.5 18.4 %collective-permute-done.46.refs_1_.refs_0_ = bf16[344,2048]{1,0:T(8,128)(2,1)S(1)} collective-permute-done((bf16[344,2048]{1,0:T(8,128)(2,1)S(1)}, bf16[344,2048]{1,0:T(8,128)(2,1)S(1)}, u32[]{:S(2)}, u32[]{:S(2)}) %collective-permute-start.46) | collective-permute-done | bytes 1409056 | tf_op jit(solution)/shard_map/ppermute | solution.py:650
  293.3 3.9 collective-permute-start.48
  301.7 5.8 collective-permute-done.52
  309.7 4.7 collective-permute-done.51
  321.7 7.0 %collective-permute-done.48.refs_1_ = bf16[344,2048]{1,0:T(8,128)(2,1)S(1)} collective-permute-done((bf16[344,2048]{1,0:T(8,128)(2,1)S(1)}, bf16[344,2048]{1,0:T(8,128)(2,1)S(1)}, u32[]{:S(2)}, u32[]{:S(2)}) %collective-permute-start.48) | collective-permute-done | bytes 1409056 | tf_op jit(solution)/shard_map/ppermute | solution.py:650
  328.6 2.7 turn.15
  331.4 3.2 fusion.45
  336.7 3.7 collective-permute-start.57
  342.8 5.1 convert_bitcast_fusion
  347.9 2.6 fusion.44.dOT
  350.6 21.1 %collective-permute-done.57.refs_1_.refs_0_ = bf16[344,2048]{1,0:T(8,128)(2,1)} collective-permute-done((bf16[344,2048]{1,0:T(8,128)(2,1)}, bf16[344,2048]{1,0:T(8,128)(2,1)}, u32[]{:S(2)}, u32[]{:S(2)}) %collective-permute-start.57) | collective-permute-done | bytes 1409056 | tf_op jit(solution)/shard_map/ppermute | solution.py:650
  373.0 3.2 turn.16
  378.4 3.8 collective-permute-start.62
  392.7 20.0 %mix_backward.2 = (bf16[256,1024]{1,0:T(8,128)(2,1)S(1)}, bf16[256,1024]{1,0:T(8,128)(2,1)S(1)}, bf16[256,1024]{1,0:T(8,128)(2,1)S(1)}, f32[4,512]{1,0:T(4,128)S...) custom-call(s32[64]{0:T(128)S(1)} %or_convert_fusion.reset, ...), custom_call_target="tpu_custom_call" | custom-call | flops 131072 | bytes 2048 | tf_op jit(solution)/shard_map/mix_backward/pallas_call | solution.py:261
  416.2 2.6 collective-permute-start.64
  421.7 20.5 %mix_backward.3 = (bf16[256,1024]{1,0:T(8,128)(2,1)S(1)}, bf16[256,1024]{1,0:T(8,128)(2,1)S(1)}, bf16[256,1024]{1,0:T(8,128)(2,1)S(1)}, f32[4,512]{1,0:T(4,128)S...) custom-call(s32[64]{0:T(128)S(1)} %or_convert_fusion.reset, ...), custom_call_target="tpu_custom_call", output_to_operand_aliasing={{0}: (12, {}), {1}: (13, {}), {2}: (14, {})} | custom-call | flops 131072 | bytes 2048 | tf_op jit(solution)/shard_map/mix_backward/pallas_call | solution.py:261
  461.2 2.8 collective-permute-start.66
  465.2 9.8 %parts.5 = (bf16[4,256,1024]{2,1,0:T(8,128)(2,1)S(1)}, bf16[4,256,1024]{2,1,0:T(8,128)(2,1)S(1)}, f32[1,1024]{1,0:T(1,128)S(1)}) custom-call(s32[1]{0:T(128)} %bitcast.35.core, bf16[1040,2048]{1,0:T(8,128)(2,1)S(1)} %copy-done.99, bf16[1040,1024]{1,0:T(8,128)(2,1)S(1)} %pad_dynamic-update-slice_fusion.1.refs_1_, bf16[2048,1024]{1,0:T(8,128)(2,1)S(1)} %copy-done.4), custom_call_target="tpu_custom_call" | custom-call | flops 10000000000 | bytes 10000000 | tf_op jit(solution)/shard_map/parts/pallas_call | solution.py:573
  475.1 18.0 %collective-permute-done.66.refs_1_ = bf16[344,2048]{1,0:T(8,128)(2,1)S(1)} collective-permute-done((bf16[344,2048]{1,0:T(8,128)(2,1)S(1)}, bf16[344,2048]{1,0:T(8,128)(2,1)S(1)}, u32[]{:S(2)}, u32[]{:S(2)}) %collective-permute-start.66) | collective-permute-done | bytes 1409056 | tf_op jit(solution)/shard_map/ppermute | solution.py:650
  493.1 2.5 turn.19
  503.7 3.2 add_convert_fusion
  511.1 4.8 collective-permute-done.72
  525.2 3.4 fusion.89
  532.4 4.2 turn.20
  541.1 3.6 fusion.21
  549.0 10.6 %collective-permute-done.80.refs_1_.refs_0_ = bf16[256,2048]{1,0:T(8,128)(2,1)S(1)} collective-permute-done((bf16[256,2048]{1,0:T(8,128)(2,1)}, bf16[256,2048]{1,0:T(8,128)(2,1)S(1)}, u32[]{:S(2)}, u32[]{:S(2)}) %collective-permute-start.80) | collective-permute-done | bytes 1048608 | tf_op jit(solution)/shard_map/ppermute | solution.py:650
  561.9 2.8 turn.21
  564.8 2.8 collective-permute-start.82
  568.8 3.2 finish.8
  572.0 5.9 finish.9
  577.9 3.2 finish.10
  581.1 3.9 finish.11
  584.9 3.6 finish.12
  590.4 4.8 collective-permute-start.84
  597.2 18.1 %collective-permute-done.84.refs_0_ = bf16[256,2048]{1,0:T(8,128)(2,1)S(1)} collective-permute-done((bf16[256,2048]{1,0:T(8,128)(2,1)S(1)}, bf16[256,2048]{1,0:T(8,128)(2,1)S(1)}, u32[]{:S(2)}, u32[]{:S(2)}) %collective-permute-start.84) | collective-permute-done | bytes 1048608 | tf_op jit(solution)/shard_map/ppermute | solution.py:650
  620.7 17.3 %collective-permute-done.86.refs_0_ = bf16[272,2048]{1,0:T(8,128)(2,1)S(1)} collective-permute-done((bf16[272,2048]{1,0:T(8,128)(2,1)S(1)}, bf16[272,2048]{1,0:T(8,128)(2,1)S(1)}, u32[]{:S(2)}, u32[]{:S(2)}) %collective-permute-start.86) | collective-permute-done | bytes 1114144 | tf_op jit(solution)/shard_map/ppermute | solution.py:650
  (640 shorter events, 212.4 us)
Async XLA Ops:
  7.3 96.3 %all-gather.2.cloned.1.call-start = ((), (), s32[]{:S(2)}) async-start(), calls=%async_computation.1 | async-start | bytes 4718592 | tf_op jit(solution)/shard_map/all_gather | solution.py:692
  10.9 20.0 %collective-permute-start.4 = (bf16[256,1024]{1,0:T(8,128)(2,1)}, bf16[256,1024]{1,0:T(8,128)(2,1)S(1)}, u32[]{:S(2)}, u32[]{:S(2)}) collective-permute-start(bf16[256,1024]{1,0:T(8,128)(2,1)} %refs_0_.3), channel_id=1, source_target_pairs={{0,2},{1,3},{2,0},{3,1},{4,6},{5,7},{6,4},{7,5},{8,10},{9,11},{10,... | collective-permute-start | bytes 1572872 | tf_op jit(solution)/shard_map/ppermute | solution.py:370
  13.5 18.5 %collective-permute-start.6 = (bf16[256,1024]{1,0:T(8,128)(2,1)}, bf16[256,1024]{1,0:T(8,128)(2,1)S(1)}, u32[]{:S(2)}, u32[]{:S(2)}) collective-permute-start(bf16[256,1024]{1,0:T(8,128)(2,1)} %refs_0_.3), channel_id=1, source_target_pairs={{0,4},{1,5},{2,6},{3,7},{4,0},{5,1},{6,2},{7,3},{8,12},{9,13},{10,... | collective-permute-start | bytes 1572872 | tf_op jit(solution)/shard_map/ppermute | solution.py:370
  15.0 14.0 %collective-permute-start.1 = (bf16[2,256,128]{2,1,0:T(8,128)(2,1)S(1)}, bf16[2,256,128]{2,1,0:T(8,128)(2,1)S(1)}, u32[]{:S(2)}, u32[]{:S(2)}) collective-permute-start(bf16[2,256,128]{2,1,0:T(8,128)(2,1)S(1)} %pad_maximum_fusion.3), channel_id=1, source_target_pairs={{0,2},{1,3},{2,0},{3,1},{4,6},{5,7},{6,4},{7,5},{8,10},{9,11},{10,... | collective-permute-start | bytes 393224 | tf_op jit(solution)/shard_map/ppermute | solution.py:430
  29.1 9.3 %collective-permute-start.2 = (bf16[4,256,128]{2,1,0:T(8,128)(2,1)S(1)}, bf16[4,256,128]{2,1,0:T(8,128)(2,1)S(1)}, u32[]{:S(2)}, u32[]{:S(2)}) collective-permute-start(bf16[4,256,128]{2,1,0:T(8,128)(2,1)S(1)} %pad_maximum_fusion.2), channel_id=1, source_target_pairs={{0,4},{1,5},{2,6},{3,7},{4,0},{5,1},{6,2},{7,3},{8,12},{9,13},{10,... | collective-permute-start | bytes 786440 | tf_op jit(solution)/shard_map/ppermute | solution.py:430
  31.7 11.2 %collective-permute-start.8 = (bf16[128,1024]{1,0:T(8,128)(2,1)S(1)}, bf16[128,1024]{1,0:T(8,128)(2,1)}, u32[]{:S(2)}, u32[]{:S(2)}) collective-permute-start(bf16[128,1024]{1,0:T(8,128)(2,1)S(1)} %slice.296), channel_id=1, source_target_pairs={{0,4},{1,5},{2,6},{3,7},{4,0},{5,1},{6,2},{7,3},{8,12},{9,13},{10,... | collective-permute-start | bytes 786440 | tf_op jit(solution)/shard_map/ppermute | solution.py:370
  32.8 10.1 %collective-permute-start.9 = (bf16[128,1024]{1,0:T(8,128)(2,1)S(1)}, bf16[128,1024]{1,0:T(8,128)(2,1)}, u32[]{:S(2)}, u32[]{:S(2)}) collective-permute-start(bf16[128,1024]{1,0:T(8,128)(2,1)S(1)} %slice.297), channel_id=1, source_target_pairs={{0,2},{1,3},{2,0},{3,1},{4,6},{5,7},{6,4},{7,5},{8,10},{9,11},{10,... | collective-permute-start | bytes 786440 | tf_op jit(solution)/shard_map/ppermute | solution.py:370
  42.9 410.7 %reduce-scatter.2.cloned.1.call-start = ((), (), s32[]{:S(2)}) async-start(), calls=%async_computation.2 | async-start | bytes 4718592 | tf_op jit(solution)/shard_map/reduce_scatter | solution.py:795
  114.2 12.1 %collective-permute-start.16 = (bf16[256,1024]{1,0:T(8,128)(2,1)S(1)}, bf16[256,1024]{1,0:T(8,128)(2,1)S(1)}, u32[]{:S(2)}, u32[]{:S(2)}) collective-permute-start(bf16[256,1024]{1,0:T(8,128)(2,1)S(1)} %fusion.40.refs_0_), channel_id=1, source_target_pairs={{0,2},{1,3},{2,0},{3,1},{4,6},{5,7},{6,4},{7,5},{8,10},{9,11},{10,... | collective-permute-start | bytes 1572872 | tf_op jit(solution)/shard_map/ppermute | solution.py:370
  115.8 12.9 %collective-permute-start.18 = (bf16[256,1024]{1,0:T(8,128)(2,1)S(1)}, bf16[256,1024]{1,0:T(8,128)(2,1)S(1)}, u32[]{:S(2)}, u32[]{:S(2)}) collective-permute-start(bf16[256,1024]{1,0:T(8,128)(2,1)S(1)} %fusion.40.refs_0_), channel_id=1, source_target_pairs={{0,4},{1,5},{2,6},{3,7},{4,0},{5,1},{6,2},{7,3},{8,12},{9,13},{10,... | collective-permute-start | bytes 1572872 | tf_op jit(solution)/shard_map/ppermute | solution.py:370
  117.3 17.9 %collective-permute-start.15 = (bf16[256,1024]{1,0:T(8,128)(2,1)S(1)}, bf16[256,1024]{1,0:T(8,128)(2,1)S(1)}, u32[]{:S(2)}, u32[]{:S(2)}) collective-permute-start(bf16[256,1024]{1,0:T(8,128)(2,1)S(1)} %fusion.40.refs_0_), channel_id=1, source_target_pairs={{0,1},{1,0},{2,3},{3,2},{4,5},{5,4},{6,7},{7,6},{8,9},{9,8},{10,11... | collective-permute-start | bytes 1572872 | tf_op jit(solution)/shard_map/ppermute | solution.py:370
  126.3 6.8 %collective-permute-start.20 = (bf16[128,1024]{1,0:T(8,128)(2,1)S(1)}, bf16[128,1024]{1,0:T(8,128)(2,1)S(1)}, u32[]{:S(2)}, u32[]{:S(2)}) collective-permute-start(bf16[128,1024]{1,0:T(8,128)(2,1)S(1)} %slice.304), channel_id=1, source_target_pairs={{0,4},{1,5},{2,6},{3,7},{4,0},{5,1},{6,2},{7,3},{8,12},{9,13},{10,... | collective-permute-start | bytes 786440 | tf_op jit(solution)/shard_map/ppermute | solution.py:370
  129.4 7.3 %collective-permute-start.17 = (bf16[256,1024]{1,0:T(8,128)(2,1)S(1)}, bf16[256,1024]{1,0:T(8,128)(2,1)S(1)}, u32[]{:S(2)}, u32[]{:S(2)}) collective-permute-start(bf16[256,1024]{1,0:T(8,128)(2,1)S(1)} %collective-permute-done.16.refs_2_), channel_id=1, source_target_pairs={{0,1},{1,0},{2,3},{3,2},{4,5},{5,4},{6,7},{7,6},{8,9},{9,8},{10,11... | collective-permute-start | bytes 1572872 | tf_op jit(solution)/shard_map/ppermute | solution.py:370
  129.4 7.3 %collective-permute-start.19 = (bf16[256,1024]{1,0:T(8,128)(2,1)S(1)}, bf16[256,1024]{1,0:T(8,128)(2,1)S(1)}, u32[]{:S(2)}, u32[]{:S(2)}) collective-permute-start(bf16[256,1024]{1,0:T(8,128)(2,1)S(1)} %collective-permute-done.18.refs_4_), channel_id=1, source_target_pairs={{0,1},{1,0},{2,3},{3,2},{4,5},{5,4},{6,7},{7,6},{8,9},{9,8},{10,11... | collective-permute-start | bytes 1572872 | tf_op jit(solution)/shard_map/ppermute | solution.py:370
  140.2 14.3 %collective-permute-start.25 = (bf16[256,1024]{1,0:T(8,128)(2,1)}, bf16[256,1024]{1,0:T(8,128)(2,1)}, u32[]{:S(2)}, u32[]{:S(2)}) collective-permute-start(bf16[256,1024]{1,0:T(8,128)(2,1)} %get-tuple-element.484.refs_0_), channel_id=1, source_target_pairs={{0,2},{1,3},{2,0},{3,1},{4,6},{5,7},{6,4},{7,5},{8,10},{9,11},{10,... | collective-permute-start | bytes 1572872 | tf_op jit(solution)/shard_map/ppermute | solution.py:370
  140.8 16.3 %collective-permute-start.27 = (bf16[256,1024]{1,0:T(8,128)(2,1)}, bf16[256,1024]{1,0:T(8,128)(2,1)}, u32[]{:S(2)}, u32[]{:S(2)}) collective-permute-start(bf16[256,1024]{1,0:T(8,128)(2,1)} %get-tuple-element.484.refs_0_), channel_id=1, source_target_pairs={{0,4},{1,5},{2,6},{3,7},{4,0},{5,1},{6,2},{7,3},{8,12},{9,13},{10,... | collective-permute-start | bytes 1572872 | tf_op jit(solution)/shard_map/ppermute | solution.py:370
  141.8 25.0 %collective-permute-start.24 = (bf16[256,1024]{1,0:T(8,128)(2,1)}, bf16[256,1024]{1,0:T(8,128)(2,1)}, u32[]{:S(2)}, u32[]{:S(2)}) collective-permute-start(bf16[256,1024]{1,0:T(8,128)(2,1)} %get-tuple-element.484.refs_0_), channel_id=1, source_target_pairs={{0,1},{1,0},{2,3},{3,2},{4,5},{5,4},{6,7},{7,6},{8,9},{9,8},{10,11... | collective-permute-start | bytes 1572872 | tf_op jit(solution)/shard_map/ppermute | solution.py:370
  155.5 7.7 %collective-permute-start.29 = (bf16[128,1024]{1,0:T(8,128)(2,1)S(1)}, bf16[128,1024]{1,0:T(8,128)(2,1)}, u32[]{:S(2)}, u32[]{:S(2)}) collective-permute-start(bf16[128,1024]{1,0:T(8,128)(2,1)S(1)} %slice.306), channel_id=1, source_target_pairs={{0,4},{1,5},{2,6},{3,7},{4,0},{5,1},{6,2},{7,3},{8,12},{9,13},{10,... | collective-permute-start | bytes 786440 | tf_op jit(solution)/shard_map/ppermute | solution.py:370
  158.1 7.4 %collective-permute-start.30 = (bf16[128,1024]{1,0:T(8,128)(2,1)S(1)}, bf16[128,1024]{1,0:T(8,128)(2,1)}, u32[]{:S(2)}, u32[]{:S(2)}) collective-permute-start(bf16[128,1024]{1,0:T(8,128)(2,1)S(1)} %slice.307), channel_id=1, source_target_pairs={{0,2},{1,3},{2,0},{3,1},{4,6},{5,7},{6,4},{7,5},{8,10},{9,11},{10,... | collective-permute-start | bytes 786440 | tf_op jit(solution)/shard_map/ppermute | solution.py:370
  158.5 8.9 %collective-permute-start.26 = (bf16[256,1024]{1,0:T(8,128)(2,1)}, bf16[256,1024]{1,0:T(8,128)(2,1)}, u32[]{:S(2)}, u32[]{:S(2)}) collective-permute-start(bf16[256,1024]{1,0:T(8,128)(2,1)} %collective-permute-done.25.refs_2_), channel_id=1, source_target_pairs={{0,1},{1,0},{2,3},{3,2},{4,5},{5,4},{6,7},{7,6},{8,9},{9,8},{10,11... | collective-permute-start | bytes 1572872 | tf_op jit(solution)/shard_map/ppermute | solution.py:370
  158.5 8.9 %collective-permute-start.28 = (bf16[256,1024]{1,0:T(8,128)(2,1)}, bf16[256,1024]{1,0:T(8,128)(2,1)}, u32[]{:S(2)}, u32[]{:S(2)}) collective-permute-start(bf16[256,1024]{1,0:T(8,128)(2,1)} %collective-permute-done.27.refs_4_), channel_id=1, source_target_pairs={{0,1},{1,0},{2,3},{3,2},{4,5},{5,4},{6,7},{7,6},{8,9},{9,8},{10,11... | collective-permute-start | bytes 1572872 | tf_op jit(solution)/shard_map/ppermute | solution.py:370
  184.5 33.0 %collective-permute-start.33 = (bf16[344,2048]{1,0:T(8,128)(2,1)S(1)}, bf16[344,2048]{1,0:T(8,128)(2,1)S(1)}, u32[]{:S(2)}, u32[]{:S(2)}) collective-permute-start(bf16[344,2048]{1,0:T(8,128)(2,1)S(1)} %weight_gradient.11.refs_0_), channel_id=1, source_target_pairs={{0,8},{8,0},{16,24},{24,16},{1,9},{9,1},{17,25},{25,17},{2,10},{10... | collective-permute-start | bytes 4227080 | tf_op jit(solution)/shard_map/ppermute | solution.py:650
  219.3 39.7 %collective-permute-start.35 = (bf16[344,2048]{1,0:T(8,128)(2,1)}, bf16[344,2048]{1,0:T(8,128)(2,1)}, u32[]{:S(2)}, u32[]{:S(2)}) collective-permute-start(bf16[344,2048]{1,0:T(8,128)(2,1)} %copy-done.36), channel_id=1, source_target_pairs={{8,16},{16,8},{9,17},{17,9},{10,18},{18,10},{11,19},{19,11},{12,20... | collective-permute-start | bytes 4227080 | tf_op jit(solution)/shard_map/ppermute | solution.py:646
  221.4 37.6 %collective-permute-start.34 = (bf16[344,2048]{1,0:T(8,128)(2,1)}, bf16[344,2048]{1,0:T(8,128)(2,1)}, u32[]{:S(2)}, u32[]{:S(2)}) collective-permute-start(bf16[344,2048]{1,0:T(8,128)(2,1)} %copy-done.42), channel_id=1, source_target_pairs={{0,8},{8,0},{16,24},{24,16},{1,9},{9,1},{17,25},{25,17},{2,10},{10... | collective-permute-start | bytes 4227080 | tf_op jit(solution)/shard_map/ppermute | solution.py:650
  230.3 10.7 %collective-permute-start.38 = (bf16[128,1024]{1,0:T(8,128)(2,1)}, bf16[128,1024]{1,0:T(8,128)(2,1)}, u32[]{:S(2)}, u32[]{:S(2)}) collective-permute-start(bf16[128,1024]{1,0:T(8,128)(2,1)} %get-tuple-element.449), channel_id=1, source_target_pairs={{0,4},{1,5},{2,6},{3,7},{4,0},{5,1},{6,2},{7,3},{8,12},{9,13},{10,... | collective-permute-start | bytes 786440 | tf_op jit(solution)/shard_map/ppermute | solution.py:397
  230.9 11.8 %collective-permute-start.40 = (bf16[128,1024]{1,0:T(8,128)(2,1)}, bf16[128,1024]{1,0:T(8,128)(2,1)}, u32[]{:S(2)}, u32[]{:S(2)}) collective-permute-start(bf16[128,1024]{1,0:T(8,128)(2,1)} %get-tuple-element.448), channel_id=1, source_target_pairs={{0,2},{1,3},{2,0},{3,1},{4,6},{5,7},{6,4},{7,5},{8,10},{9,11},{10,... | collective-permute-start | bytes 786440 | tf_op jit(solution)/shard_map/ppermute | solution.py:397
  232.0 7.8 %collective-permute-start.44 = (f32[2,1024]{1,0:T(2,128)}, f32[2,1024]{1,0:T(2,128)}, u32[]{:S(2)}, u32[]{:S(2)}) collective-permute-start(f32[2,1024]{1,0:T(2,128)} %fusion.73), channel_id=1, source_target_pairs={{0,2},{1,3},{2,0},{3,1},{4,6},{5,7},{6,4},{7,5},{8,10},{9,11},{10,... | collective-permute-start | bytes 24584 | tf_op jit(solution)/shard_map/ppermute | solution.py:698
  239.8 9.5 %collective-permute-start.37 = (bf16[128,1024]{1,0:T(8,128)(2,1)}, bf16[128,1024]{1,0:T(8,128)(2,1)S(1)}, u32[]{:S(2)}, u32[]{:S(2)}) collective-permute-start(bf16[128,1024]{1,0:T(8,128)(2,1)} %get-tuple-element.450), channel_id=1, source_target_pairs={{0,2},{1,3},{2,0},{3,1},{4,6},{5,7},{6,4},{7,5},{8,10},{9,11},{10,... | collective-permute-start | bytes 786440 | tf_op jit(solution)/shard_map/ppermute | solution.py:397
  242.7 15.0 %collective-permute-start.42 = (bf16[128,1024]{1,0:T(8,128)(2,1)}, bf16[128,1024]{1,0:T(8,128)(2,1)S(1)}, u32[]{:S(2)}, u32[]{:S(2)}) collective-permute-start(bf16[128,1024]{1,0:T(8,128)(2,1)} %get-tuple-element.451), channel_id=1, source_target_pairs={{0,4},{1,5},{2,6},{3,7},{4,0},{5,1},{6,2},{7,3},{8,12},{9,13},{10,... | collective-permute-start | bytes 786440 | tf_op jit(solution)/shard_map/ppermute | solution.py:397
  244.8 12.8 %collective-permute-start.39 = (bf16[128,1024]{1,0:T(8,128)(2,1)S(1)}, bf16[128,1024]{1,0:T(8,128)(2,1)S(1)}, u32[]{:S(2)}, u32[]{:S(2)}) collective-permute-start(bf16[128,1024]{1,0:T(8,128)(2,1)S(1)} %get-tuple-element.447), channel_id=1, source_target_pairs={{0,2},{1,3},{2,0},{3,1},{4,6},{5,7},{6,4},{7,5},{8,10},{9,11},{10,... | collective-permute-start | bytes 786440 | tf_op jit(solution)/shard_map/ppermute | solution.py:397
  249.2 8.4 %collective-permute-start.41 = (bf16[128,1024]{1,0:T(8,128)(2,1)S(1)}, bf16[128,1024]{1,0:T(8,128)(2,1)S(1)}, u32[]{:S(2)}, u32[]{:S(2)}) collective-permute-start(bf16[128,1024]{1,0:T(8,128)(2,1)S(1)} %get-tuple-element.446), channel_id=1, source_target_pairs={{0,4},{1,5},{2,6},{3,7},{4,0},{5,1},{6,2},{7,3},{8,12},{9,13},{10,... | collective-permute-start | bytes 786440 | tf_op jit(solution)/shard_map/ppermute | solution.py:397
  262.3 29.6 %collective-permute-start.46 = (bf16[344,2048]{1,0:T(8,128)(2,1)S(1)}, bf16[344,2048]{1,0:T(8,128)(2,1)S(1)}, u32[]{:S(2)}, u32[]{:S(2)}) collective-permute-start(bf16[344,2048]{1,0:T(8,128)(2,1)S(1)} %get-tuple-element.256.refs_2_), channel_id=1, source_target_pairs={{0,8},{8,0},{16,24},{24,16},{1,9},{9,1},{17,25},{25,17},{2,10},{10... | collective-permute-start | bytes 4227080 | tf_op jit(solution)/shard_map/ppermute | solution.py:650
  262.4 29.5 %collective-permute-start.47 = (bf16[344,2048]{1,0:T(8,128)(2,1)S(1)}, bf16[344,2048]{1,0:T(8,128)(2,1)S(1)}, u32[]{:S(2)}, u32[]{:S(2)}) collective-permute-start(bf16[344,2048]{1,0:T(8,128)(2,1)S(1)} %get-tuple-element.257.refs_3_), channel_id=1, source_target_pairs={{8,16},{16,8},{9,17},{17,9},{10,18},{18,10},{11,19},{19,11},{12,20... | collective-permute-start | bytes 4227080 | tf_op jit(solution)/shard_map/ppermute | solution.py:646
  293.3 35.4 %collective-permute-start.48 = (bf16[344,2048]{1,0:T(8,128)(2,1)S(1)}, bf16[344,2048]{1,0:T(8,128)(2,1)S(1)}, u32[]{:S(2)}, u32[]{:S(2)}) collective-permute-start(bf16[344,2048]{1,0:T(8,128)(2,1)S(1)} %get-tuple-element.273.refs_3_), channel_id=1, source_target_pairs={{0,8},{8,0},{16,24},{24,16},{1,9},{9,1},{17,25},{25,17},{2,10},{10... | collective-permute-start | bytes 4227080 | tf_op jit(solution)/shard_map/ppermute | solution.py:650
  297.2 31.5 %collective-permute-start.49 = (bf16[344,2048]{1,0:T(8,128)(2,1)S(1)}, bf16[344,2048]{1,0:T(8,128)(2,1)S(1)}, u32[]{:S(2)}, u32[]{:S(2)}) collective-permute-start(bf16[344,2048]{1,0:T(8,128)(2,1)S(1)} %get-tuple-element.274.refs_3_), channel_id=1, source_target_pairs={{8,16},{16,8},{9,17},{17,9},{10,18},{18,10},{11,19},{19,11},{12,20... | collective-permute-start | bytes 4227080 | tf_op jit(solution)/shard_map/ppermute | solution.py:646
  299.0 8.4 %collective-permute-start.52 = (bf16[128,1024]{1,0:T(8,128)(2,1)S(1)}, bf16[128,1024]{1,0:T(8,128)(2,1)S(1)}, u32[]{:S(2)}, u32[]{:S(2)}) collective-permute-start(bf16[128,1024]{1,0:T(8,128)(2,1)S(1)} %get-tuple-element.443), channel_id=1, source_target_pairs={{0,4},{1,5},{2,6},{3,7},{4,0},{5,1},{6,2},{7,3},{8,12},{9,13},{10,... | collective-permute-start | bytes 786440 | tf_op jit(solution)/shard_map/ppermute | solution.py:397
  299.6 9.2 %collective-permute-start.54 = (bf16[128,1024]{1,0:T(8,128)(2,1)S(1)}, bf16[128,1024]{1,0:T(8,128)(2,1)S(1)}, u32[]{:S(2)}, u32[]{:S(2)}) collective-permute-start(bf16[128,1024]{1,0:T(8,128)(2,1)S(1)} %get-tuple-element.442), channel_id=1, source_target_pairs={{0,2},{1,3},{2,0},{3,1},{4,6},{5,7},{6,4},{7,5},{8,10},{9,11},{10,... | collective-permute-start | bytes 786440 | tf_op jit(solution)/shard_map/ppermute | solution.py:397
  300.3 14.2 %collective-permute-start.51 = (bf16[128,1024]{1,0:T(8,128)(2,1)S(1)}, bf16[128,1024]{1,0:T(8,128)(2,1)S(1)}, u32[]{:S(2)}, u32[]{:S(2)}) collective-permute-start(bf16[128,1024]{1,0:T(8,128)(2,1)S(1)} %get-tuple-element.444), channel_id=1, source_target_pairs={{0,2},{1,3},{2,0},{3,1},{4,6},{5,7},{6,4},{7,5},{8,10},{9,11},{10,... | collective-permute-start | bytes 786440 | tf_op jit(solution)/shard_map/ppermute | solution.py:397
  307.5 13.9 %collective-permute-start.56 = (bf16[128,1024]{1,0:T(8,128)(2,1)S(1)}, bf16[128,1024]{1,0:T(8,128)(2,1)S(1)}, u32[]{:S(2)}, u32[]{:S(2)}) collective-permute-start(bf16[128,1024]{1,0:T(8,128)(2,1)S(1)} %get-tuple-element.445), channel_id=1, source_target_pairs={{0,4},{1,5},{2,6},{3,7},{4,0},{5,1},{6,2},{7,3},{8,12},{9,13},{10,... | collective-permute-start | bytes 786440 | tf_op jit(solution)/shard_map/ppermute | solution.py:397
  309.0 12.4 %collective-permute-start.53 = (bf16[128,1024]{1,0:T(8,128)(2,1)S(1)}, bf16[128,1024]{1,0:T(8,128)(2,1)S(1)}, u32[]{:S(2)}, u32[]{:S(2)}) collective-permute-start(bf16[128,1024]{1,0:T(8,128)(2,1)S(1)} %get-tuple-element.441), channel_id=1, source_target_pairs={{0,2},{1,3},{2,0},{3,1},{4,6},{5,7},{6,4},{7,5},{8,10},{9,11},{10,... | collective-permute-start | bytes 786440 | tf_op jit(solution)/shard_map/ppermute | solution.py:397
  314.4 6.9 %collective-permute-start.55 = (bf16[128,1024]{1,0:T(8,128)(2,1)S(1)}, bf16[128,1024]{1,0:T(8,128)(2,1)S(1)}, u32[]{:S(2)}, u32[]{:S(2)}) collective-permute-start(bf16[128,1024]{1,0:T(8,128)(2,1)S(1)} %get-tuple-element.440), channel_id=1, source_target_pairs={{0,4},{1,5},{2,6},{3,7},{4,0},{5,1},{6,2},{7,3},{8,12},{9,13},{10,... | collective-permute-start | bytes 786440 | tf_op jit(solution)/shard_map/ppermute | solution.py:397
  336.7 35.0 %collective-permute-start.57 = (bf16[344,2048]{1,0:T(8,128)(2,1)}, bf16[344,2048]{1,0:T(8,128)(2,1)}, u32[]{:S(2)}, u32[]{:S(2)}) collective-permute-start(bf16[344,2048]{1,0:T(8,128)(2,1)} %get-tuple-element.286.refs_2_), channel_id=1, source_target_pairs={{0,8},{8,0},{16,24},{24,16},{1,9},{9,1},{17,25},{25,17},{2,10},{10... | collective-permute-start | bytes 4227080 | tf_op jit(solution)/shard_map/ppermute | solution.py:650
  340.4 31.2 %collective-permute-start.58 = (bf16[344,2048]{1,0:T(8,128)(2,1)}, bf16[344,2048]{1,0:T(8,128)(2,1)}, u32[]{:S(2)}, u32[]{:S(2)}) collective-permute-start(bf16[344,2048]{1,0:T(8,128)(2,1)} %get-tuple-element.287.refs_3_), channel_id=1, source_target_pairs={{8,16},{16,8},{9,17},{17,9},{10,18},{18,10},{11,19},{19,11},{12,20... | collective-permute-start | bytes 4227080 | tf_op jit(solution)/shard_map/ppermute | solution.py:646
  378.4 36.3 %collective-permute-start.62 = (bf16[344,2048]{1,0:T(8,128)(2,1)}, bf16[344,2048]{1,0:T(8,128)(2,1)S(1)}, u32[]{:S(2)}, u32[]{:S(2)}) collective-permute-start(bf16[344,2048]{1,0:T(8,128)(2,1)} %copy-done.80), channel_id=1, source_target_pairs={{0,8},{8,0},{16,24},{24,16},{1,9},{9,1},{17,25},{25,17},{2,10},{10... | collective-permute-start | bytes 4227080 | tf_op jit(solution)/shard_map/ppermute | solution.py:650
  382.2 32.5 %collective-permute-start.63 = (bf16[344,2048]{1,0:T(8,128)(2,1)}, bf16[344,2048]{1,0:T(8,128)(2,1)S(1)}, u32[]{:S(2)}, u32[]{:S(2)}) collective-permute-start(bf16[344,2048]{1,0:T(8,128)(2,1)} %copy-done.71), channel_id=1, source_target_pairs={{8,16},{16,8},{9,17},{17,9},{10,18},{18,10},{11,19},{19,11},{12,20... | collective-permute-start | bytes 4227080 | tf_op jit(solution)/shard_map/ppermute | solution.py:646
  416.2 35.2 %collective-permute-start.64 = (bf16[344,2048]{1,0:T(8,128)(2,1)S(1)}, bf16[344,2048]{1,0:T(8,128)(2,1)S(1)}, u32[]{:S(2)}, u32[]{:S(2)}) collective-permute-start(bf16[344,2048]{1,0:T(8,128)(2,1)S(1)} %get-tuple-element.320.refs_2_), channel_id=1, source_target_pairs={{0,8},{8,0},{16,24},{24,16},{1,9},{9,1},{17,25},{25,17},{2,10},{10... | collective-permute-start | bytes 4227080 | tf_op jit(solution)/shard_map/ppermute | solution.py:650
  418.8 33.7 %collective-permute-start.65 = (bf16[344,2048]{1,0:T(8,128)(2,1)S(1)}, bf16[344,2048]{1,0:T(8,128)(2,1)S(1)}, u32[]{:S(2)}, u32[]{:S(2)}) collective-permute-start(bf16[344,2048]{1,0:T(8,128)(2,1)S(1)} %get-tuple-element.321.refs_3_), channel_id=1, source_target_pairs={{8,16},{16,8},{9,17},{17,9},{10,18},{18,10},{11,19},{19,11},{12,20... | collective-permute-start | bytes 4227080 | tf_op jit(solution)/shard_map/ppermute | solution.py:646
  461.2 31.9 %collective-permute-start.66 = (bf16[344,2048]{1,0:T(8,128)(2,1)S(1)}, bf16[344,2048]{1,0:T(8,128)(2,1)S(1)}, u32[]{:S(2)}, u32[]{:S(2)}) collective-permute-start(bf16[344,2048]{1,0:T(8,128)(2,1)S(1)} %get-tuple-element.349.refs_3_), channel_id=1, source_target_pairs={{0,8},{8,0},{16,24},{24,16},{1,9},{9,1},{17,25},{25,17},{2,10},{10... | collective-permute-start | bytes 4227080 | tf_op jit(solution)/shard_map/ppermute | solution.py:650
  464.0 11.1 %collective-permute-start.67 = (bf16[256,2048]{1,0:T(8,128)(2,1)S(1)}, bf16[256,2048]{1,0:T(8,128)(2,1)S(1)}, u32[]{:S(2)}, u32[]{:S(2)}) collective-permute-start(bf16[256,2048]{1,0:T(8,128)(2,1)S(1)} %get-tuple-element.348.refs_3_), channel_id=1, source_target_pairs={{8,16},{16,8},{9,17},{17,9},{10,18},{18,10},{11,19},{19,11},{12,20... | collective-permute-start | bytes 3145736 | tf_op jit(solution)/shard_map/ppermute | solution.py:646
  495.6 8.1 %collective-permute-start.70 = (bf16[4,256,1024]{2,1,0:T(8,128)(2,1)S(1)}, bf16[4,256,1024]{2,1,0:T(8,128)(2,1)}, u32[]{:S(2)}, u32[]{:S(2)}) collective-permute-start(bf16[4,256,1024]{2,1,0:T(8,128)(2,1)S(1)} %get-tuple-element.372), channel_id=1, source_target_pairs={{0,1},{1,0},{2,3},{3,2},{4,5},{5,4},{6,7},{7,6},{8,9},{9,8},{10,11... | collective-permute-start | bytes 6291464 | tf_op jit(solution)/shard_map/ppermute | solution.py:397
  498.7 33.7 %collective-permute-start.68 = (bf16[256,2048]{1,0:T(8,128)(2,1)}, bf16[256,2048]{1,0:T(8,128)(2,1)}, u32[]{:S(2)}, u32[]{:S(2)}) collective-permute-start(bf16[256,2048]{1,0:T(8,128)(2,1)} %get-tuple-element.364.refs_1_), channel_id=1, source_target_pairs={{0,8},{8,0},{16,24},{24,16},{1,9},{9,1},{17,25},{25,17},{2,10},{10... | collective-permute-start | bytes 3145736 | tf_op jit(solution)/shard_map/ppermute | solution.py:650
  500.6 31.8 %collective-permute-start.69 = (bf16[256,2048]{1,0:T(8,128)(2,1)}, bf16[256,2048]{1,0:T(8,128)(2,1)}, u32[]{:S(2)}, u32[]{:S(2)}) collective-permute-start(bf16[256,2048]{1,0:T(8,128)(2,1)} %get-tuple-element.365.refs_3_), channel_id=1, source_target_pairs={{8,16},{16,8},{9,17},{17,9},{10,18},{18,10},{11,19},{19,11},{12,20... | collective-permute-start | bytes 3145736 | tf_op jit(solution)/shard_map/ppermute | solution.py:646
  508.0 7.9 %collective-permute-start.72 = (bf16[128,1024]{1,0:T(8,128)(2,1)}, bf16[128,1024]{1,0:T(8,128)(2,1)S(1)}, u32[]{:S(2)}, u32[]{:S(2)}) collective-permute-start(bf16[128,1024]{1,0:T(8,128)(2,1)} %get-tuple-element.437), channel_id=1, source_target_pairs={{0,4},{1,5},{2,6},{3,7},{4,0},{5,1},{6,2},{7,3},{8,12},{9,13},{10,... | collective-permute-start | bytes 786440 | tf_op jit(solution)/shard_map/ppermute | solution.py:397
  508.4 9.6 %collective-permute-start.74 = (bf16[128,1024]{1,0:T(8,128)(2,1)}, bf16[128,1024]{1,0:T(8,128)(2,1)}, u32[]{:S(2)}, u32[]{:S(2)}) collective-permute-start(bf16[128,1024]{1,0:T(8,128)(2,1)} %get-tuple-element.436), channel_id=1, source_target_pairs={{0,2},{1,3},{2,0},{3,1},{4,6},{5,7},{6,4},{7,5},{8,10},{9,11},{10,... | collective-permute-start | bytes 786440 | tf_op jit(solution)/shard_map/ppermute | solution.py:397
  508.9 14.5 %collective-permute-start.71 = (bf16[128,1024]{1,0:T(8,128)(2,1)S(1)}, bf16[128,1024]{1,0:T(8,128)(2,1)}, u32[]{:S(2)}, u32[]{:S(2)}) collective-permute-start(bf16[128,1024]{1,0:T(8,128)(2,1)S(1)} %get-tuple-element.438), channel_id=1, source_target_pairs={{0,2},{1,3},{2,0},{3,1},{4,6},{5,7},{6,4},{7,5},{8,10},{9,11},{10,... | collective-permute-start | bytes 786440 | tf_op jit(solution)/shard_map/ppermute | solution.py:397
  518.0 10.6 %collective-permute-start.76 = (bf16[128,1024]{1,0:T(8,128)(2,1)S(1)}, bf16[128,1024]{1,0:T(8,128)(2,1)S(1)}, u32[]{:S(2)}, u32[]{:S(2)}) collective-permute-start(bf16[128,1024]{1,0:T(8,128)(2,1)S(1)} %get-tuple-element.439), channel_id=1, source_target_pairs={{0,4},{1,5},{2,6},{3,7},{4,0},{5,1},{6,2},{7,3},{8,12},{9,13},{10,... | collective-permute-start | bytes 786440 | tf_op jit(solution)/shard_map/ppermute | solution.py:397
  520.7 7.9 %collective-permute-start.73 = (bf16[128,1024]{1,0:T(8,128)(2,1)S(1)}, bf16[128,1024]{1,0:T(8,128)(2,1)S(1)}, u32[]{:S(2)}, u32[]{:S(2)}) collective-permute-start(bf16[128,1024]{1,0:T(8,128)(2,1)S(1)} %get-tuple-element.435), channel_id=1, source_target_pairs={{0,2},{1,3},{2,0},{3,1},{4,6},{5,7},{6,4},{7,5},{8,10},{9,11},{10,... | collective-permute-start | bytes 786440 | tf_op jit(solution)/shard_map/ppermute | solution.py:397
  536.7 23.0 %collective-permute-start.80 = (bf16[256,2048]{1,0:T(8,128)(2,1)}, bf16[256,2048]{1,0:T(8,128)(2,1)S(1)}, u32[]{:S(2)}, u32[]{:S(2)}) collective-permute-start(bf16[256,2048]{1,0:T(8,128)(2,1)} %get-tuple-element.381.refs_1_), channel_id=1, source_target_pairs={{0,8},{8,0},{16,24},{24,16},{1,9},{9,1},{17,25},{25,17},{2,10},{10... | collective-permute-start | bytes 3145736 | tf_op jit(solution)/shard_map/ppermute | solution.py:650
  538.8 21.9 %collective-permute-start.81 = (bf16[256,2048]{1,0:T(8,128)(2,1)}, bf16[256,2048]{1,0:T(8,128)(2,1)}, u32[]{:S(2)}, u32[]{:S(2)}) collective-permute-start(bf16[256,2048]{1,0:T(8,128)(2,1)} %get-tuple-element.380.refs_3_), channel_id=1, source_target_pairs={{8,16},{16,8},{9,17},{17,9},{10,18},{18,10},{11,19},{19,11},{12,20... | collective-permute-start | bytes 3145736 | tf_op jit(solution)/shard_map/ppermute | solution.py:646
  564.8 23.9 %collective-permute-start.82 = (bf16[272,2048]{1,0:T(8,128)(2,1)S(1)}, bf16[272,2048]{1,0:T(8,128)(2,1)S(1)}, u32[]{:S(2)}, u32[]{:S(2)}) collective-permute-start(bf16[272,2048]{1,0:T(8,128)(2,1)S(1)} %get-tuple-element.398.refs_1_), channel_id=1, source_target_pairs={{0,8},{8,0},{16,24},{24,16},{1,9},{9,1},{17,25},{25,17},{2,10},{10... | collective-permute-start | bytes 3342344 | tf_op jit(solution)/shard_map/ppermute | solution.py:650
  567.6 21.0 %collective-permute-start.83 = (bf16[256,2048]{1,0:T(8,128)(2,1)S(1)}, bf16[256,2048]{1,0:T(8,128)(2,1)S(1)}, u32[]{:S(2)}, u32[]{:S(2)}) collective-permute-start(bf16[256,2048]{1,0:T(8,128)(2,1)S(1)} %get-tuple-element.399.refs_2_), channel_id=1, source_target_pairs={{8,16},{16,8},{9,17},{17,9},{10,18},{18,10},{11,19},{19,11},{12,20... | collective-permute-start | bytes 3145736 | tf_op jit(solution)/shard_map/ppermute | solution.py:646
  589.7 25.6 %collective-permute-start.85 = (bf16[272,2048]{1,0:T(8,128)(2,1)S(1)}, bf16[272,2048]{1,0:T(8,128)(2,1)S(1)}, u32[]{:S(2)}, u32[]{:S(2)}) collective-permute-start(bf16[272,2048]{1,0:T(8,128)(2,1)S(1)} %get-tuple-element.402.refs_0_), channel_id=1, source_target_pairs={{8,16},{16,8},{9,17},{17,9},{10,18},{18,10},{11,19},{19,11},{12,20... | collective-permute-start | bytes 3342344 | tf_op jit(solution)/shard_map/ppermute | solution.py:646
  590.4 24.9 %collective-permute-start.84 = (bf16[256,2048]{1,0:T(8,128)(2,1)S(1)}, bf16[256,2048]{1,0:T(8,128)(2,1)S(1)}, u32[]{:S(2)}, u32[]{:S(2)}) collective-permute-start(bf16[256,2048]{1,0:T(8,128)(2,1)S(1)} %get-tuple-element.403.refs_1_), channel_id=1, source_target_pairs={{0,8},{8,0},{16,24},{24,16},{1,9},{9,1},{17,25},{25,17},{2,10},{10... | collective-permute-start | bytes 3145736 | tf_op jit(solution)/shard_map/ppermute | solution.py:650
  615.9 22.0 %collective-permute-start.86 = (bf16[272,2048]{1,0:T(8,128)(2,1)S(1)}, bf16[272,2048]{1,0:T(8,128)(2,1)S(1)}, u32[]{:S(2)}, u32[]{:S(2)}) collective-permute-start(bf16[272,2048]{1,0:T(8,128)(2,1)S(1)} %turn.23.refs_1_), channel_id=1, source_target_pairs={{0,8},{8,0},{16,24},{24,16},{1,9},{9,1},{17,25},{25,17},{2,10},{10... | collective-permute-start | bytes 3342344 | tf_op jit(solution)/shard_map/ppermute | solution.py:650
  (183 other events, 1650.4 us)
Sparse Core Ops, SparseCore 0:
  43.0 38.0 all-gather.1
  378.5 52.4 reduce-scatter.1

commit v6 on v5

--- a/solution.py
+++ b/solution.py
@@ -107,7 +107,7 @@
         z2=yk-rr[:,:L]
         return z2,jnp.where(rs,w0,wt-rw),jnp.where(rs,c0,ct-rc)
     zt=nn(w0.astype(BF),spread(ka_o[0][:HD],heads))+c0
-    lax.fori_loop(0,nb,body,(zt,w0,c0),unroll=4)
+    lax.fori_loop(0,nb,body,(zt,w0,c0),unroll=8)
     def post(gr,_):
         outs=[]
         for p in range(8):
@@ -219,7 +219,7 @@
     la=jnp.zeros((HD,heads*HD),F32) if last else li[...]
     lc=jnp.zeros((HD,L),F32) if last else lci[...]
     ht=nn(la.astype(BF),spread(ka_i[nb-1][:HD],heads))+lc
-    ht,la,lc=lax.fori_loop(0,nb,body,(ht,la,lc))
+    ht,la,lc=lax.fori_loop(0,nb,body,(ht,la,lc),unroll=4)
     lo[...]=la; lco[...]=lc
     def post(gr,_):
         dqs=[];dks=[];dvs=[];des=[]

time: 664 us -> 664 us (level)
  no operation moved by 1% of the time
where the time goes in v6:
time: 664 us; the launch traced here: 653 us
  waiting for transfers between devices  215 us (32%)
  Pallas kernels  181 us (27%)
  starting transfers between devices  96.5 us (15%)
  local copies, waits for them, and re-layouts  71 us (11%)
  other arithmetic  40.4 us (6%)
  matrix products  29.6 us (4%)
  between operations  18.8 us (3%)
    ppermute x13, waiting for transfers between devices, tick(): lax.ppermute(load, 'dp', [(0, 1), (1, 0), (2, 3), (3, 2)])  122 us
    ppermute x48, waiting for transfers between devices, swap(): return lax.ppermute(v, 'head', [(i, i ^ bit) for i in range(8)])  64.8 us
    unnamed x337, local copies, waits for them, and re-layouts  52.2 us
    pallas_call x2, Pallas kernels, ttt_bwd(): pl.pallas_call(functools.partial(bwd_kernel, heads, nb, part * nb, last),...  40.7 us
    ppermute x13, starting transfers between devices, tick(): lax.ppermute(load, 'dp', [(0, 1), (1, 0), (2, 3), (3, 2)])  35.5 us
    ppermute x48, starting transfers between devices, swap(): return lax.ppermute(v, 'head', [(i, i ^ bit) for i in range(8)])  34.2 us
    pallas_call x3, Pallas kernels, parts(): pl.pallas_call(functools.partial(parts_kernel, n), grid_spec=spec, out_sh...  27.5 us
    pallas_call x1, Pallas kernels, ttt_fwd(): pl.pallas_call(functools.partial(fwd_kernel, heads, nb), out_shape=outs,...  26.2 us
  transfers between devices with their start and end apart: 89, of which 37 were waited for; matrix products, arithmetic and copies ran while one was open for 11% of the time, Pallas kernels for 23%

profile of v6, /device:TPU:0, one launch (start us, length us, event | category | flops | bytes accessed | tf_op | source)
XLA Modules:
  0.0 652.6 jit_solution(6391613694323307849)
XLA Ops:
  10.9 2.6 collective-permute-start.4
  15.6 13.4 %collective-permute-done.1 = bf16[2,256,128]{2,1,0:T(8,128)(2,1)S(1)} collective-permute-done((bf16[2,256,128]{2,1,0:T(8,128)(2,1)S(1)}, bf16[2,256,128]{2,1,0:T(8,128)(2,1)S(1)}, u32[]{:S(2)}, u32[]{:S(2)}) %collective-permute-start.1) | collective-permute-done | bytes 131104 | tf_op jit(solution)/shard_map/ppermute | solution.py:430
  34.7 3.6 collective-permute-done.2
  39.2 3.7 collective-permute-done.8.refs_6_
  53.0 6.0 rms_rows.2
  59.8 2.6 convert_multiply_fusion.1
  68.5 26.2 %mix_forward.1 = (bf16[256,1024]{1,0:T(8,128)(2,1)S(1)}, f32[64,64,64]{2,1,0:T(8,128)S(1)}, f32[64,64,64]{2,1,0:T(8,128)S(1)}, f32[64,64,64]{2,1,0:T(8,128)S(1)}...) custom-call(s32[64]{0:T(128)S(1)} %or_convert_fusion.reset, ...), custom_call_target="tpu_custom_call" | custom-call | flops 262144 | bytes 4096 | tf_op jit(solution)/shard_map/mix_forward/pallas_call | solution.py:141
  116.6 8.9 %collective-permute-done.16.refs_2_ = bf16[256,1024]{1,0:T(8,128)(2,1)S(1)} collective-permute-done((bf16[256,1024]{1,0:T(8,128)(2,1)S(1)}, bf16[256,1024]{1,0:T(8,128)(2,1)S(1)}, u32[]{:S(2)}, u32[]{:S(2)}) %collective-permute-start.16) | collective-permute-done | bytes 524320 | tf_op jit(solution)/shard_map/ppermute | solution.py:370
  129.2 3.2 collective-permute-done.20.refs_6_
  137.0 2.5 fusion.88
  141.1 12.7 %collective-permute-done.25.refs_2_ = bf16[256,1024]{1,0:T(8,128)(2,1)} collective-permute-done((bf16[256,1024]{1,0:T(8,128)(2,1)}, bf16[256,1024]{1,0:T(8,128)(2,1)}, u32[]{:S(2)}, u32[]{:S(2)}) %collective-permute-start.25) | collective-permute-done | bytes 524320 | tf_op jit(solution)/shard_map/ppermute | solution.py:370
  158.2 4.2 collective-permute-done.29.refs_6_
  167.7 6.8 %rms_rows.3 = (bf16[2048,1024]{1,0:T(8,128)(2,1)S(1)}, f32[1,1024]{1,0:T(1,128)S(1)}, bf16[16,128]{1,0:T(8,128)(2,1)}) custom-call(s32[10]{0:T(128)S(1)} %stack.70.spots, bf16[2048,128]{1,0:T(8,128)(2,1)S(1)} %copy-done.95, bf16[256,1024]{1,0:T(8,128)(2,1)} %get-tuple-element.484.refs_0_, bf16[256,1024]{1,0:T(8,128)(2,1)} %collective-permute-done.24.refs_1_, ...), custom_call_target="tpu_custom_call" | custom-call | flops 16777216 | bytes 8388608 | tf_op jit(solution)/shard_map/rms_rows/pallas_call | solution.py:337
  174.5 3.1 fusion.90
  177.8 3.3 fusion.5
  185.3 3.9 fusion.4
  189.3 2.4 weight_gradient.12.refs_0_
  192.8 12.0 %parts.3 = (bf16[4,256,1024]{2,1,0:T(8,128)(2,1)S(1)}, bf16[4,256,1024]{2,1,0:T(8,128)(2,1)}, f32[1,1024]{1,0:T(1,128)S(1)}) custom-call(s32[1]{0:T(128)} %bitcast.35.core, bf16[688,2048]{1,0:T(8,128)(2,1)S(1)} %copy-done.114, bf16[688,2048]{1,0:T(8,128)(2,1)S(1)} %copy-done.115, bf16[688,1024]{1,0:T(8,128)(2,1)S(1)} %get-tuple-element.247.refs_2_, ...), custom_call_target="tpu_custom_call" | custom-call | flops 10000000000 | bytes 10000000 | tf_op jit(solution)/shard_map/parts/pallas_call | solution.py:573
  204.8 11.9 %collective-permute-done.33.refs_1_ = bf16[344,2048]{1,0:T(8,128)(2,1)S(1)} collective-permute-done((bf16[344,2048]{1,0:T(8,128)(2,1)S(1)}, bf16[344,2048]{1,0:T(8,128)(2,1)S(1)}, u32[]{:S(2)}, u32[]{:S(2)}) %collective-permute-start.33) | collective-permute-done | bytes 1409056 | tf_op jit(solution)/shard_map/ppermute | solution.py:650
  220.7 3.3 collective-permute-start.34
  224.0 3.2 add_convert_fusion.2
  233.3 5.7 collective-permute-done.44
  245.5 3.0 collective-permute-done.37
  251.4 2.4 weight_gradient.14.refs_2_.refs_0_
  253.8 2.4 weight_gradient.13.refs_2_.refs_0_
  258.3 3.3 turn.13
  262.6 2.4 weight_gradient.15.refs_2_.refs_0_
  267.1 5.7 parts.4
  272.7 18.4 %collective-permute-done.46.refs_1_.refs_0_ = bf16[344,2048]{1,0:T(8,128)(2,1)S(1)} collective-permute-done((bf16[344,2048]{1,0:T(8,128)(2,1)S(1)}, bf16[344,2048]{1,0:T(8,128)(2,1)S(1)}, u32[]{:S(2)}, u32[]{:S(2)}) %collective-permute-start.46) | collective-permute-done | bytes 1409056 | tf_op jit(solution)/shard_map/ppermute | solution.py:650
  292.5 3.9 collective-permute-start.48
  300.9 5.8 collective-permute-done.52
  309.0 4.7 collective-permute-done.51
  320.9 7.0 %collective-permute-done.48.refs_1_ = bf16[344,2048]{1,0:T(8,128)(2,1)S(1)} collective-permute-done((bf16[344,2048]{1,0:T(8,128)(2,1)S(1)}, bf16[344,2048]{1,0:T(8,128)(2,1)S(1)}, u32[]{:S(2)}, u32[]{:S(2)}) %collective-permute-start.48) | collective-permute-done | bytes 1409056 | tf_op jit(solution)/shard_map/ppermute | solution.py:650
  327.9 2.7 turn.15
  330.6 3.2 fusion.45
  335.9 3.7 collective-permute-start.57
  342.1 5.1 convert_bitcast_fusion
  347.2 2.6 fusion.44.dOT
  349.8 21.1 %collective-permute-done.57.refs_1_.refs_0_ = bf16[344,2048]{1,0:T(8,128)(2,1)} collective-permute-done((bf16[344,2048]{1,0:T(8,128)(2,1)}, bf16[344,2048]{1,0:T(8,128)(2,1)}, u32[]{:S(2)}, u32[]{:S(2)}) %collective-permute-start.57) | collective-permute-done | bytes 1409056 | tf_op jit(solution)/shard_map/ppermute | solution.py:650
  372.2 3.2 turn.16
  377.7 3.8 collective-permute-start.62
  391.9 20.1 %mix_backward.2 = (bf16[256,1024]{1,0:T(8,128)(2,1)S(1)}, bf16[256,1024]{1,0:T(8,128)(2,1)S(1)}, bf16[256,1024]{1,0:T(8,128)(2,1)S(1)}, f32[4,512]{1,0:T(4,128)S...) custom-call(s32[64]{0:T(128)S(1)} %or_convert_fusion.reset, ...), custom_call_target="tpu_custom_call" | custom-call | flops 131072 | bytes 2048 | tf_op jit(solution)/shard_map/mix_backward/pallas_call | solution.py:261
  415.6 2.6 collective-permute-start.64
  421.2 20.6 %mix_backward.3 = (bf16[256,1024]{1,0:T(8,128)(2,1)S(1)}, bf16[256,1024]{1,0:T(8,128)(2,1)S(1)}, bf16[256,1024]{1,0:T(8,128)(2,1)S(1)}, f32[4,512]{1,0:T(4,128)S...) custom-call(s32[64]{0:T(128)S(1)} %or_convert_fusion.reset, ...), custom_call_target="tpu_custom_call", output_to_operand_aliasing={{0}: (12, {}), {1}: (13, {}), {2}: (14, {})} | custom-call | flops 131072 | bytes 2048 | tf_op jit(solution)/shard_map/mix_backward/pallas_call | solution.py:261
  460.9 3.0 collective-permute-start.66
  465.0 9.8 %parts.5 = (bf16[4,256,1024]{2,1,0:T(8,128)(2,1)S(1)}, bf16[4,256,1024]{2,1,0:T(8,128)(2,1)S(1)}, f32[1,1024]{1,0:T(1,128)S(1)}) custom-call(s32[1]{0:T(128)} %bitcast.35.core, bf16[1040,2048]{1,0:T(8,128)(2,1)S(1)} %copy-done.99, bf16[1040,1024]{1,0:T(8,128)(2,1)S(1)} %pad_dynamic-update-slice_fusion.1.refs_1_, bf16[2048,1024]{1,0:T(8,128)(2,1)S(1)} %copy-done.4), custom_call_target="tpu_custom_call" | custom-call | flops 10000000000 | bytes 10000000 | tf_op jit(solution)/shard_map/parts/pallas_call | solution.py:573
  474.8 18.0 %collective-permute-done.66.refs_1_ = bf16[344,2048]{1,0:T(8,128)(2,1)S(1)} collective-permute-done((bf16[344,2048]{1,0:T(8,128)(2,1)S(1)}, bf16[344,2048]{1,0:T(8,128)(2,1)S(1)}, u32[]{:S(2)}, u32[]{:S(2)}) %collective-permute-start.66) | collective-permute-done | bytes 1409056 | tf_op jit(solution)/shard_map/ppermute | solution.py:650
  492.9 2.5 turn.19
  503.4 3.2 add_convert_fusion
  510.9 4.8 collective-permute-done.72
  524.9 3.4 fusion.89
  532.2 4.2 turn.20
  541.1 3.6 fusion.21
  549.0 10.4 %collective-permute-done.80.refs_1_.refs_0_ = bf16[256,2048]{1,0:T(8,128)(2,1)S(1)} collective-permute-done((bf16[256,2048]{1,0:T(8,128)(2,1)}, bf16[256,2048]{1,0:T(8,128)(2,1)S(1)}, u32[]{:S(2)}, u32[]{:S(2)}) %collective-permute-start.80) | collective-permute-done | bytes 1048608 | tf_op jit(solution)/shard_map/ppermute | solution.py:650
  561.7 2.8 turn.21
  564.5 2.8 collective-permute-start.82
  568.2 3.2 finish.8
  571.5 5.9 finish.9
  577.4 3.2 finish.10
  580.6 3.9 finish.11
  584.4 3.6 finish.12
  590.2 4.8 collective-permute-start.84
  596.9 18.1 %collective-permute-done.84.refs_0_ = bf16[256,2048]{1,0:T(8,128)(2,1)S(1)} collective-permute-done((bf16[256,2048]{1,0:T(8,128)(2,1)S(1)}, bf16[256,2048]{1,0:T(8,128)(2,1)S(1)}, u32[]{:S(2)}, u32[]{:S(2)}) %collective-permute-start.84) | collective-permute-done | bytes 1048608 | tf_op jit(solution)/shard_map/ppermute | solution.py:650
  620.4 17.0 %collective-permute-done.86.refs_0_ = bf16[272,2048]{1,0:T(8,128)(2,1)S(1)} collective-permute-done((bf16[272,2048]{1,0:T(8,128)(2,1)S(1)}, bf16[272,2048]{1,0:T(8,128)(2,1)S(1)}, u32[]{:S(2)}, u32[]{:S(2)}) %collective-permute-start.86) | collective-permute-done | bytes 1114144 | tf_op jit(solution)/shard_map/ppermute | solution.py:650
  (640 shorter events, 212.7 us)
Async XLA Ops:
  7.3 95.6 %all-gather.2.cloned.1.call-start = ((), (), s32[]{:S(2)}) async-start(), calls=%async_computation.1 | async-start | bytes 4718592 | tf_op jit(solution)/shard_map/all_gather | solution.py:692
  10.9 20.0 %collective-permute-start.4 = (bf16[256,1024]{1,0:T(8,128)(2,1)}, bf16[256,1024]{1,0:T(8,128)(2,1)S(1)}, u32[]{:S(2)}, u32[]{:S(2)}) collective-permute-start(bf16[256,1024]{1,0:T(8,128)(2,1)} %refs_0_.3), channel_id=1, source_target_pairs={{0,2},{1,3},{2,0},{3,1},{4,6},{5,7},{6,4},{7,5},{8,10},{9,11},{10,... | collective-permute-start | bytes 1572872 | tf_op jit(solution)/shard_map/ppermute | solution.py:370
  13.5 18.5 %collective-permute-start.6 = (bf16[256,1024]{1,0:T(8,128)(2,1)}, bf16[256,1024]{1,0:T(8,128)(2,1)S(1)}, u32[]{:S(2)}, u32[]{:S(2)}) collective-permute-start(bf16[256,1024]{1,0:T(8,128)(2,1)} %refs_0_.3), channel_id=1, source_target_pairs={{0,4},{1,5},{2,6},{3,7},{4,0},{5,1},{6,2},{7,3},{8,12},{9,13},{10,... | collective-permute-start | bytes 1572872 | tf_op jit(solution)/shard_map/ppermute | solution.py:370
  15.0 14.0 %collective-permute-start.1 = (bf16[2,256,128]{2,1,0:T(8,128)(2,1)S(1)}, bf16[2,256,128]{2,1,0:T(8,128)(2,1)S(1)}, u32[]{:S(2)}, u32[]{:S(2)}) collective-permute-start(bf16[2,256,128]{2,1,0:T(8,128)(2,1)S(1)} %pad_maximum_fusion.3), channel_id=1, source_target_pairs={{0,2},{1,3},{2,0},{3,1},{4,6},{5,7},{6,4},{7,5},{8,10},{9,11},{10,... | collective-permute-start | bytes 393224 | tf_op jit(solution)/shard_map/ppermute | solution.py:430
  29.1 9.3 %collective-permute-start.2 = (bf16[4,256,128]{2,1,0:T(8,128)(2,1)S(1)}, bf16[4,256,128]{2,1,0:T(8,128)(2,1)S(1)}, u32[]{:S(2)}, u32[]{:S(2)}) collective-permute-start(bf16[4,256,128]{2,1,0:T(8,128)(2,1)S(1)} %pad_maximum_fusion.2), channel_id=1, source_target_pairs={{0,4},{1,5},{2,6},{3,7},{4,0},{5,1},{6,2},{7,3},{8,12},{9,13},{10,... | collective-permute-start | bytes 786440 | tf_op jit(solution)/shard_map/ppermute | solution.py:430
  31.7 11.2 %collective-permute-start.8 = (bf16[128,1024]{1,0:T(8,128)(2,1)S(1)}, bf16[128,1024]{1,0:T(8,128)(2,1)}, u32[]{:S(2)}, u32[]{:S(2)}) collective-permute-start(bf16[128,1024]{1,0:T(8,128)(2,1)S(1)} %slice.296), channel_id=1, source_target_pairs={{0,4},{1,5},{2,6},{3,7},{4,0},{5,1},{6,2},{7,3},{8,12},{9,13},{10,... | collective-permute-start | bytes 786440 | tf_op jit(solution)/shard_map/ppermute | solution.py:370
  32.8 10.1 %collective-permute-start.9 = (bf16[128,1024]{1,0:T(8,128)(2,1)S(1)}, bf16[128,1024]{1,0:T(8,128)(2,1)}, u32[]{:S(2)}, u32[]{:S(2)}) collective-permute-start(bf16[128,1024]{1,0:T(8,128)(2,1)S(1)} %slice.297), channel_id=1, source_target_pairs={{0,2},{1,3},{2,0},{3,1},{4,6},{5,7},{6,4},{7,5},{8,10},{9,11},{10,... | collective-permute-start | bytes 786440 | tf_op jit(solution)/shard_map/ppermute | solution.py:370
  42.9 410.4 %reduce-scatter.2.cloned.1.call-start = ((), (), s32[]{:S(2)}) async-start(), calls=%async_computation.2 | async-start | bytes 4718592 | tf_op jit(solution)/shard_map/reduce_scatter | solution.py:795
  113.4 12.1 %collective-permute-start.16 = (bf16[256,1024]{1,0:T(8,128)(2,1)S(1)}, bf16[256,1024]{1,0:T(8,128)(2,1)S(1)}, u32[]{:S(2)}, u32[]{:S(2)}) collective-permute-start(bf16[256,1024]{1,0:T(8,128)(2,1)S(1)} %fusion.40.refs_0_), channel_id=1, source_target_pairs={{0,2},{1,3},{2,0},{3,1},{4,6},{5,7},{6,4},{7,5},{8,10},{9,11},{10,... | collective-permute-start | bytes 1572872 | tf_op jit(solution)/shard_map/ppermute | solution.py:370
  115.0 12.9 %collective-permute-start.18 = (bf16[256,1024]{1,0:T(8,128)(2,1)S(1)}, bf16[256,1024]{1,0:T(8,128)(2,1)S(1)}, u32[]{:S(2)}, u32[]{:S(2)}) collective-permute-start(bf16[256,1024]{1,0:T(8,128)(2,1)S(1)} %fusion.40.refs_0_), channel_id=1, source_target_pairs={{0,4},{1,5},{2,6},{3,7},{4,0},{5,1},{6,2},{7,3},{8,12},{9,13},{10,... | collective-permute-start | bytes 1572872 | tf_op jit(solution)/shard_map/ppermute | solution.py:370
  116.6 17.9 %collective-permute-start.15 = (bf16[256,1024]{1,0:T(8,128)(2,1)S(1)}, bf16[256,1024]{1,0:T(8,128)(2,1)S(1)}, u32[]{:S(2)}, u32[]{:S(2)}) collective-permute-start(bf16[256,1024]{1,0:T(8,128)(2,1)S(1)} %fusion.40.refs_0_), channel_id=1, source_target_pairs={{0,1},{1,0},{2,3},{3,2},{4,5},{5,4},{6,7},{7,6},{8,9},{9,8},{10,11... | collective-permute-start | bytes 1572872 | tf_op jit(solution)/shard_map/ppermute | solution.py:370
  125.5 6.8 %collective-permute-start.20 = (bf16[128,1024]{1,0:T(8,128)(2,1)S(1)}, bf16[128,1024]{1,0:T(8,128)(2,1)S(1)}, u32[]{:S(2)}, u32[]{:S(2)}) collective-permute-start(bf16[128,1024]{1,0:T(8,128)(2,1)S(1)} %slice.304), channel_id=1, source_target_pairs={{0,4},{1,5},{2,6},{3,7},{4,0},{5,1},{6,2},{7,3},{8,12},{9,13},{10,... | collective-permute-start | bytes 786440 | tf_op jit(solution)/shard_map/ppermute | solution.py:370
  128.7 7.3 %collective-permute-start.17 = (bf16[256,1024]{1,0:T(8,128)(2,1)S(1)}, bf16[256,1024]{1,0:T(8,128)(2,1)S(1)}, u32[]{:S(2)}, u32[]{:S(2)}) collective-permute-start(bf16[256,1024]{1,0:T(8,128)(2,1)S(1)} %collective-permute-done.16.refs_2_), channel_id=1, source_target_pairs={{0,1},{1,0},{2,3},{3,2},{4,5},{5,4},{6,7},{7,6},{8,9},{9,8},{10,11... | collective-permute-start | bytes 1572872 | tf_op jit(solution)/shard_map/ppermute | solution.py:370
  128.7 7.3 %collective-permute-start.19 = (bf16[256,1024]{1,0:T(8,128)(2,1)S(1)}, bf16[256,1024]{1,0:T(8,128)(2,1)S(1)}, u32[]{:S(2)}, u32[]{:S(2)}) collective-permute-start(bf16[256,1024]{1,0:T(8,128)(2,1)S(1)} %collective-permute-done.18.refs_4_), channel_id=1, source_target_pairs={{0,1},{1,0},{2,3},{3,2},{4,5},{5,4},{6,7},{7,6},{8,9},{9,8},{10,11... | collective-permute-start | bytes 1572872 | tf_op jit(solution)/shard_map/ppermute | solution.py:370
  139.5 14.3 %collective-permute-start.25 = (bf16[256,1024]{1,0:T(8,128)(2,1)}, bf16[256,1024]{1,0:T(8,128)(2,1)}, u32[]{:S(2)}, u32[]{:S(2)}) collective-permute-start(bf16[256,1024]{1,0:T(8,128)(2,1)} %get-tuple-element.484.refs_0_), channel_id=1, source_target_pairs={{0,2},{1,3},{2,0},{3,1},{4,6},{5,7},{6,4},{7,5},{8,10},{9,11},{10,... | collective-permute-start | bytes 1572872 | tf_op jit(solution)/shard_map/ppermute | solution.py:370
  140.1 16.3 %collective-permute-start.27 = (bf16[256,1024]{1,0:T(8,128)(2,1)}, bf16[256,1024]{1,0:T(8,128)(2,1)}, u32[]{:S(2)}, u32[]{:S(2)}) collective-permute-start(bf16[256,1024]{1,0:T(8,128)(2,1)} %get-tuple-element.484.refs_0_), channel_id=1, source_target_pairs={{0,4},{1,5},{2,6},{3,7},{4,0},{5,1},{6,2},{7,3},{8,12},{9,13},{10,... | collective-permute-start | bytes 1572872 | tf_op jit(solution)/shard_map/ppermute | solution.py:370
  141.1 25.0 %collective-permute-start.24 = (bf16[256,1024]{1,0:T(8,128)(2,1)}, bf16[256,1024]{1,0:T(8,128)(2,1)}, u32[]{:S(2)}, u32[]{:S(2)}) collective-permute-start(bf16[256,1024]{1,0:T(8,128)(2,1)} %get-tuple-element.484.refs_0_), channel_id=1, source_target_pairs={{0,1},{1,0},{2,3},{3,2},{4,5},{5,4},{6,7},{7,6},{8,9},{9,8},{10,11... | collective-permute-start | bytes 1572872 | tf_op jit(solution)/shard_map/ppermute | solution.py:370
  154.7 7.7 %collective-permute-start.29 = (bf16[128,1024]{1,0:T(8,128)(2,1)S(1)}, bf16[128,1024]{1,0:T(8,128)(2,1)}, u32[]{:S(2)}, u32[]{:S(2)}) collective-permute-start(bf16[128,1024]{1,0:T(8,128)(2,1)S(1)} %slice.306), channel_id=1, source_target_pairs={{0,4},{1,5},{2,6},{3,7},{4,0},{5,1},{6,2},{7,3},{8,12},{9,13},{10,... | collective-permute-start | bytes 786440 | tf_op jit(solution)/shard_map/ppermute | solution.py:370
  157.4 7.4 %collective-permute-start.30 = (bf16[128,1024]{1,0:T(8,128)(2,1)S(1)}, bf16[128,1024]{1,0:T(8,128)(2,1)}, u32[]{:S(2)}, u32[]{:S(2)}) collective-permute-start(bf16[128,1024]{1,0:T(8,128)(2,1)S(1)} %slice.307), channel_id=1, source_target_pairs={{0,2},{1,3},{2,0},{3,1},{4,6},{5,7},{6,4},{7,5},{8,10},{9,11},{10,... | collective-permute-start | bytes 786440 | tf_op jit(solution)/shard_map/ppermute | solution.py:370
  157.7 8.9 %collective-permute-start.26 = (bf16[256,1024]{1,0:T(8,128)(2,1)}, bf16[256,1024]{1,0:T(8,128)(2,1)}, u32[]{:S(2)}, u32[]{:S(2)}) collective-permute-start(bf16[256,1024]{1,0:T(8,128)(2,1)} %collective-permute-done.25.refs_2_), channel_id=1, source_target_pairs={{0,1},{1,0},{2,3},{3,2},{4,5},{5,4},{6,7},{7,6},{8,9},{9,8},{10,11... | collective-permute-start | bytes 1572872 | tf_op jit(solution)/shard_map/ppermute | solution.py:370
  157.7 8.9 %collective-permute-start.28 = (bf16[256,1024]{1,0:T(8,128)(2,1)}, bf16[256,1024]{1,0:T(8,128)(2,1)}, u32[]{:S(2)}, u32[]{:S(2)}) collective-permute-start(bf16[256,1024]{1,0:T(8,128)(2,1)} %collective-permute-done.27.refs_4_), channel_id=1, source_target_pairs={{0,1},{1,0},{2,3},{3,2},{4,5},{5,4},{6,7},{7,6},{8,9},{9,8},{10,11... | collective-permute-start | bytes 1572872 | tf_op jit(solution)/shard_map/ppermute | solution.py:370
  183.7 33.0 %collective-permute-start.33 = (bf16[344,2048]{1,0:T(8,128)(2,1)S(1)}, bf16[344,2048]{1,0:T(8,128)(2,1)S(1)}, u32[]{:S(2)}, u32[]{:S(2)}) collective-permute-start(bf16[344,2048]{1,0:T(8,128)(2,1)S(1)} %weight_gradient.11.refs_0_), channel_id=1, source_target_pairs={{0,8},{8,0},{16,24},{24,16},{1,9},{9,1},{17,25},{25,17},{2,10},{10... | collective-permute-start | bytes 4227080 | tf_op jit(solution)/shard_map/ppermute | solution.py:650
  218.5 39.7 %collective-permute-start.35 = (bf16[344,2048]{1,0:T(8,128)(2,1)}, bf16[344,2048]{1,0:T(8,128)(2,1)}, u32[]{:S(2)}, u32[]{:S(2)}) collective-permute-start(bf16[344,2048]{1,0:T(8,128)(2,1)} %copy-done.36), channel_id=1, source_target_pairs={{8,16},{16,8},{9,17},{17,9},{10,18},{18,10},{11,19},{19,11},{12,20... | collective-permute-start | bytes 4227080 | tf_op jit(solution)/shard_map/ppermute | solution.py:646
  220.7 37.6 %collective-permute-start.34 = (bf16[344,2048]{1,0:T(8,128)(2,1)}, bf16[344,2048]{1,0:T(8,128)(2,1)}, u32[]{:S(2)}, u32[]{:S(2)}) collective-permute-start(bf16[344,2048]{1,0:T(8,128)(2,1)} %copy-done.42), channel_id=1, source_target_pairs={{0,8},{8,0},{16,24},{24,16},{1,9},{9,1},{17,25},{25,17},{2,10},{10... | collective-permute-start | bytes 4227080 | tf_op jit(solution)/shard_map/ppermute | solution.py:650
  229.6 10.7 %collective-permute-start.38 = (bf16[128,1024]{1,0:T(8,128)(2,1)}, bf16[128,1024]{1,0:T(8,128)(2,1)}, u32[]{:S(2)}, u32[]{:S(2)}) collective-permute-start(bf16[128,1024]{1,0:T(8,128)(2,1)} %get-tuple-element.449), channel_id=1, source_target_pairs={{0,4},{1,5},{2,6},{3,7},{4,0},{5,1},{6,2},{7,3},{8,12},{9,13},{10,... | collective-permute-start | bytes 786440 | tf_op jit(solution)/shard_map/ppermute | solution.py:397
  230.1 11.8 %collective-permute-start.40 = (bf16[128,1024]{1,0:T(8,128)(2,1)}, bf16[128,1024]{1,0:T(8,128)(2,1)}, u32[]{:S(2)}, u32[]{:S(2)}) collective-permute-start(bf16[128,1024]{1,0:T(8,128)(2,1)} %get-tuple-element.448), channel_id=1, source_target_pairs={{0,2},{1,3},{2,0},{3,1},{4,6},{5,7},{6,4},{7,5},{8,10},{9,11},{10,... | collective-permute-start | bytes 786440 | tf_op jit(solution)/shard_map/ppermute | solution.py:397
  231.3 7.8 %collective-permute-start.44 = (f32[2,1024]{1,0:T(2,128)}, f32[2,1024]{1,0:T(2,128)}, u32[]{:S(2)}, u32[]{:S(2)}) collective-permute-start(f32[2,1024]{1,0:T(2,128)} %fusion.73), channel_id=1, source_target_pairs={{0,2},{1,3},{2,0},{3,1},{4,6},{5,7},{6,4},{7,5},{8,10},{9,11},{10,... | collective-permute-start | bytes 24584 | tf_op jit(solution)/shard_map/ppermute | solution.py:698
  239.0 9.5 %collective-permute-start.37 = (bf16[128,1024]{1,0:T(8,128)(2,1)}, bf16[128,1024]{1,0:T(8,128)(2,1)S(1)}, u32[]{:S(2)}, u32[]{:S(2)}) collective-permute-start(bf16[128,1024]{1,0:T(8,128)(2,1)} %get-tuple-element.450), channel_id=1, source_target_pairs={{0,2},{1,3},{2,0},{3,1},{4,6},{5,7},{6,4},{7,5},{8,10},{9,11},{10,... | collective-permute-start | bytes 786440 | tf_op jit(solution)/shard_map/ppermute | solution.py:397
  241.9 15.0 %collective-permute-start.42 = (bf16[128,1024]{1,0:T(8,128)(2,1)}, bf16[128,1024]{1,0:T(8,128)(2,1)S(1)}, u32[]{:S(2)}, u32[]{:S(2)}) collective-permute-start(bf16[128,1024]{1,0:T(8,128)(2,1)} %get-tuple-element.451), channel_id=1, source_target_pairs={{0,4},{1,5},{2,6},{3,7},{4,0},{5,1},{6,2},{7,3},{8,12},{9,13},{10,... | collective-permute-start | bytes 786440 | tf_op jit(solution)/shard_map/ppermute | solution.py:397
  244.1 12.8 %collective-permute-start.39 = (bf16[128,1024]{1,0:T(8,128)(2,1)S(1)}, bf16[128,1024]{1,0:T(8,128)(2,1)S(1)}, u32[]{:S(2)}, u32[]{:S(2)}) collective-permute-start(bf16[128,1024]{1,0:T(8,128)(2,1)S(1)} %get-tuple-element.447), channel_id=1, source_target_pairs={{0,2},{1,3},{2,0},{3,1},{4,6},{5,7},{6,4},{7,5},{8,10},{9,11},{10,... | collective-permute-start | bytes 786440 | tf_op jit(solution)/shard_map/ppermute | solution.py:397
  248.5 8.4 %collective-permute-start.41 = (bf16[128,1024]{1,0:T(8,128)(2,1)S(1)}, bf16[128,1024]{1,0:T(8,128)(2,1)S(1)}, u32[]{:S(2)}, u32[]{:S(2)}) collective-permute-start(bf16[128,1024]{1,0:T(8,128)(2,1)S(1)} %get-tuple-element.446), channel_id=1, source_target_pairs={{0,4},{1,5},{2,6},{3,7},{4,0},{5,1},{6,2},{7,3},{8,12},{9,13},{10,... | collective-permute-start | bytes 786440 | tf_op jit(solution)/shard_map/ppermute | solution.py:397
  261.6 29.6 %collective-permute-start.46 = (bf16[344,2048]{1,0:T(8,128)(2,1)S(1)}, bf16[344,2048]{1,0:T(8,128)(2,1)S(1)}, u32[]{:S(2)}, u32[]{:S(2)}) collective-permute-start(bf16[344,2048]{1,0:T(8,128)(2,1)S(1)} %get-tuple-element.256.refs_2_), channel_id=1, source_target_pairs={{0,8},{8,0},{16,24},{24,16},{1,9},{9,1},{17,25},{25,17},{2,10},{10... | collective-permute-start | bytes 4227080 | tf_op jit(solution)/shard_map/ppermute | solution.py:650
  261.6 29.5 %collective-permute-start.47 = (bf16[344,2048]{1,0:T(8,128)(2,1)S(1)}, bf16[344,2048]{1,0:T(8,128)(2,1)S(1)}, u32[]{:S(2)}, u32[]{:S(2)}) collective-permute-start(bf16[344,2048]{1,0:T(8,128)(2,1)S(1)} %get-tuple-element.257.refs_3_), channel_id=1, source_target_pairs={{8,16},{16,8},{9,17},{17,9},{10,18},{18,10},{11,19},{19,11},{12,20... | collective-permute-start | bytes 4227080 | tf_op jit(solution)/shard_map/ppermute | solution.py:646
  292.5 35.4 %collective-permute-start.48 = (bf16[344,2048]{1,0:T(8,128)(2,1)S(1)}, bf16[344,2048]{1,0:T(8,128)(2,1)S(1)}, u32[]{:S(2)}, u32[]{:S(2)}) collective-permute-start(bf16[344,2048]{1,0:T(8,128)(2,1)S(1)} %get-tuple-element.273.refs_3_), channel_id=1, source_target_pairs={{0,8},{8,0},{16,24},{24,16},{1,9},{9,1},{17,25},{25,17},{2,10},{10... | collective-permute-start | bytes 4227080 | tf_op jit(solution)/shard_map/ppermute | solution.py:650
  296.4 31.5 %collective-permute-start.49 = (bf16[344,2048]{1,0:T(8,128)(2,1)S(1)}, bf16[344,2048]{1,0:T(8,128)(2,1)S(1)}, u32[]{:S(2)}, u32[]{:S(2)}) collective-permute-start(bf16[344,2048]{1,0:T(8,128)(2,1)S(1)} %get-tuple-element.274.refs_3_), channel_id=1, source_target_pairs={{8,16},{16,8},{9,17},{17,9},{10,18},{18,10},{11,19},{19,11},{12,20... | collective-permute-start | bytes 4227080 | tf_op jit(solution)/shard_map/ppermute | solution.py:646
  298.3 8.4 %collective-permute-start.52 = (bf16[128,1024]{1,0:T(8,128)(2,1)S(1)}, bf16[128,1024]{1,0:T(8,128)(2,1)S(1)}, u32[]{:S(2)}, u32[]{:S(2)}) collective-permute-start(bf16[128,1024]{1,0:T(8,128)(2,1)S(1)} %get-tuple-element.443), channel_id=1, source_target_pairs={{0,4},{1,5},{2,6},{3,7},{4,0},{5,1},{6,2},{7,3},{8,12},{9,13},{10,... | collective-permute-start | bytes 786440 | tf_op jit(solution)/shard_map/ppermute | solution.py:397
  298.9 9.2 %collective-permute-start.54 = (bf16[128,1024]{1,0:T(8,128)(2,1)S(1)}, bf16[128,1024]{1,0:T(8,128)(2,1)S(1)}, u32[]{:S(2)}, u32[]{:S(2)}) collective-permute-start(bf16[128,1024]{1,0:T(8,128)(2,1)S(1)} %get-tuple-element.442), channel_id=1, source_target_pairs={{0,2},{1,3},{2,0},{3,1},{4,6},{5,7},{6,4},{7,5},{8,10},{9,11},{10,... | collective-permute-start | bytes 786440 | tf_op jit(solution)/shard_map/ppermute | solution.py:397
  299.5 14.2 %collective-permute-start.51 = (bf16[128,1024]{1,0:T(8,128)(2,1)S(1)}, bf16[128,1024]{1,0:T(8,128)(2,1)S(1)}, u32[]{:S(2)}, u32[]{:S(2)}) collective-permute-start(bf16[128,1024]{1,0:T(8,128)(2,1)S(1)} %get-tuple-element.444), channel_id=1, source_target_pairs={{0,2},{1,3},{2,0},{3,1},{4,6},{5,7},{6,4},{7,5},{8,10},{9,11},{10,... | collective-permute-start | bytes 786440 | tf_op jit(solution)/shard_map/ppermute | solution.py:397
  306.7 13.9 %collective-permute-start.56 = (bf16[128,1024]{1,0:T(8,128)(2,1)S(1)}, bf16[128,1024]{1,0:T(8,128)(2,1)S(1)}, u32[]{:S(2)}, u32[]{:S(2)}) collective-permute-start(bf16[128,1024]{1,0:T(8,128)(2,1)S(1)} %get-tuple-element.445), channel_id=1, source_target_pairs={{0,4},{1,5},{2,6},{3,7},{4,0},{5,1},{6,2},{7,3},{8,12},{9,13},{10,... | collective-permute-start | bytes 786440 | tf_op jit(solution)/shard_map/ppermute | solution.py:397
  308.3 12.4 %collective-permute-start.53 = (bf16[128,1024]{1,0:T(8,128)(2,1)S(1)}, bf16[128,1024]{1,0:T(8,128)(2,1)S(1)}, u32[]{:S(2)}, u32[]{:S(2)}) collective-permute-start(bf16[128,1024]{1,0:T(8,128)(2,1)S(1)} %get-tuple-element.441), channel_id=1, source_target_pairs={{0,2},{1,3},{2,0},{3,1},{4,6},{5,7},{6,4},{7,5},{8,10},{9,11},{10,... | collective-permute-start | bytes 786440 | tf_op jit(solution)/shard_map/ppermute | solution.py:397
  313.7 6.9 %collective-permute-start.55 = (bf16[128,1024]{1,0:T(8,128)(2,1)S(1)}, bf16[128,1024]{1,0:T(8,128)(2,1)S(1)}, u32[]{:S(2)}, u32[]{:S(2)}) collective-permute-start(bf16[128,1024]{1,0:T(8,128)(2,1)S(1)} %get-tuple-element.440), channel_id=1, source_target_pairs={{0,4},{1,5},{2,6},{3,7},{4,0},{5,1},{6,2},{7,3},{8,12},{9,13},{10,... | collective-permute-start | bytes 786440 | tf_op jit(solution)/shard_map/ppermute | solution.py:397
  335.9 35.0 %collective-permute-start.57 = (bf16[344,2048]{1,0:T(8,128)(2,1)}, bf16[344,2048]{1,0:T(8,128)(2,1)}, u32[]{:S(2)}, u32[]{:S(2)}) collective-permute-start(bf16[344,2048]{1,0:T(8,128)(2,1)} %get-tuple-element.286.refs_2_), channel_id=1, source_target_pairs={{0,8},{8,0},{16,24},{24,16},{1,9},{9,1},{17,25},{25,17},{2,10},{10... | collective-permute-start | bytes 4227080 | tf_op jit(solution)/shard_map/ppermute | solution.py:650
  339.6 31.2 %collective-permute-start.58 = (bf16[344,2048]{1,0:T(8,128)(2,1)}, bf16[344,2048]{1,0:T(8,128)(2,1)}, u32[]{:S(2)}, u32[]{:S(2)}) collective-permute-start(bf16[344,2048]{1,0:T(8,128)(2,1)} %get-tuple-element.287.refs_3_), channel_id=1, source_target_pairs={{8,16},{16,8},{9,17},{17,9},{10,18},{18,10},{11,19},{19,11},{12,20... | collective-permute-start | bytes 4227080 | tf_op jit(solution)/shard_map/ppermute | solution.py:646
  377.7 36.5 %collective-permute-start.62 = (bf16[344,2048]{1,0:T(8,128)(2,1)}, bf16[344,2048]{1,0:T(8,128)(2,1)S(1)}, u32[]{:S(2)}, u32[]{:S(2)}) collective-permute-start(bf16[344,2048]{1,0:T(8,128)(2,1)} %copy-done.80), channel_id=1, source_target_pairs={{0,8},{8,0},{16,24},{24,16},{1,9},{9,1},{17,25},{25,17},{2,10},{10... | collective-permute-start | bytes 4227080 | tf_op jit(solution)/shard_map/ppermute | solution.py:650
  381.5 32.7 %collective-permute-start.63 = (bf16[344,2048]{1,0:T(8,128)(2,1)}, bf16[344,2048]{1,0:T(8,128)(2,1)S(1)}, u32[]{:S(2)}, u32[]{:S(2)}) collective-permute-start(bf16[344,2048]{1,0:T(8,128)(2,1)} %copy-done.71), channel_id=1, source_target_pairs={{8,16},{16,8},{9,17},{17,9},{10,18},{18,10},{11,19},{19,11},{12,20... | collective-permute-start | bytes 4227080 | tf_op jit(solution)/shard_map/ppermute | solution.py:646
  415.6 35.5 %collective-permute-start.64 = (bf16[344,2048]{1,0:T(8,128)(2,1)S(1)}, bf16[344,2048]{1,0:T(8,128)(2,1)S(1)}, u32[]{:S(2)}, u32[]{:S(2)}) collective-permute-start(bf16[344,2048]{1,0:T(8,128)(2,1)S(1)} %get-tuple-element.320.refs_2_), channel_id=1, source_target_pairs={{0,8},{8,0},{16,24},{24,16},{1,9},{9,1},{17,25},{25,17},{2,10},{10... | collective-permute-start | bytes 4227080 | tf_op jit(solution)/shard_map/ppermute | solution.py:650
  418.2 34.0 %collective-permute-start.65 = (bf16[344,2048]{1,0:T(8,128)(2,1)S(1)}, bf16[344,2048]{1,0:T(8,128)(2,1)S(1)}, u32[]{:S(2)}, u32[]{:S(2)}) collective-permute-start(bf16[344,2048]{1,0:T(8,128)(2,1)S(1)} %get-tuple-element.321.refs_3_), channel_id=1, source_target_pairs={{8,16},{16,8},{9,17},{17,9},{10,18},{18,10},{11,19},{19,11},{12,20... | collective-permute-start | bytes 4227080 | tf_op jit(solution)/shard_map/ppermute | solution.py:646
  460.9 31.9 %collective-permute-start.66 = (bf16[344,2048]{1,0:T(8,128)(2,1)S(1)}, bf16[344,2048]{1,0:T(8,128)(2,1)S(1)}, u32[]{:S(2)}, u32[]{:S(2)}) collective-permute-start(bf16[344,2048]{1,0:T(8,128)(2,1)S(1)} %get-tuple-element.349.refs_3_), channel_id=1, source_target_pairs={{0,8},{8,0},{16,24},{24,16},{1,9},{9,1},{17,25},{25,17},{2,10},{10... | collective-permute-start | bytes 4227080 | tf_op jit(solution)/shard_map/ppermute | solution.py:650
  464.0 10.8 %collective-permute-start.67 = (bf16[256,2048]{1,0:T(8,128)(2,1)S(1)}, bf16[256,2048]{1,0:T(8,128)(2,1)S(1)}, u32[]{:S(2)}, u32[]{:S(2)}) collective-permute-start(bf16[256,2048]{1,0:T(8,128)(2,1)S(1)} %get-tuple-element.348.refs_3_), channel_id=1, source_target_pairs={{8,16},{16,8},{9,17},{17,9},{10,18},{18,10},{11,19},{19,11},{12,20... | collective-permute-start | bytes 3145736 | tf_op jit(solution)/shard_map/ppermute | solution.py:646
  495.3 8.1 %collective-permute-start.70 = (bf16[4,256,1024]{2,1,0:T(8,128)(2,1)S(1)}, bf16[4,256,1024]{2,1,0:T(8,128)(2,1)}, u32[]{:S(2)}, u32[]{:S(2)}) collective-permute-start(bf16[4,256,1024]{2,1,0:T(8,128)(2,1)S(1)} %get-tuple-element.372), channel_id=1, source_target_pairs={{0,1},{1,0},{2,3},{3,2},{4,5},{5,4},{6,7},{7,6},{8,9},{9,8},{10,11... | collective-permute-start | bytes 6291464 | tf_op jit(solution)/shard_map/ppermute | solution.py:397
  498.4 33.8 %collective-permute-start.68 = (bf16[256,2048]{1,0:T(8,128)(2,1)}, bf16[256,2048]{1,0:T(8,128)(2,1)}, u32[]{:S(2)}, u32[]{:S(2)}) collective-permute-start(bf16[256,2048]{1,0:T(8,128)(2,1)} %get-tuple-element.364.refs_1_), channel_id=1, source_target_pairs={{0,8},{8,0},{16,24},{24,16},{1,9},{9,1},{17,25},{25,17},{2,10},{10... | collective-permute-start | bytes 3145736 | tf_op jit(solution)/shard_map/ppermute | solution.py:650
  500.3 31.9 %collective-permute-start.69 = (bf16[256,2048]{1,0:T(8,128)(2,1)}, bf16[256,2048]{1,0:T(8,128)(2,1)}, u32[]{:S(2)}, u32[]{:S(2)}) collective-permute-start(bf16[256,2048]{1,0:T(8,128)(2,1)} %get-tuple-element.365.refs_3_), channel_id=1, source_target_pairs={{8,16},{16,8},{9,17},{17,9},{10,18},{18,10},{11,19},{19,11},{12,20... | collective-permute-start | bytes 3145736 | tf_op jit(solution)/shard_map/ppermute | solution.py:646
  507.7 7.9 %collective-permute-start.72 = (bf16[128,1024]{1,0:T(8,128)(2,1)}, bf16[128,1024]{1,0:T(8,128)(2,1)S(1)}, u32[]{:S(2)}, u32[]{:S(2)}) collective-permute-start(bf16[128,1024]{1,0:T(8,128)(2,1)} %get-tuple-element.437), channel_id=1, source_target_pairs={{0,4},{1,5},{2,6},{3,7},{4,0},{5,1},{6,2},{7,3},{8,12},{9,13},{10,... | collective-permute-start | bytes 786440 | tf_op jit(solution)/shard_map/ppermute | solution.py:397
  508.2 9.6 %collective-permute-start.74 = (bf16[128,1024]{1,0:T(8,128)(2,1)}, bf16[128,1024]{1,0:T(8,128)(2,1)}, u32[]{:S(2)}, u32[]{:S(2)}) collective-permute-start(bf16[128,1024]{1,0:T(8,128)(2,1)} %get-tuple-element.436), channel_id=1, source_target_pairs={{0,2},{1,3},{2,0},{3,1},{4,6},{5,7},{6,4},{7,5},{8,10},{9,11},{10,... | collective-permute-start | bytes 786440 | tf_op jit(solution)/shard_map/ppermute | solution.py:397
  508.6 14.6 %collective-permute-start.71 = (bf16[128,1024]{1,0:T(8,128)(2,1)S(1)}, bf16[128,1024]{1,0:T(8,128)(2,1)}, u32[]{:S(2)}, u32[]{:S(2)}) collective-permute-start(bf16[128,1024]{1,0:T(8,128)(2,1)S(1)} %get-tuple-element.438), channel_id=1, source_target_pairs={{0,2},{1,3},{2,0},{3,1},{4,6},{5,7},{6,4},{7,5},{8,10},{9,11},{10,... | collective-permute-start | bytes 786440 | tf_op jit(solution)/shard_map/ppermute | solution.py:397
  517.8 10.6 %collective-permute-start.76 = (bf16[128,1024]{1,0:T(8,128)(2,1)S(1)}, bf16[128,1024]{1,0:T(8,128)(2,1)S(1)}, u32[]{:S(2)}, u32[]{:S(2)}) collective-permute-start(bf16[128,1024]{1,0:T(8,128)(2,1)S(1)} %get-tuple-element.439), channel_id=1, source_target_pairs={{0,4},{1,5},{2,6},{3,7},{4,0},{5,1},{6,2},{7,3},{8,12},{9,13},{10,... | collective-permute-start | bytes 786440 | tf_op jit(solution)/shard_map/ppermute | solution.py:397
  520.5 7.9 %collective-permute-start.73 = (bf16[128,1024]{1,0:T(8,128)(2,1)S(1)}, bf16[128,1024]{1,0:T(8,128)(2,1)S(1)}, u32[]{:S(2)}, u32[]{:S(2)}) collective-permute-start(bf16[128,1024]{1,0:T(8,128)(2,1)S(1)} %get-tuple-element.435), channel_id=1, source_target_pairs={{0,2},{1,3},{2,0},{3,1},{4,6},{5,7},{6,4},{7,5},{8,10},{9,11},{10,... | collective-permute-start | bytes 786440 | tf_op jit(solution)/shard_map/ppermute | solution.py:397
  536.4 22.9 %collective-permute-start.80 = (bf16[256,2048]{1,0:T(8,128)(2,1)}, bf16[256,2048]{1,0:T(8,128)(2,1)S(1)}, u32[]{:S(2)}, u32[]{:S(2)}) collective-permute-start(bf16[256,2048]{1,0:T(8,128)(2,1)} %get-tuple-element.381.refs_1_), channel_id=1, source_target_pairs={{0,8},{8,0},{16,24},{24,16},{1,9},{9,1},{17,25},{25,17},{2,10},{10... | collective-permute-start | bytes 3145736 | tf_op jit(solution)/shard_map/ppermute | solution.py:650
  538.6 21.9 %collective-permute-start.81 = (bf16[256,2048]{1,0:T(8,128)(2,1)}, bf16[256,2048]{1,0:T(8,128)(2,1)}, u32[]{:S(2)}, u32[]{:S(2)}) collective-permute-start(bf16[256,2048]{1,0:T(8,128)(2,1)} %get-tuple-element.380.refs_3_), channel_id=1, source_target_pairs={{8,16},{16,8},{9,17},{17,9},{10,18},{18,10},{11,19},{19,11},{12,20... | collective-permute-start | bytes 3145736 | tf_op jit(solution)/shard_map/ppermute | solution.py:646
  564.5 23.9 %collective-permute-start.82 = (bf16[272,2048]{1,0:T(8,128)(2,1)S(1)}, bf16[272,2048]{1,0:T(8,128)(2,1)S(1)}, u32[]{:S(2)}, u32[]{:S(2)}) collective-permute-start(bf16[272,2048]{1,0:T(8,128)(2,1)S(1)} %get-tuple-element.398.refs_1_), channel_id=1, source_target_pairs={{0,8},{8,0},{16,24},{24,16},{1,9},{9,1},{17,25},{25,17},{2,10},{10... | collective-permute-start | bytes 3342344 | tf_op jit(solution)/shard_map/ppermute | solution.py:650
  567.3 20.7 %collective-permute-start.83 = (bf16[256,2048]{1,0:T(8,128)(2,1)S(1)}, bf16[256,2048]{1,0:T(8,128)(2,1)S(1)}, u32[]{:S(2)}, u32[]{:S(2)}) collective-permute-start(bf16[256,2048]{1,0:T(8,128)(2,1)S(1)} %get-tuple-element.399.refs_2_), channel_id=1, source_target_pairs={{8,16},{16,8},{9,17},{17,9},{10,18},{18,10},{11,19},{19,11},{12,20... | collective-permute-start | bytes 3145736 | tf_op jit(solution)/shard_map/ppermute | solution.py:646
  589.4 25.6 %collective-permute-start.85 = (bf16[272,2048]{1,0:T(8,128)(2,1)S(1)}, bf16[272,2048]{1,0:T(8,128)(2,1)S(1)}, u32[]{:S(2)}, u32[]{:S(2)}) collective-permute-start(bf16[272,2048]{1,0:T(8,128)(2,1)S(1)} %get-tuple-element.402.refs_0_), channel_id=1, source_target_pairs={{8,16},{16,8},{9,17},{17,9},{10,18},{18,10},{11,19},{19,11},{12,20... | collective-permute-start | bytes 3342344 | tf_op jit(solution)/shard_map/ppermute | solution.py:646
  590.2 24.9 %collective-permute-start.84 = (bf16[256,2048]{1,0:T(8,128)(2,1)S(1)}, bf16[256,2048]{1,0:T(8,128)(2,1)S(1)}, u32[]{:S(2)}, u32[]{:S(2)}) collective-permute-start(bf16[256,2048]{1,0:T(8,128)(2,1)S(1)} %get-tuple-element.403.refs_1_), channel_id=1, source_target_pairs={{0,8},{8,0},{16,24},{24,16},{1,9},{9,1},{17,25},{25,17},{2,10},{10... | collective-permute-start | bytes 3145736 | tf_op jit(solution)/shard_map/ppermute | solution.py:650
  615.6 21.8 %collective-permute-start.86 = (bf16[272,2048]{1,0:T(8,128)(2,1)S(1)}, bf16[272,2048]{1,0:T(8,128)(2,1)S(1)}, u32[]{:S(2)}, u32[]{:S(2)}) collective-permute-start(bf16[272,2048]{1,0:T(8,128)(2,1)S(1)} %turn.23.refs_1_), channel_id=1, source_target_pairs={{0,8},{8,0},{16,24},{24,16},{1,9},{9,1},{17,25},{25,17},{2,10},{10... | collective-permute-start | bytes 3342344 | tf_op jit(solution)/shard_map/ppermute | solution.py:650
  (183 other events, 1650.8 us)
Sparse Core Ops, SparseCore 0:
  43.0 38.1 all-gather.1
  377.8 52.5 reduce-scatter.1
